TPU v7x, 32 devices: a whole 2x2x4 slice. The times are simulated.
32 devices in a mesh: dp: 8 (over y, x, core), mp: 4 (over z).
Axes of the slice: x: 2, y: 2, z: 4, core: 2. Of those that a mesh axis runs over, the one named last changes fastest.
Arguments:
- target_ids: int32 [16, 1024], P('dp', 'mp'), may hold values from 0 to 131071
- tgt_lengths: int32 [16], P('dp'), may hold values from 1 to 1024, 12288 in all
- encoder_states: bfloat16 [16, 1024, 1024], P('dp', 'mp'), may hold values from -6 to 6
- src_lengths: int32 [16], P('dp'), may hold values from 1 to 1024, 12288 in all
- table: bfloat16 [1024, 131072], P(('dp', 'mp')), may hold values from -0.1875 to 0.1875
- pos_table: bfloat16 [1024, 1024], P('dp', 'mp'), may hold values from -3 to 3
- self_query_key_value_weight: bfloat16 [1024, 3, 1024], P('dp', None, 'mp'), may hold values from -0.1875 to 0.1875
- self_output_weight: bfloat16 [1024, 1024], P('dp', 'mp'), may hold values from -0.75 to 0.75
- cross_query_weight: bfloat16 [1024, 1024], P('dp', 'mp'), may hold values from -0.1875 to 0.1875
- cross_key_value_weight: bfloat16 [1024, 2, 1024], P('dp', None, 'mp'), may hold values from -0.1875 to 0.1875
- cross_output_weight: bfloat16 [1024, 1024], P('dp', 'mp'), may hold values from -0.75 to 0.75
- feedforward_input_weight: bfloat16 [1024, 4096], P('dp', 'mp'), may hold values from -0.1875 to 0.1875
- feedforward_output_weight: bfloat16 [1024, 4096], P('dp', 'mp'), may hold values from -0.09375 to 0.09375
- norm_gains: float32 [5, 1024], replicated, may hold values from 0.5 to 1.5
- norm_biases: float32 [5, 1024], replicated, may hold values from -1.25 to 1.25
- out_grad: float32 [16, 1024, 1024], P('dp', 'mp'), may hold values from -6 to 6
Outputs:
- hidden_out: float32 [16, 1024, 1024], P('dp', 'mp')
- table_grad: float32 [1024, 131072], P(('dp', 'mp'))
- pos_grad: float32 [1024, 1024], P('dp', 'mp')
- self_qkv_grad: float32 [1024, 3, 1024], P('dp', None, 'mp')
- self_out_grad: float32 [1024, 1024], P('dp', 'mp')
- cross_q_grad: float32 [1024, 1024], P('dp', 'mp')
- cross_kv_grad: float32 [1024, 2, 1024], P('dp', None, 'mp')
- cross_out_grad: float32 [1024, 1024], P('dp', 'mp')
- ffn_in_grad: float32 [1024, 4096], P('dp', 'mp')
- ffn_out_grad: float32 [1024, 4096], P('dp', 'mp')
- gains_grad: float32 [5, 1024], replicated
- biases_grad: float32 [5, 1024], replicated
- encoder_grad: float32 [16, 1024, 1024], P('dp', 'mp')
Inputs may be any that keep to these rules, and one draw needn't show every extreme that they name: `tgt_lengths`: some target sequence has all 1024 tokens. `src_lengths`: some source sequence has all 1024 tokens.
All inputs are finite; a program needn't handle non-finite values. No bound on the sum of `tgt_lengths` or of `src_lengths` on one device may be relied on, other than what follows from the above.
Results may differ from a plain program's by a relative error of at most 0.02.
Values may be sent and summed in bfloat16 or wider, within the bound.
No kernel may reach another device: no remote copies, remote signals or barrier semaphores. Data moves between devices by JAX's collectives and lax.ppermute only.
A program may use at most 256 MiB of HBM per device.

v0:
```python
import jax
import jax.numpy as jnp
from jax import lax
from jax.sharding import PartitionSpec as P

D = 1024
HEAD_DIM = 64


EPSILON = 1e-05
NEGATIVE = -1e30


def layer_norm(values, gains, shifts):
    average = jnp.mean(values, axis=-1, keepdims=True)
    centred = values - average
    variance = jnp.mean(centred * centred, axis=-1, keepdims=True)
    return centred * lax.rsqrt(variance + EPSILON) * gains + shifts


def norm_back(values, gains, shifts, grad_out):
    unused, pullback = jax.vjp(layer_norm, values, gains, shifts)
    return pullback(grad_out)


def gelu_exact(values):
    return jax.nn.gelu(values, approximate=False)


def split_heads(values):
    return values.reshape(values.shape[:2] + (values.shape[2] // HEAD_DIM, HEAD_DIM))


def merge_heads(values):
    return values.reshape(values.shape[:2] + (values.shape[2] * values.shape[3],))


def split_blocks(values, block_rows):
    shaped = values.reshape(
        (values.shape[0], values.shape[1] // block_rows, block_rows) + values.shape[2:]
    )
    return jnp.moveaxis(shaped, 1, 0)


def join_blocks(values):
    moved = jnp.moveaxis(values, 0, 1)
    return moved.reshape((moved.shape[0], moved.shape[1] * moved.shape[2]) + moved.shape[3:])


def block_scores(query_block, keys, lengths, start, causal, scale):
    scores = (
        jnp.einsum("sqhd,skhd->shqk", query_block, keys, preferred_element_type=jnp.float32) * scale
    )
    key_pos = jnp.arange(keys.shape[1], dtype=jnp.int32)
    allowed = key_pos[None, None, None, :] < lengths[:, None, None, None]
    if causal:
        query_pos = start + jnp.arange(query_block.shape[1], dtype=jnp.int32)
        allowed = allowed & (key_pos[None, None, None, :] <= query_pos[None, None, :, None])
    return jnp.where(allowed, scores, NEGATIVE)


def attend(queries, keys, values, lengths, causal):
    block_rows = min(512, queries.shape[1])
    scale = queries.shape[3] ** (-0.5)
    starts = jnp.arange(queries.shape[1] // block_rows, dtype=jnp.int32) * block_rows

    def one_block(inputs):
        query_block, start = inputs
        scores = block_scores(query_block, keys, lengths, start, causal, scale)
        top_score = jnp.max(scores, axis=-1, keepdims=True)
        raw_weights = jnp.exp(scores - top_score)
        totals = jnp.sum(raw_weights, axis=-1, keepdims=True)
        probs = raw_weights / totals
        log_total = top_score[..., 0] + jnp.log(totals[..., 0])
        mixed = jnp.einsum(
            "shqk,skhd->sqhd",
            probs.astype(jnp.bfloat16),
            values,
            preferred_element_type=jnp.float32,
        ).astype(jnp.bfloat16)
        return (mixed, log_total)

    mixed, log_totals = lax.map(one_block, (split_blocks(queries, block_rows), starts))
    return (join_blocks(mixed), log_totals)


def attend_back(queries, keys, values, lengths, causal, log_totals, grad_mixed):
    block_rows = min(512, queries.shape[1])
    scale = queries.shape[3] ** (-0.5)
    starts = jnp.arange(queries.shape[1] // block_rows, dtype=jnp.int32) * block_rows

    def one_block(carry, inputs):
        grad_keys, grad_values = carry
        query_block, grad_block, log_block, start = inputs
        scores = block_scores(query_block, keys, lengths, start, causal, scale)
        probs = jnp.exp(scores - log_block[..., None])
        grad_values = grad_values + jnp.einsum(
            "shqk,sqhd->skhd",
            probs.astype(jnp.bfloat16),
            grad_block,
            preferred_element_type=jnp.float32,
        )
        grad_probs = jnp.einsum(
            "sqhd,skhd->shqk", grad_block, values, preferred_element_type=jnp.float32
        )
        inner = jnp.sum(grad_probs * probs, axis=-1, keepdims=True)
        grad_scores = (probs * (grad_probs - inner)).astype(jnp.bfloat16)
        query_row_gradient = (
            jnp.einsum("shqk,skhd->sqhd", grad_scores, keys, preferred_element_type=jnp.float32)
            * scale
        )
        grad_keys = (
            grad_keys
            + jnp.einsum(
                "shqk,sqhd->skhd", grad_scores, query_block, preferred_element_type=jnp.float32
            )
            * scale
        )
        return ((grad_keys, grad_values), query_row_gradient)

    zero_keys = jnp.zeros(keys.shape, jnp.float32)
    carried, grad_queries = lax.scan(
        one_block,
        (zero_keys, zero_keys),
        (
            split_blocks(queries, block_rows),
            split_blocks(grad_mixed, block_rows),
            log_totals,
            starts,
        ),
    )
    return (join_blocks(grad_queries), carried[0], carried[1])


def spread(values):
    return lax.all_gather(values, "mp", axis=1, tiled=True)


def collect(partial_sums):
    return lax.psum_scatter(partial_sums, "mp", scatter_dimension=1, tiled=True)


def spread_grad(grads):
    return lax.all_gather(grads.astype(jnp.bfloat16), "mp", axis=1, tiled=True)


def body(
    target_ids,
    tgt_lengths,
    encoder_states,
    src_lengths,
    table,
    pos_table,
    self_query_key_value_weight,
    self_output_weight,
    cross_query_weight,
    cross_key_value_weight,
    cross_output_weight,
    feedforward_input_weight,
    feedforward_output_weight,
    norm_gains,
    norm_biases,
    out_grad,
):
    seq_count, local_len = target_ids.shape
    single_float = jnp.float32
    bf16 = jnp.bfloat16
    all_ids = lax.all_gather(target_ids.reshape(-1), ("dp", "mp"), axis=0, tiled=True)
    picked = jnp.take(table, all_ids, axis=1)
    embedded = lax.all_to_all(picked, ("dp", "mp"), split_axis=1, concat_axis=0, tiled=True)
    embedded = embedded.astype(single_float).T.reshape(seq_count, local_len, D) * 32.0
    fetched = (
        lax.all_gather(pos_table, "dp", axis=0, tiled=True),
        lax.all_gather(self_query_key_value_weight, "dp", axis=0, tiled=True),
        lax.all_gather(self_output_weight, "dp", axis=0, tiled=True),
        lax.all_gather(cross_query_weight, "dp", axis=0, tiled=True),
        lax.all_gather(cross_key_value_weight, "dp", axis=0, tiled=True),
        lax.all_gather(cross_output_weight, "dp", axis=0, tiled=True),
        lax.all_gather(feedforward_input_weight, "dp", axis=0, tiled=True),
        lax.all_gather(feedforward_output_weight, "dp", axis=0, tiled=True),
    )
    (
        positions,
        query_key_value_matrix,
        self_output_matrix,
        cross_query_matrix,
        cross_key_value_matrix,
        cross_output_matrix,
        feedforward_input_matrix,
        feedforward_output_matrix,
    ) = fetched
    state_zero = embedded + positions.astype(single_float).T[None]
    hidden_state_one = layer_norm(state_zero, norm_gains[0], norm_biases[0])
    self_normalized = spread(
        layer_norm(hidden_state_one, norm_gains[1], norm_biases[1]).astype(bf16)
    )
    projected_rows = jnp.einsum(
        "uvb,bqn->uvqn",
        self_normalized,
        query_key_value_matrix,
        preferred_element_type=single_float,
    ).astype(bf16)
    self_queries = split_heads(projected_rows[:, :, 0])
    self_keys = split_heads(projected_rows[:, :, 1])
    self_values = split_heads(projected_rows[:, :, 2])
    self_attended, self_logs = attend(self_queries, self_keys, self_values, tgt_lengths, True)
    self_flattened = merge_heads(self_attended)
    hidden_state_two = hidden_state_one + collect(
        jnp.einsum(
            "zvr,nr->zvn", self_flattened, self_output_matrix, preferred_element_type=single_float
        )
    )
    cross_normalized = spread(
        layer_norm(hidden_state_two, norm_gains[2], norm_biases[2]).astype(bf16)
    )
    source_row_states = spread(encoder_states)
    cross_query_rows = jnp.einsum(
        "hzc,cv->hzv", cross_normalized, cross_query_matrix, preferred_element_type=single_float
    ).astype(bf16)
    source_key_value = jnp.einsum(
        "uvb,bqn->uvqn",
        source_row_states,
        cross_key_value_matrix,
        preferred_element_type=single_float,
    ).astype(bf16)
    cross_queries = split_heads(cross_query_rows)
    cross_keys = split_heads(source_key_value[:, :, 0])
    cross_values = split_heads(source_key_value[:, :, 1])
    cross_attended, cross_logs = attend(cross_queries, cross_keys, cross_values, src_lengths, False)
    cross_flattened = merge_heads(cross_attended)
    hidden_state_three = hidden_state_two + collect(
        jnp.einsum(
            "zvr,nr->zvn", cross_flattened, cross_output_matrix, preferred_element_type=single_float
        )
    )
    feedforward_normalized = layer_norm(hidden_state_three, norm_gains[3], norm_biases[3]).astype(
        bf16
    )
    feedforward_rows = spread(feedforward_normalized)
    preactivation = jnp.einsum(
        "rqo,og->rqg",
        feedforward_rows,
        feedforward_input_matrix,
        preferred_element_type=single_float,
    )
    activation_rows = gelu_exact(preactivation).astype(bf16)
    hidden_state_four = hidden_state_three + collect(
        jnp.einsum(
            "hbc,nc->hbn",
            activation_rows,
            feedforward_output_matrix,
            preferred_element_type=single_float,
        )
    )
    hidden_out = layer_norm(hidden_state_four, norm_gains[4], norm_biases[4])
    refetched = (
        lax.all_gather(self_query_key_value_weight, "dp", axis=0, tiled=True),
        lax.all_gather(self_output_weight, "dp", axis=0, tiled=True),
        lax.all_gather(cross_query_weight, "dp", axis=0, tiled=True),
        lax.all_gather(cross_key_value_weight, "dp", axis=0, tiled=True),
        lax.all_gather(cross_output_weight, "dp", axis=0, tiled=True),
        lax.all_gather(feedforward_input_weight, "dp", axis=0, tiled=True),
        lax.all_gather(feedforward_output_weight, "dp", axis=0, tiled=True),
    )
    (
        reverse_query_key_value,
        reverse_self_output,
        reverse_cross_query,
        reverse_cross_key_value,
        reverse_cross_output,
        reverse_feedforward_input,
        reverse_feedforward_output,
    ) = refetched
    grad_four, gain_four, shift_four = norm_back(
        hidden_state_four, norm_gains[4], norm_biases[4], out_grad
    )
    unused, gelu_pull = jax.vjp(gelu_exact, preactivation)
    gradient_rows = spread_grad(grad_four)
    activation_gradient = jnp.einsum(
        "rqo,og->rqg",
        gradient_rows,
        reverse_feedforward_output,
        preferred_element_type=single_float,
    )
    feedforward_output_gradient = jnp.einsum(
        "xku,xko->uo", gradient_rows, activation_rows, preferred_element_type=single_float
    )
    preactivation_gradient = gelu_pull(activation_gradient)[0].astype(bf16)
    feedforward_input_gradient = jnp.einsum(
        "xku,xko->uo", feedforward_rows, preactivation_gradient, preferred_element_type=single_float
    )
    grad_normed = collect(
        jnp.einsum(
            "hbc,nc->hbn",
            preactivation_gradient,
            reverse_feedforward_input,
            preferred_element_type=single_float,
        )
    )
    grad_part, gain_three, shift_three = norm_back(
        hidden_state_three, norm_gains[3], norm_biases[3], grad_normed
    )
    grad_three = grad_four + grad_part
    gradient_rows = spread_grad(grad_three)
    grad_mixed = jnp.einsum(
        "hzc,cv->hzv", gradient_rows, reverse_cross_output, preferred_element_type=single_float
    ).astype(bf16)
    cross_output_gradient = jnp.einsum(
        "cvh,cvz->hz", gradient_rows, cross_flattened, preferred_element_type=single_float
    )
    grad_q, grad_k, grad_v = attend_back(
        cross_queries,
        cross_keys,
        cross_values,
        src_lengths,
        False,
        cross_logs,
        split_heads(grad_mixed),
    )
    query_row_gradient = merge_heads(grad_q).astype(bf16)
    key_value_gradient = jnp.stack([merge_heads(grad_k), merge_heads(grad_v)], axis=2).astype(bf16)
    cross_query_gradient = jnp.einsum(
        "cvh,cvz->hz", cross_normalized, query_row_gradient, preferred_element_type=single_float
    )
    cross_key_value_gradient = jnp.einsum(
        "yxa,yxkq->akq", source_row_states, key_value_gradient, preferred_element_type=single_float
    )
    grad_normed = collect(
        jnp.einsum(
            "zvr,nr->zvn",
            query_row_gradient,
            reverse_cross_query,
            preferred_element_type=single_float,
        )
    )
    encoder_grad = collect(
        jnp.einsum(
            "guwi,bwi->gub",
            key_value_gradient,
            reverse_cross_key_value,
            preferred_element_type=single_float,
        )
    )
    grad_part, gain_two, shift_two = norm_back(
        hidden_state_two, norm_gains[2], norm_biases[2], grad_normed
    )
    grad_two = grad_three + grad_part
    gradient_rows = spread_grad(grad_two)
    grad_mixed = jnp.einsum(
        "hzc,cv->hzv", gradient_rows, reverse_self_output, preferred_element_type=single_float
    ).astype(bf16)
    self_output_gradient = jnp.einsum(
        "cvh,cvz->hz", gradient_rows, self_flattened, preferred_element_type=single_float
    )
    grad_q, grad_k, grad_v = attend_back(
        self_queries, self_keys, self_values, tgt_lengths, True, self_logs, split_heads(grad_mixed)
    )
    projected_gradient = jnp.stack(
        [merge_heads(grad_q), merge_heads(grad_k), merge_heads(grad_v)], axis=2
    ).astype(bf16)
    query_key_value_gradient = jnp.einsum(
        "yxa,yxkq->akq", self_normalized, projected_gradient, preferred_element_type=single_float
    )
    grad_normed = collect(
        jnp.einsum(
            "guwi,bwi->gub",
            projected_gradient,
            reverse_query_key_value,
            preferred_element_type=single_float,
        )
    )
    grad_part, gain_one, shift_one = norm_back(
        hidden_state_one, norm_gains[1], norm_biases[1], grad_normed
    )
    grad_one = grad_two + grad_part
    grad_zero, gain_zero, shift_zero = norm_back(
        state_zero, norm_gains[0], norm_biases[0], grad_one
    )
    token_grads = (grad_zero * 32.0).reshape(seq_count * local_len, D).T
    arrived = lax.all_to_all(
        token_grads.astype(jnp.bfloat16), ("dp", "mp"), split_axis=0, concat_axis=1, tiled=True
    ).astype(token_grads.dtype)
    table_grad = (
        jnp.zeros((table.shape[0], table.shape[1]), single_float).at[:, all_ids].add(arrived)
    )
    grad_pos = jnp.sum(grad_zero, axis=0).T
    summed = (
        lax.psum_scatter(
            grad_pos.astype(jnp.bfloat16), "dp", scatter_dimension=0, tiled=True
        ).astype(jnp.float32),
        lax.psum_scatter(
            query_key_value_gradient.astype(jnp.bfloat16), "dp", scatter_dimension=0, tiled=True
        ).astype(jnp.float32),
        lax.psum_scatter(
            self_output_gradient.astype(jnp.bfloat16), "dp", scatter_dimension=0, tiled=True
        ).astype(jnp.float32),
        lax.psum_scatter(
            cross_query_gradient.astype(jnp.bfloat16), "dp", scatter_dimension=0, tiled=True
        ).astype(jnp.float32),
        lax.psum_scatter(
            cross_key_value_gradient.astype(jnp.bfloat16), "dp", scatter_dimension=0, tiled=True
        ).astype(jnp.float32),
        lax.psum_scatter(
            cross_output_gradient.astype(jnp.bfloat16), "dp", scatter_dimension=0, tiled=True
        ).astype(jnp.float32),
        lax.psum_scatter(
            feedforward_input_gradient.astype(jnp.bfloat16), "dp", scatter_dimension=0, tiled=True
        ).astype(jnp.float32),
        lax.psum_scatter(
            feedforward_output_gradient.astype(jnp.bfloat16), "dp", scatter_dimension=0, tiled=True
        ).astype(jnp.float32),
    )
    gain_grads = jnp.stack([gain_zero, gain_one, gain_two, gain_three, gain_four])
    shift_grads = jnp.stack([shift_zero, shift_one, shift_two, shift_three, shift_four])
    gains_grad, biases_grad = lax.psum((gain_grads, shift_grads), ("dp", "mp"))
    return (
        hidden_out,
        table_grad,
        summed[0],
        summed[1],
        summed[2],
        summed[3],
        summed[4],
        summed[5],
        summed[6],
        summed[7],
        gains_grad,
        biases_grad,
        encoder_grad,
    )


def solution(mesh):
    placed = (
        P("dp", "mp"),
        P("dp"),
        P("dp", "mp", None),
        P("dp"),
        P(("dp", "mp"), None),
        P("dp", "mp"),
        P("dp", None, "mp"),
        P("dp", "mp"),
        P("dp", "mp"),
        P("dp", None, "mp"),
        P("dp", "mp"),
        P("dp", "mp"),
        P("dp", "mp"),
        P(),
        P(),
        P("dp", "mp", None),
    )
    return jax.shard_map(
        body,
        mesh=mesh,
        in_specs=placed,
        out_specs=(
            P("dp", "mp", None),
            P(("dp", "mp"), None),
            P("dp", "mp"),
            P("dp", None, "mp"),
            P("dp", "mp"),
            P("dp", "mp"),
            P("dp", None, "mp"),
            P("dp", "mp"),
            P("dp", "mp"),
            P("dp", "mp"),
            P(),
            P(),
            P("dp", "mp", None),
        ),
        check_vma=False,
    )
```

profile of v0, /device:TPU:0, one launch (start us, length us, event | category | flops | bytes accessed | tf_op | source)
XLA Modules:
  0.0 2915.1 jit_solution(9910737201195608067)
XLA Ops:
  7.9 70.1 %all-gather = s32[32,1,512]{2,1,0:T(1,128)S(1)} all-gather(s32[1,1,512]{2,1,0:T(1,128)S(1)} %reshape.486), channel_id=1, replica_groups=mesh['dp'=8,'mp'=4] {'dp','mp'}, dimensions={0}, use_global_device_ids=true | all-gather | bytes 67584 | tf_op jit(solution)/shard_map/all_gather | solution.py:168
  78.7 25.2 copy.182
  103.9 247.6 %gather_fusion = bf16[16384,32]{1,0:T(8,128)(2,1)} fusion(bf16[32,131072]{0,1:T(8,128)(2,1)} %copy.182, s32[16384]{0:T(1024)S(1)} %get-tuple-element.592), kind=kCustom, calls=%fused_computation | custom fusion | bytes 2162688 | tf_op jit(solution)/shard_map/jit(_take)/gather | solution.py:169
  406.2 69.4 %all-gather.13.cloned.1.call-done = bf16[2,1024,1024]{2,1,0:T(8,128)(2,1)} async-done(((bf16[2,256,1024]{2,1,0:T(8,128)(2,1)}), bf16[2,1024,1024]{2,1,0:T(8,128)(2,1)}) %all-gather.13.cloned.1.call-update) | async-done | bytes 4194320 | tf_op jit(solution)/shard_map/all_gather | solution.py:136
  486.7 33.8 %while.54 = (s32[]{:T(128)}, bf16[2,2,512,4,64]{2,4,3,1,0:T(8,128)(2,1)}, f32[2,2,4,512]{3,2,1,0:T(4,128)S(1)}, s32[2]{0:T(128)S(1)}, s32[2]{0:T(128)S(1)}, /*in...) while((s32[]{:T(128)}, ...), condition=%wide.region_7.8_spmd, body=%wide.region_4.0_spmd.sunk | while | flops 1125906944 | bytes 67248320 | solution.py:83
  535.7 140.9 %reduce-scatter.20.cloned.1.call-done = f32[2,256,1024]{2,1,0:T(8,128)} async-done(((f32[2,1024,1024]{2,1,0:T(8,128)}), f32[2,256,1024]{2,1,0:T(8,128)}) %reduce-scatter.20.cloned.1.call-update) | async-done | bytes 2097168 | tf_op jit(solution)/shard_map/reduce_scatter | solution.py:140
  687.6 20.4 all_gather.61
  718.8 66.7 %all-gather.19.cloned.1.call-done = bf16[2,1024,1024]{2,1,0:T(8,128)(2,1)} async-done(((bf16[2,256,1024]{2,1,0:T(8,128)(2,1)}), bf16[2,1024,1024]{2,1,0:T(8,128)(2,1)}) %all-gather.19.cloned.1.call-update) | async-done | bytes 4194320 | tf_op jit(solution)/shard_map/all_gather | solution.py:136
  790.5 76.3 %all-gather.17.cloned.1.call-done = bf16[2,1024,1024]{2,1,0:T(8,128)(2,1)} async-done(((bf16[2,256,1024]{2,1,0:T(8,128)(2,1)}), bf16[2,1024,1024]{2,1,0:T(8,128)(2,1)}) %all-gather.17.cloned.1.call-update) | async-done | bytes 4194320 | tf_op jit(solution)/shard_map/all_gather | solution.py:136
  876.8 24.6 while.55
  914.9 142.3 %reduce-scatter.22.cloned.1.call-done = f32[2,256,1024]{2,1,0:T(8,128)} async-done(((f32[2,1024,1024]{2,1,0:T(8,128)}), f32[2,256,1024]{2,1,0:T(8,128)}) %reduce-scatter.22.cloned.1.call-update) | async-done | bytes 2097168 | tf_op jit(solution)/shard_map/reduce_scatter | solution.py:140
  1062.2 25.6 all-gather.25.cloned.1.call-done
  1087.8 82.9 %all-gather.23.cloned.1.call-done = bf16[2,1024,1024]{2,1,0:T(8,128)(2,1)} async-done(((bf16[2,256,1024]{2,1,0:T(8,128)(2,1)}), bf16[2,1024,1024]{2,1,0:T(8,128)(2,1)}) %all-gather.23.cloned.1.call-update) | async-done | bytes 4194320 | tf_op jit(solution)/shard_map/all_gather | solution.py:136
  1215.5 142.9 %reduce-scatter.24.cloned.1.call-done = f32[2,256,1024]{2,1,0:T(8,128)} async-done(((f32[2,1024,1024]{2,1,0:T(8,128)}), f32[2,256,1024]{2,1,0:T(8,128)}) %reduce-scatter.24.cloned.1.call-update) | async-done | bytes 2097168 | tf_op jit(solution)/shard_map/reduce_scatter | solution.py:140
  1366.9 81.6 %all-gather.29.cloned.1.call-done = bf16[2,1024,1024]{2,1,0:T(8,128)(2,1)} async-done(((bf16[2,256,1024]{2,1,0:T(8,128)(2,1)}), bf16[2,1024,1024]{2,1,0:T(8,128)(2,1)}) %all-gather.29.cloned.1.call-update) | async-done | bytes 4194320 | tf_op jit(solution)/shard_map/all_gather | solution.py:144
  1469.2 143.1 %reduce-scatter.26.cloned.1.call-done = f32[2,256,1024]{2,1,0:T(8,128)} async-done(((f32[2,1024,1024]{2,1,0:T(8,128)}), f32[2,256,1024]{2,1,0:T(8,128)}) %reduce-scatter.26.cloned.1.call-update) | async-done | bytes 2097168 | tf_op jit(solution)/shard_map/reduce_scatter | solution.py:140
  1619.3 81.6 %all-gather.31.cloned.1.call-done = bf16[2,1024,1024]{2,1,0:T(8,128)(2,1)} async-done(((bf16[2,256,1024]{2,1,0:T(8,128)(2,1)}), bf16[2,1024,1024]{2,1,0:T(8,128)(2,1)}) %all-gather.31.cloned.1.call-update) | async-done | bytes 4194320 | tf_op jit(solution)/shard_map/all_gather | solution.py:144
  1708.5 85.2 %while.56 = (s32[]{:T(128)}, f32[2,1024,4,64]{1,3,2,0:T(8,128)}, f32[2,1024,4,64]{1,3,2,0:T(8,128)}, bf16[2,2,512,4,64]{2,4,3,1,0:T(8,128)(2,1)}, bf16[2,2,512,4...) while((s32[]{:T(128)}, f32[2,1024,4,64]{1,3,2,0:T(8,128)}, ...), condition=%wide.region_28.29_spmd.clone, body=%wide.region_26.28_spmd.clone.sunk | while | flops 2750150656 | bytes 195488112 | solution.py:122
  1801.7 143.1 %reduce-scatter.28.cloned.1.call-done = f32[2,256,1024]{2,1,0:T(8,128)} async-done(((f32[2,1024,1024]{2,1,0:T(8,128)}), f32[2,256,1024]{2,1,0:T(8,128)}) %reduce-scatter.28.cloned.1.call-update) | async-done | bytes 2097168 | tf_op jit(solution)/shard_map/reduce_scatter | solution.py:140
  1951.3 81.6 %all-gather.33.cloned.1.call-done = bf16[2,1024,1024]{2,1,0:T(8,128)(2,1)} async-done(((bf16[2,256,1024]{2,1,0:T(8,128)(2,1)}), bf16[2,1024,1024]{2,1,0:T(8,128)(2,1)}) %all-gather.33.cloned.1.call-update) | async-done | bytes 4194320 | tf_op jit(solution)/shard_map/all_gather | solution.py:144
  2045.9 93.4 %while.57 = (s32[]{:T(128)}, f32[2,1024,4,64]{1,3,2,0:T(8,128)S(1)}, f32[2,1024,4,64]{1,3,2,0:T(8,128)}, bf16[2,2,512,4,64]{2,4,3,1,0:T(8,128)(2,1)}, bf16[2,2,5...) while((s32[]{:T(128)}, ...), condition=%wide.region_34.35_spmd.clone, body=%wide.region_32.34_spmd.clone.sunk | while | flops 2751724032 | bytes 250732976 | solution.py:122
  2207.7 95.3 %reduce-scatter.30.cloned.1.call-done = f32[2,256,1024]{2,1,0:T(8,128)} async-done(((f32[2,1024,1024]{2,1,0:T(8,128)}), f32[2,256,1024]{2,1,0:T(8,128)}) %reduce-scatter.30.cloned.1.call-update) | async-done | bytes 2097168 | tf_op jit(solution)/shard_map/reduce_scatter | solution.py:140
  2336.9 21.2 reduce-scatter.42.cloned.1.call-done
  2359.9 42.9 %reduce-scatter.40.cloned.1.call-done = bf16[128,1024]{1,0:T(8,128)(2,1)} async-done(((bf16[1024,1024]{1,0:T(8,128)(2,1)}), bf16[128,1024]{1,0:T(8,128)(2,1)}) %reduce-scatter.40.cloned.1.call-update) | async-done | bytes 262160 | tf_op jit(solution)/shard_map/reduce_scatter | solution.py:406
  2404.6 35.3 %reduce-scatter.38.cloned.1.call-done = bf16[128,256]{1,0:T(8,128)(2,1)} async-done(((bf16[1024,256]{1,0:T(8,128)(2,1)}), bf16[128,256]{1,0:T(8,128)(2,1)}) %reduce-scatter.38.cloned.1.call-update) | async-done | bytes 65552 | tf_op jit(solution)/shard_map/reduce_scatter | solution.py:403
  2441.4 36.0 %reduce-scatter.36.cloned.1.call-done = bf16[128,256]{1,0:T(8,128)(2,1)} async-done(((bf16[1024,256]{1,0:T(8,128)(2,1)}), bf16[128,256]{1,0:T(8,128)(2,1)}) %reduce-scatter.36.cloned.1.call-update) | async-done | bytes 65552 | tf_op jit(solution)/shard_map/reduce_scatter | solution.py:397
  2478.9 37.7 %reduce-scatter.48.cloned.1.call-done = bf16[128,512]{1,0:T(8,128)(2,1)} async-done(((bf16[1024,512]{1,0:T(8,128)(2,1)}), bf16[128,512]{1,0:T(8,128)(2,1)}) %reduce-scatter.48.cloned.1.call-update) | async-done | bytes 131088
  2518.5 35.4 %reduce-scatter.34.cloned.1.call-done = bf16[128,256]{1,0:T(8,128)(2,1)} async-done(((bf16[1024,256]{1,0:T(8,128)(2,1)}), bf16[128,256]{1,0:T(8,128)(2,1)}) %reduce-scatter.34.cloned.1.call-update) | async-done | bytes 65552 | tf_op jit(solution)/shard_map/reduce_scatter | solution.py:394
  2555.3 40.5 %reduce-scatter.32.cloned.1.call-done = bf16[128,3,256]{2,0,1:T(8,128)(2,1)} async-done(((bf16[1024,3,256]{2,0,1:T(8,128)(2,1)}), bf16[128,3,256]{2,0,1:T(8,128)(2,1)}) %reduce-scatter.32.cloned.1.call-update) | async-done | bytes 196624 | tf_op jit(solution)/shard_map/reduce_scatter | solution.py:391
  2597.6 40.3 %all-reduce = (f32[5,1024]{1,0:T(8,128)}, f32[5,1024]{1,0:T(8,128)}) all-reduce(f32[5,1024]{1,0:T(8,128)S(1)} %stack.51, f32[5,1024]{1,0:T(8,128)S(1)} %stack.57), channel_id=1, replica_groups=mesh['dp'=8,'mp'=4] {'dp','mp'}, use_global_device_ids=true, to_apply=%region_55.56 | all-reduce | flops 10240 | bytes 81920 | tf_op jit(solution)/shard_map/psum | solution.py:415
  2644.9 222.8 %scatter_custom_fusion = f32[32,131072]{0,1:T(8,128)} fusion(s32[16384]{0:T(1024)S(1)} %get-tuple-element.463, f32[]{:T(128)} %constant.79.clone.1, f32[16384,32]{1,0:T(8,128)} %copy.210, s32[16384]{0:T(1024)S(1)} %broadcast_clamp_fusion), kind=kCustom, calls=%fused_computation.101 | custom fusion | flops 524288 | bytes 16777728 | tf_op jit(solution)/shard_map/scatter-add | solution.py:384
  2867.7 40.4 %copy.223 = f32[32,131072]{1,0:T(8,128)} copy(f32[32,131072]{0,1:T(8,128)} %scatter_custom_fusion) | data formatting | bytes 33554432
  (558 shorter events, 609.2 us)
Async XLA Ops:
  356.1 28.4 all-to-all-start
  359.5 46.7 %all-gather.15.cloned.1.call-start = ((), (), s32[]{:S(2)}) async-start(), calls=%async_computation.18 | async-start | bytes 1769472 | tf_op jit(solution)/shard_map/all_gather | solution.py:174
  360.4 115.3 %all-gather.13.cloned.1.call-start = ((), (), s32[]{:S(2)}) async-start(), calls=%async_computation.17 | async-start | bytes 5242880 | tf_op jit(solution)/shard_map/all_gather | solution.py:136
  394.7 281.9 %reduce-scatter.20.cloned.1.call-start = ((), (), s32[]{:S(2)}) async-start(), calls=%async_computation.19 | async-start | bytes 10485760 | tf_op jit(solution)/shard_map/reduce_scatter | solution.py:140
  533.4 185.4 %all-gather.21.cloned.1.call-start = ((), (), s32[]{:S(2)}) async-start(), calls=%async_computation.22 | async-start | bytes 1179648 | tf_op jit(solution)/shard_map/all_gather | solution.py:177
  535.1 250.4 %all-gather.19.cloned.1.call-start = ((), (), s32[]{:S(2)}) async-start(), calls=%async_computation.21 | async-start | bytes 5242880 | tf_op jit(solution)/shard_map/all_gather | solution.py:136
  535.6 331.1 %all-gather.17.cloned.1.call-start = ((), (), s32[]{:S(2)}) async-start(), calls=%async_computation.20 | async-start | bytes 5242880 | tf_op jit(solution)/shard_map/all_gather | solution.py:136
  687.6 369.6 %reduce-scatter.22.cloned.1.call-start = ((), (), s32[]{:S(2)}) async-start(), calls=%async_computation.23 | async-start | bytes 10485760 | tf_op jit(solution)/shard_map/reduce_scatter | solution.py:140
  914.1 173.7 %all-gather.25.cloned.1.call-start = ((), (), s32[]{:S(2)}) async-start(), calls=%async_computation.25 | async-start | bytes 2359296 | tf_op jit(solution)/shard_map/all_gather | solution.py:179
  914.8 255.9 %all-gather.23.cloned.1.call-start = ((), (), s32[]{:S(2)}) async-start(), calls=%async_computation.24 | async-start | bytes 5242880 | tf_op jit(solution)/shard_map/all_gather | solution.py:136
  1061.5 143.0 %all-gather.27.cloned.1.call-start = ((), (), s32[]{:S(2)}) async-start(), calls=%async_computation.26 | async-start | bytes 2359296 | tf_op jit(solution)/shard_map/all_gather | solution.py:180
  1062.1 296.3 %reduce-scatter.24.cloned.1.call-start = ((), (), s32[]{:S(2)}) async-start(), calls=%async_computation.27 | async-start | bytes 10485760 | tf_op jit(solution)/shard_map/reduce_scatter | solution.py:140
  1215.3 233.2 %all-gather.29.cloned.1.call-start = ((), (), s32[]{:S(2)}) async-start(), calls=%async_computation.28 | async-start | bytes 5242880 | tf_op jit(solution)/shard_map/all_gather | solution.py:144
  1366.9 245.5 %reduce-scatter.26.cloned.1.call-start = ((), (), s32[]{:S(2)}) async-start(), calls=%async_computation.29 | async-start | bytes 10485760 | tf_op jit(solution)/shard_map/reduce_scatter | solution.py:140
  1469.2 231.7 %all-gather.31.cloned.1.call-start = ((), (), s32[]{:S(2)}) async-start(), calls=%async_computation.30 | async-start | bytes 5242880 | tf_op jit(solution)/shard_map/all_gather | solution.py:144
  1619.2 325.5 %reduce-scatter.28.cloned.1.call-start = ((), (), s32[]{:S(2)}) async-start(), calls=%async_computation.31 | async-start | bytes 10485760 | tf_op jit(solution)/shard_map/reduce_scatter | solution.py:140
  1801.6 231.2 %all-gather.33.cloned.1.call-start = ((), (), s32[]{:S(2)}) async-start(), calls=%async_computation.32 | async-start | bytes 5242880 | tf_op jit(solution)/shard_map/all_gather | solution.py:144
  1951.2 351.8 %reduce-scatter.30.cloned.1.call-start = ((), (), s32[]{:S(2)}) async-start(), calls=%async_computation.33 | async-start | bytes 10485760 | tf_op jit(solution)/shard_map/reduce_scatter | solution.py:140
  2159.9 198.3 %reduce-scatter.42.cloned.1.call-start = ((), (), s32[]{:S(2)}) async-start(), calls=%async_computation.39 | async-start | bytes 2359296 | tf_op jit(solution)/shard_map/reduce_scatter | solution.py:409
  2169.4 233.4 %reduce-scatter.40.cloned.1.call-start = ((), (), s32[]{:S(2)}) async-start(), calls=%async_computation.38 | async-start | bytes 2359296 | tf_op jit(solution)/shard_map/reduce_scatter | solution.py:406
  2179.2 260.6 %reduce-scatter.38.cloned.1.call-start = ((), (), s32[]{:S(2)}) async-start(), calls=%async_computation.37 | async-start | bytes 589824 | tf_op jit(solution)/shard_map/reduce_scatter | solution.py:403
  2183.7 293.7 %reduce-scatter.36.cloned.1.call-start = ((), (), s32[]{:S(2)}) async-start(), calls=%async_computation.36 | async-start | bytes 589824 | tf_op jit(solution)/shard_map/reduce_scatter | solution.py:397
  2188.4 328.3 %reduce-scatter.48.cloned.1.call-start = ((), (), s32[]{:S(2)}) async-start(), calls=%async_computation.42 | async-start | bytes 1179648
  2195.4 358.5 %reduce-scatter.34.cloned.1.call-start = ((), (), s32[]{:S(2)}) async-start(), calls=%async_computation.35 | async-start | bytes 589824 | tf_op jit(solution)/shard_map/reduce_scatter | solution.py:394
  2199.9 395.9 %reduce-scatter.32.cloned.1.call-start = ((), (), s32[]{:S(2)}) async-start(), calls=%async_computation.34 | async-start | bytes 1769472 | tf_op jit(solution)/shard_map/reduce_scatter | solution.py:391
  2207.7 430.2 %reduce-scatter.46.cloned.1.call-start = ((), (), s32[]{:S(2)}) async-start(), calls=%async_computation.41 | async-start | bytes 589824
  2315.0 593.1 %reduce-scatter.44.cloned.1.call-start = ((), (), s32[]{:S(2)}) async-start(), calls=%async_computation.40 | async-start | bytes 10485760 | tf_op jit(solution)/shard_map/reduce_scatter | solution.py:140
  2324.2 273.4 %copy-start.110 = (f32[1024]{0:T(1024)S(1)}, f32[1024]{0:T(1024)}, u32[]{:S(2)}) copy-start(f32[1024]{0:T(1024)} %get-tuple-element.471) | copy-start | bytes 12292
  2324.2 273.4 %copy-start.105 = (f32[1024]{0:T(1024)S(1)}, f32[1024]{0:T(1024)}, u32[]{:S(2)}) copy-start(f32[1024]{0:T(1024)} %get-tuple-element.478) | copy-start | bytes 12292
  2324.2 273.4 %copy-start.106 = (f32[1024]{0:T(1024)S(1)}, f32[1024]{0:T(1024)}, u32[]{:S(2)}) copy-start(f32[1024]{0:T(1024)} %get-tuple-element.477) | copy-start | bytes 12292
  2324.2 273.4 %copy-start.109 = (f32[1024]{0:T(1024)S(1)}, f32[1024]{0:T(1024)}, u32[]{:S(2)}) copy-start(f32[1024]{0:T(1024)} %get-tuple-element.480) | copy-start | bytes 12292
  2324.2 315.5 %all-to-all-start.1 = ((bf16[32,32,512]{2,1,0:T(8,128)(2,1)}), bf16[32,32,512]{2,1,0:T(8,128)(2,1)S(1)}, u32[]{:S(2)}, u32[]{:S(2)}) async-start(bf16[32,32,512]{2,1,0:T(8,128)(2,1)} %bitcast.60), calls=%async_computation.7 | async-start | bytes 2097152 | tf_op jit(solution)/shard_map/all_to_all | solution.py:380
  (133 other events, 3833.8 us)
Sparse Core Ops, SparseCore 0:
  362.8 29.1 all-gather.14
  394.9 80.7 all-gather.12
  533.6 143.0 reduce-scatter.19
  678.9 24.2 all-gather.20
  704.7 80.7 all-gather.18
  787.5 79.2 all-gather.16
  914.2 142.9 reduce-scatter.21
  1059.1 28.6 all-gather.24
  1089.9 80.7 all-gather.22
  1172.4 26.4 all-gather.26
  1215.4 142.9 reduce-scatter.23
  1367.0 81.4 all-gather.28
  1469.3 143.0 reduce-scatter.25
  1619.4 81.4 all-gather.30
  1801.8 142.9 reduce-scatter.27
  1951.4 81.4 all-gather.32
  2160.0 143.0 reduce-scatter.29
  2306.2 51.9 reduce-scatter.41
  2361.8 40.9 reduce-scatter.39
  2405.7 34.0 reduce-scatter.37
  2443.2 34.1 reduce-scatter.35
  2480.6 35.9 reduce-scatter.47
  2519.7 34.0 reduce-scatter.33
  2557.3 38.4 reduce-scatter.31
  2599.2 34.1 reduce-scatter.45
  2636.1 144.4 reduce-scatter.43
where the time goes:
time: 2930 us; the launch traced here: 2920 us
  waiting for transfers between devices  1630 us (56%)
  local copies, waits for them, and re-layouts  422 us (14%)
  other arithmetic  384 us (13%)
  matrix products  283 us (10%)
  blocking collectives  168 us (6%)
    reduce_scatter x7, waiting for transfers between devices, collect(): return lax.psum_scatter(partial_sums, 'mp', scatter_dimension=1, tiled=True)  808 us
    all_gather x4, waiting for transfers between devices, spread(): return lax.all_gather(values, 'mp', axis=1, tiled=True)  295 us
    gather x2, local copies, waits for them, and re-layouts, body(): picked = jnp.take(table, all_ids, axis=1)  251 us
    all_gather x3, waiting for transfers between devices, spread_grad(): return lax.all_gather(grads.astype(jnp.bfloat16), 'mp', axis=1, tiled=True)  245 us
    scatter-add x3, other arithmetic, body(): jnp.zeros((table.shape[0], table.shape[1]), single_float).at[:, all_ids]  230 us
    unnamed x211, local copies, waits for them, and re-layouts  90.7 us
    all_gather x1, blocking collectives, body(): lax.all_gather(target_ids.reshape(-1), ('dp', 'mp'), axis=0, tiled=True)  70.1 us
  transfers between devices with their start and end apart: 28, of which 22 were waited for; matrix products, arithmetic and copies ran while one was open for 14% of the time, Pallas kernels for 0%

commit v1 on v0

v1 whole, which is shorter than its diff:
```python
import functools

import jax
import jax.numpy as jnp
from jax import lax
from jax.experimental import pallas as pl
from jax.experimental.pallas import tpu as pltpu
from jax.sharding import Mesh
from jax.sharding import PartitionSpec as P

HEAD_DIM = 64
EPSILON = 1e-05
NEGATIVE = -1e30
LANES = 128
ALL = ("chip", "core", "mp")
LINE = ("core", "mp")
CORES = 2

f32 = jnp.float32
bf16 = jnp.bfloat16
i32 = jnp.int32

NT = (((1,), (1,)), ((), ()))
NN = (((1,), (0,)), ((), ()))
TN = (((0,), (0,)), ((), ()))


def dot(a, b, dims=NN):
    return lax.dot_general(a, b, dims, preferred_element_type=f32)


def params(mib=56):
    return pltpu.CompilerParams(vmem_limit_bytes=mib << 20)


def cost(flops, moved, trans=0):
    return pl.CostEstimate(flops=int(flops), bytes_accessed=int(moved), transcendentals=int(trans))


def normed(values):
    centred = values - jnp.mean(values, axis=-1, keepdims=True)
    inverse = lax.rsqrt(jnp.mean(centred * centred, axis=-1, keepdims=True) + EPSILON)
    return centred * inverse, inverse


def norm_back(values, gain, grad):
    hat, inverse = normed(values)
    scaled = grad * gain
    first = jnp.mean(scaled, axis=-1, keepdims=True)
    second = jnp.mean(scaled * hat, axis=-1, keepdims=True)
    back = inverse * (scaled - first - hat * second)
    gain_grad = jnp.sum(grad * hat, axis=0, keepdims=True)
    bias_grad = jnp.sum(grad, axis=0, keepdims=True)
    return back, gain_grad, bias_grad


def columns(w_ref, m):
    block = w_ref[:, pl.ds(m, 1)]
    return block.reshape(block.shape[0] * block.shape[3], block.shape[4])


def whole_weight(w_ref):
    parts = [columns(w_ref, m) for m in range(w_ref.shape[1])]
    return jnp.concatenate(parts, axis=1)


def project(x, w_ref, store):
    width = w_ref.shape[4]

    def step(m, carry):
        store(pl.multiple_of(m * width, width), dot(x, columns(w_ref, m)))
        return carry

    lax.fori_loop(0, w_ref.shape[1], step, 0)


def weight_spec(weights, index):
    shape = weights.shape
    return pl.BlockSpec(
        (shape[0], shape[1], 1, shape[3], shape[4]), lambda *a: (0, 0, index(a[0]), 0, 0)
    )


def full(shape):
    return pl.BlockSpec(shape, lambda *a: (0,) * len(shape))


def gather_kernel(groups, fill, rows_ref, group_ref, *refs):
    tables, out_ref, turned, picked = refs[:groups], refs[groups], refs[-2], refs[-1]
    step = pl.program_id(0)
    feats, width = tables[0].shape
    tokens = picked.shape[0]

    @pl.when(step < fill)
    def _():
        stacked = jnp.concatenate([t[...].astype(f32) for t in tables], axis=0).astype(bf16)
        row = lax.broadcasted_iota(i32, (256, 256), 0)
        eye = jnp.where(row == lax.broadcasted_iota(i32, (256, 256), 1), 1.0, 0.0).astype(bf16)
        for k in range(width // 256):
            at = pl.multiple_of(step * width + k * 256, 256)
            turned[pl.ds(at, 256), :] = dot(eye, stacked[:, k * 256 : (k + 1) * 256], NT)

    @pl.when(step >= fill)
    def _():
        base = (step - fill) * tokens

        def some(k, carry):
            for u in range(16):
                t = k * 16 + u
                picked[pl.ds(t, 1), :] = turned[pl.ds(rows_ref[base + t], 1), :]
            return carry

        lax.fori_loop(0, tokens // 16, some, 0)
        row = lax.broadcasted_iota(i32, (LANES, LANES), 0)
        eye = jnp.where(row == lax.broadcasted_iota(i32, (LANES, LANES), 1), 1.0, 0.0)
        across = dot(eye.astype(bf16), picked[...].astype(bf16), NT)
        own = lax.broadcasted_iota(i32, (LANES, tokens), 0) // feats == group_ref[0]
        kept = jnp.where(own, across, 0.0)
        total = kept[:feats]
        for g in range(1, groups):
            total = total + kept[g * feats : (g + 1) * feats]
        out_ref[0] = total.astype(out_ref.dtype)


def gather_tokens(table, rows, group):
    feats, vocab = table.shape
    groups = LANES // feats
    height = vocab // groups
    n, _, tokens = group.shape
    width = min(2048, height)
    fill = height // width

    def table_spec(g):
        return pl.BlockSpec(
            (feats, width), lambda s, r, g=g: (0, g * fill + jnp.minimum(s, fill - 1))
        )

    return pl.pallas_call(
        functools.partial(gather_kernel, groups, fill),
        out_shape=jax.ShapeDtypeStruct((n, feats, tokens), bf16),
        grid_spec=pltpu.PrefetchScalarGridSpec(
            num_scalar_prefetch=1,
            grid=(fill + n,),
            in_specs=[pl.BlockSpec((1, 1, tokens), lambda s, r: (jnp.maximum(s - fill, 0), 0, 0))]
            + [table_spec(g) for g in range(groups)],
            out_specs=pl.BlockSpec(
                (1, feats, tokens), lambda s, r: (jnp.maximum(s - fill, 0), 0, 0)
            ),
            scratch_shapes=[pltpu.VMEM((height, LANES), f32), pltpu.VMEM((tokens, LANES), f32)],
        ),
        compiler_params=params(),
        cost_estimate=cost(4 * vocab * LANES * 64, 2 * feats * vocab + 400 * n * tokens),
        name="gather_tokens",
    )(rows, group, *([table] * groups))


BATCH = 16


def scatter_kernel(
    groups, per_core, rows_ref, row_ref, group_ref, grad_ref, out_ref, pos_ref, acc, update, turned, sem
):
    step = pl.program_id(0)
    feats, tokens = grad_ref.shape[1:]
    height = acc.shape[0]
    width = turned.shape[2]

    @pl.when(step == 0)
    def _():
        def clear(k, carry):
            acc[pl.ds(pl.multiple_of(k * 256, 256), 256), :] = jnp.zeros((256, LANES), f32)
            return carry

        lax.fori_loop(0, height // 256, clear, 0)
        pos_ref[...] = jnp.zeros_like(pos_ref)

    grads = grad_ref[0].astype(f32)
    core = lax.rem(lax.div(step, per_core), CORES)
    pos_ref[core] += grads
    tall = jnp.concatenate([grads] * groups, axis=0)
    own = lax.broadcasted_iota(i32, (LANES, tokens), 0) // feats == group_ref[0]
    tall = jnp.where(own, tall, 0.0).astype(bf16)
    row = lax.broadcasted_iota(i32, (LANES, LANES), 0)
    col = lax.broadcasted_iota(i32, (LANES, LANES), 1)
    near = row // BATCH == col // BATCH
    for b in range(tokens // LANES):
        at = slice(b * LANES, (b + 1) * LANES)
        along = jnp.broadcast_to(row_ref[0][:, at].astype(f32), (LANES, LANES))
        same = jnp.where((along == along.T) & near, 1.0, 0.0).astype(bf16)
        update[at, :] = dot(same, tall[:, at], NT)
    base = step * tokens

    def some(k, carry):
        where = [rows_ref[base + k * BATCH + u] for u in range(BATCH)]
        fresh = [
            acc[pl.ds(where[u], 1), :] + update[pl.ds(k * BATCH + u, 1), :] for u in range(BATCH)
        ]
        for u in range(BATCH):
            acc[pl.ds(where[u], 1), :] = fresh[u]
        return carry

    lax.fori_loop(0, tokens // BATCH, some, 0)

    @pl.when(step == pl.num_programs(0) - 1)
    def _():
        def copy(i, slot, g):
            at = pl.multiple_of(g * height + i * width, width)
            return pltpu.make_async_copy(
                turned.at[slot, pl.ds(g * feats, feats)],
                out_ref.at[:, pl.ds(at, width)],
                sem.at[slot, g],
            )

        def turn(i, carry):
            slot = lax.rem(i, 2)

            @pl.when(i >= 2)
            def _():
                for g in range(groups):
                    copy(i - 2, slot, g).wait()

            at = pl.multiple_of(i * width, width)
            turned[slot] = (acc[pl.ds(at, width), :] * 32.0).T
            for g in range(groups):
                copy(i, slot, g).start()
            return carry

        count = height // width
        lax.fori_loop(0, count, turn, 0)
        for i in range(max(count - 2, 0), count):
            for g in range(groups):
                copy(i, i % 2, g).wait()


def scatter_tokens(grads, rows, row, group, vocab, per_core):
    n, feats, tokens = grads.shape
    groups = LANES // feats
    height = vocab // groups
    width = min(1024, height)
    token_spec = pl.BlockSpec((1, 1, tokens), lambda s, r: (s, 0, 0))
    return pl.pallas_call(
        functools.partial(scatter_kernel, groups, per_core),
        out_shape=(
            jax.ShapeDtypeStruct((feats, vocab), f32),
            jax.ShapeDtypeStruct((CORES, feats, tokens), f32),
        ),
        grid_spec=pltpu.PrefetchScalarGridSpec(
            num_scalar_prefetch=1,
            grid=(n,),
            in_specs=[
                token_spec,
                token_spec,
                pl.BlockSpec((1, feats, tokens), lambda s, r: (s, 0, 0)),
            ],
            out_specs=(
                pl.BlockSpec(memory_space=pl.ANY),
                full((CORES, feats, tokens)),
            ),
            scratch_shapes=[
                pltpu.VMEM((height, LANES), f32),
                pltpu.VMEM((tokens, LANES), f32),
                pltpu.VMEM((2, LANES, width), f32),
                pltpu.SemaphoreType.DMA((2, groups)),
            ],
        ),
        compiler_params=params(),
        cost_estimate=cost(n * tokens * LANES * 256, 4 * feats * vocab + 1000 * n * tokens),
        name="scatter_tokens",
    )(rows, row, group, grads)


def entry_kernel(
    info_ref, emb_ref, pos_a, pos_b, w_ref, gain_ref, bias_ref, x0_ref, x1_ref, a_ref, q_ref, kv_ref
):
    step = pl.program_id(0)
    half = x0_ref.shape[0] // 2

    @pl.when(step == 0)
    def _():
        for i, pos in enumerate((pos_a, pos_b)):
            at = slice(i * half, (i + 1) * half)
            places = pos[...].reshape(pos.shape[0] * pos.shape[3], pos.shape[4])
            x0 = (emb_ref[:, at].astype(f32) * 32.0 + places.astype(f32)).T
            x1 = normed(x0)[0] * gain_ref[0:1] + bias_ref[0:1]
            a = normed(x1)[0] * gain_ref[1:2] + bias_ref[1:2]
            x0_ref[at] = x0
            x1_ref[at] = x1
            a_ref[at] = a.astype(bf16)

    x = a_ref[...]

    @pl.when(step == 0)
    def _():
        def store(at, y):
            q_ref[0, :, pl.ds(at, w_ref.shape[4])] = (y * HEAD_DIM**-0.5).astype(bf16)

        project(x, w_ref, store)

    @pl.when(step > 0)
    def _():
        def store(at, y):
            kv_ref[0, :, pl.ds(at, w_ref.shape[4])] = y.astype(bf16)

        project(x, w_ref, store)


def entry(info, emb, first, gains, biases):
    width, tokens = emb.shape
    half = tokens // 2
    shape = first.shape

    def pos_spec(i):
        return pl.BlockSpec(
            (shape[0], 1, 1, shape[3], shape[4]), lambda s, info, i=i: (0, info[3 + i], 0, 0, 0)
        )

    rows = jax.ShapeDtypeStruct((tokens, width), f32)
    return pl.pallas_call(
        entry_kernel,
        out_shape=(
            rows,
            rows,
            jax.ShapeDtypeStruct((tokens, width), bf16),
            jax.ShapeDtypeStruct((1, tokens, width), bf16),
            jax.ShapeDtypeStruct((2, tokens, width), bf16),
        ),
        grid_spec=pltpu.PrefetchScalarGridSpec(
            num_scalar_prefetch=1,
            grid=(3,),
            in_specs=[
                full(emb.shape),
                pos_spec(0),
                pos_spec(1),
                weight_spec(first, lambda s: s + 1),
                full(gains.shape),
                full(biases.shape),
            ],
            out_specs=(
                full((tokens, width)),
                full((tokens, width)),
                full((tokens, width)),
                full((1, tokens, width)),
                pl.BlockSpec((1, tokens, width), lambda s, info: (jnp.maximum(s - 1, 0), 0, 0)),
            ),
        ),
        compiler_params=params(),
        cost_estimate=cost(6 * tokens * width * width, 20 * tokens * width + 6 * width * width),
        name="entry",
    )(info, emb, first, first, first, gains, biases)


def source_kernel(x_ref, w_ref, kv_ref):
    def store(at, y):
        kv_ref[0, :, pl.ds(at, w_ref.shape[4])] = y.astype(bf16)

    project(x_ref[...], w_ref, store)


def source_keys(states, second):
    tokens, width = states.shape
    return pl.pallas_call(
        source_kernel,
        out_shape=jax.ShapeDtypeStruct((2, tokens, width), bf16),
        grid=(2,),
        in_specs=[full(states.shape), weight_spec(second, lambda s: s + 2)],
        out_specs=pl.BlockSpec((1, tokens, width), lambda s: (s, 0, 0)),
        compiler_params=params(),
        cost_estimate=cost(4 * tokens * width * width, 6 * tokens * width + 4 * width * width),
        name="source_keys",
    )(states, second)


def attend_kernel(causal, info_ref, q_ref, own_ref, par_ref, o_ref, p_ref, hide):
    tokens = q_ref.shape[1]
    half = tokens // 2
    core = info_ref[0]

    @pl.when(pl.program_id(0) == 0)
    def _():
        length = info_ref[1] if causal else info_ref[2]
        key = lax.broadcasted_iota(i32, (tokens, tokens), 0)
        query = lax.broadcasted_iota(i32, (tokens, tokens), 1)
        upper = key >= half
        own = key + jnp.where(upper, info_ref[4] - 1, info_ref[3]) * half
        par = key + jnp.where(upper, info_ref[6] - 1, info_ref[5]) * half
        at = query + jnp.where(query >= half, info_ref[4] - 1, info_ref[3]) * half
        for i, place in enumerate((own, par)):
            seen = place < length
            if causal:
                seen = seen & (place <= at)
            hide[i] = jnp.where(seen, 0.0, NEGATIVE)

    outs = []
    for h in range(LANES // HEAD_DIM):
        lanes = slice(h * HEAD_DIM, (h + 1) * HEAD_DIM)
        q = q_ref[0][:, lanes]
        s_own = dot(own_ref[0][:, lanes], q, NT) + hide[0]
        s_par = dot(par_ref[0][:, lanes], q, NT) + hide[1]
        top = jnp.maximum(
            jnp.max(s_own, axis=0, keepdims=True), jnp.max(s_par, axis=0, keepdims=True)
        )
        e_own = jnp.exp(s_own - top)
        e_par = jnp.exp(s_par - top)
        total = jnp.sum(e_own, axis=0, keepdims=True) + jnp.sum(e_par, axis=0, keepdims=True)
        scale = 1.0 / total
        p_own = (e_own * scale).astype(bf16)
        p_par = (e_par * scale).astype(bf16)
        p_ref[h, 0] = p_own
        p_ref[h, 1] = p_par
        outs.append(dot(own_ref[1][:, lanes], p_own, TN) + dot(par_ref[1][:, lanes], p_par, TN))
    o_ref[0] = jnp.concatenate(outs, axis=0).T.astype(bf16)


def attend(info, q, own, par, causal):
    _, tokens, width = q.shape
    heads = width // HEAD_DIM
    pair = LANES // HEAD_DIM
    one = pl.BlockSpec((1, tokens, LANES), lambda s, info: (0, 0, s))
    two = pl.BlockSpec((2, tokens, LANES), lambda s, info: (0, 0, s))
    return pl.pallas_call(
        functools.partial(attend_kernel, causal),
        out_shape=(
            jax.ShapeDtypeStruct((1, tokens, width), bf16),
            jax.ShapeDtypeStruct((heads, 2, tokens, tokens), bf16),
        ),
        grid_spec=pltpu.PrefetchScalarGridSpec(
            num_scalar_prefetch=1,
            grid=(heads // pair,),
            in_specs=[one, two, two],
            out_specs=(
                one,
                pl.BlockSpec((pair, 2, tokens, tokens), lambda s, info: (s, 0, 0, 0)),
            ),
            scratch_shapes=[pltpu.VMEM((2, tokens, tokens), f32)],
        ),
        compiler_params=params(),
        cost_estimate=cost(
            32 * tokens * tokens * width, 4 * heads * tokens * tokens, 2 * heads * tokens * tokens
        ),
        name="attend",
    )(info, q, own, par)


def middle_kernel(o_ref, w_ref, x_ref, wq_ref, gain_ref, bias_ref, x2_ref, c_ref, q_ref):
    x2 = x_ref[...] + dot(o_ref[0], whole_weight(w_ref), NT)
    x2_ref[...] = x2
    c = (normed(x2)[0] * gain_ref[2:3] + bias_ref[2:3]).astype(bf16)
    c_ref[...] = c

    def store(at, y):
        q_ref[0, :, pl.ds(at, wq_ref.shape[4])] = (y * HEAD_DIM**-0.5).astype(bf16)

    project(c, wq_ref, store)


def middle(o, second, x1, gains, biases):
    _, tokens, width = o.shape
    return pl.pallas_call(
        middle_kernel,
        out_shape=(
            jax.ShapeDtypeStruct((tokens, width), f32),
            jax.ShapeDtypeStruct((tokens, width), bf16),
            jax.ShapeDtypeStruct((1, tokens, width), bf16),
        ),
        grid=(1,),
        in_specs=[
            full(o.shape),
            weight_spec(second, lambda s: 0),
            full(x1.shape),
            weight_spec(second, lambda s: 1),
            full(gains.shape),
            full(biases.shape),
        ],
        out_specs=(full((tokens, width)), full((tokens, width)), full((1, tokens, width))),
        compiler_params=params(),
        cost_estimate=cost(4 * tokens * width * width, 14 * tokens * width + 4 * width * width),
        name="middle",
    )(o, second, x1, second, gains, biases)


def feed_kernel(
    o_ref,
    wo_ref,
    x_ref,
    w1_ref,
    w2_ref,
    og_ref,
    gain_ref,
    bias_ref,
    x3_ref,
    f_ref,
    g_ref,
    slope_ref,
    hid_ref,
    g4_ref,
    g4b_ref,
    sums_ref,
    total,
):
    step = pl.program_id(0)

    @pl.when(step == 0)
    def _():
        x3 = x_ref[...] + dot(o_ref[0], whole_weight(wo_ref), NT)
        x3_ref[...] = x3
        f_ref[...] = (normed(x3)[0] * gain_ref[3:4] + bias_ref[3:4]).astype(bf16)
        total[...] = x3

    def store(at, u):
        bell = 0.5 + 0.5 * lax.erf(u * 0.7071067811865476)
        lanes = pl.ds(at, w1_ref.shape[4])
        g_ref[0, :, lanes] = (u * bell).astype(bf16)
        slope = bell + u * (0.3989422804014327 * jnp.exp(-0.5 * u * u))
        slope_ref[0, :, lanes] = slope.astype(bf16)

    project(f_ref[...], w1_ref, store)
    total[...] += dot(g_ref[0], whole_weight(w2_ref), NT)

    @pl.when(step == pl.num_programs(0) - 1)
    def _():
        x4 = total[...]
        grad = og_ref[...].astype(f32)
        hid_ref[...] = (normed(x4)[0] * gain_ref[4:5] + bias_ref[4:5]).astype(hid_ref.dtype)
        g4, gain_grad, bias_grad = norm_back(x4, gain_ref[4:5], grad)
        g4_ref[...] = g4
        g4b_ref[...] = g4.astype(bf16)
        sums_ref[0:1] = gain_grad
        sums_ref[1:2] = bias_grad


def feed(o, second, x2, third, og, gains, biases):
    _, tokens, width = o.shape
    blocks = third.shape[2] // 2
    row = full((tokens, width))
    part = pl.BlockSpec((1, tokens, width), lambda s: (s, 0, 0))
    wide = jax.ShapeDtypeStruct((tokens, width), f32)
    slim = jax.ShapeDtypeStruct((tokens, width), bf16)
    many = jax.ShapeDtypeStruct((blocks, tokens, width), bf16)
    return pl.pallas_call(
        feed_kernel,
        out_shape=(wide, slim, many, many, slim, wide, slim, jax.ShapeDtypeStruct((2, width), f32)),
        grid=(blocks,),
        in_specs=[
            full(o.shape),
            weight_spec(second, lambda s: 4),
            row,
            weight_spec(third, lambda s: s),
            weight_spec(third, lambda s: s + blocks),
            row,
            full(gains.shape),
            full(biases.shape),
        ],
        out_specs=(row, row, part, part, row, row, row, full((2, width))),
        scratch_shapes=[pltpu.VMEM((tokens, width), f32)],
        compiler_params=params(60),
        cost_estimate=cost(
            (4 * blocks + 2) * tokens * width * width,
            (22 + 4 * blocks) * tokens * width + (2 + 4 * blocks) * width * width,
            2 * blocks * tokens * width,
        ),
        name="feed",
    )(o, second, x2, third, third, og, gains, biases)


def feed_back_kernel(
    g4_ref,
    g4b_ref,
    slope_ref,
    w1_ref,
    w2_ref,
    x3_ref,
    wo_ref,
    gain_ref,
    du_ref,
    g3_ref,
    g3b_ref,
    do_ref,
    sums_ref,
    total,
):
    step = pl.program_id(0)

    def store(at, y):
        lanes = pl.ds(at, w2_ref.shape[4])
        du_ref[0, :, lanes] = (y * slope_ref[0, :, lanes].astype(f32)).astype(bf16)

    project(g4b_ref[...], w2_ref, store)
    part = dot(du_ref[0], whole_weight(w1_ref), NT)

    @pl.when(step == 0)
    def _():
        total[...] = part

    @pl.when(step > 0)
    def _():
        total[...] += part

    @pl.when(step == pl.num_programs(0) - 1)
    def _():
        back, gain_grad, bias_grad = norm_back(x3_ref[...], gain_ref[3:4], total[...])
        g3 = g4_ref[...] + back
        g3_ref[...] = g3
        g3b = g3.astype(bf16)
        g3b_ref[...] = g3b
        sums_ref[0:1] = gain_grad
        sums_ref[1:2] = bias_grad

        def keep(at, y):
            do_ref[0, :, pl.ds(at, wo_ref.shape[4])] = y.astype(bf16)

        project(g3b, wo_ref, keep)


def feed_back(g4, g4b, slope, second, x3, third, gains):
    blocks, tokens, width = slope.shape
    row = full((tokens, width))
    part = pl.BlockSpec((1, tokens, width), lambda s: (s, 0, 0))
    wide = jax.ShapeDtypeStruct((tokens, width), f32)
    slim = jax.ShapeDtypeStruct((tokens, width), bf16)
    return pl.pallas_call(
        feed_back_kernel,
        out_shape=(
            jax.ShapeDtypeStruct((blocks, tokens, width), bf16),
            wide,
            slim,
            jax.ShapeDtypeStruct((1, tokens, width), bf16),
            jax.ShapeDtypeStruct((2, width), f32),
        ),
        grid=(blocks,),
        in_specs=[
            row,
            row,
            part,
            weight_spec(third, lambda s: s),
            weight_spec(third, lambda s: s + blocks),
            row,
            weight_spec(second, lambda s: 4),
            full(gains.shape),
        ],
        out_specs=(part, row, row, full((1, tokens, width)), full((2, width))),
        scratch_shapes=[pltpu.VMEM((tokens, width), f32)],
        compiler_params=params(60),
        cost_estimate=cost(
            (4 * blocks + 2) * tokens * width * width,
            (18 + 4 * blocks) * tokens * width + (2 + 4 * blocks) * width * width,
        ),
        name="feed_back",
    )(g4, g4b, slope, third, third, x3, second, gains)


def attend_back_kernel(
    q_ref, own_ref, par_ref, p_ref, o_ref, do_ref, dq_ref, down_ref, dpar_ref
):
    flat = do_ref[0].astype(f32).T * o_ref[0].astype(f32).T
    outs = []
    for h in range(LANES // HEAD_DIM):
        lanes = slice(h * HEAD_DIM, (h + 1) * HEAD_DIM)
        q = q_ref[0][:, lanes]
        grad = do_ref[0][:, lanes]
        inner = jnp.sum(flat[lanes], axis=0, keepdims=True)
        back = None
        for i, (kv_ref, d_ref) in enumerate(((own_ref, down_ref), (par_ref, dpar_ref))):
            keys = kv_ref[0][:, lanes]
            probs = p_ref[h, i]
            d_probs = dot(kv_ref[1][:, lanes], grad, NT)
            d_scores = (probs.astype(f32) * (d_probs - inner)).astype(bf16)
            d_ref[1, :, lanes] = dot(probs, grad).astype(bf16)
            d_ref[0, :, lanes] = dot(d_scores, q).astype(bf16)
            some = dot(keys, d_scores, TN)
            back = some if back is None else back + some
        outs.append(back)
    dq_ref[0] = (jnp.concatenate(outs, axis=0).T * HEAD_DIM**-0.5).astype(bf16)


def attend_back(q, own, par, probs, o, do):
    _, tokens, width = q.shape
    heads = width // HEAD_DIM
    pair = LANES // HEAD_DIM
    one = pl.BlockSpec((1, tokens, LANES), lambda s: (0, 0, s))
    two = pl.BlockSpec((2, tokens, LANES), lambda s: (0, 0, s))
    kv = jax.ShapeDtypeStruct((2, tokens, width), bf16)
    return pl.pallas_call(
        attend_back_kernel,
        out_shape=(jax.ShapeDtypeStruct((1, tokens, width), bf16), kv, kv),
        grid=(heads // pair,),
        in_specs=[
            one,
            two,
            two,
            pl.BlockSpec((pair, 2, tokens, tokens), lambda s: (s, 0, 0, 0)),
            one,
            one,
        ],
        out_specs=(one, two, two),
        compiler_params=params(),
        cost_estimate=cost(64 * tokens * tokens * width, 4 * heads * tokens * tokens),
        name="attend_back",
    )(q, own, par, probs, o, do)


def middle_back_kernel(
    dq_ref, wq_ref, x2_ref, g3_ref, wo_ref, gain_ref, g2_ref, g2b_ref, do_ref, sums_ref
):
    d_normed = dot(dq_ref[0], whole_weight(wq_ref), NT)
    back, gain_grad, bias_grad = norm_back(x2_ref[...], gain_ref[2:3], d_normed)
    g2 = g3_ref[...] + back
    g2_ref[...] = g2
    g2b = g2.astype(bf16)
    g2b_ref[...] = g2b
    sums_ref[0:1] = gain_grad
    sums_ref[1:2] = bias_grad

    def keep(at, y):
        do_ref[0, :, pl.ds(at, wo_ref.shape[4])] = y.astype(bf16)

    project(g2b, wo_ref, keep)


def middle_back(dq, second, x2, g3, gains):
    _, tokens, width = dq.shape
    row = full((tokens, width))
    return pl.pallas_call(
        middle_back_kernel,
        out_shape=(
            jax.ShapeDtypeStruct((tokens, width), f32),
            jax.ShapeDtypeStruct((tokens, width), bf16),
            jax.ShapeDtypeStruct((1, tokens, width), bf16),
            jax.ShapeDtypeStruct((2, width), f32),
        ),
        grid=(1,),
        in_specs=[
            full(dq.shape),
            weight_spec(second, lambda s: 1),
            row,
            row,
            weight_spec(second, lambda s: 0),
            full(gains.shape),
        ],
        out_specs=(row, row, full((1, tokens, width)), full((2, width))),
        compiler_params=params(),
        cost_estimate=cost(4 * tokens * width * width, 18 * tokens * width + 4 * width * width),
        name="middle_back",
    )(dq, second, x2, g3, second, gains)


def source_back_kernel(mine_ref, came_ref, w_ref, out_ref, sum_ref, total):
    step = pl.program_id(0)
    grads = (mine_ref[0].astype(f32) + came_ref[0].astype(f32)).astype(bf16)
    sum_ref[0] = grads
    part = dot(grads, whole_weight(w_ref), NT)

    @pl.when(step == 0)
    def _():
        total[...] = part

    @pl.when(step == pl.num_programs(0) - 1)
    def _():
        out_ref[...] = (total[...] + part).astype(bf16)


def source_back(mine, came, second):
    parts, tokens, width = mine.shape
    part = pl.BlockSpec((1, tokens, width), lambda s: (s, 0, 0))
    return pl.pallas_call(
        source_back_kernel,
        out_shape=(
            jax.ShapeDtypeStruct((tokens, width), bf16),
            jax.ShapeDtypeStruct((parts, tokens, width), bf16),
        ),
        grid=(parts,),
        in_specs=[part, part, weight_spec(second, lambda s: s + 2)],
        out_specs=(full((tokens, width)), part),
        scratch_shapes=[pltpu.VMEM((tokens, width), f32)],
        compiler_params=params(),
        cost_estimate=cost(4 * tokens * width * width, 14 * tokens * width + 4 * width * width),
        name="source_back",
    )(mine, came, second)


def exit_kernel(
    dq_ref, mine_ref, came_ref, w_ref, x1_ref, x0_ref, g2_ref, gain_ref, g0_ref, sum_ref, sums_ref, total
):
    step = pl.program_id(0)

    @pl.when(step == 0)
    def _():
        total[...] = dot(dq_ref[0], whole_weight(w_ref), NT)

    @pl.when(step > 0)
    def _():
        grads = (mine_ref[0].astype(f32) + came_ref[0].astype(f32)).astype(bf16)
        sum_ref[0] = grads
        total[...] += dot(grads, whole_weight(w_ref), NT)

    @pl.when(step == pl.num_programs(0) - 1)
    def _():
        back, gain_one, bias_one = norm_back(x1_ref[...], gain_ref[1:2], total[...])
        g1 = g2_ref[...] + back
        g0, gain_zero, bias_zero = norm_back(x0_ref[...], gain_ref[0:1], g1)
        g0_ref[...] = g0.T.astype(bf16)
        sums_ref[0:1] = gain_zero
        sums_ref[1:2] = bias_zero
        sums_ref[2:3] = gain_one
        sums_ref[3:4] = bias_one


def exit_back(dq, mine, came, first, x1, x0, g2, gains):
    _, tokens, width = dq.shape
    row = full((tokens, width))
    part = pl.BlockSpec((1, tokens, width), lambda s: (jnp.maximum(s - 1, 0), 0, 0))
    return pl.pallas_call(
        exit_kernel,
        out_shape=(
            jax.ShapeDtypeStruct((width, tokens), bf16),
            jax.ShapeDtypeStruct((2, tokens, width), bf16),
            jax.ShapeDtypeStruct((4, width), f32),
        ),
        grid=(3,),
        in_specs=[
            full(dq.shape),
            part,
            part,
            weight_spec(first, lambda s: s + 1),
            row,
            row,
            row,
            full(gains.shape),
        ],
        out_specs=(full((width, tokens)), part, full((4, width))),
        scratch_shapes=[pltpu.VMEM((tokens, width), f32)],
        compiler_params=params(),
        cost_estimate=cost(6 * tokens * width * width, 28 * tokens * width + 6 * width * width),
        name="exit_back",
    )(dq, mine, came, first, x1, x0, g2, gains)


def weight_grad_kernel(chips, aliased, info_ref, xo_ref, xp_ref, yo_ref, yp_ref, *refs):
    out_ref, turned = refs[-2], refs[-1]
    tokens, width = xo_ref.shape
    rows = width // (chips * CORES)
    core = info_ref[0]

    @pl.when(pl.program_id(0) == 0)
    def _():
        for i, x_ref in enumerate((xo_ref, xp_ref)):
            at = slice(i * tokens, (i + 1) * tokens)
            if rows % LANES == 0:
                for j in range(chips):
                    lanes = pl.ds(pl.multiple_of((2 * j + core) * rows, rows), rows)
                    turned[j * rows : (j + 1) * rows, at] = x_ref[:, lanes].astype(f32).T.astype(bf16)
            else:
                tall = x_ref[...].astype(f32).T.reshape(chips, CORES, rows, tokens)
                mine = jnp.where(core == 0, tall[:, 0], tall[:, 1])
                turned[:, at] = mine.reshape(chips * rows, tokens).astype(bf16)

    y_own, y_par = yo_ref[0], yp_ref[0]
    blocks, span = out_ref.shape[1], out_ref.shape[4]
    result = dot(turned[:, :tokens], y_own) + dot(turned[:, tokens:], y_par)
    for m in range(blocks):
        part = result[:, m * span : (m + 1) * span].astype(bf16)
        out_ref[:, m, 0] = part.reshape(chips, rows, span)


def weight_grad(info, x_own, x_par, y_own, y_par, shape, at, before=None):
    parts, tokens, width = y_own.shape
    chips = shape[0]
    row = full(x_own.shape)
    part = pl.BlockSpec((1, tokens, width), lambda s, info: (s, 0, 0))
    extra = [] if before is None else [before]
    return pl.pallas_call(
        functools.partial(weight_grad_kernel, chips, before is not None),
        out_shape=jax.ShapeDtypeStruct(shape, bf16),
        grid_spec=pltpu.PrefetchScalarGridSpec(
            num_scalar_prefetch=1,
            grid=(parts,),
            in_specs=[row, row, part, part] + [pl.BlockSpec(memory_space=pl.ANY) for _ in extra],
            out_specs=pl.BlockSpec(
                (chips, shape[1], 1, shape[3], shape[4]), lambda s, info: (0, 0, s + at, 0, 0)
            ),
            scratch_shapes=[pltpu.VMEM((x_own.shape[1] // 2, 2 * tokens), bf16)],
        ),
        input_output_aliases={} if before is None else {5: 0},
        compiler_params=params(),
        cost_estimate=cost(
            2 * parts * tokens * width * width, 5 * parts * tokens * width + 4 * tokens * width
        ),
        name="weight_grad",
    )(info, x_own, x_par, y_own, y_par, *extra)


def swap(value):
    return lax.ppermute(value, "core", [(0, 1), (1, 0)])


def line_moves(mp):
    rounds = []
    for turn in range(2):
        moves = []
        for c in range(CORES):
            for m in range(mp):
                target, slot = (1 if m in (1, 2) else 0), m // 2
                moves.append((c * mp + m, target * mp + 2 * c + (slot ^ turn)))
        rounds.append(moves)
    return rounds


def to_chips(value, mp):
    m = lax.axis_index("mp")
    slot, odd = m // 2, m % 2
    came = []
    for turn, moves in enumerate(line_moves(mp)):
        sent = jnp.where((slot ^ turn) == 0, value[0], value[1])
        came.append(lax.ppermute(sent, LINE, moves))
    return jnp.concatenate(
        [jnp.where(odd == 0, came[0], came[1]), jnp.where(odd == 0, came[1], came[0])], axis=0
    )


def from_chips(value, mp):
    m = lax.axis_index("mp")
    slot, odd = m // 2, m % 2
    half = value.shape[0] // 2
    came = []
    for turn, moves in enumerate(line_moves(mp)):
        sent = jnp.where((odd ^ turn) == 0, value[:half], value[half:])
        came.append(lax.ppermute(sent, LINE, [(b, a) for a, b in moves]))
    return jnp.stack(
        [jnp.where(slot == 0, came[0], came[1]), jnp.where(slot == 0, came[1], came[0])]
    )


def packed(*weights):
    return jnp.concatenate([w.reshape(-1, w.shape[-1]) for w in weights], axis=0)


def gathered(rows, dp, mp, parts):
    value = lax.all_gather(rows, ALL, axis=0, tiled=False)
    return value.reshape(dp, mp, parts, rows.shape[0] // parts, rows.shape[1])


def scattered(grads):
    part = lax.psum_scatter(grads, "chip", scatter_dimension=0, tiled=False)
    return lax.psum_scatter(part, "mp", scatter_dimension=0, tiled=False).astype(f32)


def body(
    chips,
    mp,
    target_ids,
    tgt_lengths,
    encoder_states,
    src_lengths,
    table,
    pos_table,
    self_query_key_value_weight,
    self_output_weight,
    cross_query_weight,
    cross_key_value_weight,
    cross_output_weight,
    feedforward_input_weight,
    feedforward_output_weight,
    norm_gains,
    norm_biases,
    out_grad,
):
    dp = chips * CORES
    n = dp * mp
    seqs, block = target_ids.shape
    assert seqs * CORES == mp == 4
    tokens = seqs * block
    width = norm_gains.shape[1]
    vocab = table.shape[1]
    feats = table.shape[0]
    rows = pos_table.shape[0]
    core, m = lax.axis_index("core"), lax.axis_index("mp")

    def split(weight):
        return weight.reshape(rows, -1, block).transpose(1, 0, 2)

    all_ids = lax.all_gather(target_ids.reshape(-1), "mp", axis=0, tiled=False)
    all_ids = lax.all_gather(all_ids, ("chip", "core"), axis=0, tiled=False)
    first = gathered(packed(pos_table, split(self_query_key_value_weight)), dp, mp, 4)
    second = gathered(
        packed(
            self_output_weight, cross_query_weight, split(cross_key_value_weight), cross_output_weight
        ),
        dp,
        mp,
        5,
    )
    sub = feedforward_input_weight.shape[1] // block
    third = gathered(
        packed(split(feedforward_input_weight), split(feedforward_output_weight)), dp, mp, 2 * sub
    )

    lengths = jnp.stack([tgt_lengths, src_lengths])
    other = swap(lengths)
    lengths = jnp.where(
        core == 0,
        jnp.concatenate([lengths, other], axis=1),
        jnp.concatenate([other, lengths], axis=1),
    )
    lengths = lax.dynamic_index_in_dim(lengths, m, axis=1, keepdims=False)
    info = jnp.stack(
        [core, lengths[0], lengths[1], core, 3 - core, 1 - core, 2 + core, jnp.zeros_like(core)]
    ).astype(i32)

    ids = all_ids.reshape(chips, CORES, mp, seqs, block)
    ids = jnp.stack([ids[:, :, 0], ids[:, :, 3], ids[:, :, 1], ids[:, :, 2]], axis=2)
    ids = ids.reshape(chips, CORES, CORES, 2, seqs, block).transpose(0, 2, 1, 4, 3, 5)
    ids = ids.reshape(n, 1, tokens)
    height = vocab // (LANES // feats)
    row, group = ids % height, ids // height
    flat_row = row.reshape(-1)

    picked = gather_tokens(table, flat_row, group)
    emb = lax.all_to_all(picked, ALL, split_axis=0, concat_axis=0, tiled=True)
    emb = emb.reshape(width, tokens)

    states = to_chips(encoder_states, mp)
    og = to_chips(out_grad.astype(bf16), mp)

    x0, x1, a, q, kv = entry(info, emb, first, norm_gains, norm_biases)
    kv_par = swap(kv)
    ckv = source_keys(states, second)
    ckv_par = swap(ckv)
    o, probs = attend(info, q, kv, kv_par, True)
    x2, c, cq = middle(o, second, x1, norm_gains, norm_biases)
    oc, cprobs = attend(info, cq, ckv, ckv_par, False)
    x3, f, g, slope, hid, g4, g4b, sums4 = feed(
        oc, second, x2, third, og, norm_gains, norm_biases
    )
    hidden_out = from_chips(hid, mp).astype(f32)

    du, g3, g3b, doc, sums3 = feed_back(g4, g4b, slope, second, x3, third, norm_gains)
    shape = (chips, mp, 2 * sub, rows, block)
    grads = weight_grad(info, f, swap(f), du, swap(du), shape, 0)
    grads = weight_grad(info, g4b, swap(g4b), g, swap(g), shape, sub, grads)
    feed_grads = scattered(grads)

    dcq, dckv_own, dckv_par = attend_back(cq, ckv, ckv_par, cprobs, oc, doc)
    dckv_came = swap(dckv_par)
    g2, g2b, do, sums2 = middle_back(dcq, second, x2, g3, norm_gains)
    enc_grad, dckv = source_back(dckv_own, dckv_came, second)
    encoder_grad = from_chips(enc_grad, mp).astype(f32)
    shape = (chips, mp, 4, rows, block)
    grads = weight_grad(info, g3b, swap(g3b), oc, swap(oc), shape, 0)
    grads = weight_grad(info, c, swap(c), dcq, swap(dcq), shape, 1, grads)
    grads = weight_grad(info, states, swap(states), dckv, swap(dckv), shape, 2, grads)
    cross_grads = scattered(grads)

    dq, dkv_own, dkv_par = attend_back(q, kv, kv_par, probs, o, do)
    dkv_came = swap(dkv_par)
    g0, dkv, sums01 = exit_back(dq, dkv_own, dkv_came, first, x1, x0, g2, norm_gains)
    sent = g0.reshape(n, feats, tokens)
    arrived = lax.all_to_all(sent, ALL, split_axis=0, concat_axis=0, tiled=True)
    grads = weight_grad(info, g2b, swap(g2b), o, swap(o), shape, 0)
    grads = weight_grad(info, a, swap(a), dq, swap(dq), shape, 1, grads)
    grads = weight_grad(info, a, swap(a), dkv, swap(dkv), shape, 2, grads)
    self_grads = scattered(grads)

    table_grad, places = scatter_tokens(arrived, flat_row, row, group, vocab, mp)

    blocks = places.reshape(CORES, feats, 2, block).transpose(0, 2, 1, 3).reshape(4, feats, block)
    blocks = jnp.stack([blocks[0], blocks[2], blocks[3], blocks[1]])
    parts = []
    for k in range(mp):
        mine = lax.dynamic_index_in_dim(blocks, (m + k) % mp, axis=0, keepdims=False)
        parts.append(
            mine if k == 0 else lax.ppermute(mine, "mp", [(i, (i + k) % mp) for i in range(mp)])
        )
    pos_grad = []
    for source in range(mp):
        value = parts[0]
        for k in range(1, mp):
            value = jnp.where((m - source) % mp == k, parts[k], value)
        pos_grad.append(value)
    pos_grad = jnp.concatenate(pos_grad, axis=0)

    sums = jnp.concatenate([sums01, sums2, sums3, sums4], axis=0)
    sums = lax.psum(sums, ALL)

    def join(parts):
        return parts.transpose(1, 0, 2)

    return (
        hidden_out,
        table_grad,
        pos_grad,
        join(self_grads[1:4]),
        self_grads[0],
        cross_grads[1],
        join(cross_grads[2:4]),
        cross_grads[0],
        join(feed_grads[:sub]).reshape(rows, -1),
        join(feed_grads[sub:]).reshape(rows, -1),
        sums[0::2],
        sums[1::2],
        encoder_grad,
    )


def solution(mesh):
    dp, mp = mesh.devices.shape
    chips = dp // CORES
    fine = Mesh(mesh.devices.reshape(chips, CORES, mp), ALL)
    both = ("chip", "core")
    placed = (
        P(both, "mp"),
        P(both),
        P(both, "mp", None),
        P(both),
        P(ALL, None),
        P(both, "mp"),
        P(both, None, "mp"),
        P(both, "mp"),
        P(both, "mp"),
        P(both, None, "mp"),
        P(both, "mp"),
        P(both, "mp"),
        P(both, "mp"),
        P(),
        P(),
        P(both, "mp", None),
    )
    return jax.shard_map(
        functools.partial(body, chips, mp),
        mesh=fine,
        in_specs=placed,
        out_specs=(
            P(both, "mp", None),
            P(ALL, None),
            P(both, "mp"),
            P(both, None, "mp"),
            P(both, "mp"),
            P(both, "mp"),
            P(both, None, "mp"),
            P(both, "mp"),
            P(both, "mp"),
            P(both, "mp"),
            P(),
            P(),
            P(both, "mp", None),
        ),
        check_vma=False,
    )
```

time: 2930 us -> 860 us (0.29)
  waiting for transfers between devices: 1630 us -> 297 us
  local copies, waits for them, and re-layouts: 422 us -> 34.6 us
  other arithmetic: 384 us -> 20.4 us
  Pallas kernels: 0 us -> 352 us
  matrix products: 283 us -> 0 us
  blocking collectives: 168 us -> 88.5 us
  starting transfers between devices: 10.8 us -> 45.3 us
    reduce_scatter x13 -> x3, waiting for transfers between devices: 1020 us -> 0.01 us  [scattered(): lax.psum_scatter(part, 'mp', scatter_dimension=0, tiled=False).astype(f32)]
    all_gather x11 -> x3, waiting for transfers between devices: 566 us -> 79.2 us  [gathered(): value = lax.all_gather(rows, ALL, axis=0, tiled=False)]
    pallas_call x0 -> x22, Pallas kernels: none -> 352 us  [the longest x1 56.7 us: scatter_tokens(): pl.pallas_call(functools.partial(scatter_kernel, groups, per_core), out_s...]
    dot_general x49 -> x0, matrix products: 283 us -> none  [the longest x4 47.9 us: one_block(): jnp.einsum('sqhd,skhd->shqk', grad_block, values, preferred_element_type=...]
    gather x2 -> x0, local copies, waits for them, and re-layouts: 251 us -> none  [body(): picked = jnp.take(table, all_ids, axis=1)]
    scatter-add x3 -> x0, other arithmetic: 230 us -> none  [body(): jnp.zeros((table.shape[0], table.shape[1]), single_float).at[:, all_ids]]
    all_gather x5 -> x2, blocking collectives: 127 us -> 22.8 us  [the longest x1 13.6 us: body(): all_ids = lax.all_gather(target_ids.reshape(-1), 'mp', axis=0, tiled=False)]
    ppermute x0 -> x31, waiting for transfers between devices: none -> 87.5 us  [the longest x20 31.9 us: swap(): return lax.ppermute(value, 'core', [(0, 1), (1, 0)])]
  transfers between devices with their start and end apart: 28 -> 42, of which waited for: 22 -> 14; matrix products, arithmetic and copies ran while one was open for 14% -> 4% of each run, Pallas kernels for 0% -> 32%
where the time goes in v1:
time: 860 us; the launch traced here: 852 us
  Pallas kernels  352 us (41%)
  waiting for transfers between devices  297 us (35%)
  blocking collectives  88.5 us (10%)
  starting transfers between devices  45.3 us (5%)
  local copies, waits for them, and re-layouts  34.6 us (4%)
  other arithmetic  20.4 us (2%)
  between operations  14.8 us (2%)
    unnamed x12, waiting for transfers between devices  106 us
    all_gather x3, waiting for transfers between devices, gathered(): value = lax.all_gather(rows, ALL, axis=0, tiled=False)  79.2 us
    psum x1, blocking collectives, body(): sums = lax.psum(sums, ALL)  65.7 us
    pallas_call x1, Pallas kernels, scatter_tokens(): pl.pallas_call(functools.partial(scatter_kernel, groups, per_core), out_s...  56.7 us
    pallas_call x8, Pallas kernels, weight_grad(): pl.pallas_call(functools.partial(weight_grad_kernel, chips, before is not...  54.9 us
    pallas_call x1, Pallas kernels, gather_tokens(): pl.pallas_call(functools.partial(gather_kernel, groups, fill), out_shape=...  45.7 us
    pallas_call x2, Pallas kernels, attend(): pl.pallas_call(functools.partial(attend_kernel, causal), out_shape=(jax.S...  43.5 us
    pallas_call x2, Pallas kernels, attend_back(): pl.pallas_call(attend_back_kernel, out_shape=(jax.ShapeDtypeStruct((1, to...  41.9 us
  transfers between devices with their start and end apart: 42, of which 14 were waited for; matrix products, arithmetic and copies ran while one was open for 4% of the time, Pallas kernels for 32%

profile of v1, /device:TPU:0, one launch (start us, length us, event | category | flops | bytes accessed | tf_op | source)
XLA Modules:
  0.0 851.8 jit_solution(10374328958190411664)
XLA Ops:
  13.0 13.6 %all-gather.4 = s32[4,1,512]{2,1,0:T(1,128)S(1)} all-gather(s32[1,1,512]{2,1,0:T(1,128)S(1)} %reshape.272), channel_id=1, replica_groups=mesh['chip'=4,'core'=2,'mp'=4] {'mp'}, dimensions={0}, use_global_device_ids=true | all-gather | bytes 10240 | tf_op jit(solution)/shard_map/all_gather | solution.py:980
  26.6 9.2 %all-gather.5 = s32[8,4,512]{2,1,0:T(4,128)S(1)} all-gather(s32[1,4,512]{2,1,0:T(4,128)S(1)} %copy.58), channel_id=2, replica_groups=mesh['chip'=4,'core'=2,'mp'=4] {'chip','core'}, dimensions={0}, use_global_device_ids=true | all-gather | bytes 73728 | tf_op jit(solution)/shard_map/all_gather | solution.py:981
  38.5 45.7 %gather_tokens.1 = bf16[32,32,512]{2,1,0:T(8,128)(2,1)} custom-call(s32[16384]{0:T(1024)} %add_select_fusion.rows_ref, s32[32,1,512]{2,1,0:T(1,128)} %and_select_fusion.1.group_ref, bf16[32,131072]{1,0:T(8,128)(2,1)} %refs_3_.1, bf16[32,131072]{1,0:T(8,128)(2,1)} %refs_3_.1, bf16[32,131072]{1,0:T(8,128)(2,1)} %refs_3_.1, bf16[32,131072]{1,0:T(8,128)(2,1)} %refs_3_.1), custom_call_target="tpu_custom_call" | custom-call | flops 4294967296 | bytes 14942208 | tf_op jit(solution)/shard_map/gather_tokens/pallas_call | solution.py:138
  99.0 23.7 %all-to-all-done = bf16[32,32,512]{2,1,0:T(8,128)(2,1)S(1)} async-done(((bf16[32,32,512]{2,1,0:T(8,128)(2,1)}), bf16[32,32,512]{2,1,0:T(8,128)(2,1)S(1)}, u32[]{:S(2)}, u32[]{:S(2)}) %all-to-all-start) | async-done | bytes 1048608 | tf_op jit(solution)/shard_map/all_to_all | solution.py:1017
  123.6 13.8 %entry.1 = (f32[512,1024]{1,0:T(8,128)}, f32[512,1024]{1,0:T(8,128)}, bf16[512,1024]{1,0:T(8,128)(2,1)}, bf16[1,512,1024]{2,1,0:T(8,128)(2,1)}, bf16[2,512,1024]{2,1,0:T(8,128)(2,1)}) custom-call(s32[8]{0:T(128)} %stack.58.info_ref, bf16[1024,512]{1,0:T(8,128)(2,1)} %bitcast.119, bf16[8,4,4,128,256]{4,3,2,1,0:T(8,128)(2,1)} %bitcast.114, ...), custom_call_target="tpu_custom_call" | custom-call | flops 3221225472 | bytes 16777216 | tf_op jit(solution)/shard_map/entry/pallas_call | solution.py:318
  142.1 48.6 %all-gather.12.cloned.1.call-done = bf16[20480,256]{1,0:T(8,128)(2,1)} async-done(((bf16[640,256]{1,0:T(8,128)(2,1)}), bf16[20480,256]{1,0:T(8,128)(2,1)}) %all-gather.12.cloned.1.call-update) | async-done | bytes 10485776 | tf_op jit(solution)/shard_map/all_gather | solution.py:937
  190.7 6.5 source_keys.1.own_ref
  203.5 29.3 %collective-permute-done.6 = bf16[256,1024]{1,0:T(8,128)(2,1)S(1)} collective-permute-done((bf16[256,1024]{1,0:T(8,128)(2,1)S(1)}, bf16[256,1024]{1,0:T(8,128)(2,1)S(1)}, u32[]{:S(2)}, u32[]{:S(2)}) %collective-permute-start.6) | collective-permute-done | bytes 524320 | tf_op jit(solution)/shard_map/ppermute | solution.py:913
  233.9 21.7 %attend.2 = (bf16[1,512,1024]{2,1,0:T(8,128)(2,1)}, bf16[16,2,512,512]{3,2,1,0:T(8,128)(2,1)}) custom-call(s32[8]{0:T(128)} %stack.58.info_ref, bf16[1,512,1024]{2,1,0:T(8,128)(2,1)} %get-tuple-element.55.q_ref, bf16[2,512,1024]{2,1,0:T(8,128)(2,1)} %get-tuple-element.56.own_ref, bf16[2,512,1024]{2,1,0:T(8,128)(2,1)} %collective-permute-done.1.par_ref), custom_call_target="tpu_custom_call" | custom-call | flops 8589934592 | bytes 16777216 | tf_op jit(solution)/shard_map/attend/pallas_call | solution.py:420
  255.6 8.4 middle.1
  265.4 21.8 %attend.3 = (bf16[1,512,1024]{2,1,0:T(8,128)(2,1)}, bf16[16,2,512,512]{3,2,1,0:T(8,128)(2,1)}) custom-call(s32[8]{0:T(128)} %stack.58.info_ref, bf16[1,512,1024]{2,1,0:T(8,128)(2,1)} %get-tuple-element.59.q_ref, bf16[2,512,1024]{2,1,0:T(8,128)(2,1)} %source_keys.1.own_ref, bf16[2,512,1024]{2,1,0:T(8,128)(2,1)} %copy-done.37), custom_call_target="tpu_custom_call" | custom-call | flops 8589934592 | bytes 16777216 | tf_op jit(solution)/shard_map/attend/pallas_call | solution.py:420
  287.2 30.6 %all-gather.14.cloned.1.call-done = bf16[32768,256]{1,0:T(8,128)(2,1)} async-done(((bf16[1024,256]{1,0:T(8,128)(2,1)}), bf16[32768,256]{1,0:T(8,128)(2,1)}) %all-gather.14.cloned.1.call-update) | async-done | bytes 16777232 | tf_op jit(solution)/shard_map/all_gather | solution.py:937
  317.7 25.9 %feed.1 = (f32[512,1024]{1,0:T(8,128)}, bf16[512,1024]{1,0:T(8,128)(2,1)}, bf16[4,512,1024]{2,1,0:T(8,128)(2,1)}, bf16[4,512,1024]{2,1,0:T(8,128)(2,1)}, bf16[51...) custom-call(bf16[1,512,1024]{2,1,0:T(8,128)(2,1)} %get-tuple-element.60.o_ref.yo_ref, ...), custom_call_target="tpu_custom_call" | custom-call | flops 9663676416 | bytes 38797312 | tf_op jit(solution)/shard_map/feed/pallas_call | solution.py:539
  343.7 24.3 %feed_back.1 = (bf16[4,512,1024]{2,1,0:T(8,128)(2,1)}, f32[512,1024]{1,0:T(8,128)}, bf16[512,1024]{1,0:T(8,128)(2,1)}, bf16[1,512,1024]{2,1,0:T(8,128)(2,1)}, f32[2,1024]{1,0:T(2,128)}) custom-call(f32[512,1024]{1,0:T(8,128)} %get-tuple-element.65.g4_ref, bf16[512,1024]{1,0:T(8,128)(2,1)} %get-tuple-element.66.g4b_ref.xo_ref, ...), custom_call_target="tpu_custom_call" | custom-call | flops 9663676416 | bytes 36700160 | tf_op jit(solution)/shard_map/feed_back/pallas_call | solution.py:620
  368.0 21.0 %attend_back.2 = (bf16[1,512,1024]{2,1,0:T(8,128)(2,1)}, bf16[2,512,1024]{2,1,0:T(8,128)(2,1)}, bf16[2,512,1024]{2,1,0:T(8,128)(2,1)}) custom-call(bf16[1,512,1024]{2,1,0:T(8,128)(2,1)} %get-tuple-element.59.q_ref, bf16[2,512,1024]{2,1,0:T(8,128)(2,1)} %source_keys.1.own_ref, bf16[2,512,1024]{2,1,0:T(8,128)(2,1)} %copy-done.37, ...), custom_call_target="tpu_custom_call" | custom-call | flops 17179869184 | bytes 16777216 | tf_op jit(solution)/shard_map/attend_back/pallas_call | solution.py:682
  395.1 6.7 source_back.1
  403.1 5.9 collective-permute-done.23.xp_ref
  421.7 6.7 weight_grad.13
  428.6 9.5 %middle_back.1 = (f32[512,1024]{1,0:T(8,128)}, bf16[512,1024]{1,0:T(8,128)(2,1)}, bf16[1,512,1024]{2,1,0:T(8,128)(2,1)}, f32[2,1024]{1,0:T(2,128)}) custom-call(bf16[1,512,1024]{2,1,0:T(8,128)(2,1)} %get-tuple-element.70.dq_ref.yo_ref, bf16[8,4,5,128,256]{4,3,2,1,0:T(8,128)(2,1)} %bitcast.108, f32[512,1024]{1,0:T(8,128)} %get-tuple-element.61.x_ref.x2_ref, ...), custom_call_target="tpu_custom_call" | custom-call | flops 2147483648 | bytes 13631488 | tf_op jit(solution)/shard_map/middle_back/pallas_call | solution.py:722
  438.0 20.9 %attend_back.3 = (bf16[1,512,1024]{2,1,0:T(8,128)(2,1)}, bf16[2,512,1024]{2,1,0:T(8,128)(2,1)}, bf16[2,512,1024]{2,1,0:T(8,128)(2,1)}) custom-call(bf16[1,512,1024]{2,1,0:T(8,128)(2,1)} %get-tuple-element.55.q_ref, bf16[2,512,1024]{2,1,0:T(8,128)(2,1)} %get-tuple-element.56.own_ref, bf16[2,512,1024]{2,1,0:T(8,128)(2,1)} %collective-permute-done.1.par_ref, ...), custom_call_target="tpu_custom_call" | custom-call | flops 17179869184 | bytes 16777216 | tf_op jit(solution)/shard_map/attend_back/pallas_call | solution.py:682
  464.7 13.8 %exit_back.1 = (bf16[1024,512]{1,0:T(8,128)(2,1)}, bf16[2,512,1024]{2,1,0:T(8,128)(2,1)}, f32[4,1024]{1,0:T(4,128)}) custom-call(bf16[1,512,1024]{2,1,0:T(8,128)(2,1)} %get-tuple-element.73.dq_ref.yo_ref, bf16[2,512,1024]{2,1,0:T(8,128)(2,1)} %get-tuple-element.74.mine_ref, bf16[2,512,1024]{2,1,0:T(8,128)(2,1)} %copy-done.10, ...), custom_call_target="tpu_custom_call" | custom-call | flops 3221225472 | bytes 20971520 | tf_op jit(solution)/shard_map/exit_back/pallas_call | solution.py:811
  479.8 5.6 collective-permute-done.17.yp_ref
  499.2 6.8 weight_grad.10
  507.8 12.0 %collective-permute-done.27.xp_ref = bf16[512,1024]{1,0:T(8,128)(2,1)S(1)} collective-permute-done((bf16[512,1024]{1,0:T(8,128)(2,1)S(1)}, bf16[512,1024]{1,0:T(8,128)(2,1)S(1)}, u32[]{:S(2)}, u32[]{:S(2)}) %collective-permute-start.27) | collective-permute-done | bytes 1048608 | tf_op jit(solution)/shard_map/ppermute | solution.py:892
  520.7 10.4 %weight_grad.14.refs_0_ = bf16[4,4,8,128,256]{4,3,2,1,0:T(8,128)(2,1)} custom-call(s32[8]{0:T(128)} %stack.58.info_ref, bf16[512,1024]{1,0:T(8,128)(2,1)} %get-tuple-element.90.xo_ref, bf16[512,1024]{1,0:T(8,128)(2,1)} %copy-done.26, bf16[4,512,1024]{2,1,0:T(8,128)(2,1)} %get-tuple-element.91.yo_ref, bf16[4,512,1024]{2,1,0:T(8,128)(2,1)} %collective-permute-done.28.yp_ref), custom_call_target="tpu_custom_call" | custom-call | flops 4294967296 | bytes 12582912 | tf_op jit(solution)/shard_map/weight_grad/pallas_call | solution.py:870
  534.2 10.2 %weight_grad.15 = bf16[4,4,8,128,256]{4,3,2,1,0:T(8,128)(2,1)} custom-call(s32[8]{0:T(128)} %stack.58.info_ref, bf16[512,1024]{1,0:T(8,128)(2,1)} %get-tuple-element.66.g4b_ref.xo_ref, bf16[512,1024]{1,0:T(8,128)(2,1)} %copy-done.20, bf16[4,512,1024]{2,1,0:T(8,128)(2,1)} %get-tuple-element.89.yo_ref, ...), custom_call_target="tpu_custom_call", output_to_operand_aliasing={{}: (5, {})} | custom-call | flops 4294967296 | bytes 12582912 | tf_op jit(solution)/shard_map/weight_grad/pallas_call | solution.py:870
  545.1 13.5 %reduce-scatter.19.cloned.1.call-done = bf16[1,4,4,128,256]{4,3,2,1,0:T(8,128)(2,1)} async-done(((bf16[4,4,4,128,256]{4,3,2,1,0:T(8,128)(2,1)}), bf16[1,4,4,128,256]{4,3,2,1,0:T(8,128)(2,1)}) %reduce-scatter.19.cloned.1.call-update) | async-done | bytes 1048592
  563.3 92.0 %reduce-scatter.23.cloned.1.call-done = bf16[1,4,8,128,256]{4,3,2,1,0:T(8,128)(2,1)} async-done(((bf16[4,4,8,128,256]{4,3,2,1,0:T(8,128)(2,1)}), bf16[1,4,8,128,256]{4,3,2,1,0:T(8,128)(2,1)}) %reduce-scatter.23.cloned.1.call-update) | async-done | bytes 2097168
  663.2 5.5 collective-permute-start.8
  675.5 22.6 %collective-permute-done.8 = bf16[256,1024]{1,0:T(8,128)(2,1)S(1)} collective-permute-done((bf16[256,1024]{1,0:T(8,128)(2,1)}, bf16[256,1024]{1,0:T(8,128)(2,1)S(1)}, u32[]{:S(2)}, u32[]{:S(2)}) %collective-permute-start.8) | collective-permute-done | bytes 524320 | tf_op jit(solution)/shard_map/ppermute | solution.py:926
  699.8 65.7 %psum.7 = f32[10,1024]{1,0:T(8,128)S(1)} all-reduce(f32[10,1024]{1,0:T(8,128)S(1)} %pad_maximum_fusion.8), channel_id=1, replica_groups=mesh['chip'=4,'core'=2,'mp'=4] {'chip','core','mp'}, use_global_device_ids=true, to_apply=%region_6.7 | all-reduce | flops 10240 | bytes 81920 | tf_op jit(solution)/shard_map/psum | solution.py:1081
  769.8 56.7 %scatter_tokens.1 = (f32[32,131072]{1,0:T(8,128)}, f32[2,32,512]{2,1,0:T(8,128)}) custom-call(s32[16384]{0:T(1024)} %add_select_fusion.rows_ref, s32[32,1,512]{2,1,0:T(1,128)} %get-tuple-element.149.row_ref, s32[32,1,512]{2,1,0:T(1,128)} %and_select_fusion.1.group_ref, bf16[32,32,512]{2,1,0:T(8,128)(2,1)} %copy-done.21), custom_call_target="tpu_custom_call" | custom-call | flops 536870912 | bytes 33161216 | tf_op jit(solution)/shard_map/scatter_tokens/pallas_call | solution.py:241
  (222 shorter events, 128.4 us)
Async XLA Ops:
  7.2 115.5 %all-gather.10.cloned.1.call-start = ((), (), s32[]{:S(2)}) async-start(), calls=%async_computation.11 | async-start | bytes 8650752 | tf_op jit(solution)/shard_map/all_gather | solution.py:937
  9.0 181.7 %all-gather.12.cloned.1.call-start = ((), (), s32[]{:S(2)}) async-start(), calls=%async_computation.12 | async-start | bytes 10813440 | tf_op jit(solution)/shard_map/all_gather | solution.py:937
  11.6 306.1 %all-gather.14.cloned.1.call-start = ((), (), s32[]{:S(2)}) async-start(), calls=%async_computation.13 | async-start | bytes 17301504 | tf_op jit(solution)/shard_map/all_gather | solution.py:937
  84.2 38.5 %all-to-all-start = ((bf16[32,32,512]{2,1,0:T(8,128)(2,1)}), bf16[32,32,512]{2,1,0:T(8,128)(2,1)S(1)}, u32[]{:S(2)}, u32[]{:S(2)}) async-start(bf16[32,32,512]{2,1,0:T(8,128)(2,1)} %gather_tokens.1), calls=%async_computation | async-start | bytes 2097152 | tf_op jit(solution)/shard_map/all_to_all | solution.py:1017
  87.6 456.8 %reduce-scatter.21.cloned.1.call-start = ((), (), s32[]{:S(2)}) async-start(), calls=%async_computation.15 | async-start | bytes 5242880
  89.0 50.7 %collective-permute-start.2 = (bf16[256,1024]{1,0:T(8,128)(2,1)}, bf16[256,1024]{1,0:T(8,128)(2,1)}, u32[]{:S(2)}, u32[]{:S(2)}) collective-permute-start(bf16[256,1024]{1,0:T(8,128)(2,1)} %get-tuple-element.165), channel_id=1, source_target_pairs={{0,0},{1,4},{2,5},{3,1},{4,2},{5,6},{6,7},{7,3},{8,8},{9,12},{10,1... | collective-permute-start | bytes 1572872 | tf_op jit(solution)/shard_map/ppermute | solution.py:913
  94.4 45.3 %collective-permute-start.3 = (bf16[256,1024]{1,0:T(8,128)(2,1)}, bf16[256,1024]{1,0:T(8,128)(2,1)}, u32[]{:S(2)}, u32[]{:S(2)}) collective-permute-start(bf16[256,1024]{1,0:T(8,128)(2,1)} %get-tuple-element.166), channel_id=1, source_target_pairs={{0,1},{1,5},{2,4},{3,0},{4,3},{5,7},{6,6},{7,2},{8,9},{9,13},{10,1... | collective-permute-start | bytes 1572872 | tf_op jit(solution)/shard_map/ppermute | solution.py:913
  137.4 96.5 %collective-permute-start.1 = (bf16[2,512,1024]{2,1,0:T(8,128)(2,1)}, bf16[2,512,1024]{2,1,0:T(8,128)(2,1)}, u32[]{:S(2)}, u32[]{:S(2)}) collective-permute-start(bf16[2,512,1024]{2,1,0:T(8,128)(2,1)} %get-tuple-element.56.own_ref), channel_id=1, source_target_pairs={{0,4},{4,0},{1,5},{5,1},{2,6},{6,2},{3,7},{7,3},{8,12},{12,8},{9,1... | collective-permute-start | bytes 6291464 | tf_op jit(solution)/shard_map/ppermute | solution.py:892
  197.2 66.8 %collective-permute-start.4 = (bf16[2,512,1024]{2,1,0:T(8,128)(2,1)}, bf16[2,512,1024]{2,1,0:T(8,128)(2,1)S(1)}, u32[]{:S(2)}, u32[]{:S(2)}) collective-permute-start(bf16[2,512,1024]{2,1,0:T(8,128)(2,1)} %source_keys.1.own_ref), channel_id=1, source_target_pairs={{0,4},{4,0},{1,5},{5,1},{2,6},{6,2},{3,7},{7,3},{8,12},{12,8},{9,1... | collective-permute-start | bytes 6291464 | tf_op jit(solution)/shard_map/ppermute | solution.py:892
  198.2 34.5 %collective-permute-start.6 = (bf16[256,1024]{1,0:T(8,128)(2,1)S(1)}, bf16[256,1024]{1,0:T(8,128)(2,1)S(1)}, u32[]{:S(2)}, u32[]{:S(2)}) collective-permute-start(bf16[256,1024]{1,0:T(8,128)(2,1)S(1)} %get-tuple-element.162), channel_id=1, source_target_pairs={{0,1},{1,5},{2,4},{3,0},{4,3},{5,7},{6,6},{7,2},{8,9},{9,13},{10,1... | collective-permute-start | bytes 1572872 | tf_op jit(solution)/shard_map/ppermute | solution.py:913
  389.3 13.5 %collective-permute-start.24 = (bf16[1,512,1024]{2,1,0:T(8,128)(2,1)S(1)}, bf16[1,512,1024]{2,1,0:T(8,128)(2,1)}, u32[]{:S(2)}, u32[]{:S(2)}) collective-permute-start(bf16[1,512,1024]{2,1,0:T(8,128)(2,1)S(1)} %copy-done.5), channel_id=1, source_target_pairs={{0,4},{4,0},{1,5},{5,1},{2,6},{6,2},{3,7},{7,3},{8,12},{12,8},{9,1... | collective-permute-start | bytes 3145736 | tf_op jit(solution)/shard_map/ppermute | solution.py:892
  401.7 17.7 %collective-permute-start.20 = (bf16[2,512,1024]{2,1,0:T(8,128)(2,1)}, bf16[2,512,1024]{2,1,0:T(8,128)(2,1)S(1)}, u32[]{:S(2)}, u32[]{:S(2)}) collective-permute-start(bf16[2,512,1024]{2,1,0:T(8,128)(2,1)} %get-tuple-element.86.yo_ref), channel_id=1, source_target_pairs={{0,4},{4,0},{1,5},{5,1},{2,6},{6,2},{3,7},{7,3},{8,12},{12,8},{9,1... | collective-permute-start | bytes 6291464 | tf_op jit(solution)/shard_map/ppermute | solution.py:892
  402.3 12.0 %collective-permute-start.21 = (bf16[512,1024]{1,0:T(8,128)(2,1)S(1)}, bf16[512,1024]{1,0:T(8,128)(2,1)}, u32[]{:S(2)}, u32[]{:S(2)}) collective-permute-start(bf16[512,1024]{1,0:T(8,128)(2,1)S(1)} %copy-done.15), channel_id=1, source_target_pairs={{0,4},{4,0},{1,5},{5,1},{2,6},{6,2},{3,7},{7,3},{8,12},{12,8},{9,1... | collective-permute-start | bytes 3145736 | tf_op jit(solution)/shard_map/ppermute | solution.py:892
  402.6 11.7 %collective-permute-start.22 = (bf16[1,512,1024]{2,1,0:T(8,128)(2,1)S(1)}, bf16[1,512,1024]{2,1,0:T(8,128)(2,1)}, u32[]{:S(2)}, u32[]{:S(2)}) collective-permute-start(bf16[1,512,1024]{2,1,0:T(8,128)(2,1)S(1)} %copy-done.4), channel_id=1, source_target_pairs={{0,4},{4,0},{1,5},{5,1},{2,6},{6,2},{3,7},{7,3},{8,12},{12,8},{9,1... | collective-permute-start | bytes 3145736 | tf_op jit(solution)/shard_map/ppermute | solution.py:892
  402.8 16.7 %collective-permute-start.18 = (bf16[512,1024]{1,0:T(8,128)(2,1)S(1)}, bf16[512,1024]{1,0:T(8,128)(2,1)S(1)}, u32[]{:S(2)}, u32[]{:S(2)}) collective-permute-start(bf16[512,1024]{1,0:T(8,128)(2,1)S(1)} %copy-done), channel_id=1, source_target_pairs={{0,4},{4,0},{1,5},{5,1},{2,6},{6,2},{3,7},{7,3},{8,12},{12,8},{9,1... | collective-permute-start | bytes 3145736 | tf_op jit(solution)/shard_map/ppermute | solution.py:892
  428.5 130.1 %reduce-scatter.19.cloned.1.call-start = ((), (), s32[]{:S(2)}) async-start(), calls=%async_computation.14 | async-start | bytes 5242880
  478.5 19.3 %collective-permute-start.14 = (bf16[2,512,1024]{2,1,0:T(8,128)(2,1)}, bf16[2,512,1024]{2,1,0:T(8,128)(2,1)S(1)}, u32[]{:S(2)}, u32[]{:S(2)}) collective-permute-start(bf16[2,512,1024]{2,1,0:T(8,128)(2,1)} %get-tuple-element.82.yo_ref), channel_id=1, source_target_pairs={{0,4},{4,0},{1,5},{5,1},{2,6},{6,2},{3,7},{7,3},{8,12},{12,8},{9,1... | collective-permute-start | bytes 6291464 | tf_op jit(solution)/shard_map/ppermute | solution.py:892
  479.3 12.4 %collective-permute-start.13 = (bf16[512,1024]{1,0:T(8,128)(2,1)S(1)}, bf16[512,1024]{1,0:T(8,128)(2,1)S(1)}, u32[]{:S(2)}, u32[]{:S(2)}) collective-permute-start(bf16[512,1024]{1,0:T(8,128)(2,1)S(1)} %copy-done.1), channel_id=1, source_target_pairs={{0,4},{4,0},{1,5},{5,1},{2,6},{6,2},{3,7},{7,3},{8,12},{12,8},{9,1... | collective-permute-start | bytes 3145736 | tf_op jit(solution)/shard_map/ppermute | solution.py:892
  479.5 12.1 %collective-permute-start.15 = (bf16[1,512,1024]{2,1,0:T(8,128)(2,1)S(1)}, bf16[1,512,1024]{2,1,0:T(8,128)(2,1)}, u32[]{:S(2)}, u32[]{:S(2)}) collective-permute-start(bf16[1,512,1024]{2,1,0:T(8,128)(2,1)S(1)} %copy-done.6), channel_id=1, source_target_pairs={{0,4},{4,0},{1,5},{5,1},{2,6},{6,2},{3,7},{7,3},{8,12},{12,8},{9,1... | collective-permute-start | bytes 3145736 | tf_op jit(solution)/shard_map/ppermute | solution.py:892
  506.0 149.3 %reduce-scatter.23.cloned.1.call-start = ((), (), s32[]{:S(2)}) async-start(), calls=%async_computation.16 | async-start | bytes 10485760
  506.0 14.7 %collective-permute-start.28 = (bf16[4,512,1024]{2,1,0:T(8,128)(2,1)}, bf16[4,512,1024]{2,1,0:T(8,128)(2,1)}, u32[]{:S(2)}, u32[]{:S(2)}) collective-permute-start(bf16[4,512,1024]{2,1,0:T(8,128)(2,1)} %get-tuple-element.91.yo_ref), channel_id=1, source_target_pairs={{0,4},{4,0},{1,5},{5,1},{2,6},{6,2},{3,7},{7,3},{8,12},{12,8},{9,1... | collective-permute-start | bytes 12582920 | tf_op jit(solution)/shard_map/ppermute | solution.py:892
  506.4 24.8 %collective-permute-start.26 = (bf16[4,512,1024]{2,1,0:T(8,128)(2,1)}, bf16[4,512,1024]{2,1,0:T(8,128)(2,1)S(1)}, u32[]{:S(2)}, u32[]{:S(2)}) collective-permute-start(bf16[4,512,1024]{2,1,0:T(8,128)(2,1)} %get-tuple-element.89.yo_ref), channel_id=1, source_target_pairs={{0,4},{4,0},{1,5},{5,1},{2,6},{6,2},{3,7},{7,3},{8,12},{12,8},{9,1... | collective-permute-start | bytes 12582920 | tf_op jit(solution)/shard_map/ppermute | solution.py:892
  507.2 12.6 %collective-permute-start.27 = (bf16[512,1024]{1,0:T(8,128)(2,1)S(1)}, bf16[512,1024]{1,0:T(8,128)(2,1)S(1)}, u32[]{:S(2)}, u32[]{:S(2)}) collective-permute-start(bf16[512,1024]{1,0:T(8,128)(2,1)S(1)} %copy-done.25), channel_id=1, source_target_pairs={{0,4},{4,0},{1,5},{5,1},{2,6},{6,2},{3,7},{7,3},{8,12},{12,8},{9,1... | collective-permute-start | bytes 3145736 | tf_op jit(solution)/shard_map/ppermute | solution.py:892
  507.5 23.6 %collective-permute-start.25 = (bf16[512,1024]{1,0:T(8,128)(2,1)S(1)}, bf16[512,1024]{1,0:T(8,128)(2,1)S(1)}, u32[]{:S(2)}, u32[]{:S(2)}) collective-permute-start(bf16[512,1024]{1,0:T(8,128)(2,1)S(1)} %copy-done.2), channel_id=1, source_target_pairs={{0,4},{4,0},{1,5},{5,1},{2,6},{6,2},{3,7},{7,3},{8,12},{12,8},{9,1... | collective-permute-start | bytes 3145736 | tf_op jit(solution)/shard_map/ppermute | solution.py:892
  544.3 292.5 %reduce-scatter.15.cloned.1.call-start = ((), (), s32[]{:S(2)}) async-start(), calls=%async_computation.9 | async-start | bytes 1310720 | tf_op jit(solution)/shard_map/reduce_scatter | solution.py:943
  545.1 293.7 %reduce-scatter.13.cloned.1.call-start = ((), (), s32[]{:S(2)}) async-start(), calls=%async_computation.8 | async-start | bytes 1310720 | tf_op jit(solution)/shard_map/reduce_scatter | solution.py:943
  558.6 210.2 %all-to-all-start.1 = ((bf16[32,32,512]{2,1,0:T(8,128)(2,1)}), bf16[32,32,512]{2,1,0:T(8,128)(2,1)S(1)}, u32[]{:S(2)}, u32[]{:S(2)}) async-start(bf16[32,32,512]{2,1,0:T(8,128)(2,1)} %bitcast.29), calls=%async_computation.1 | async-start | bytes 2097152 | tf_op jit(solution)/shard_map/all_to_all | solution.py:1056
  563.2 278.7 %reduce-scatter.17.cloned.1.call-start = ((), (), s32[]{:S(2)}) async-start(), calls=%async_computation.10 | async-start | bytes 2621440 | tf_op jit(solution)/shard_map/reduce_scatter | solution.py:943
  661.5 14.0 %collective-permute-start.7 = (bf16[256,1024]{1,0:T(8,128)(2,1)}, bf16[256,1024]{1,0:T(8,128)(2,1)S(1)}, u32[]{:S(2)}, u32[]{:S(2)}) collective-permute-start(bf16[256,1024]{1,0:T(8,128)(2,1)} %get-tuple-element.157), channel_id=1, source_target_pairs={{0,0},{4,1},{5,2},{1,3},{2,4},{6,5},{7,6},{3,7},{8,8},{12,9},{13,1... | collective-permute-start | bytes 1572872 | tf_op jit(solution)/shard_map/ppermute | solution.py:926
  663.2 35.0 %collective-permute-start.8 = (bf16[256,1024]{1,0:T(8,128)(2,1)}, bf16[256,1024]{1,0:T(8,128)(2,1)S(1)}, u32[]{:S(2)}, u32[]{:S(2)}) collective-permute-start(bf16[256,1024]{1,0:T(8,128)(2,1)} %get-tuple-element.158), channel_id=1, source_target_pairs={{1,0},{5,1},{4,2},{0,3},{3,4},{7,5},{6,6},{2,7},{9,8},{13,9},{12,1... | collective-permute-start | bytes 1572872 | tf_op jit(solution)/shard_map/ppermute | solution.py:926
  669.8 96.9 %collective-permute-start.29 = (bf16[256,1024]{1,0:T(8,128)(2,1)}, bf16[256,1024]{1,0:T(8,128)(2,1)S(1)}, u32[]{:S(2)}, u32[]{:S(2)}) collective-permute-start(bf16[256,1024]{1,0:T(8,128)(2,1)} %get-tuple-element.153), channel_id=1, source_target_pairs={{0,0},{4,1},{5,2},{1,3},{2,4},{6,5},{7,6},{3,7},{8,8},{12,9},{13,1... | collective-permute-start | bytes 1572872 | tf_op jit(solution)/shard_map/ppermute | solution.py:926
  671.5 96.0 %collective-permute-start.30 = (bf16[256,1024]{1,0:T(8,128)(2,1)}, bf16[256,1024]{1,0:T(8,128)(2,1)}, u32[]{:S(2)}, u32[]{:S(2)}) collective-permute-start(bf16[256,1024]{1,0:T(8,128)(2,1)} %get-tuple-element.154), channel_id=1, source_target_pairs={{1,0},{5,1},{4,2},{0,3},{3,4},{7,5},{6,6},{2,7},{9,8},{13,9},{12,1... | collective-permute-start | bytes 1572872 | tf_op jit(solution)/shard_map/ppermute | solution.py:926
  (48 other events, 242.3 us)
Sparse Core Ops, SparseCore 0:
  11.5 80.0 all-gather.9
  95.1 95.5 all-gather.11
  193.7 124.0 all-gather.13
  428.6 50.8 reduce-scatter.20
  506.1 52.4 reduce-scatter.18
  562.1 93.1 reduce-scatter.22
  657.7 41.7 reduce-scatter.14
  701.8 40.7 reduce-scatter.12
  744.9 44.9 reduce-scatter.16

commit v2 on v1

--- a/solution.py
+++ b/solution.py
@@ -33,8 +33,8 @@
     return pltpu.CompilerParams(vmem_limit_bytes=mib << 20)
 
 
-def cost(flops, moved, trans=0):
-    return pl.CostEstimate(flops=int(flops), bytes_accessed=int(moved), transcendentals=int(trans))
+def cost(microseconds):
+    return pl.CostEstimate(flops=0, bytes_accessed=int(microseconds * 3.2e6), transcendentals=0)
 
 
 def normed(values):
@@ -54,31 +54,78 @@
     return back, gain_grad, bias_grad
 
 
-def columns(w_ref, m):
-    block = w_ref[:, pl.ds(m, 1)]
-    return block.reshape(block.shape[0] * block.shape[3], block.shape[4])
-
-
-def whole_weight(w_ref):
-    parts = [columns(w_ref, m) for m in range(w_ref.shape[1])]
+def in_order(pieces, info_ref):
+    for bit, place in ((0, 0), (1, 7), (2, 8)):
+        far = info_ref[place] == 1
+        turned = []
+        for i, piece in enumerate(pieces):
+            turned.append(jnp.where(far, pieces[i ^ (1 << bit)], piece))
+        pieces = turned
+    return pieces
+
+
+def joined(blocks, info_ref):
+    flat = [b.reshape(-1, b.shape[-1]) for b in blocks]
+    return flat[0] if len(flat) == 1 else jnp.concatenate(in_order(flat, info_ref), axis=0)
+
+
+def columns(w_refs, m, info_ref):
+    return joined([w[:, pl.ds(m, 1)] for w in w_refs], info_ref)
+
+
+def whole_weight(w_refs, info_ref):
+    parts = [columns(w_refs, m, info_ref) for m in range(w_refs[0].shape[1])]
     return jnp.concatenate(parts, axis=1)
 
 
-def project(x, w_ref, store):
-    width = w_ref.shape[4]
+def project(x, w_refs, info_ref, store):
+    width = w_refs[0].shape[4]
 
     def step(m, carry):
-        store(pl.multiple_of(m * width, width), dot(x, columns(w_ref, m)))
+        store(pl.multiple_of(m * width, width), dot(x, columns(w_refs, m, info_ref)))
         return carry
 
-    lax.fori_loop(0, w_ref.shape[1], step, 0)
-
-
-def weight_spec(weights, index):
-    shape = weights.shape
-    return pl.BlockSpec(
-        (shape[0], shape[1], 1, shape[3], shape[4]), lambda *a: (0, 0, index(a[0]), 0, 0)
-    )
+    lax.fori_loop(0, w_refs[0].shape[1], step, 0)
+
+
+def weight_specs(weights, index):
+    return [
+        pl.BlockSpec(
+            (w.shape[0], w.shape[1], 1, w.shape[3], w.shape[4]),
+            lambda s, info, skip=skip: (0, 0, index(s) + skip, 0, 0),
+        )
+        for w, skip in weights
+    ]
+
+
+def call(kernel, info, grid, operands, outs, scratch=(), mib=56, **others):
+    arrays, specs, sizes = [], [], []
+    for value, spec in operands:
+        group = isinstance(value, (list, tuple))
+        sizes.append(len(value) if group else None)
+        arrays.extend([w for w, _ in value] if group else [value])
+        specs.extend(spec if group else [spec])
+
+    def body(info_ref, *refs):
+        given, rest, at = [], refs, 0
+        for size in sizes:
+            given.append(refs[at] if size is None else list(refs[at : at + size]))
+            at += 1 if size is None else size
+        kernel(info_ref, *given, *rest[at:])
+
+    return pl.pallas_call(
+        body,
+        out_shape=[o for o, _ in outs],
+        grid_spec=pltpu.PrefetchScalarGridSpec(
+            num_scalar_prefetch=1,
+            grid=grid,
+            in_specs=specs,
+            out_specs=[o for _, o in outs],
+            scratch_shapes=list(scratch),
+        ),
+        compiler_params=params(mib),
+        **others,
+    )(info, *arrays)
 
 
 def full(shape):
@@ -149,7 +196,7 @@
             scratch_shapes=[pltpu.VMEM((height, LANES), f32), pltpu.VMEM((tokens, LANES), f32)],
         ),
         compiler_params=params(),
-        cost_estimate=cost(4 * vocab * LANES * 64, 2 * feats * vocab + 400 * n * tokens),
+        cost_estimate=cost(45),
         name="gather_tokens",
     )(rows, group, *([table] * groups))
 
@@ -264,13 +311,13 @@
             ],
         ),
         compiler_params=params(),
-        cost_estimate=cost(n * tokens * LANES * 256, 4 * feats * vocab + 1000 * n * tokens),
+        cost_estimate=cost(57),
         name="scatter_tokens",
     )(rows, row, group, grads)
 
 
 def entry_kernel(
-    info_ref, emb_ref, pos_a, pos_b, w_ref, gain_ref, bias_ref, x0_ref, x1_ref, a_ref, q_ref, kv_ref
+    info_ref, emb_ref, pos_a, pos_b, wq_ref, wkv_ref, gain_ref, bias_ref, x0_ref, x1_ref, a_ref, q_ref, kv_ref
 ):
     step = pl.program_id(0)
     half = x0_ref.shape[0] // 2
@@ -279,7 +326,7 @@
     def _():
         for i, pos in enumerate((pos_a, pos_b)):
             at = slice(i * half, (i + 1) * half)
-            places = pos[...].reshape(pos.shape[0] * pos.shape[3], pos.shape[4])
+            places = joined([p[...] for p in pos], info_ref)
             x0 = (emb_ref[:, at].astype(f32) * 32.0 + places.astype(f32)).T
             x1 = normed(x0)[0] * gain_ref[0:1] + bias_ref[0:1]
             a = normed(x1)[0] * gain_ref[1:2] + bias_ref[1:2]
@@ -288,86 +335,115 @@
             a_ref[at] = a.astype(bf16)
 
     x = a_ref[...]
+    span = wq_ref[0].shape[4]
 
     @pl.when(step == 0)
     def _():
         def store(at, y):
-            q_ref[0, :, pl.ds(at, w_ref.shape[4])] = (y * HEAD_DIM**-0.5).astype(bf16)
-
-        project(x, w_ref, store)
+            q_ref[0, :, pl.ds(at, span)] = (y * HEAD_DIM**-0.5).astype(bf16)
+
+        project(x, wq_ref, info_ref, store)
 
     @pl.when(step > 0)
     def _():
         def store(at, y):
-            kv_ref[0, :, pl.ds(at, w_ref.shape[4])] = y.astype(bf16)
-
-        project(x, w_ref, store)
+            kv_ref[0, :, pl.ds(at, span)] = y.astype(bf16)
+
+        project(x, wkv_ref, info_ref, store)
 
 
 def entry(info, emb, first, gains, biases):
     width, tokens = emb.shape
-    half = tokens // 2
-    shape = first.shape
-
-    def pos_spec(i):
-        return pl.BlockSpec(
-            (shape[0], 1, 1, shape[3], shape[4]), lambda s, info, i=i: (0, info[3 + i], 0, 0, 0)
-        )
-
+    wq, wkv = first
+
+    def pos_specs(i):
+        return [
+            pl.BlockSpec(
+                (w.shape[0], 1, 1, w.shape[3], w.shape[4]),
+                lambda s, info, skip=skip: (0, info[3 + i], skip, 0, 0),
+            )
+            for w, skip in wq
+        ]
+
+    row = full((tokens, width))
     rows = jax.ShapeDtypeStruct((tokens, width), f32)
-    return pl.pallas_call(
+    return call(
         entry_kernel,
-        out_shape=(
-            rows,
-            rows,
-            jax.ShapeDtypeStruct((tokens, width), bf16),
-            jax.ShapeDtypeStruct((1, tokens, width), bf16),
-            jax.ShapeDtypeStruct((2, tokens, width), bf16),
-        ),
-        grid_spec=pltpu.PrefetchScalarGridSpec(
-            num_scalar_prefetch=1,
-            grid=(3,),
-            in_specs=[
-                full(emb.shape),
-                pos_spec(0),
-                pos_spec(1),
-                weight_spec(first, lambda s: s + 1),
-                full(gains.shape),
-                full(biases.shape),
-            ],
-            out_specs=(
-                full((tokens, width)),
-                full((tokens, width)),
-                full((tokens, width)),
-                full((1, tokens, width)),
+        info,
+        (3,),
+        [
+            (emb, full(emb.shape)),
+            (wq, pos_specs(0)),
+            (wq, pos_specs(1)),
+            (wq, weight_specs(wq, lambda s: 1)),
+            (wkv, weight_specs(wkv, lambda s: jnp.maximum(s - 1, 0))),
+            (gains, full(gains.shape)),
+            (biases, full(biases.shape)),
+        ],
+        [
+            (rows, row),
+            (rows, row),
+            (jax.ShapeDtypeStruct((tokens, width), bf16), row),
+            (jax.ShapeDtypeStruct((1, tokens, width), bf16), full((1, tokens, width))),
+            (
+                jax.ShapeDtypeStruct((2, tokens, width), bf16),
                 pl.BlockSpec((1, tokens, width), lambda s, info: (jnp.maximum(s - 1, 0), 0, 0)),
             ),
-        ),
-        compiler_params=params(),
-        cost_estimate=cost(6 * tokens * width * width, 20 * tokens * width + 6 * width * width),
+        ],
+        cost_estimate=cost(15),
         name="entry",
-    )(info, emb, first, first, first, gains, biases)
-
-
-def source_kernel(x_ref, w_ref, kv_ref):
+    )
+
+
+def slots(pair, info_ref):
+    odd = info_ref[9] == 1
+    one, two = pair[0][...], pair[1][...]
+    return jnp.where(odd, two, one), jnp.where(odd, one, two)
+
+
+def put_slots(pair, info_ref, values):
+    for odd in range(2):
+
+        @pl.when(info_ref[9] == odd)
+        def _():
+            pair[odd][...] = values[0].astype(bf16)
+            pair[1 - odd][...] = values[1].astype(bf16)
+
+
+def source_kernel(info_ref, came_a, came_b, w_refs, x_ref, kv_ref):
+    @pl.when(pl.program_id(0) == 0)
+    def _():
+        half = came_a.shape[0]
+        x_ref[:half], x_ref[half:] = slots((came_a, came_b), info_ref)
+
     def store(at, y):
-        kv_ref[0, :, pl.ds(at, w_ref.shape[4])] = y.astype(bf16)
-
-    project(x_ref[...], w_ref, store)
-
-
-def source_keys(states, second):
-    tokens, width = states.shape
-    return pl.pallas_call(
+        kv_ref[0, :, pl.ds(at, w_refs[0].shape[4])] = y.astype(bf16)
+
+    project(x_ref[...], w_refs, info_ref, store)
+
+
+def source_keys(info, came, weights):
+    half, width = came[0].shape
+    tokens = 2 * half
+    return call(
         source_kernel,
-        out_shape=jax.ShapeDtypeStruct((2, tokens, width), bf16),
-        grid=(2,),
-        in_specs=[full(states.shape), weight_spec(second, lambda s: s + 2)],
-        out_specs=pl.BlockSpec((1, tokens, width), lambda s: (s, 0, 0)),
-        compiler_params=params(),
-        cost_estimate=cost(4 * tokens * width * width, 6 * tokens * width + 4 * width * width),
+        info,
+        (2,),
+        [
+            (came[0], full((half, width))),
+            (came[1], full((half, width))),
+            (weights, weight_specs(weights, lambda s: s)),
+        ],
+        [
+            (jax.ShapeDtypeStruct((tokens, width), bf16), full((tokens, width))),
+            (
+                jax.ShapeDtypeStruct((2, tokens, width), bf16),
+                pl.BlockSpec((1, tokens, width), lambda s, info: (s, 0, 0)),
+            ),
+        ],
+        cost_estimate=cost(8),
         name="source_keys",
-    )(states, second)
+    )
 
 
 def attend_kernel(causal, info_ref, q_ref, own_ref, par_ref, o_ref, p_ref, hide):
@@ -434,143 +510,126 @@
             scratch_shapes=[pltpu.VMEM((2, tokens, tokens), f32)],
         ),
         compiler_params=params(),
-        cost_estimate=cost(
-            32 * tokens * tokens * width, 4 * heads * tokens * tokens, 2 * heads * tokens * tokens
-        ),
+        cost_estimate=cost(22),
         name="attend",
     )(info, q, own, par)
 
 
-def middle_kernel(o_ref, w_ref, x_ref, wq_ref, gain_ref, bias_ref, x2_ref, c_ref, q_ref):
-    x2 = x_ref[...] + dot(o_ref[0], whole_weight(w_ref), NT)
+def middle_kernel(info_ref, o_ref, w_ref, x_ref, wq_ref, gain_ref, bias_ref, x2_ref, c_ref, q_ref):
+    x2 = x_ref[...] + dot(o_ref[0], whole_weight(w_ref, info_ref), NT)
     x2_ref[...] = x2
     c = (normed(x2)[0] * gain_ref[2:3] + bias_ref[2:3]).astype(bf16)
     c_ref[...] = c
 
     def store(at, y):
-        q_ref[0, :, pl.ds(at, wq_ref.shape[4])] = (y * HEAD_DIM**-0.5).astype(bf16)
-
-    project(c, wq_ref, store)
-
-
-def middle(o, second, x1, gains, biases):
+        q_ref[0, :, pl.ds(at, wq_ref[0].shape[4])] = (y * HEAD_DIM**-0.5).astype(bf16)
+
+    project(c, wq_ref, info_ref, store)
+
+
+def middle(info, o, weights, x1, gains, biases):
     _, tokens, width = o.shape
-    return pl.pallas_call(
+    row = full((tokens, width))
+    return call(
         middle_kernel,
-        out_shape=(
-            jax.ShapeDtypeStruct((tokens, width), f32),
-            jax.ShapeDtypeStruct((tokens, width), bf16),
-            jax.ShapeDtypeStruct((1, tokens, width), bf16),
-        ),
-        grid=(1,),
-        in_specs=[
-            full(o.shape),
-            weight_spec(second, lambda s: 0),
-            full(x1.shape),
-            weight_spec(second, lambda s: 1),
-            full(gains.shape),
-            full(biases.shape),
-        ],
-        out_specs=(full((tokens, width)), full((tokens, width)), full((1, tokens, width))),
-        compiler_params=params(),
-        cost_estimate=cost(4 * tokens * width * width, 14 * tokens * width + 4 * width * width),
+        info,
+        (1,),
+        [
+            (o, full(o.shape)),
+            (weights, weight_specs(weights, lambda s: 0)),
+            (x1, row),
+            (weights, weight_specs(weights, lambda s: 1)),
+            (gains, full(gains.shape)),
+            (biases, full(biases.shape)),
+        ],
+        [
+            (jax.ShapeDtypeStruct((tokens, width), f32), row),
+            (jax.ShapeDtypeStruct((tokens, width), bf16), row),
+            (jax.ShapeDtypeStruct((1, tokens, width), bf16), full((1, tokens, width))),
+        ],
+        cost_estimate=cost(9),
         name="middle",
-    )(o, second, x1, second, gains, biases)
+    )
 
 
 def feed_kernel(
+    info_ref,
     o_ref,
     wo_ref,
     x_ref,
     w1_ref,
     w2_ref,
-    og_ref,
     gain_ref,
     bias_ref,
     x3_ref,
     f_ref,
     g_ref,
     slope_ref,
-    hid_ref,
-    g4_ref,
-    g4b_ref,
-    sums_ref,
-    total,
+    x4_ref,
 ):
     step = pl.program_id(0)
 
     @pl.when(step == 0)
     def _():
-        x3 = x_ref[...] + dot(o_ref[0], whole_weight(wo_ref), NT)
+        x3 = x_ref[...] + dot(o_ref[0], whole_weight(wo_ref, info_ref), NT)
         x3_ref[...] = x3
         f_ref[...] = (normed(x3)[0] * gain_ref[3:4] + bias_ref[3:4]).astype(bf16)
-        total[...] = x3
+        x4_ref[...] = x3
 
     def store(at, u):
         bell = 0.5 + 0.5 * lax.erf(u * 0.7071067811865476)
-        lanes = pl.ds(at, w1_ref.shape[4])
+        lanes = pl.ds(at, w1_ref[0].shape[4])
         g_ref[0, :, lanes] = (u * bell).astype(bf16)
         slope = bell + u * (0.3989422804014327 * jnp.exp(-0.5 * u * u))
         slope_ref[0, :, lanes] = slope.astype(bf16)
 
-    project(f_ref[...], w1_ref, store)
-    total[...] += dot(g_ref[0], whole_weight(w2_ref), NT)
-
-    @pl.when(step == pl.num_programs(0) - 1)
-    def _():
-        x4 = total[...]
-        grad = og_ref[...].astype(f32)
-        hid_ref[...] = (normed(x4)[0] * gain_ref[4:5] + bias_ref[4:5]).astype(hid_ref.dtype)
-        g4, gain_grad, bias_grad = norm_back(x4, gain_ref[4:5], grad)
-        g4_ref[...] = g4
-        g4b_ref[...] = g4.astype(bf16)
-        sums_ref[0:1] = gain_grad
-        sums_ref[1:2] = bias_grad
-
-
-def feed(o, second, x2, third, og, gains, biases):
+    project(f_ref[...], w1_ref, info_ref, store)
+    x4_ref[...] += dot(g_ref[0], whole_weight(w2_ref, info_ref), NT)
+
+
+def feed(info, o, wo, x2, w1, w2, gains, biases, slabs):
     _, tokens, width = o.shape
-    blocks = third.shape[2] // 2
+    blocks = slabs
     row = full((tokens, width))
-    part = pl.BlockSpec((1, tokens, width), lambda s: (s, 0, 0))
+    part = pl.BlockSpec((1, tokens, width), lambda s, info: (s, 0, 0))
     wide = jax.ShapeDtypeStruct((tokens, width), f32)
     slim = jax.ShapeDtypeStruct((tokens, width), bf16)
     many = jax.ShapeDtypeStruct((blocks, tokens, width), bf16)
-    return pl.pallas_call(
+    return call(
         feed_kernel,
-        out_shape=(wide, slim, many, many, slim, wide, slim, jax.ShapeDtypeStruct((2, width), f32)),
-        grid=(blocks,),
-        in_specs=[
-            full(o.shape),
-            weight_spec(second, lambda s: 4),
-            row,
-            weight_spec(third, lambda s: s),
-            weight_spec(third, lambda s: s + blocks),
-            row,
-            full(gains.shape),
-            full(biases.shape),
-        ],
-        out_specs=(row, row, part, part, row, row, row, full((2, width))),
-        scratch_shapes=[pltpu.VMEM((tokens, width), f32)],
-        compiler_params=params(60),
-        cost_estimate=cost(
-            (4 * blocks + 2) * tokens * width * width,
-            (22 + 4 * blocks) * tokens * width + (2 + 4 * blocks) * width * width,
-            2 * blocks * tokens * width,
-        ),
+        info,
+        (blocks,),
+        [
+            (o, full(o.shape)),
+            (wo, weight_specs(wo, lambda s: 2)),
+            (x2, row),
+            (w1, weight_specs(w1, lambda s: s)),
+            (w2, weight_specs(w2, lambda s: s)),
+            (gains, full(gains.shape)),
+            (biases, full(biases.shape)),
+        ],
+        [(wide, row), (slim, row), (many, part), (many, part), (wide, row)],
+        mib=60,
+        cost_estimate=cost(28),
         name="feed",
-    )(o, second, x2, third, third, og, gains, biases)
+    )
 
 
 def feed_back_kernel(
-    g4_ref,
-    g4b_ref,
+    info_ref,
+    x4_ref,
+    og_a,
+    og_b,
     slope_ref,
     w1_ref,
     w2_ref,
     x3_ref,
     wo_ref,
     gain_ref,
+    bias_ref,
+    hid_a,
+    hid_b,
+    g4b_ref,
     du_ref,
     g3_ref,
     g3b_ref,
@@ -580,12 +639,25 @@
 ):
     step = pl.program_id(0)
 
+    @pl.when(step == 0)
+    def _():
+        x4 = x4_ref[...]
+        half = og_a.shape[0]
+        hidden = normed(x4)[0] * gain_ref[4:5] + bias_ref[4:5]
+        put_slots((hid_a, hid_b), info_ref, (hidden[:half], hidden[half:]))
+        out_grad = jnp.concatenate(slots((og_a, og_b), info_ref), axis=0).astype(f32)
+        g4, gain_grad, bias_grad = norm_back(x4, gain_ref[4:5], out_grad)
+        g3_ref[...] = g4
+        g4b_ref[...] = g4.astype(bf16)
+        sums_ref[2:3] = gain_grad
+        sums_ref[3:4] = bias_grad
+
     def store(at, y):
-        lanes = pl.ds(at, w2_ref.shape[4])
+        lanes = pl.ds(at, w2_ref[0].shape[4])
         du_ref[0, :, lanes] = (y * slope_ref[0, :, lanes].astype(f32)).astype(bf16)
 
-    project(g4b_ref[...], w2_ref, store)
-    part = dot(du_ref[0], whole_weight(w1_ref), NT)
+    project(g4b_ref[...], w2_ref, info_ref, store)
+    part = dot(du_ref[0], whole_weight(w1_ref, info_ref), NT)
 
     @pl.when(step == 0)
     def _():
@@ -598,7 +670,7 @@
     @pl.when(step == pl.num_programs(0) - 1)
     def _():
         back, gain_grad, bias_grad = norm_back(x3_ref[...], gain_ref[3:4], total[...])
-        g3 = g4_ref[...] + back
+        g3 = g3_ref[...] + back
         g3_ref[...] = g3
         g3b = g3.astype(bf16)
         g3b_ref[...] = g3b
@@ -606,46 +678,50 @@
         sums_ref[1:2] = bias_grad
 
         def keep(at, y):
-            do_ref[0, :, pl.ds(at, wo_ref.shape[4])] = y.astype(bf16)
-
-        project(g3b, wo_ref, keep)
-
-
-def feed_back(g4, g4b, slope, second, x3, third, gains):
+            do_ref[0, :, pl.ds(at, wo_ref[0].shape[4])] = y.astype(bf16)
+
+        project(g3b, wo_ref, info_ref, keep)
+
+
+def feed_back(info, x4, og, slope, wo, x3, w1, w2, gains, biases):
     blocks, tokens, width = slope.shape
     row = full((tokens, width))
-    part = pl.BlockSpec((1, tokens, width), lambda s: (s, 0, 0))
+    part_row = full((tokens // 2, width))
+    part_shape = jax.ShapeDtypeStruct((tokens // 2, width), bf16)
+    part = pl.BlockSpec((1, tokens, width), lambda s, info: (s, 0, 0))
     wide = jax.ShapeDtypeStruct((tokens, width), f32)
     slim = jax.ShapeDtypeStruct((tokens, width), bf16)
-    return pl.pallas_call(
+    return call(
         feed_back_kernel,
-        out_shape=(
-            jax.ShapeDtypeStruct((blocks, tokens, width), bf16),
-            wide,
-            slim,
-            jax.ShapeDtypeStruct((1, tokens, width), bf16),
-            jax.ShapeDtypeStruct((2, width), f32),
-        ),
-        grid=(blocks,),
-        in_specs=[
-            row,
-            row,
-            part,
-            weight_spec(third, lambda s: s),
-            weight_spec(third, lambda s: s + blocks),
-            row,
-            weight_spec(second, lambda s: 4),
-            full(gains.shape),
-        ],
-        out_specs=(part, row, row, full((1, tokens, width)), full((2, width))),
-        scratch_shapes=[pltpu.VMEM((tokens, width), f32)],
-        compiler_params=params(60),
-        cost_estimate=cost(
-            (4 * blocks + 2) * tokens * width * width,
-            (18 + 4 * blocks) * tokens * width + (2 + 4 * blocks) * width * width,
-        ),
+        info,
+        (blocks,),
+        [
+            (x4, row),
+            (og[0], part_row),
+            (og[1], part_row),
+            (slope, part),
+            (w1, weight_specs(w1, lambda s: s)),
+            (w2, weight_specs(w2, lambda s: s)),
+            (x3, row),
+            (wo, weight_specs(wo, lambda s: 2)),
+            (gains, full(gains.shape)),
+            (biases, full(biases.shape)),
+        ],
+        [
+            (part_shape, part_row),
+            (part_shape, part_row),
+            (slim, row),
+            (jax.ShapeDtypeStruct((blocks, tokens, width), bf16), part),
+            (wide, row),
+            (slim, row),
+            (jax.ShapeDtypeStruct((1, tokens, width), bf16), full((1, tokens, width))),
+            (jax.ShapeDtypeStruct((4, width), f32), full((4, width))),
+        ],
+        [pltpu.VMEM((tokens, width), f32)],
+        60,
+        cost_estimate=cost(28),
         name="feed_back",
-    )(g4, g4b, slope, third, third, x3, second, gains)
+    )
 
 
 def attend_back_kernel(
@@ -693,15 +769,15 @@
         ],
         out_specs=(one, two, two),
         compiler_params=params(),
-        cost_estimate=cost(64 * tokens * tokens * width, 4 * heads * tokens * tokens),
+        cost_estimate=cost(21),
         name="attend_back",
     )(q, own, par, probs, o, do)
 
 
 def middle_back_kernel(
-    dq_ref, wq_ref, x2_ref, g3_ref, wo_ref, gain_ref, g2_ref, g2b_ref, do_ref, sums_ref
+    info_ref, dq_ref, wq_ref, x2_ref, g3_ref, wo_ref, gain_ref, g2_ref, g2b_ref, do_ref, sums_ref
 ):
-    d_normed = dot(dq_ref[0], whole_weight(wq_ref), NT)
+    d_normed = dot(dq_ref[0], whole_weight(wq_ref, info_ref), NT)
     back, gain_grad, bias_grad = norm_back(x2_ref[...], gain_ref[2:3], d_normed)
     g2 = g3_ref[...] + back
     g2_ref[...] = g2
@@ -711,43 +787,42 @@
     sums_ref[1:2] = bias_grad
 
     def keep(at, y):
-        do_ref[0, :, pl.ds(at, wo_ref.shape[4])] = y.astype(bf16)
-
-    project(g2b, wo_ref, keep)
-
-
-def middle_back(dq, second, x2, g3, gains):
+        do_ref[0, :, pl.ds(at, wo_ref[0].shape[4])] = y.astype(bf16)
+
+    project(g2b, wo_ref, info_ref, keep)
+
+
+def middle_back(info, dq, weights, x2, g3, gains):
     _, tokens, width = dq.shape
     row = full((tokens, width))
-    return pl.pallas_call(
+    return call(
         middle_back_kernel,
-        out_shape=(
-            jax.ShapeDtypeStruct((tokens, width), f32),
-            jax.ShapeDtypeStruct((tokens, width), bf16),
-            jax.ShapeDtypeStruct((1, tokens, width), bf16),
-            jax.ShapeDtypeStruct((2, width), f32),
-        ),
-        grid=(1,),
-        in_specs=[
-            full(dq.shape),
-            weight_spec(second, lambda s: 1),
-            row,
-            row,
-            weight_spec(second, lambda s: 0),
-            full(gains.shape),
-        ],
-        out_specs=(row, row, full((1, tokens, width)), full((2, width))),
-        compiler_params=params(),
-        cost_estimate=cost(4 * tokens * width * width, 18 * tokens * width + 4 * width * width),
+        info,
+        (1,),
+        [
+            (dq, full(dq.shape)),
+            (weights, weight_specs(weights, lambda s: 1)),
+            (x2, row),
+            (g3, row),
+            (weights, weight_specs(weights, lambda s: 0)),
+            (gains, full(gains.shape)),
+        ],
+        [
+            (jax.ShapeDtypeStruct((tokens, width), f32), row),
+            (jax.ShapeDtypeStruct((tokens, width), bf16), row),
+            (jax.ShapeDtypeStruct((1, tokens, width), bf16), full((1, tokens, width))),
+            (jax.ShapeDtypeStruct((2, width), f32), full((2, width))),
+        ],
+        cost_estimate=cost(10),
         name="middle_back",
-    )(dq, second, x2, g3, second, gains)
-
-
-def source_back_kernel(mine_ref, came_ref, w_ref, out_ref, sum_ref, total):
+    )
+
+
+def source_back_kernel(info_ref, mine_ref, came_ref, w_ref, out_a, out_b, sum_ref, total):
     step = pl.program_id(0)
     grads = (mine_ref[0].astype(f32) + came_ref[0].astype(f32)).astype(bf16)
     sum_ref[0] = grads
-    part = dot(grads, whole_weight(w_ref), NT)
+    part = dot(grads, whole_weight(w_ref, info_ref), NT)
 
     @pl.when(step == 0)
     def _():
@@ -755,42 +830,57 @@
 
     @pl.when(step == pl.num_programs(0) - 1)
     def _():
-        out_ref[...] = (total[...] + part).astype(bf16)
-
-
-def source_back(mine, came, second):
+        half = out_a.shape[0]
+        both = total[...] + part
+        put_slots((out_a, out_b), info_ref, (both[:half], both[half:]))
+
+
+def source_back(info, mine, came, weights):
     parts, tokens, width = mine.shape
-    part = pl.BlockSpec((1, tokens, width), lambda s: (s, 0, 0))
-    return pl.pallas_call(
+    part = pl.BlockSpec((1, tokens, width), lambda s, info: (s, 0, 0))
+    return call(
         source_back_kernel,
-        out_shape=(
-            jax.ShapeDtypeStruct((tokens, width), bf16),
-            jax.ShapeDtypeStruct((parts, tokens, width), bf16),
-        ),
-        grid=(parts,),
-        in_specs=[part, part, weight_spec(second, lambda s: s + 2)],
-        out_specs=(full((tokens, width)), part),
-        scratch_shapes=[pltpu.VMEM((tokens, width), f32)],
-        compiler_params=params(),
-        cost_estimate=cost(4 * tokens * width * width, 14 * tokens * width + 4 * width * width),
+        info,
+        (parts,),
+        [(mine, part), (came, part), (weights, weight_specs(weights, lambda s: s))],
+        [
+            (jax.ShapeDtypeStruct((tokens // 2, width), bf16), full((tokens // 2, width))),
+            (jax.ShapeDtypeStruct((tokens // 2, width), bf16), full((tokens // 2, width))),
+            (jax.ShapeDtypeStruct((parts, tokens, width), bf16), part),
+        ],
+        [pltpu.VMEM((tokens, width), f32)],
+        cost_estimate=cost(7),
         name="source_back",
-    )(mine, came, second)
+    )
 
 
 def exit_kernel(
-    dq_ref, mine_ref, came_ref, w_ref, x1_ref, x0_ref, g2_ref, gain_ref, g0_ref, sum_ref, sums_ref, total
+    info_ref,
+    dq_ref,
+    mine_ref,
+    came_ref,
+    wq_ref,
+    wkv_ref,
+    x1_ref,
+    x0_ref,
+    g2_ref,
+    gain_ref,
+    g0_ref,
+    sum_ref,
+    sums_ref,
+    total,
 ):
     step = pl.program_id(0)
 
     @pl.when(step == 0)
     def _():
-        total[...] = dot(dq_ref[0], whole_weight(w_ref), NT)
+        total[...] = dot(dq_ref[0], whole_weight(wq_ref, info_ref), NT)
 
     @pl.when(step > 0)
     def _():
         grads = (mine_ref[0].astype(f32) + came_ref[0].astype(f32)).astype(bf16)
         sum_ref[0] = grads
-        total[...] += dot(grads, whole_weight(w_ref), NT)
+        total[...] += dot(grads, whole_weight(wkv_ref, info_ref), NT)
 
     @pl.when(step == pl.num_programs(0) - 1)
     def _():
@@ -804,34 +894,35 @@
         sums_ref[3:4] = bias_one
 
 
-def exit_back(dq, mine, came, first, x1, x0, g2, gains):
+def exit_back(info, dq, mine, came, first, x1, x0, g2, gains):
     _, tokens, width = dq.shape
+    wq, wkv = first
     row = full((tokens, width))
-    part = pl.BlockSpec((1, tokens, width), lambda s: (jnp.maximum(s - 1, 0), 0, 0))
-    return pl.pallas_call(
+    part = pl.BlockSpec((1, tokens, width), lambda s, info: (jnp.maximum(s - 1, 0), 0, 0))
+    return call(
         exit_kernel,
-        out_shape=(
-            jax.ShapeDtypeStruct((width, tokens), bf16),
-            jax.ShapeDtypeStruct((2, tokens, width), bf16),
-            jax.ShapeDtypeStruct((4, width), f32),
-        ),
-        grid=(3,),
-        in_specs=[
-            full(dq.shape),
-            part,
-            part,
-            weight_spec(first, lambda s: s + 1),
-            row,
-            row,
-            row,
-            full(gains.shape),
-        ],
-        out_specs=(full((width, tokens)), part, full((4, width))),
-        scratch_shapes=[pltpu.VMEM((tokens, width), f32)],
-        compiler_params=params(),
-        cost_estimate=cost(6 * tokens * width * width, 28 * tokens * width + 6 * width * width),
+        info,
+        (3,),
+        [
+            (dq, full(dq.shape)),
+            (mine, part),
+            (came, part),
+            (wq, weight_specs(wq, lambda s: 1)),
+            (wkv, weight_specs(wkv, lambda s: jnp.maximum(s - 1, 0))),
+            (x1, row),
+            (x0, row),
+            (g2, row),
+            (gains, full(gains.shape)),
+        ],
+        [
+            (jax.ShapeDtypeStruct((width, tokens), bf16), full((width, tokens))),
+            (jax.ShapeDtypeStruct((2, tokens, width), bf16), part),
+            (jax.ShapeDtypeStruct((4, width), f32), full((4, width))),
+        ],
+        [pltpu.VMEM((tokens, width), f32)],
+        cost_estimate=cost(15),
         name="exit_back",
-    )(dq, mine, came, first, x1, x0, g2, gains)
+    )
 
 
 def weight_grad_kernel(chips, aliased, info_ref, xo_ref, xp_ref, yo_ref, yp_ref, *refs):
@@ -881,9 +972,7 @@
         ),
         input_output_aliases={} if before is None else {5: 0},
         compiler_params=params(),
-        cost_estimate=cost(
-            2 * parts * tokens * width * width, 5 * parts * tokens * width + 4 * tokens * width
-        ),
+        cost_estimate=cost(3 + 2 * parts),
         name="weight_grad",
     )(info, x_own, x_par, y_own, y_par, *extra)
 
@@ -905,42 +994,115 @@
 
 
 def to_chips(value, mp):
-    m = lax.axis_index("mp")
-    slot, odd = m // 2, m % 2
-    came = []
-    for turn, moves in enumerate(line_moves(mp)):
-        sent = jnp.where((slot ^ turn) == 0, value[0], value[1])
-        came.append(lax.ppermute(sent, LINE, moves))
-    return jnp.concatenate(
-        [jnp.where(odd == 0, came[0], came[1]), jnp.where(odd == 0, came[1], came[0])], axis=0
-    )
-
-
-def from_chips(value, mp):
-    m = lax.axis_index("mp")
-    slot, odd = m // 2, m % 2
-    half = value.shape[0] // 2
-    came = []
-    for turn, moves in enumerate(line_moves(mp)):
-        sent = jnp.where((odd ^ turn) == 0, value[:half], value[half:])
-        came.append(lax.ppermute(sent, LINE, [(b, a) for a, b in moves]))
-    return jnp.stack(
-        [jnp.where(slot == 0, came[0], came[1]), jnp.where(slot == 0, came[1], came[0])]
-    )
+    slot = lax.axis_index("mp") // 2
+    return [
+        lax.ppermute(jnp.where((slot ^ turn) == 0, value[0], value[1]), LINE, moves)
+        for turn, moves in enumerate(line_moves(mp))
+    ]
+
+
+def from_chips(pair, mp):
+    return [
+        lax.ppermute(sent, LINE, [(b, a) for a, b in moves])
+        for sent, moves in zip(pair, line_moves(mp))
+    ]
+
+
+def placed_again(came):
+    slot = lax.axis_index("mp") // 2
+    one, two = [c.astype(f32) for c in came]
+    return jnp.stack([jnp.where(slot == 0, one, two), jnp.where(slot == 0, two, one)])
 
 
 def packed(*weights):
     return jnp.concatenate([w.reshape(-1, w.shape[-1]) for w in weights], axis=0)
 
 
-def gathered(rows, dp, mp, parts):
+X_SWAP = [(0, 1), (1, 0), (2, 3), (3, 2)]
+Y_SWAP = [(0, 2), (2, 0), (1, 3), (3, 1)]
+def gathered(rows, unit, chips, mp):
     value = lax.all_gather(rows, ALL, axis=0, tiled=False)
-    return value.reshape(dp, mp, parts, rows.shape[0] // parts, rows.shape[1])
-
-
-def scattered(grads):
-    part = lax.psum_scatter(grads, "chip", scatter_dimension=0, tiled=False)
-    return lax.psum_scatter(part, "mp", scatter_dimension=0, tiled=False).astype(f32)
+    return value.reshape(chips * CORES, mp, -1, unit, rows.shape[-1])
+
+
+def gathered_line(rows, unit, mp):
+    value = lax.all_gather(rows, "mp", axis=0, tiled=False)
+    return value.reshape(mp, -1, unit, rows.shape[-1])
+
+
+class Spread:
+    def __init__(self, value, cut):
+        self.own, self.cut = [value], cut
+        self.near, self.far, self.both = [], [], []
+        self.swapped = {}
+
+    def begin(self, *others):
+        self.own = tied(self.own, *others)
+        sets = [self.own[0][:, : self.cut], self.own[0][:, self.cut :]]
+        self.near = [lax.ppermute(w, "chip", p) for w, p in zip(sets, (X_SWAP, Y_SWAP))]
+        self.far = [lax.ppermute(w, "chip", p) for w, p in zip(sets, (Y_SWAP, X_SWAP))]
+
+    def finish(self, *others):
+        self.near = tied(self.near, *others)
+        self.both = [lax.ppermute(w, "chip", p) for w, p in zip(self.near, (Y_SWAP, X_SWAP))]
+
+    def swap(self, *names):
+        for name in names:
+            self.swapped[name] = [swap(w) for w in getattr(self, name)]
+
+    def hold(self, *others):
+        state = [self.own, self.near, self.far, self.both, self.swapped]
+        state, others = lax.optimization_barrier((state, others))
+        self.own, self.near, self.far, self.both, self.swapped = state
+        return others if len(others) > 1 else others[0]
+
+    def pieces(self):
+        found = []
+        for i in range(2):
+            pieces = []
+            for name in ("own", "near", "far", "both") if i == 0 else ("own", "far", "near", "both"):
+                at, skip = (0, i * self.cut) if name == "own" else (i, 0)
+                for group in (getattr(self, name), self.swapped[name]):
+                    pieces.append((group[at][None], skip))
+            found.append(pieces)
+        return found
+
+
+def tied(value, *others):
+    return after(value, *others) if others else value
+
+
+def scattered(grads, axis):
+    return lax.psum_scatter(grads, axis, scatter_dimension=0, tiled=False)
+
+
+def sent_over(grads, axis, size):
+    me = lax.axis_index(axis)
+    terms = []
+    for k in range(size):
+        if axis == "chip" and size == 4:
+            to, perm = me ^ k, [(i, i ^ k) for i in range(size)]
+        else:
+            to, perm = (me + k) % size, [(i, (i + k) % size) for i in range(size)]
+        part = lax.dynamic_index_in_dim(grads, to, axis=0, keepdims=False)
+        terms.append(part if k == 0 else lax.ppermute(part, axis, perm))
+    return terms
+
+
+def summed(terms):
+    return sum([t.astype(f32) for t in terms[1:]], start=terms[0].astype(f32))
+
+
+def total_over(value, axis, size):
+    terms = [
+        lax.ppermute(value, axis, [(i, (i + k) % size) for i in range(size)])
+        for k in range(1, size)
+    ]
+    return sum(terms, start=value)
+
+
+def after(value, *others):
+    return lax.optimization_barrier((value, others))[0]
 
 
 def body(
@@ -972,26 +1134,31 @@
     vocab = table.shape[1]
     feats = table.shape[0]
     rows = pos_table.shape[0]
-    core, m = lax.axis_index("core"), lax.axis_index("mp")
+    core, m, chip = lax.axis_index("core"), lax.axis_index("mp"), lax.axis_index("chip")
 
     def split(weight):
         return weight.reshape(rows, -1, block).transpose(1, 0, 2)
 
-    all_ids = lax.all_gather(target_ids.reshape(-1), "mp", axis=0, tiled=False)
-    all_ids = lax.all_gather(all_ids, ("chip", "core"), axis=0, tiled=False)
-    first = gathered(packed(pos_table, split(self_query_key_value_weight)), dp, mp, 4)
-    second = gathered(
-        packed(
-            self_output_weight, cross_query_weight, split(cross_key_value_weight), cross_output_weight
-        ),
-        dp,
-        mp,
-        5,
-    )
+    own_ids = jnp.broadcast_to(target_ids.reshape(1, tokens), (n, tokens))
+    all_ids = lax.all_to_all(own_ids, ALL, split_axis=0, concat_axis=0, tiled=True)
     sub = feedforward_input_weight.shape[1] // block
-    third = gathered(
-        packed(split(feedforward_input_weight), split(feedforward_output_weight)), dp, mp, 2 * sub
-    )
+    first = packed(pos_table, split(self_query_key_value_weight))
+    second = packed(
+        self_output_weight, cross_query_weight, split(cross_key_value_weight), cross_output_weight
+    )
+    third = packed(split(feedforward_input_weight), split(feedforward_output_weight))
+    sub = feedforward_input_weight.shape[1] // block
+    late = gathered(jnp.concatenate([second, third]), rows, chips, mp)
+    second = [(late, 0)], [(late, 2)]
+    third = [(late, 5)], [(late, 5 + sub)]
+    stepped = chips == 4
+    if stepped:
+        copies = jnp.broadcast_to(first[None], (mp,) + first.shape)
+        copies = lax.all_to_all(after(copies, all_ids), "mp", split_axis=0, concat_axis=0, tiled=True)
+        first = Spread(copies.reshape(mp, -1, rows, block), 2)
+    else:
+        first = gathered(first, rows, chips, mp)
+        first = [(first, 0)], [(first, 2)]
 
     lengths = jnp.stack([tgt_lengths, src_lengths])
     other = swap(lengths)
@@ -1002,7 +1169,18 @@
     )
     lengths = lax.dynamic_index_in_dim(lengths, m, axis=1, keepdims=False)
     info = jnp.stack(
-        [core, lengths[0], lengths[1], core, 3 - core, 1 - core, 2 + core, jnp.zeros_like(core)]
+        [
+            core,
+            lengths[0],
+            lengths[1],
+            core,
+            3 - core,
+            1 - core,
+            2 + core,
+            chip % 2,
+            chip // 2,
+            m % 2,
+        ]
     ).astype(i32)
 
     ids = all_ids.reshape(chips, CORES, mp, seqs, block)
@@ -1014,52 +1192,99 @@
     flat_row = row.reshape(-1)
 
     picked = gather_tokens(table, flat_row, group)
+    if stepped:
+        picked = first.hold(picked)
+        first.begin(picked)
+        first.finish()
+        first.swap("own", "near", "far", "both")
+        first = first.pieces()
     emb = lax.all_to_all(picked, ALL, split_axis=0, concat_axis=0, tiled=True)
     emb = emb.reshape(width, tokens)
 
-    states = to_chips(encoder_states, mp)
-    og = to_chips(out_grad.astype(bf16), mp)
-
     x0, x1, a, q, kv = entry(info, emb, first, norm_gains, norm_biases)
+    states = to_chips(after(encoder_states, a), mp)
     kv_par = swap(kv)
-    ckv = source_keys(states, second)
+    outs = attend(info, q, kv, kv_par, True)
+    (o, probs), states = lax.optimization_barrier((outs, states))
+    states, ckv = source_keys(info, states, second[1])
     ckv_par = swap(ckv)
-    o, probs = attend(info, q, kv, kv_par, True)
-    x2, c, cq = middle(o, second, x1, norm_gains, norm_biases)
+    x2, c, cq = middle(info, after(o, ckv), second[0], x1, norm_gains, norm_biases)
     oc, cprobs = attend(info, cq, ckv, ckv_par, False)
-    x3, f, g, slope, hid, g4, g4b, sums4 = feed(
-        oc, second, x2, third, og, norm_gains, norm_biases
-    )
-    hidden_out = from_chips(hid, mp).astype(f32)
-
-    du, g3, g3b, doc, sums3 = feed_back(g4, g4b, slope, second, x3, third, norm_gains)
-    shape = (chips, mp, 2 * sub, rows, block)
-    grads = weight_grad(info, f, swap(f), du, swap(du), shape, 0)
-    grads = weight_grad(info, g4b, swap(g4b), g, swap(g), shape, sub, grads)
-    feed_grads = scattered(grads)
-
-    dcq, dckv_own, dckv_par = attend_back(cq, ckv, ckv_par, cprobs, oc, doc)
-    dckv_came = swap(dckv_par)
-    g2, g2b, do, sums2 = middle_back(dcq, second, x2, g3, norm_gains)
-    enc_grad, dckv = source_back(dckv_own, dckv_came, second)
-    encoder_grad = from_chips(enc_grad, mp).astype(f32)
+    og = to_chips(after(out_grad.astype(bf16), oc), mp)
+    w1, w2 = third
+    oc_par, c_par = swap(oc), swap(after(c, oc))
+    outs = feed(info, oc, second[1], x2, w1, w2, norm_gains, norm_biases, sub)
+    (x3, f, g, slope, x4), og, oc_par, c_par = lax.optimization_barrier((outs, og, oc_par, c_par))
+    f_par, g_par = swap(f), swap(g)
+    a_par, o_par, states_par = [swap(after(v, x4)) for v in (a, o, states)]
+    outs = feed_back(info, x4, og, slope, second[1], x3, w1, w2, norm_gains, norm_biases)
+    outs, f_par, g_par, a_par, o_par, states_par = lax.optimization_barrier(
+        (outs, f_par, g_par, a_par, o_par, states_par)
+    )
+    *hid, g4b, du, g3, g3b, doc, sums34 = outs
+    g4b_par, g3b_par, du_par = swap(g4b), swap(g3b), swap(du)
+    hidden_out = from_chips(tied(hid, g4b_par), mp)
+    shape = (chips, mp, sub, rows, block)
+    grads = weight_grad(info, g4b, g4b_par, g, g_par, shape, 0)
+    part_one = scattered(grads, "chip")
+    shape = (chips, mp, sub + 1, rows, block)
+    grads = weight_grad(info, after(g3b, grads), g3b_par, oc, oc_par, shape, sub)
+    grads = weight_grad(info, after(f, grads), f_par, du, du_par, shape, 0, grads)
+    doc, hidden_out = lax.optimization_barrier((after(doc, grads), hidden_out))
+
+    outs = attend_back(cq, ckv, ckv_par, cprobs, oc, doc)
+    (dcq, dckv_own, dckv_par), part_one = lax.optimization_barrier((outs, part_one))
+    part_one = scattered(part_one, "mp")
+    hidden_out = placed_again(hidden_out)
+    dckv_came, dcq_par = swap(dckv_par), swap(dcq)
+    outs = middle_back(info, dcq, second[0], x2, g3, norm_gains)
+    (g2, g2b, do, sums2), dckv_came, dcq_par, dckv_own = lax.optimization_barrier(
+        (outs, dckv_came, dcq_par, dckv_own)
+    )
+    g2b_par = swap(g2b)
+    outs = source_back(info, dckv_own, dckv_came, second[1])
+    outs, part_one = lax.optimization_barrier((outs, part_one))
+    part_two = scattered(after(grads, part_one), "chip")
+    *enc_grad, dckv = outs
+    dckv_after = swap(dckv)
     shape = (chips, mp, 4, rows, block)
-    grads = weight_grad(info, g3b, swap(g3b), oc, swap(oc), shape, 0)
-    grads = weight_grad(info, c, swap(c), dcq, swap(dcq), shape, 1, grads)
-    grads = weight_grad(info, states, swap(states), dckv, swap(dckv), shape, 2, grads)
-    cross_grads = scattered(grads)
-
-    dq, dkv_own, dkv_par = attend_back(q, kv, kv_par, probs, o, do)
+    grads = weight_grad(info, c, c_par, after(dcq, dckv), dcq_par, shape, 0)
+    grads = weight_grad(info, g2b, g2b_par, o, o_par, shape, 1, grads)
+    grads = weight_grad(info, states, states_par, dckv, dckv_after, shape, 2, grads)
+    do = after(do, grads)
+    cross_terms = lax.all_to_all(grads, "chip", split_axis=0, concat_axis=0, tiled=True)
+    encoder_grad = from_chips(tied(enc_grad, grads), mp)
+
+    outs = attend_back(q, kv, kv_par, probs, o, do)
+    (dq, dkv_own, dkv_par), encoder_grad = lax.optimization_barrier((outs, encoder_grad))
     dkv_came = swap(dkv_par)
-    g0, dkv, sums01 = exit_back(dq, dkv_own, dkv_came, first, x1, x0, g2, norm_gains)
+    dq_par = swap(dq)
+    outs = exit_back(info, dq, dkv_own, dkv_came, first, x1, x0, g2, norm_gains)
+    (g0, dkv, sums01), dq_par, cross_terms = lax.optimization_barrier((outs, dq_par, cross_terms))
     sent = g0.reshape(n, feats, tokens)
     arrived = lax.all_to_all(sent, ALL, split_axis=0, concat_axis=0, tiled=True)
-    grads = weight_grad(info, g2b, swap(g2b), o, swap(o), shape, 0)
-    grads = weight_grad(info, a, swap(a), dq, swap(dq), shape, 1, grads)
-    grads = weight_grad(info, a, swap(a), dkv, swap(dkv), shape, 2, grads)
-    self_grads = scattered(grads)
-
-    table_grad, places = scatter_tokens(arrived, flat_row, row, group, vocab, mp)
+    encoder_grad = placed_again(encoder_grad)
+    cross_part = jnp.sum(cross_terms.astype(f32), axis=0).astype(bf16)
+    sums = jnp.concatenate((sums01, sums2, sums34), axis=0)
+    sums_par = swap(sums)
+    shape = (chips, mp, 3, rows, block)
+    dkv_after = swap(dkv)
+    grads = weight_grad(info, a, a_par, dq, dq_par, shape, 0)
+    grads, sums_par = lax.optimization_barrier((grads, sums_par))
+    sums = total_over(sums + sums_par, "chip", chips)
+    grads = weight_grad(info, a, a_par, dkv, dkv_after, shape, 1, grads)
+    sums, grads, arrived, part_two = lax.optimization_barrier((sums, grads, arrived, part_two))
+    sums_up = scattered(jnp.concatenate([part_two, cross_part], axis=1), "mp")
+    self_terms = lax.all_to_all(grads, "chip", split_axis=0, concat_axis=0, tiled=True)
+    sums = total_over(sums, "mp", mp)
+
+    outs = scatter_tokens(arrived, flat_row, row, group, vocab, mp)
+    (table_grad, places), self_terms, sums = lax.optimization_barrier((outs, self_terms, sums))
+    self_part = jnp.sum(self_terms.astype(f32), axis=0).astype(bf16)
+    self_grads = summed(sent_over(self_part, "mp", mp))
+    sums_up = sums_up.astype(f32)
+    feed_out_grads = part_one.astype(f32)
+    feed_in_grads, cross_grads = sums_up[: sub + 1], sums_up[sub + 1 :]
 
     blocks = places.reshape(CORES, feats, 2, block).transpose(0, 2, 1, 3).reshape(4, feats, block)
     blocks = jnp.stack([blocks[0], blocks[2], blocks[3], blocks[1]])
@@ -1077,9 +1302,6 @@
         pos_grad.append(value)
     pos_grad = jnp.concatenate(pos_grad, axis=0)
 
-    sums = jnp.concatenate([sums01, sums2, sums3, sums4], axis=0)
-    sums = lax.psum(sums, ALL)
-
     def join(parts):
         return parts.transpose(1, 0, 2)
 
@@ -1087,13 +1309,13 @@
         hidden_out,
         table_grad,
         pos_grad,
-        join(self_grads[1:4]),
-        self_grads[0],
+        join(self_grads),
         cross_grads[1],
+        cross_grads[0],
         join(cross_grads[2:4]),
-        cross_grads[0],
-        join(feed_grads[:sub]).reshape(rows, -1),
-        join(feed_grads[sub:]).reshape(rows, -1),
+        feed_in_grads[sub],
+        join(feed_in_grads[:sub]).reshape(rows, -1),
+        join(feed_out_grads).reshape(rows, -1),
         sums[0::2],
         sums[1::2],
         encoder_grad,

time: 860 us -> 679 us (0.79)
  waiting for transfers between devices: 297 us -> 152 us
  blocking collectives: 88.5 us -> 0 us
  starting transfers between devices: 45.3 us -> 82.6 us
    unnamed x12 -> x7, waiting for transfers between devices: 106 us -> 3.01 us
    psum x1 -> x0, blocking collectives: 65.7 us -> none  [body(): sums = lax.psum(sums, ALL)]
    all_gather x3 -> x1, waiting for transfers between devices: 79.2 us -> 38.2 us  [gathered(): value = lax.all_gather(rows, ALL, axis=0, tiled=False)]
    ppermute x8 -> x23, waiting for transfers between devices: 51.9 us -> 75.7 us  [the longest x4 38.9 us: begin(): lax.ppermute(w, 'chip', p)]
    all_to_all x1, waiting for transfers between devices: 23.7 us -> 0.01 us  [body(): emb = lax.all_to_all(picked, ALL, split_axis=0, concat_axis=0, tiled=True)]
    all_gather x2 -> x0, blocking collectives: 22.8 us -> none  [the longest x1 13.6 us: body(): all_ids = lax.all_gather(target_ids.reshape(-1), 'mp', axis=0, tiled=False)]
    ppermute x20 -> x28, waiting for transfers between devices: 31.9 us -> 10 us  [swap(): return lax.ppermute(value, 'core', [(0, 1), (1, 0)])]
    all_to_all x0 -> x4, starting transfers between devices: none -> 19.5 us  [the longest x2 8.69 us: body(): lax.all_to_all(grads, 'chip', split_axis=0, concat_axis=0, tiled=True)]
  transfers between devices with their start and end apart: 42 -> 65, of which waited for: 14 -> 22; matrix products, arithmetic and copies ran while one was open for 4% -> 5% of each run, Pallas kernels for 32% -> 47%
where the time goes in v2:
time: 679 us; the launch traced here: 671 us
  Pallas kernels  357 us (53%)
  waiting for transfers between devices  152 us (22%)
  starting transfers between devices  82.6 us (12%)
  local copies, waits for them, and re-layouts  40.5 us (6%)
  other arithmetic  22.9 us (3%)
  between operations  15.5 us (2%)
    pallas_call x8, Pallas kernels, call(): pl.pallas_call(body, out_shape=[o for o, _ in outs], grid_spec=pltpu.Pref...  115 us
    pallas_call x1, Pallas kernels, scatter_tokens(): pl.pallas_call(functools.partial(scatter_kernel, groups, per_core), out_s...  56.7 us
    pallas_call x8, Pallas kernels, weight_grad(): pl.pallas_call(functools.partial(weight_grad_kernel, chips, before is not...  54.7 us
    pallas_call x1, Pallas kernels, gather_tokens(): pl.pallas_call(functools.partial(gather_kernel, groups, fill), out_shape=...  45.6 us
    pallas_call x2, Pallas kernels, attend(): pl.pallas_call(functools.partial(attend_kernel, causal), out_shape=(jax.S...  43.5 us
    pallas_call x2, Pallas kernels, attend_back(): pl.pallas_call(attend_back_kernel, out_shape=(jax.ShapeDtypeStruct((1, to...  42.2 us
    ppermute x4, waiting for transfers between devices, begin(): lax.ppermute(w, 'chip', p)  38.9 us
    all_gather x1, waiting for transfers between devices, gathered(): value = lax.all_gather(rows, ALL, axis=0, tiled=False)  38.2 us
  transfers between devices with their start and end apart: 65, of which 22 were waited for; matrix products, arithmetic and copies ran while one was open for 5% of the time, Pallas kernels for 47%

profile of v2, /device:TPU:0, one launch (start us, length us, event | category | flops | bytes accessed | tf_op | source)
XLA Modules:
  0.0 670.8 jit_solution(1272838051930859242)
XLA Ops:
  12.5 7.3 %all-to-all-start.1 = ((s32[32,1,512]{2,1,0:T(1,128)}), s32[32,1,512]{2,1,0:T(1,128)S(1)}, u32[]{:S(2)}, u32[]{:S(2)}) async-start(s32[32,1,512]{2,1,0:T(1,128)} %broadcast_in_dim.59), calls=%async_computation.1 | async-start | bytes 131072 | tf_op jit(solution)/shard_map/all_to_all | solution.py:1143
  20.9 6.4 all-to-all-done.1
  33.6 45.6 %gather_tokens.1 = bf16[32,32,512]{2,1,0:T(8,128)(2,1)} custom-call(s32[16384]{0:T(1024)} %add_select_fusion.rows_ref, s32[32,1,512]{2,1,0:T(1,128)} %and_select_fusion.1.group_ref, bf16[32,131072]{1,0:T(8,128)(2,1)} %refs_3_.1, bf16[32,131072]{1,0:T(8,128)(2,1)} %refs_3_.1, bf16[32,131072]{1,0:T(8,128)(2,1)} %refs_3_.1, bf16[32,131072]{1,0:T(8,128)(2,1)} %refs_3_.1), custom_call_target="tpu_custom_call" | custom-call | bytes 144000000 | tf_op jit(solution)/shard_map/gather_tokens/pallas_call | solution.py:185
  89.4 17.2 %collective-permute-done.10 = bf16[4,2,128,256]{3,2,1,0:T(8,128)(2,1)S(1)} collective-permute-done((bf16[4,2,128,256]{3,2,1,0:T(8,128)(2,1)S(1)}, bf16[4,2,128,256]{3,2,1,0:T(8,128)(2,1)S(1)}, u32[]{:S(2)}, u32[]{:S(2)}) %collective-permute-start.10) | collective-permute-done | bytes 524320 | tf_op jit(solution)/shard_map/ppermute | solution.py:1042
  106.9 9.6 %collective-permute-done.8 = bf16[4,2,128,256]{3,2,1,0:T(8,128)(2,1)S(1)} collective-permute-done((bf16[4,2,128,256]{3,2,1,0:T(8,128)(2,1)S(1)}, bf16[4,2,128,256]{3,2,1,0:T(8,128)(2,1)S(1)}, u32[]{:S(2)}, u32[]{:S(2)}) %collective-permute-start.8) | collective-permute-done | bytes 524320 | tf_op jit(solution)/shard_map/ppermute | solution.py:1043
  119.4 9.2 %collective-permute-done.2 = bf16[4,2,128,256]{3,2,1,0:T(8,128)(2,1)S(1)} collective-permute-done((bf16[4,2,128,256]{3,2,1,0:T(8,128)(2,1)S(1)}, bf16[4,2,128,256]{3,2,1,0:T(8,128)(2,1)S(1)}, u32[]{:S(2)}, u32[]{:S(2)}) %collective-permute-start.2) | collective-permute-done | bytes 524320 | tf_op jit(solution)/shard_map/ppermute | solution.py:1042
  130.0 12.1 %collective-permute-done.12 = bf16[4,2,128,256]{3,2,1,0:T(8,128)(2,1)} collective-permute-done((bf16[4,2,128,256]{3,2,1,0:T(8,128)(2,1)S(1)}, bf16[4,2,128,256]{3,2,1,0:T(8,128)(2,1)}, u32[]{:S(2)}, u32[]{:S(2)}) %collective-permute-start.12) | collective-permute-done | bytes 524320 | tf_op jit(solution)/shard_map/ppermute | solution.py:1047
  151.5 15.2 %entry.1 = (f32[512,1024]{1,0:T(8,128)}, f32[512,1024]{1,0:T(8,128)}, bf16[512,1024]{1,0:T(8,128)(2,1)}, bf16[1,512,1024]{2,1,0:T(8,128)(2,1)}, bf16[2,512,1024]{2,1,0:T(8,128)(2,1)}) custom-call(s32[10]{0:T(128)} %stack.70.info_ref, bf16[1024,512]{1,0:T(8,128)(2,1)} %bitcast.16.refs_0_, bf16[1,4,4,128,256]{4,3,2,1,0:T(8,128)(2,1)} %bitcast.138, ...), custom_call_target="tpu_custom_call" | custom-call | bytes 48000000 | tf_op jit(solution)/shard_map/entry/pallas_call | solution.py:116
  174.0 21.7 %attend.2 = (bf16[1,512,1024]{2,1,0:T(8,128)(2,1)}, bf16[16,2,512,512]{3,2,1,0:T(8,128)(2,1)}) custom-call(s32[10]{0:T(128)} %stack.70.info_ref, bf16[1,512,1024]{2,1,0:T(8,128)(2,1)} %get-tuple-element.144.q_ref, bf16[2,512,1024]{2,1,0:T(8,128)(2,1)} %get-tuple-element.145.own_ref, bf16[2,512,1024]{2,1,0:T(8,128)(2,1)} %copy-done.5), custom_call_target="tpu_custom_call" | custom-call | bytes 70400000 | tf_op jit(solution)/shard_map/attend/pallas_call | solution.py:496
  198.1 38.2 %all-gather.3.cloned.1.call-done = bf16[53248,256]{1,0:T(8,128)(2,1)} async-done(((bf16[1664,256]{1,0:T(8,128)(2,1)}), bf16[53248,256]{1,0:T(8,128)(2,1)}) %all-gather.3.cloned.1.call-update) | async-done | bytes 27262992 | tf_op jit(solution)/shard_map/all_gather | solution.py:1024
  236.3 7.6 %source_keys.1 = (bf16[512,1024]{1,0:T(8,128)(2,1)}, bf16[2,512,1024]{2,1,0:T(8,128)(2,1)}) custom-call(s32[10]{0:T(128)} %stack.70.info_ref, bf16[256,1024]{1,0:T(8,128)(2,1)} %copy-done.39, bf16[256,1024]{1,0:T(8,128)(2,1)} %copy-done.38, bf16[8,4,13,128,256]{4,3,2,1,0:T(8,128)(2,1)} %bitcast.124), custom_call_target="tpu_custom_call" | custom-call | bytes 25600000 | tf_op jit(solution)/shard_map/source_keys/pallas_call | solution.py:116
  244.2 9.1 %middle.1 = (f32[512,1024]{1,0:T(8,128)}, bf16[512,1024]{1,0:T(8,128)(2,1)}, bf16[1,512,1024]{2,1,0:T(8,128)(2,1)}) custom-call(s32[10]{0:T(128)} %stack.70.info_ref, bf16[1,512,1024]{2,1,0:T(8,128)(2,1)} %get-tuple-element.183.refs_0_.yo_ref.o_ref, bf16[8,4,13,128,256]{4,3,2,1,0:T(8,128)(2,1)} %bitcast.125, ...), custom_call_target="tpu_custom_call" | custom-call | bytes 28800000 | tf_op jit(solution)/shard_map/middle/pallas_call | solution.py:116
  254.6 21.8 %attend.3 = (bf16[1,512,1024]{2,1,0:T(8,128)(2,1)}, bf16[16,2,512,512]{3,2,1,0:T(8,128)(2,1)}) custom-call(s32[10]{0:T(128)} %stack.70.info_ref, bf16[1,512,1024]{2,1,0:T(8,128)(2,1)} %get-tuple-element.156.q_ref, bf16[2,512,1024]{2,1,0:T(8,128)(2,1)} %get-tuple-element.153.own_ref, bf16[2,512,1024]{2,1,0:T(8,128)(2,1)} %copy-done.6), custom_call_target="tpu_custom_call" | custom-call | bytes 70400000 | tf_op jit(solution)/shard_map/attend/pallas_call | solution.py:496
  280.1 5.7 collective-permute-start.18
  285.9 23.2 %feed.1 = (f32[512,1024]{1,0:T(8,128)}, bf16[512,1024]{1,0:T(8,128)(2,1)}, bf16[4,512,1024]{2,1,0:T(8,128)(2,1)}, bf16[4,512,1024]{2,1,0:T(8,128)(2,1)}, f32[512,1024]{1,0:T(8,128)}) custom-call(s32[10]{0:T(128)} %stack.70.info_ref, bf16[1,512,1024]{2,1,0:T(8,128)(2,1)} %get-tuple-element.157.refs_0_.yo_ref.o_ref, bf16[8,4,13,128,256]{4,3,2,1,0:T(8,128)(2,1)} %bitcast.127, ...), custom_call_target="tpu_custom_call" | custom-call | bytes 89600000 | tf_op jit(solution)/shard_map/feed/pallas_call | solution.py:116
  310.3 27.1 %feed_back.1 = (bf16[256,1024]{1,0:T(8,128)(2,1)}, bf16[256,1024]{1,0:T(8,128)(2,1)}, bf16[512,1024]{1,0:T(8,128)(2,1)}, bf16[4,512,1024]{2,1,0:T(8,128)(2,1)}, ...) custom-call(s32[10]{0:T(128)} %stack.70.info_ref, ...), custom_call_target="tpu_custom_call" | custom-call | bytes 89600000 | tf_op jit(solution)/shard_map/feed_back/pallas_call | solution.py:116
  341.4 10.1 %weight_grad.8 = bf16[4,4,4,128,256]{4,3,2,1,0:T(8,128)(2,1)} custom-call(s32[10]{0:T(128)} %stack.70.info_ref, bf16[512,1024]{1,0:T(8,128)(2,1)} %get-tuple-element.188.xo_ref, bf16[512,1024]{1,0:T(8,128)(2,1)} %copy-done.30, bf16[4,512,1024]{2,1,0:T(8,128)(2,1)} %get-tuple-element.181.yo_ref, bf16[4,512,1024]{2,1,0:T(8,128)(2,1)} %collective-permute-done.23.yp_ref), custom_call_target="tpu_custom_call" | custom-call | bytes 35200000 | tf_op jit(solution)/shard_map/weight_grad/pallas_call | solution.py:961
  361.3 5.4 weight_grad.9.refs_0_
  368.8 10.1 %weight_grad.10 = bf16[4,4,5,128,256]{4,3,2,1,0:T(8,128)(2,1)} custom-call(s32[10]{0:T(128)} %stack.70.info_ref, bf16[512,1024]{1,0:T(8,128)(2,1)} %get-tuple-element.192.xo_ref, bf16[512,1024]{1,0:T(8,128)(2,1)} %collective-permute-done.22.xp_ref, bf16[4,512,1024]{2,1,0:T(8,128)(2,1)} %get-tuple-element.194.yo_ref, ...), custom_call_target="tpu_custom_call", output_to_operand_aliasing={{}: (5, {})} | custom-call | bytes 35200000 | tf_op jit(solution)/shard_map/weight_grad/pallas_call | solution.py:961
  378.9 21.3 %attend_back.2 = (bf16[1,512,1024]{2,1,0:T(8,128)(2,1)}, bf16[2,512,1024]{2,1,0:T(8,128)(2,1)}, bf16[2,512,1024]{2,1,0:T(8,128)(2,1)}) custom-call(bf16[1,512,1024]{2,1,0:T(8,128)(2,1)} %get-tuple-element.156.q_ref, bf16[2,512,1024]{2,1,0:T(8,128)(2,1)} %get-tuple-element.153.own_ref, bf16[2,512,1024]{2,1,0:T(8,128)(2,1)} %copy-done.6, ...), custom_call_target="tpu_custom_call" | custom-call | bytes 67200000 | tf_op jit(solution)/shard_map/attend_back/pallas_call | solution.py:758
  406.2 10.0 %middle_back.1 = (f32[512,1024]{1,0:T(8,128)}, bf16[512,1024]{1,0:T(8,128)(2,1)}, bf16[1,512,1024]{2,1,0:T(8,128)(2,1)}, f32[2,1024]{1,0:T(2,128)}) custom-call(s32[10]{0:T(128)} %stack.70.info_ref, bf16[1,512,1024]{2,1,0:T(8,128)(2,1)} %get-tuple-element.228.refs_0_.yo_ref, bf16[8,4,13,128,256]{4,3,2,1,0:T(8,128)(2,1)} %bitcast.133, ...), custom_call_target="tpu_custom_call" | custom-call | bytes 32000000 | tf_op jit(solution)/shard_map/middle_back/pallas_call | solution.py:116
  418.5 7.3 %source_back.1 = (bf16[256,1024]{1,0:T(8,128)(2,1)}, bf16[256,1024]{1,0:T(8,128)(2,1)}, bf16[2,512,1024]{2,1,0:T(8,128)(2,1)}) custom-call(s32[10]{0:T(128)} %stack.70.info_ref, bf16[2,512,1024]{2,1,0:T(8,128)(2,1)} %get-tuple-element.218.refs_0_, bf16[2,512,1024]{2,1,0:T(8,128)(2,1)} %copy-done.15, bf16[8,4,13,128,256]{4,3,2,1,0:T(8,128)(2,1)} %bitcast.135), custom_call_target="tpu_custom_call" | custom-call | bytes 22400000 | tf_op jit(solution)/shard_map/source_back/pallas_call | solution.py:116
  425.7 7.2 %reduce-scatter.9.cloned.1.call-done = bf16[1,4,128,256]{2,3,1,0:T(8,128)(2,1)} async-done(((bf16[4,4,128,256]{2,3,1,0:T(8,128)(2,1)}), bf16[1,4,128,256]{2,3,1,0:T(8,128)(2,1)}) %reduce-scatter.9.cloned.1.call-update) | async-done | bytes 262160 | tf_op jit(solution)/shard_map/reduce_scatter | solution.py:1076
  447.8 6.8 %weight_grad.13 = bf16[4,4,4,128,256]{4,3,2,1,0:T(8,128)(2,1)} custom-call(s32[10]{0:T(128)} %stack.70.info_ref, bf16[512,1024]{1,0:T(8,128)(2,1)} %get-tuple-element.185.xo_ref, bf16[512,1024]{1,0:T(8,128)(2,1)} %collective-permute-done.26.xp_ref, bf16[2,512,1024]{2,1,0:T(8,128)(2,1)} %get-tuple-element.224.yo_ref, ...), custom_call_target="tpu_custom_call", output_to_operand_aliasing={{}: (5, {})} | custom-call | bytes 22400000 | tf_op jit(solution)/shard_map/weight_grad/pallas_call | solution.py:961
  460.3 5.5 collective-permute-start.37
  465.8 20.9 %attend_back.3 = (bf16[1,512,1024]{2,1,0:T(8,128)(2,1)}, bf16[2,512,1024]{2,1,0:T(8,128)(2,1)}, bf16[2,512,1024]{2,1,0:T(8,128)(2,1)}) custom-call(bf16[1,512,1024]{2,1,0:T(8,128)(2,1)} %get-tuple-element.144.q_ref, bf16[2,512,1024]{2,1,0:T(8,128)(2,1)} %get-tuple-element.145.own_ref, bf16[2,512,1024]{2,1,0:T(8,128)(2,1)} %copy-done.5, ...), custom_call_target="tpu_custom_call" | custom-call | bytes 67200000 | tf_op jit(solution)/shard_map/attend_back/pallas_call | solution.py:758
  493.8 15.2 %exit_back.1 = (bf16[1024,512]{1,0:T(8,128)(2,1)}, bf16[2,512,1024]{2,1,0:T(8,128)(2,1)}, f32[4,1024]{1,0:T(4,128)}) custom-call(s32[10]{0:T(128)} %stack.70.info_ref, bf16[1,512,1024]{2,1,0:T(8,128)(2,1)} %get-tuple-element.238.refs_0_.yo_ref, bf16[2,512,1024]{2,1,0:T(8,128)(2,1)} %get-tuple-element.239.refs_1_, bf16[2,512,1024]{2,1,0:T(8,128)(2,1)} %copy-done.16, ...), custom_call_target="tpu_custom_call" | custom-call | bytes 48000000 | tf_op jit(solution)/shard_map/exit_back/pallas_call | solution.py:116
  509.1 11.4 %all-to-all-done.3 = bf16[4,4,4,128,256]{4,3,2,1,0:T(8,128)(2,1)} async-done(((bf16[4,4,4,128,256]{4,3,2,1,0:T(8,128)(2,1)}), bf16[4,4,4,128,256]{4,3,2,1,0:T(8,128)(2,1)}, u32[]{:S(2)}, u32[]{:S(2)}) %all-to-all-start.3) | async-done | bytes 4194336 | tf_op jit(solution)/shard_map/all_to_all | solution.py:1255
  525.5 5.2 weight_grad.14.refs_0_
  542.0 6.8 %weight_grad.15 = bf16[4,4,3,128,256]{4,3,2,1,0:T(8,128)(2,1)} custom-call(s32[10]{0:T(128)} %stack.70.info_ref, bf16[512,1024]{1,0:T(8,128)(2,1)} %get-tuple-element.182.xo_ref, bf16[512,1024]{1,0:T(8,128)(2,1)} %copy-done.11, bf16[2,512,1024]{2,1,0:T(8,128)(2,1)} %get-tuple-element.252.yo_ref, ...), custom_call_target="tpu_custom_call", output_to_operand_aliasing={{}: (5, {})} | custom-call | bytes 22400000 | tf_op jit(solution)/shard_map/weight_grad/pallas_call | solution.py:961
  571.6 56.7 %scatter_tokens.1 = (f32[32,131072]{1,0:T(8,128)}, f32[2,32,512]{2,1,0:T(8,128)}) custom-call(s32[16384]{0:T(1024)} %add_select_fusion.rows_ref, s32[32,1,512]{2,1,0:T(1,128)} %get-tuple-element.335.row_ref, s32[32,1,512]{2,1,0:T(1,128)} %and_select_fusion.1.group_ref, bf16[32,32,512]{2,1,0:T(8,128)(2,1)} %copy-done.8), custom_call_target="tpu_custom_call" | custom-call | bytes 182400000 | tf_op jit(solution)/shard_map/scatter_tokens/pallas_call | solution.py:288
  648.8 7.7 %collective-permute-done.52 = bf16[3,128,256]{2,1,0:T(8,128)(2,1)S(1)} collective-permute-done((bf16[3,128,256]{2,1,0:T(8,128)(2,1)S(1)}, bf16[3,128,256]{2,1,0:T(8,128)(2,1)S(1)}, u32[]{:S(2)}, u32[]{:S(2)}) %collective-permute-start.52) | collective-permute-done | bytes 196640 | tf_op jit(solution)/shard_map/ppermute | solution.py:1088
  (304 shorter events, 170.6 us)
Async XLA Ops:
  7.2 229.1 %all-gather.3.cloned.1.call-start = ((), (), s32[]{:S(2)}) async-start(), calls=%async_computation.12 | async-start | bytes 28114944 | tf_op jit(solution)/shard_map/all_gather | solution.py:1024
  27.3 52.0 %all-to-all-start = ((bf16[4,512,256]{2,1,0:T(8,128)(2,1)}), bf16[4,512,256]{2,1,0:T(8,128)(2,1)S(1)}, u32[]{:S(2)}, u32[]{:S(2)}) async-start(bf16[4,512,256]{2,1,0:T(8,128)(2,1)} %broadcast_in_dim.57), calls=%async_computation | async-start | bytes 2097152 | tf_op jit(solution)/shard_map/all_to_all | solution.py:1157
  79.3 71.3 %all-to-all-start.2 = ((bf16[32,32,512]{2,1,0:T(8,128)(2,1)}), bf16[32,32,512]{2,1,0:T(8,128)(2,1)}, u32[]{:S(2)}, u32[]{:S(2)}) async-start(bf16[32,32,512]{2,1,0:T(8,128)(2,1)} %gather_tokens.1), calls=%async_computation.2 | async-start | bytes 2097152 | tf_op jit(solution)/shard_map/all_to_all | solution.py:1201
  83.7 319.5 %reduce-scatter.13.cloned.1.call-start = ((), (), s32[]{:S(2)}) async-start(), calls=%async_computation.13 | async-start | bytes 5242880
  85.6 30.8 %collective-permute-start.8 = (bf16[4,2,128,256]{3,2,1,0:T(8,128)(2,1)S(1)}, bf16[4,2,128,256]{3,2,1,0:T(8,128)(2,1)S(1)}, u32[]{:S(2)}, u32[]{:S(2)}) collective-permute-start(bf16[4,2,128,256]{3,2,1,0:T(8,128)(2,1)S(1)} %get-tuple-element.348), channel_id=1, source_target_pairs={{0,8},{8,0},{16,24},{24,16},{1,9},{9,1},{17,25},{25,17},{2,10},{10... | collective-permute-start | bytes 1572872 | tf_op jit(solution)/shard_map/ppermute | solution.py:1043
  87.1 32.3 %collective-permute-start.4 = (bf16[4,2,128,256]{3,2,1,0:T(8,128)(2,1)S(1)}, bf16[4,2,128,256]{3,2,1,0:T(8,128)(2,1)S(1)}, u32[]{:S(2)}, u32[]{:S(2)}) collective-permute-start(bf16[4,2,128,256]{3,2,1,0:T(8,128)(2,1)S(1)} %get-tuple-element.349), channel_id=1, source_target_pairs={{0,16},{16,0},{8,24},{24,8},{1,17},{17,1},{9,25},{25,9},{2,18},{18... | collective-permute-start | bytes 1572872 | tf_op jit(solution)/shard_map/ppermute | solution.py:1043
  87.7 40.9 %collective-permute-start.2 = (bf16[4,2,128,256]{3,2,1,0:T(8,128)(2,1)S(1)}, bf16[4,2,128,256]{3,2,1,0:T(8,128)(2,1)S(1)}, u32[]{:S(2)}, u32[]{:S(2)}) collective-permute-start(bf16[4,2,128,256]{3,2,1,0:T(8,128)(2,1)S(1)} %get-tuple-element.349), channel_id=1, source_target_pairs={{0,8},{8,0},{16,24},{24,16},{1,9},{9,1},{17,25},{25,17},{2,10},{10... | collective-permute-start | bytes 1572872 | tf_op jit(solution)/shard_map/ppermute | solution.py:1042
  89.2 61.3 %collective-permute-start.1 = (bf16[4,4,128,256]{3,2,1,0:T(8,128)(2,1)S(1)}, bf16[4,4,128,256]{3,2,1,0:T(8,128)(2,1)S(1)}, u32[]{:S(2)}, u32[]{:S(2)}) collective-permute-start(bf16[4,4,128,256]{3,2,1,0:T(8,128)(2,1)S(1)} %bitcast.137), channel_id=1, source_target_pairs={{0,4},{4,0},{1,5},{5,1},{2,6},{6,2},{3,7},{7,3},{8,12},{12,8},{9,1... | collective-permute-start | bytes 3145736 | tf_op jit(solution)/shard_map/ppermute | solution.py:981
  106.6 35.5 %collective-permute-start.12 = (bf16[4,2,128,256]{3,2,1,0:T(8,128)(2,1)S(1)}, bf16[4,2,128,256]{3,2,1,0:T(8,128)(2,1)}, u32[]{:S(2)}, u32[]{:S(2)}) collective-permute-start(bf16[4,2,128,256]{3,2,1,0:T(8,128)(2,1)S(1)} %collective-permute-done.10), channel_id=1, source_target_pairs={{0,8},{8,0},{16,24},{24,16},{1,9},{9,1},{17,25},{25,17},{2,10},{10... | collective-permute-start | bytes 1572872 | tf_op jit(solution)/shard_map/ppermute | solution.py:1047
  168.6 29.6 %collective-permute-start.16 = (bf16[256,1024]{1,0:T(8,128)(2,1)S(1)}, bf16[256,1024]{1,0:T(8,128)(2,1)S(1)}, u32[]{:S(2)}, u32[]{:S(2)}) collective-permute-start(bf16[256,1024]{1,0:T(8,128)(2,1)S(1)} %get-tuple-element.346), channel_id=1, source_target_pairs={{0,1},{1,5},{2,4},{3,0},{4,3},{5,7},{6,6},{7,2},{8,9},{9,13},{10,1... | collective-permute-start | bytes 1572872 | tf_op jit(solution)/shard_map/ppermute | solution.py:999
  171.8 26.3 %collective-permute-start.15 = (bf16[256,1024]{1,0:T(8,128)(2,1)S(1)}, bf16[256,1024]{1,0:T(8,128)(2,1)S(1)}, u32[]{:S(2)}, u32[]{:S(2)}) collective-permute-start(bf16[256,1024]{1,0:T(8,128)(2,1)S(1)} %get-tuple-element.347), channel_id=1, source_target_pairs={{0,0},{1,4},{2,5},{3,1},{4,2},{5,6},{6,7},{7,3},{8,8},{9,12},{10,1... | collective-permute-start | bytes 1572872 | tf_op jit(solution)/shard_map/ppermute | solution.py:999
  276.4 32.6 %collective-permute-start.21 = (bf16[512,1024]{1,0:T(8,128)(2,1)S(1)}, bf16[512,1024]{1,0:T(8,128)(2,1)}, u32[]{:S(2)}, u32[]{:S(2)}) collective-permute-start(bf16[512,1024]{1,0:T(8,128)(2,1)S(1)} %copy-done.24), channel_id=1, source_target_pairs={{0,4},{4,0},{1,5},{5,1},{2,6},{6,2},{3,7},{7,3},{8,12},{12,8},{9,1... | collective-permute-start | bytes 3145736 | tf_op jit(solution)/shard_map/ppermute | solution.py:981
  276.7 32.4 %collective-permute-start.20 = (bf16[1,512,1024]{2,1,0:T(8,128)(2,1)}, bf16[1,512,1024]{2,1,0:T(8,128)(2,1)}, u32[]{:S(2)}, u32[]{:S(2)}) collective-permute-start(bf16[1,512,1024]{2,1,0:T(8,128)(2,1)} %get-tuple-element.157.refs_0_.yo_ref.o_ref), channel_id=1, source_target_pairs={{0,4},{4,0},{1,5},{5,1},{2,6},{6,2},{3,7},{7,3},{8,12},{12,8},{9,1... | collective-permute-start | bytes 3145736 | tf_op jit(solution)/shard_map/ppermute | solution.py:981
  278.2 30.9 %collective-permute-start.19 = (bf16[256,1024]{1,0:T(8,128)(2,1)}, bf16[256,1024]{1,0:T(8,128)(2,1)S(1)}, u32[]{:S(2)}, u32[]{:S(2)}) collective-permute-start(bf16[256,1024]{1,0:T(8,128)(2,1)} %get-tuple-element.344), channel_id=1, source_target_pairs={{0,1},{1,5},{2,4},{3,0},{4,3},{5,7},{6,6},{7,2},{8,9},{9,13},{10,1... | collective-permute-start | bytes 1572872 | tf_op jit(solution)/shard_map/ppermute | solution.py:999
  280.1 29.0 %collective-permute-start.18 = (bf16[256,1024]{1,0:T(8,128)(2,1)}, bf16[256,1024]{1,0:T(8,128)(2,1)}, u32[]{:S(2)}, u32[]{:S(2)}) collective-permute-start(bf16[256,1024]{1,0:T(8,128)(2,1)} %get-tuple-element.345), channel_id=1, source_target_pairs={{0,0},{1,4},{2,5},{3,1},{4,2},{5,6},{6,7},{7,3},{8,8},{9,12},{10,1... | collective-permute-start | bytes 1572872 | tf_op jit(solution)/shard_map/ppermute | solution.py:999
  309.1 28.4 %collective-permute-start.23 = (bf16[4,512,1024]{2,1,0:T(8,128)(2,1)}, bf16[4,512,1024]{2,1,0:T(8,128)(2,1)}, u32[]{:S(2)}, u32[]{:S(2)}) collective-permute-start(bf16[4,512,1024]{2,1,0:T(8,128)(2,1)} %get-tuple-element.181.yo_ref), channel_id=1, source_target_pairs={{0,4},{4,0},{1,5},{5,1},{2,6},{6,2},{3,7},{7,3},{8,12},{12,8},{9,1... | collective-permute-start | bytes 12582920 | tf_op jit(solution)/shard_map/ppermute | solution.py:981
  309.2 28.2 %collective-permute-start.24 = (bf16[512,1024]{1,0:T(8,128)(2,1)S(1)}, bf16[512,1024]{1,0:T(8,128)(2,1)S(1)}, u32[]{:S(2)}, u32[]{:S(2)}) collective-permute-start(bf16[512,1024]{1,0:T(8,128)(2,1)S(1)} %copy-done.10), channel_id=1, source_target_pairs={{0,4},{4,0},{1,5},{5,1},{2,6},{6,2},{3,7},{7,3},{8,12},{12,8},{9,1... | collective-permute-start | bytes 3145736 | tf_op jit(solution)/shard_map/ppermute | solution.py:981
  309.7 27.8 %collective-permute-start.25 = (bf16[1,512,1024]{2,1,0:T(8,128)(2,1)S(1)}, bf16[1,512,1024]{2,1,0:T(8,128)(2,1)}, u32[]{:S(2)}, u32[]{:S(2)}) collective-permute-start(bf16[1,512,1024]{2,1,0:T(8,128)(2,1)S(1)} %copy-done.2), channel_id=1, source_target_pairs={{0,4},{4,0},{1,5},{5,1},{2,6},{6,2},{3,7},{7,3},{8,12},{12,8},{9,1... | collective-permute-start | bytes 3145736 | tf_op jit(solution)/shard_map/ppermute | solution.py:981
  309.8 27.7 %collective-permute-start.26 = (bf16[512,1024]{1,0:T(8,128)(2,1)}, bf16[512,1024]{1,0:T(8,128)(2,1)}, u32[]{:S(2)}, u32[]{:S(2)}) collective-permute-start(bf16[512,1024]{1,0:T(8,128)(2,1)} %get-tuple-element.185.xo_ref), channel_id=1, source_target_pairs={{0,4},{4,0},{1,5},{5,1},{2,6},{6,2},{3,7},{7,3},{8,12},{12,8},{9,1... | collective-permute-start | bytes 3145736 | tf_op jit(solution)/shard_map/ppermute | solution.py:981
  310.2 27.3 %collective-permute-start.22 = (bf16[512,1024]{1,0:T(8,128)(2,1)}, bf16[512,1024]{1,0:T(8,128)(2,1)}, u32[]{:S(2)}, u32[]{:S(2)}) collective-permute-start(bf16[512,1024]{1,0:T(8,128)(2,1)} %get-tuple-element.192.xo_ref), channel_id=1, source_target_pairs={{0,4},{4,0},{1,5},{5,1},{2,6},{6,2},{3,7},{7,3},{8,12},{12,8},{9,1... | collective-permute-start | bytes 3145736 | tf_op jit(solution)/shard_map/ppermute | solution.py:981
  351.5 81.4 %reduce-scatter.9.cloned.1.call-start = ((), (), s32[]{:S(2)}) async-start(), calls=%async_computation.10 | async-start | bytes 1310720 | tf_op jit(solution)/shard_map/reduce_scatter | solution.py:1076
  353.1 25.8 %collective-permute-start.30 = (bf16[256,1024]{1,0:T(8,128)(2,1)}, bf16[256,1024]{1,0:T(8,128)(2,1)S(1)}, u32[]{:S(2)}, u32[]{:S(2)}) collective-permute-start(bf16[256,1024]{1,0:T(8,128)(2,1)} %get-tuple-element.198), channel_id=1, source_target_pairs={{0,0},{4,1},{5,2},{1,3},{2,4},{6,5},{7,6},{3,7},{8,8},{12,9},{13,1... | collective-permute-start | bytes 1572872 | tf_op jit(solution)/shard_map/ppermute | solution.py:1006
  405.6 143.3 %reduce-scatter.15.cloned.1.call-start = ((), (), s32[]{:S(2)}) async-start(), calls=%async_computation.14 | async-start | bytes 6553600
  454.6 65.9 %all-to-all-start.3 = ((bf16[4,4,4,128,256]{4,3,2,1,0:T(8,128)(2,1)}), bf16[4,4,4,128,256]{4,3,2,1,0:T(8,128)(2,1)}, u32[]{:S(2)}, u32[]{:S(2)}) async-start(bf16[4,4,4,128,256]{4,3,2,1,0:T(8,128)(2,1)} %weight_grad.13), calls=%async_computation.4 | async-start | bytes 8388608 | tf_op jit(solution)/shard_map/all_to_all | solution.py:1255
  459.6 27.2 %collective-permute-start.36 = (bf16[256,1024]{1,0:T(8,128)(2,1)S(1)}, bf16[256,1024]{1,0:T(8,128)(2,1)S(1)}, u32[]{:S(2)}, u32[]{:S(2)}) collective-permute-start(bf16[256,1024]{1,0:T(8,128)(2,1)S(1)} %copy-done.53), channel_id=1, source_target_pairs={{0,0},{4,1},{5,2},{1,3},{2,4},{6,5},{7,6},{3,7},{8,8},{12,9},{13,1... | collective-permute-start | bytes 1572872 | tf_op jit(solution)/shard_map/ppermute | solution.py:1006
  460.3 26.5 %collective-permute-start.37 = (bf16[256,1024]{1,0:T(8,128)(2,1)S(1)}, bf16[256,1024]{1,0:T(8,128)(2,1)S(1)}, u32[]{:S(2)}, u32[]{:S(2)}) collective-permute-start(bf16[256,1024]{1,0:T(8,128)(2,1)S(1)} %copy-done.52), channel_id=1, source_target_pairs={{1,0},{5,1},{4,2},{0,3},{3,4},{7,5},{6,6},{2,7},{9,8},{13,9},{12,1... | collective-permute-start | bytes 1572872 | tf_op jit(solution)/shard_map/ppermute | solution.py:1006
  520.4 30.2 %all-to-all-start.4 = ((bf16[32,32,512]{2,1,0:T(8,128)(2,1)}), bf16[32,32,512]{2,1,0:T(8,128)(2,1)S(1)}, u32[]{:S(2)}, u32[]{:S(2)}) async-start(bf16[32,32,512]{2,1,0:T(8,128)(2,1)} %bitcast.170), calls=%async_computation.5 | async-start | bytes 2097152 | tf_op jit(solution)/shard_map/all_to_all | solution.py:1265
  525.1 133.2 %reduce-scatter.11.cloned.1.call-start = ((), (), s32[]{:S(2)}) async-start(), calls=%async_computation.11 | async-start | bytes 2949120 | tf_op jit(solution)/shard_map/reduce_scatter | solution.py:1076
  552.4 76.0 %all-to-all-start.5 = ((bf16[4,4,3,128,256]{4,3,2,1,0:T(8,128)(2,1)}), bf16[4,4,3,128,256]{4,3,2,1,0:T(8,128)(2,1)S(1)}, u32[]{:S(2)}, u32[]{:S(2)}) async-start(bf16[4,4,3,128,256]{4,3,2,1,0:T(8,128)(2,1)} %weight_grad.15), calls=%async_computation.6 | async-start | bytes 6291456 | tf_op jit(solution)/shard_map/all_to_all | solution.py:1278
  563.5 64.8 %collective-permute-start.47 = (f32[10,1024]{1,0:T(8,128)S(1)}, f32[10,1024]{1,0:T(8,128)S(1)}, u32[]{:S(2)}, u32[]{:S(2)}) collective-permute-start(f32[10,1024]{1,0:T(8,128)S(1)} %add_add_fusion.1), channel_id=1, source_target_pairs={{0,3},{1,0},{2,1},{3,2},{4,7},{5,4},{6,5},{7,6},{8,11},{9,8},{10,9... | collective-permute-start | bytes 122888 | tf_op jit(solution)/shard_map/ppermute | solution.py:1098
  568.2 60.1 %collective-permute-start.46 = (f32[10,1024]{1,0:T(8,128)S(1)}, f32[10,1024]{1,0:T(8,128)S(1)}, u32[]{:S(2)}, u32[]{:S(2)}) collective-permute-start(f32[10,1024]{1,0:T(8,128)S(1)} %add_add_fusion.1), channel_id=1, source_target_pairs={{0,2},{1,3},{2,0},{3,1},{4,6},{5,7},{6,4},{7,5},{8,10},{9,11},{10,... | collective-permute-start | bytes 122888 | tf_op jit(solution)/shard_map/ppermute | solution.py:1098
  568.3 60.1 %collective-permute-start.45 = (f32[10,1024]{1,0:T(8,128)S(1)}, f32[10,1024]{1,0:T(8,128)S(1)}, u32[]{:S(2)}, u32[]{:S(2)}) collective-permute-start(f32[10,1024]{1,0:T(8,128)S(1)} %add_add_fusion.1), channel_id=1, source_target_pairs={{0,1},{1,2},{2,3},{3,0},{4,5},{5,6},{6,7},{7,4},{8,9},{9,10},{10,1... | collective-permute-start | bytes 122888 | tf_op jit(solution)/shard_map/ppermute | solution.py:1098
  (87 other events, 927.1 us)
Sparse Core Ops, SparseCore 0:
  11.9 224.3 all-gather.2
  351.7 51.5 reduce-scatter.12
  405.7 27.2 reduce-scatter.8
  435.8 104.7 reduce-scatter.14
  552.5 52.6 reduce-scatter.10

commit v3 on v2

--- a/solution.py
+++ b/solution.py
@@ -774,6 +774,71 @@
     )(q, own, par, probs, o, do)
 
 
+def causal_back_kernel(
+    info_ref, q_ref, own_ref, par_ref, p_ref, o_ref, do_ref, dq_ref, down_ref, dpar_ref, back
+):
+    tokens = q_ref.shape[1]
+    half = tokens // 2
+    low, high, every = slice(0, half), slice(half, tokens), slice(0, tokens)
+    flat = do_ref[0].astype(f32).T * o_ref[0].astype(f32).T
+    inner = [
+        jnp.sum(flat[h * HEAD_DIM : (h + 1) * HEAD_DIM], axis=0, keepdims=True)
+        for h in range(LANES // HEAD_DIM)
+    ]
+    back[...] = jnp.zeros_like(back)
+
+    def segments(i, kv_ref, d_ref, spans):
+        for h in range(LANES // HEAD_DIM):
+            lanes = slice(h * HEAD_DIM, (h + 1) * HEAD_DIM)
+            for keys, queries in spans:
+                grad = do_ref[0, queries, lanes]
+                probs = p_ref[h, i, keys, queries]
+                d_probs = dot(kv_ref[1, keys, lanes], grad, NT)
+                d_scores = (probs.astype(f32) * (d_probs - inner[h][:, queries])).astype(bf16)
+                d_ref[1, keys, lanes] = dot(probs, grad).astype(bf16)
+                d_ref[0, keys, lanes] = dot(d_scores, q_ref[0, queries, lanes]).astype(bf16)
+                back[lanes, queries] += dot(kv_ref[0, keys, lanes], d_scores, TN)
+
+    segments(0, own_ref, down_ref, [(low, every), (high, high)])
+
+    @pl.when(info_ref[0] == 0)
+    def _():
+        segments(1, par_ref, dpar_ref, [(every, high)])
+
+    @pl.when(info_ref[0] == 1)
+    def _():
+        segments(1, par_ref, dpar_ref, [(low, every)])
+        dpar_ref[:, high, :] = jnp.zeros((2, half, LANES), bf16)
+
+    dq_ref[0] = (back[...].T * HEAD_DIM**-0.5).astype(bf16)
+
+
+def causal_back(info, q, own, par, probs, o, do):
+    _, tokens, width = q.shape
+    heads = width // HEAD_DIM
+    pair = LANES // HEAD_DIM
+    one = pl.BlockSpec((1, tokens, LANES), lambda s, info: (0, 0, s))
+    two = pl.BlockSpec((2, tokens, LANES), lambda s, info: (0, 0, s))
+    kv = jax.ShapeDtypeStruct((2, tokens, width), bf16)
+    return call(
+        causal_back_kernel,
+        info,
+        (heads // pair,),
+        [
+            (q, one),
+            (own, two),
+            (par, two),
+            (probs, pl.BlockSpec((pair, 2, tokens, tokens), lambda s, info: (s, 0, 0, 0))),
+            (o, one),
+            (do, one),
+        ],
+        [(jax.ShapeDtypeStruct((1, tokens, width), bf16), one), (kv, two), (kv, two)],
+        [pltpu.VMEM((LANES, tokens), f32)],
+        cost_estimate=cost(19),
+        name="causal_back",
+    )
+
+
 def middle_back_kernel(
     info_ref, dq_ref, wq_ref, x2_ref, g3_ref, wo_ref, gain_ref, g2_ref, g2b_ref, do_ref, sums_ref
 ):
@@ -1234,8 +1299,7 @@
 
     outs = attend_back(cq, ckv, ckv_par, cprobs, oc, doc)
     (dcq, dckv_own, dckv_par), part_one = lax.optimization_barrier((outs, part_one))
-    part_one = scattered(part_one, "mp")
-    hidden_out = placed_again(hidden_out)
+    part_two = scattered(after(grads, part_one), "chip")
     dckv_came, dcq_par = swap(dckv_par), swap(dcq)
     outs = middle_back(info, dcq, second[0], x2, g3, norm_gains)
     (g2, g2b, do, sums2), dckv_came, dcq_par, dckv_own = lax.optimization_barrier(
@@ -1243,8 +1307,6 @@
     )
     g2b_par = swap(g2b)
     outs = source_back(info, dckv_own, dckv_came, second[1])
-    outs, part_one = lax.optimization_barrier((outs, part_one))
-    part_two = scattered(after(grads, part_one), "chip")
     *enc_grad, dckv = outs
     dckv_after = swap(dckv)
     shape = (chips, mp, 4, rows, block)
@@ -1255,7 +1317,7 @@
     cross_terms = lax.all_to_all(grads, "chip", split_axis=0, concat_axis=0, tiled=True)
     encoder_grad = from_chips(tied(enc_grad, grads), mp)
 
-    outs = attend_back(q, kv, kv_par, probs, o, do)
+    outs = causal_back(info, q, kv, kv_par, probs, o, do)
     (dq, dkv_own, dkv_par), encoder_grad = lax.optimization_barrier((outs, encoder_grad))
     dkv_came = swap(dkv_par)
     dq_par = swap(dq)
@@ -1263,7 +1325,6 @@
     (g0, dkv, sums01), dq_par, cross_terms = lax.optimization_barrier((outs, dq_par, cross_terms))
     sent = g0.reshape(n, feats, tokens)
     arrived = lax.all_to_all(sent, ALL, split_axis=0, concat_axis=0, tiled=True)
-    encoder_grad = placed_again(encoder_grad)
     cross_part = jnp.sum(cross_terms.astype(f32), axis=0).astype(bf16)
     sums = jnp.concatenate((sums01, sums2, sums34), axis=0)
     sums_par = swap(sums)
@@ -1274,17 +1335,22 @@
     sums = total_over(sums + sums_par, "chip", chips)
     grads = weight_grad(info, a, a_par, dkv, dkv_after, shape, 1, grads)
     sums, grads, arrived, part_two = lax.optimization_barrier((sums, grads, arrived, part_two))
-    sums_up = scattered(jnp.concatenate([part_two, cross_part], axis=1), "mp")
+    sums_up = scattered(jnp.concatenate([part_one, part_two, cross_part], axis=1), "mp")
     self_terms = lax.all_to_all(grads, "chip", split_axis=0, concat_axis=0, tiled=True)
     sums = total_over(sums, "mp", mp)
 
     outs = scatter_tokens(arrived, flat_row, row, group, vocab, mp)
     (table_grad, places), self_terms, sums = lax.optimization_barrier((outs, self_terms, sums))
+    hidden_out = placed_again(tied(hidden_out, places))
+    encoder_grad = placed_again(tied(encoder_grad, places))
     self_part = jnp.sum(self_terms.astype(f32), axis=0).astype(bf16)
     self_grads = summed(sent_over(self_part, "mp", mp))
     sums_up = sums_up.astype(f32)
-    feed_out_grads = part_one.astype(f32)
-    feed_in_grads, cross_grads = sums_up[: sub + 1], sums_up[sub + 1 :]
+    feed_out_grads, feed_in_grads, cross_grads = (
+        sums_up[:sub],
+        sums_up[sub : 2 * sub + 1],
+        sums_up[2 * sub + 1 :],
+    )
 
     blocks = places.reshape(CORES, feats, 2, block).transpose(0, 2, 1, 3).reshape(4, feats, block)
     blocks = jnp.stack([blocks[0], blocks[2], blocks[3], blocks[1]])

time: 679 us -> 662 us (0.975)
  waiting for transfers between devices: 152 us -> 138 us
    pallas_call x2 -> x1, Pallas kernels: 42.2 us -> 21.4 us  [attend_back(): pl.pallas_call(attend_back_kernel, out_shape=(jax.ShapeDtypeStruct((1, to...]
    pallas_call x8 -> x9, Pallas kernels: 115 us -> 134 us  [call(): pl.pallas_call(body, out_shape=[o for o, _ in outs], grid_spec=pltpu.Pref...]
    reduce_scatter x2 -> x1, waiting for transfers between devices: 7.21 us -> 0.01 us  [scattered(): return lax.psum_scatter(grads, axis, scatter_dimension=0, tiled=False)]
    unnamed x122 -> x114, local copies, waits for them, and re-layouts: 25.4 us -> 22.6 us
  transfers between devices with their start and end apart: 65 -> 64, of which waited for: 22 -> 18; matrix products, arithmetic and copies ran while one was open for 5% -> 4% of each run, Pallas kernels for 47% -> 48%
where the time goes in v3:
time: 662 us; the launch traced here: 653 us
  Pallas kernels  356 us (54%)
  waiting for transfers between devices  138 us (21%)
  starting transfers between devices  83.9 us (13%)
  local copies, waits for them, and re-layouts  37.7 us (6%)
  other arithmetic  22.1 us (3%)
  between operations  15.3 us (2%)
    pallas_call x9, Pallas kernels, call(): pl.pallas_call(body, out_shape=[o for o, _ in outs], grid_spec=pltpu.Pref...  134 us
    pallas_call x1, Pallas kernels, scatter_tokens(): pl.pallas_call(functools.partial(scatter_kernel, groups, per_core), out_s...  56.7 us
    pallas_call x8, Pallas kernels, weight_grad(): pl.pallas_call(functools.partial(weight_grad_kernel, chips, before is not...  55 us
    pallas_call x1, Pallas kernels, gather_tokens(): pl.pallas_call(functools.partial(gather_kernel, groups, fill), out_shape=...  45.6 us
    pallas_call x2, Pallas kernels, attend(): pl.pallas_call(functools.partial(attend_kernel, causal), out_shape=(jax.S...  43.5 us
    ppermute x4, waiting for transfers between devices, begin(): lax.ppermute(w, 'chip', p)  38.9 us
    all_gather x1, waiting for transfers between devices, gathered(): value = lax.all_gather(rows, ALL, axis=0, tiled=False)  38.1 us
    unnamed x114, local copies, waits for them, and re-layouts  22.6 us
  transfers between devices with their start and end apart: 64, of which 18 were waited for; matrix products, arithmetic and copies ran while one was open for 4% of the time, Pallas kernels for 48%

profile of v3, /device:TPU:0, one launch (start us, length us, event | category | flops | bytes accessed | tf_op | source)
XLA Modules:
  0.0 653.4 jit_solution(13825167880676822380)
XLA Ops:
  12.5 7.3 %all-to-all-start.1 = ((s32[32,1,512]{2,1,0:T(1,128)}), s32[32,1,512]{2,1,0:T(1,128)S(1)}, u32[]{:S(2)}, u32[]{:S(2)}) async-start(s32[32,1,512]{2,1,0:T(1,128)} %broadcast_in_dim.59), calls=%async_computation.1 | async-start | bytes 131072 | tf_op jit(solution)/shard_map/all_to_all | solution.py:1208
  20.9 6.4 all-to-all-done.1
  33.6 45.6 %gather_tokens.1 = bf16[32,32,512]{2,1,0:T(8,128)(2,1)} custom-call(s32[16384]{0:T(1024)} %add_select_fusion.rows_ref, s32[32,1,512]{2,1,0:T(1,128)} %and_select_fusion.1.group_ref, bf16[32,131072]{1,0:T(8,128)(2,1)} %refs_3_.1, bf16[32,131072]{1,0:T(8,128)(2,1)} %refs_3_.1, bf16[32,131072]{1,0:T(8,128)(2,1)} %refs_3_.1, bf16[32,131072]{1,0:T(8,128)(2,1)} %refs_3_.1), custom_call_target="tpu_custom_call" | custom-call | bytes 144000000 | tf_op jit(solution)/shard_map/gather_tokens/pallas_call | solution.py:185
  89.4 17.2 %collective-permute-done.10 = bf16[4,2,128,256]{3,2,1,0:T(8,128)(2,1)S(1)} collective-permute-done((bf16[4,2,128,256]{3,2,1,0:T(8,128)(2,1)S(1)}, bf16[4,2,128,256]{3,2,1,0:T(8,128)(2,1)S(1)}, u32[]{:S(2)}, u32[]{:S(2)}) %collective-permute-start.10) | collective-permute-done | bytes 524320 | tf_op jit(solution)/shard_map/ppermute | solution.py:1107
  106.9 9.6 %collective-permute-done.8 = bf16[4,2,128,256]{3,2,1,0:T(8,128)(2,1)S(1)} collective-permute-done((bf16[4,2,128,256]{3,2,1,0:T(8,128)(2,1)S(1)}, bf16[4,2,128,256]{3,2,1,0:T(8,128)(2,1)S(1)}, u32[]{:S(2)}, u32[]{:S(2)}) %collective-permute-start.8) | collective-permute-done | bytes 524320 | tf_op jit(solution)/shard_map/ppermute | solution.py:1108
  119.4 9.2 %collective-permute-done.2 = bf16[4,2,128,256]{3,2,1,0:T(8,128)(2,1)S(1)} collective-permute-done((bf16[4,2,128,256]{3,2,1,0:T(8,128)(2,1)S(1)}, bf16[4,2,128,256]{3,2,1,0:T(8,128)(2,1)S(1)}, u32[]{:S(2)}, u32[]{:S(2)}) %collective-permute-start.2) | collective-permute-done | bytes 524320 | tf_op jit(solution)/shard_map/ppermute | solution.py:1107
  129.9 12.2 %collective-permute-done.12 = bf16[4,2,128,256]{3,2,1,0:T(8,128)(2,1)} collective-permute-done((bf16[4,2,128,256]{3,2,1,0:T(8,128)(2,1)S(1)}, bf16[4,2,128,256]{3,2,1,0:T(8,128)(2,1)}, u32[]{:S(2)}, u32[]{:S(2)}) %collective-permute-start.12) | collective-permute-done | bytes 524320 | tf_op jit(solution)/shard_map/ppermute | solution.py:1112
  151.6 15.2 %entry.1 = (f32[512,1024]{1,0:T(8,128)}, f32[512,1024]{1,0:T(8,128)}, bf16[512,1024]{1,0:T(8,128)(2,1)}, bf16[1,512,1024]{2,1,0:T(8,128)(2,1)}, bf16[2,512,1024]{2,1,0:T(8,128)(2,1)}) custom-call(s32[10]{0:T(128)} %stack.70.info_ref, bf16[1024,512]{1,0:T(8,128)(2,1)} %bitcast.16.refs_0_, bf16[1,4,4,128,256]{4,3,2,1,0:T(8,128)(2,1)} %bitcast.139, ...), custom_call_target="tpu_custom_call" | custom-call | bytes 48000000 | tf_op jit(solution)/shard_map/entry/pallas_call | solution.py:116
  174.1 21.7 %attend.2 = (bf16[1,512,1024]{2,1,0:T(8,128)(2,1)}, bf16[16,2,512,512]{3,2,1,0:T(8,128)(2,1)}) custom-call(s32[10]{0:T(128)} %stack.70.info_ref, bf16[1,512,1024]{2,1,0:T(8,128)(2,1)} %get-tuple-element.144.q_ref.refs_0_, bf16[2,512,1024]{2,1,0:T(8,128)(2,1)} %get-tuple-element.145.own_ref.refs_1_, bf16[2,512,1024]{2,1,0:T(8,128)(2,1)} %copy-done.6), custom_call_target="tpu_custom_call" | custom-call | bytes 70400000 | tf_op jit(solution)/shard_map/attend/pallas_call | solution.py:496
  198.2 38.1 %all-gather.3.cloned.1.call-done = bf16[53248,256]{1,0:T(8,128)(2,1)} async-done(((bf16[1664,256]{1,0:T(8,128)(2,1)}), bf16[53248,256]{1,0:T(8,128)(2,1)}) %all-gather.3.cloned.1.call-update) | async-done | bytes 27262992 | tf_op jit(solution)/shard_map/all_gather | solution.py:1089
  236.3 7.6 %source_keys.1 = (bf16[512,1024]{1,0:T(8,128)(2,1)}, bf16[2,512,1024]{2,1,0:T(8,128)(2,1)}) custom-call(s32[10]{0:T(128)} %stack.70.info_ref, bf16[256,1024]{1,0:T(8,128)(2,1)} %copy-done.36, bf16[256,1024]{1,0:T(8,128)(2,1)} %copy-done.35, bf16[8,4,13,128,256]{4,3,2,1,0:T(8,128)(2,1)} %bitcast.125), custom_call_target="tpu_custom_call" | custom-call | bytes 25600000 | tf_op jit(solution)/shard_map/source_keys/pallas_call | solution.py:116
  244.2 9.1 %middle.1 = (f32[512,1024]{1,0:T(8,128)}, bf16[512,1024]{1,0:T(8,128)(2,1)}, bf16[1,512,1024]{2,1,0:T(8,128)(2,1)}) custom-call(s32[10]{0:T(128)} %stack.70.info_ref, bf16[1,512,1024]{2,1,0:T(8,128)(2,1)} %get-tuple-element.183.refs_0_.yo_ref.refs_4_, bf16[8,4,13,128,256]{4,3,2,1,0:T(8,128)(2,1)} %bitcast.126, ...), custom_call_target="tpu_custom_call" | custom-call | bytes 28800000 | tf_op jit(solution)/shard_map/middle/pallas_call | solution.py:116
  254.6 21.8 %attend.3 = (bf16[1,512,1024]{2,1,0:T(8,128)(2,1)}, bf16[16,2,512,512]{3,2,1,0:T(8,128)(2,1)}) custom-call(s32[10]{0:T(128)} %stack.70.info_ref, bf16[1,512,1024]{2,1,0:T(8,128)(2,1)} %get-tuple-element.156.q_ref, bf16[2,512,1024]{2,1,0:T(8,128)(2,1)} %get-tuple-element.153.own_ref, bf16[2,512,1024]{2,1,0:T(8,128)(2,1)} %copy-done.5), custom_call_target="tpu_custom_call" | custom-call | bytes 70400000 | tf_op jit(solution)/shard_map/attend/pallas_call | solution.py:496
  280.1 5.7 collective-permute-start.18
  285.8 23.1 %feed.1 = (f32[512,1024]{1,0:T(8,128)}, bf16[512,1024]{1,0:T(8,128)(2,1)}, bf16[4,512,1024]{2,1,0:T(8,128)(2,1)}, bf16[4,512,1024]{2,1,0:T(8,128)(2,1)}, f32[512,1024]{1,0:T(8,128)}) custom-call(s32[10]{0:T(128)} %stack.70.info_ref, bf16[1,512,1024]{2,1,0:T(8,128)(2,1)} %get-tuple-element.157.refs_0_.yo_ref.o_ref, bf16[8,4,13,128,256]{4,3,2,1,0:T(8,128)(2,1)} %bitcast.128, ...), custom_call_target="tpu_custom_call" | custom-call | bytes 89600000 | tf_op jit(solution)/shard_map/feed/pallas_call | solution.py:116
  310.2 27.1 %feed_back.1 = (bf16[256,1024]{1,0:T(8,128)(2,1)}, bf16[256,1024]{1,0:T(8,128)(2,1)}, bf16[512,1024]{1,0:T(8,128)(2,1)}, bf16[4,512,1024]{2,1,0:T(8,128)(2,1)}, ...) custom-call(s32[10]{0:T(128)} %stack.70.info_ref, ...), custom_call_target="tpu_custom_call" | custom-call | bytes 89600000 | tf_op jit(solution)/shard_map/feed_back/pallas_call | solution.py:116
  341.4 10.1 %weight_grad.8 = bf16[4,4,4,128,256]{4,3,2,1,0:T(8,128)(2,1)} custom-call(s32[10]{0:T(128)} %stack.70.info_ref, bf16[512,1024]{1,0:T(8,128)(2,1)} %get-tuple-element.188.xo_ref, bf16[512,1024]{1,0:T(8,128)(2,1)} %copy-done.27, bf16[4,512,1024]{2,1,0:T(8,128)(2,1)} %get-tuple-element.181.yo_ref, bf16[4,512,1024]{2,1,0:T(8,128)(2,1)} %collective-permute-done.23.yp_ref), custom_call_target="tpu_custom_call" | custom-call | bytes 35200000 | tf_op jit(solution)/shard_map/weight_grad/pallas_call | solution.py:1026
  361.3 5.4 weight_grad.9.refs_0_
  368.8 10.1 %weight_grad.10 = bf16[4,4,5,128,256]{4,3,2,1,0:T(8,128)(2,1)} custom-call(s32[10]{0:T(128)} %stack.70.info_ref, bf16[512,1024]{1,0:T(8,128)(2,1)} %get-tuple-element.192.xo_ref, bf16[512,1024]{1,0:T(8,128)(2,1)} %collective-permute-done.22.xp_ref, bf16[4,512,1024]{2,1,0:T(8,128)(2,1)} %get-tuple-element.194.yo_ref, ...), custom_call_target="tpu_custom_call", output_to_operand_aliasing={{}: (5, {})} | custom-call | bytes 35200000 | tf_op jit(solution)/shard_map/weight_grad/pallas_call | solution.py:1026
  378.9 21.4 %attend_back.1 = (bf16[1,512,1024]{2,1,0:T(8,128)(2,1)}, bf16[2,512,1024]{2,1,0:T(8,128)(2,1)}, bf16[2,512,1024]{2,1,0:T(8,128)(2,1)}) custom-call(bf16[1,512,1024]{2,1,0:T(8,128)(2,1)} %get-tuple-element.156.q_ref, bf16[2,512,1024]{2,1,0:T(8,128)(2,1)} %get-tuple-element.153.own_ref, bf16[2,512,1024]{2,1,0:T(8,128)(2,1)} %copy-done.5, ...), custom_call_target="tpu_custom_call" | custom-call | bytes 67200000 | tf_op jit(solution)/shard_map/attend_back/pallas_call | solution.py:758
  406.0 10.0 %middle_back.1 = (f32[512,1024]{1,0:T(8,128)}, bf16[512,1024]{1,0:T(8,128)(2,1)}, bf16[1,512,1024]{2,1,0:T(8,128)(2,1)}, f32[2,1024]{1,0:T(2,128)}) custom-call(s32[10]{0:T(128)} %stack.70.info_ref, bf16[1,512,1024]{2,1,0:T(8,128)(2,1)} %get-tuple-element.224.refs_0_.yo_ref, bf16[8,4,13,128,256]{4,3,2,1,0:T(8,128)(2,1)} %bitcast.134, ...), custom_call_target="tpu_custom_call" | custom-call | bytes 32000000 | tf_op jit(solution)/shard_map/middle_back/pallas_call | solution.py:116
  417.4 7.6 %source_back.1 = (bf16[256,1024]{1,0:T(8,128)(2,1)}, bf16[256,1024]{1,0:T(8,128)(2,1)}, bf16[2,512,1024]{2,1,0:T(8,128)(2,1)}) custom-call(s32[10]{0:T(128)} %stack.70.info_ref, bf16[2,512,1024]{2,1,0:T(8,128)(2,1)} %get-tuple-element.218.refs_0_, bf16[2,512,1024]{2,1,0:T(8,128)(2,1)} %copy-done.14, bf16[8,4,13,128,256]{4,3,2,1,0:T(8,128)(2,1)} %bitcast.136), custom_call_target="tpu_custom_call" | custom-call | bytes 22400000 | tf_op jit(solution)/shard_map/source_back/pallas_call | solution.py:116
  425.7 5.5 weight_grad.11.refs_0_
  432.1 5.3 weight_grad.12.refs_0_
  438.7 6.8 %weight_grad.13 = bf16[4,4,4,128,256]{4,3,2,1,0:T(8,128)(2,1)} custom-call(s32[10]{0:T(128)} %stack.70.info_ref, bf16[512,1024]{1,0:T(8,128)(2,1)} %get-tuple-element.185.xo_ref, bf16[512,1024]{1,0:T(8,128)(2,1)} %collective-permute-done.26.xp_ref, bf16[2,512,1024]{2,1,0:T(8,128)(2,1)} %get-tuple-element.220.yo_ref, ...), custom_call_target="tpu_custom_call", output_to_operand_aliasing={{}: (5, {})} | custom-call | bytes 22400000 | tf_op jit(solution)/shard_map/weight_grad/pallas_call | solution.py:1026
  451.4 6.7 %collective-permute-start.37 = (bf16[256,1024]{1,0:T(8,128)(2,1)S(1)}, bf16[256,1024]{1,0:T(8,128)(2,1)S(1)}, u32[]{:S(2)}, u32[]{:S(2)}) collective-permute-start(bf16[256,1024]{1,0:T(8,128)(2,1)S(1)} %copy-done.48), channel_id=1, source_target_pairs={{1,0},{5,1},{4,2},{0,3},{3,4},{7,5},{6,6},{2,7},{9,8},{13,9},{12,1... | collective-permute-start | bytes 1572872 | tf_op jit(solution)/shard_map/ppermute | solution.py:1071
  458.2 19.0 %causal_back.1 = (bf16[1,512,1024]{2,1,0:T(8,128)(2,1)}, bf16[2,512,1024]{2,1,0:T(8,128)(2,1)}, bf16[2,512,1024]{2,1,0:T(8,128)(2,1)}) custom-call(s32[10]{0:T(128)} %stack.70.info_ref, bf16[1,512,1024]{2,1,0:T(8,128)(2,1)} %get-tuple-element.144.q_ref.refs_0_, bf16[2,512,1024]{2,1,0:T(8,128)(2,1)} %get-tuple-element.145.own_ref.refs_1_, ...), custom_call_target="tpu_custom_call" | custom-call | bytes 60800000 | tf_op jit(solution)/shard_map/causal_back/pallas_call | solution.py:116
  485.4 15.0 %exit_back.1 = (bf16[1024,512]{1,0:T(8,128)(2,1)}, bf16[2,512,1024]{2,1,0:T(8,128)(2,1)}, f32[4,1024]{1,0:T(4,128)}) custom-call(s32[10]{0:T(128)} %stack.70.info_ref, bf16[1,512,1024]{2,1,0:T(8,128)(2,1)} %get-tuple-element.234.refs_0_.yo_ref, bf16[2,512,1024]{2,1,0:T(8,128)(2,1)} %get-tuple-element.235.refs_1_, bf16[2,512,1024]{2,1,0:T(8,128)(2,1)} %copy-done.13, ...), custom_call_target="tpu_custom_call" | custom-call | bytes 48000000 | tf_op jit(solution)/shard_map/exit_back/pallas_call | solution.py:116
  500.5 10.7 %all-to-all-done.3 = bf16[4,4,4,128,256]{4,3,2,1,0:T(8,128)(2,1)} async-done(((bf16[4,4,4,128,256]{4,3,2,1,0:T(8,128)(2,1)}), bf16[4,4,4,128,256]{4,3,2,1,0:T(8,128)(2,1)}, u32[]{:S(2)}, u32[]{:S(2)}) %all-to-all-start.3) | async-done | bytes 4194336 | tf_op jit(solution)/shard_map/all_to_all | solution.py:1317
  531.0 6.7 %weight_grad.15 = bf16[4,4,3,128,256]{4,3,2,1,0:T(8,128)(2,1)} custom-call(s32[10]{0:T(128)} %stack.70.info_ref, bf16[512,1024]{1,0:T(8,128)(2,1)} %get-tuple-element.182.xo_ref, bf16[512,1024]{1,0:T(8,128)(2,1)} %copy-done.12, bf16[2,512,1024]{2,1,0:T(8,128)(2,1)} %get-tuple-element.248.yo_ref, ...), custom_call_target="tpu_custom_call", output_to_operand_aliasing={{}: (5, {})} | custom-call | bytes 22400000 | tf_op jit(solution)/shard_map/weight_grad/pallas_call | solution.py:1026
  553.6 56.7 %scatter_tokens.1 = (f32[32,131072]{1,0:T(8,128)}, f32[2,32,512]{2,1,0:T(8,128)}) custom-call(s32[16384]{0:T(1024)} %add_select_fusion.rows_ref, s32[32,1,512]{2,1,0:T(1,128)} %get-tuple-element.335.row_ref, s32[32,1,512]{2,1,0:T(1,128)} %and_select_fusion.1.group_ref, bf16[32,32,512]{2,1,0:T(8,128)(2,1)} %copy-done.9), custom_call_target="tpu_custom_call" | custom-call | bytes 182400000 | tf_op jit(solution)/shard_map/scatter_tokens/pallas_call | solution.py:288
  629.1 8.9 %collective-permute-done.52 = bf16[3,128,256]{2,1,0:T(8,128)(2,1)S(1)} collective-permute-done((bf16[3,128,256]{2,1,0:T(8,128)(2,1)S(1)}, bf16[3,128,256]{2,1,0:T(8,128)(2,1)S(1)}, u32[]{:S(2)}, u32[]{:S(2)}) %collective-permute-start.52) | collective-permute-done | bytes 196640 | tf_op jit(solution)/shard_map/ppermute | solution.py:1153
  (292 shorter events, 155.2 us)
Async XLA Ops:
  7.2 229.1 %all-gather.3.cloned.1.call-start = ((), (), s32[]{:S(2)}) async-start(), calls=%async_computation.10 | async-start | bytes 28114944 | tf_op jit(solution)/shard_map/all_gather | solution.py:1089
  27.3 52.0 %all-to-all-start = ((bf16[4,512,256]{2,1,0:T(8,128)(2,1)}), bf16[4,512,256]{2,1,0:T(8,128)(2,1)S(1)}, u32[]{:S(2)}, u32[]{:S(2)}) async-start(bf16[4,512,256]{2,1,0:T(8,128)(2,1)} %broadcast_in_dim.57), calls=%async_computation | async-start | bytes 2097152 | tf_op jit(solution)/shard_map/all_to_all | solution.py:1222
  79.3 71.3 %all-to-all-start.2 = ((bf16[32,32,512]{2,1,0:T(8,128)(2,1)}), bf16[32,32,512]{2,1,0:T(8,128)(2,1)}, u32[]{:S(2)}, u32[]{:S(2)}) async-start(bf16[32,32,512]{2,1,0:T(8,128)(2,1)} %gather_tokens.1), calls=%async_computation.2 | async-start | bytes 2097152 | tf_op jit(solution)/shard_map/all_to_all | solution.py:1266
  83.7 319.4 %reduce-scatter.10.cloned.1.call-start = ((), (), s32[]{:S(2)}) async-start(), calls=%async_computation.11 | async-start | bytes 5242880
  85.6 30.8 %collective-permute-start.8 = (bf16[4,2,128,256]{3,2,1,0:T(8,128)(2,1)S(1)}, bf16[4,2,128,256]{3,2,1,0:T(8,128)(2,1)S(1)}, u32[]{:S(2)}, u32[]{:S(2)}) collective-permute-start(bf16[4,2,128,256]{3,2,1,0:T(8,128)(2,1)S(1)} %get-tuple-element.348), channel_id=1, source_target_pairs={{0,8},{8,0},{16,24},{24,16},{1,9},{9,1},{17,25},{25,17},{2,10},{10... | collective-permute-start | bytes 1572872 | tf_op jit(solution)/shard_map/ppermute | solution.py:1108
  87.1 32.3 %collective-permute-start.4 = (bf16[4,2,128,256]{3,2,1,0:T(8,128)(2,1)S(1)}, bf16[4,2,128,256]{3,2,1,0:T(8,128)(2,1)S(1)}, u32[]{:S(2)}, u32[]{:S(2)}) collective-permute-start(bf16[4,2,128,256]{3,2,1,0:T(8,128)(2,1)S(1)} %get-tuple-element.349), channel_id=1, source_target_pairs={{0,16},{16,0},{8,24},{24,8},{1,17},{17,1},{9,25},{25,9},{2,18},{18... | collective-permute-start | bytes 1572872 | tf_op jit(solution)/shard_map/ppermute | solution.py:1108
  87.7 40.9 %collective-permute-start.2 = (bf16[4,2,128,256]{3,2,1,0:T(8,128)(2,1)S(1)}, bf16[4,2,128,256]{3,2,1,0:T(8,128)(2,1)S(1)}, u32[]{:S(2)}, u32[]{:S(2)}) collective-permute-start(bf16[4,2,128,256]{3,2,1,0:T(8,128)(2,1)S(1)} %get-tuple-element.349), channel_id=1, source_target_pairs={{0,8},{8,0},{16,24},{24,16},{1,9},{9,1},{17,25},{25,17},{2,10},{10... | collective-permute-start | bytes 1572872 | tf_op jit(solution)/shard_map/ppermute | solution.py:1107
  89.2 61.3 %collective-permute-start.1 = (bf16[4,4,128,256]{3,2,1,0:T(8,128)(2,1)S(1)}, bf16[4,4,128,256]{3,2,1,0:T(8,128)(2,1)S(1)}, u32[]{:S(2)}, u32[]{:S(2)}) collective-permute-start(bf16[4,4,128,256]{3,2,1,0:T(8,128)(2,1)S(1)} %bitcast.138), channel_id=1, source_target_pairs={{0,4},{4,0},{1,5},{5,1},{2,6},{6,2},{3,7},{7,3},{8,12},{12,8},{9,1... | collective-permute-start | bytes 3145736 | tf_op jit(solution)/shard_map/ppermute | solution.py:1046
  106.6 35.5 %collective-permute-start.12 = (bf16[4,2,128,256]{3,2,1,0:T(8,128)(2,1)S(1)}, bf16[4,2,128,256]{3,2,1,0:T(8,128)(2,1)}, u32[]{:S(2)}, u32[]{:S(2)}) collective-permute-start(bf16[4,2,128,256]{3,2,1,0:T(8,128)(2,1)S(1)} %collective-permute-done.10), channel_id=1, source_target_pairs={{0,8},{8,0},{16,24},{24,16},{1,9},{9,1},{17,25},{25,17},{2,10},{10... | collective-permute-start | bytes 1572872 | tf_op jit(solution)/shard_map/ppermute | solution.py:1112
  116.5 25.7 %collective-permute-start.11 = (bf16[4,2,128,256]{3,2,1,0:T(8,128)(2,1)S(1)}, bf16[4,2,128,256]{3,2,1,0:T(8,128)(2,1)S(1)}, u32[]{:S(2)}, u32[]{:S(2)}) collective-permute-start(bf16[4,2,128,256]{3,2,1,0:T(8,128)(2,1)S(1)} %collective-permute-done.10), channel_id=1, source_target_pairs={{0,4},{4,0},{1,5},{5,1},{2,6},{6,2},{3,7},{7,3},{8,12},{12,8},{9,1... | collective-permute-start | bytes 1572872 | tf_op jit(solution)/shard_map/ppermute | solution.py:1046
  168.6 29.6 %collective-permute-start.16 = (bf16[256,1024]{1,0:T(8,128)(2,1)S(1)}, bf16[256,1024]{1,0:T(8,128)(2,1)S(1)}, u32[]{:S(2)}, u32[]{:S(2)}) collective-permute-start(bf16[256,1024]{1,0:T(8,128)(2,1)S(1)} %get-tuple-element.346), channel_id=1, source_target_pairs={{0,1},{1,5},{2,4},{3,0},{4,3},{5,7},{6,6},{7,2},{8,9},{9,13},{10,1... | collective-permute-start | bytes 1572872 | tf_op jit(solution)/shard_map/ppermute | solution.py:1064
  171.8 26.3 %collective-permute-start.15 = (bf16[256,1024]{1,0:T(8,128)(2,1)S(1)}, bf16[256,1024]{1,0:T(8,128)(2,1)S(1)}, u32[]{:S(2)}, u32[]{:S(2)}) collective-permute-start(bf16[256,1024]{1,0:T(8,128)(2,1)S(1)} %get-tuple-element.347), channel_id=1, source_target_pairs={{0,0},{1,4},{2,5},{3,1},{4,2},{5,6},{6,7},{7,3},{8,8},{9,12},{10,1... | collective-permute-start | bytes 1572872 | tf_op jit(solution)/shard_map/ppermute | solution.py:1064
  276.4 32.6 %collective-permute-start.21 = (bf16[512,1024]{1,0:T(8,128)(2,1)S(1)}, bf16[512,1024]{1,0:T(8,128)(2,1)}, u32[]{:S(2)}, u32[]{:S(2)}) collective-permute-start(bf16[512,1024]{1,0:T(8,128)(2,1)S(1)} %copy-done.21), channel_id=1, source_target_pairs={{0,4},{4,0},{1,5},{5,1},{2,6},{6,2},{3,7},{7,3},{8,12},{12,8},{9,1... | collective-permute-start | bytes 3145736 | tf_op jit(solution)/shard_map/ppermute | solution.py:1046
  276.7 32.3 %collective-permute-start.20 = (bf16[1,512,1024]{2,1,0:T(8,128)(2,1)}, bf16[1,512,1024]{2,1,0:T(8,128)(2,1)}, u32[]{:S(2)}, u32[]{:S(2)}) collective-permute-start(bf16[1,512,1024]{2,1,0:T(8,128)(2,1)} %get-tuple-element.157.refs_0_.yo_ref.o_ref), channel_id=1, source_target_pairs={{0,4},{4,0},{1,5},{5,1},{2,6},{6,2},{3,7},{7,3},{8,12},{12,8},{9,1... | collective-permute-start | bytes 3145736 | tf_op jit(solution)/shard_map/ppermute | solution.py:1046
  278.2 30.8 %collective-permute-start.19 = (bf16[256,1024]{1,0:T(8,128)(2,1)}, bf16[256,1024]{1,0:T(8,128)(2,1)S(1)}, u32[]{:S(2)}, u32[]{:S(2)}) collective-permute-start(bf16[256,1024]{1,0:T(8,128)(2,1)} %get-tuple-element.344), channel_id=1, source_target_pairs={{0,1},{1,5},{2,4},{3,0},{4,3},{5,7},{6,6},{7,2},{8,9},{9,13},{10,1... | collective-permute-start | bytes 1572872 | tf_op jit(solution)/shard_map/ppermute | solution.py:1064
  280.1 28.9 %collective-permute-start.18 = (bf16[256,1024]{1,0:T(8,128)(2,1)}, bf16[256,1024]{1,0:T(8,128)(2,1)}, u32[]{:S(2)}, u32[]{:S(2)}) collective-permute-start(bf16[256,1024]{1,0:T(8,128)(2,1)} %get-tuple-element.345), channel_id=1, source_target_pairs={{0,0},{1,4},{2,5},{3,1},{4,2},{5,6},{6,7},{7,3},{8,8},{9,12},{10,1... | collective-permute-start | bytes 1572872 | tf_op jit(solution)/shard_map/ppermute | solution.py:1064
  309.0 28.4 %collective-permute-start.23 = (bf16[4,512,1024]{2,1,0:T(8,128)(2,1)}, bf16[4,512,1024]{2,1,0:T(8,128)(2,1)}, u32[]{:S(2)}, u32[]{:S(2)}) collective-permute-start(bf16[4,512,1024]{2,1,0:T(8,128)(2,1)} %get-tuple-element.181.yo_ref), channel_id=1, source_target_pairs={{0,4},{4,0},{1,5},{5,1},{2,6},{6,2},{3,7},{7,3},{8,12},{12,8},{9,1... | collective-permute-start | bytes 12582920 | tf_op jit(solution)/shard_map/ppermute | solution.py:1046
  309.1 28.2 %collective-permute-start.24 = (bf16[512,1024]{1,0:T(8,128)(2,1)S(1)}, bf16[512,1024]{1,0:T(8,128)(2,1)S(1)}, u32[]{:S(2)}, u32[]{:S(2)}) collective-permute-start(bf16[512,1024]{1,0:T(8,128)(2,1)S(1)} %copy-done.11), channel_id=1, source_target_pairs={{0,4},{4,0},{1,5},{5,1},{2,6},{6,2},{3,7},{7,3},{8,12},{12,8},{9,1... | collective-permute-start | bytes 3145736 | tf_op jit(solution)/shard_map/ppermute | solution.py:1046
  309.6 27.8 %collective-permute-start.25 = (bf16[1,512,1024]{2,1,0:T(8,128)(2,1)S(1)}, bf16[1,512,1024]{2,1,0:T(8,128)(2,1)}, u32[]{:S(2)}, u32[]{:S(2)}) collective-permute-start(bf16[1,512,1024]{2,1,0:T(8,128)(2,1)S(1)} %copy-done.2), channel_id=1, source_target_pairs={{0,4},{4,0},{1,5},{5,1},{2,6},{6,2},{3,7},{7,3},{8,12},{12,8},{9,1... | collective-permute-start | bytes 3145736 | tf_op jit(solution)/shard_map/ppermute | solution.py:1046
  309.7 27.7 %collective-permute-start.26 = (bf16[512,1024]{1,0:T(8,128)(2,1)}, bf16[512,1024]{1,0:T(8,128)(2,1)}, u32[]{:S(2)}, u32[]{:S(2)}) collective-permute-start(bf16[512,1024]{1,0:T(8,128)(2,1)} %get-tuple-element.185.xo_ref), channel_id=1, source_target_pairs={{0,4},{4,0},{1,5},{5,1},{2,6},{6,2},{3,7},{7,3},{8,12},{12,8},{9,1... | collective-permute-start | bytes 3145736 | tf_op jit(solution)/shard_map/ppermute | solution.py:1046
  310.1 27.3 %collective-permute-start.22 = (bf16[512,1024]{1,0:T(8,128)(2,1)}, bf16[512,1024]{1,0:T(8,128)(2,1)}, u32[]{:S(2)}, u32[]{:S(2)}) collective-permute-start(bf16[512,1024]{1,0:T(8,128)(2,1)} %get-tuple-element.192.xo_ref), channel_id=1, source_target_pairs={{0,4},{4,0},{1,5},{5,1},{2,6},{6,2},{3,7},{7,3},{8,12},{12,8},{9,1... | collective-permute-start | bytes 3145736 | tf_op jit(solution)/shard_map/ppermute | solution.py:1046
  351.5 186.2 %reduce-scatter.12.cloned.1.call-start = ((), (), s32[]{:S(2)}) async-start(), calls=%async_computation.12 | async-start | bytes 6553600
  353.1 25.8 %collective-permute-start.30 = (bf16[256,1024]{1,0:T(8,128)(2,1)}, bf16[256,1024]{1,0:T(8,128)(2,1)S(1)}, u32[]{:S(2)}, u32[]{:S(2)}) collective-permute-start(bf16[256,1024]{1,0:T(8,128)(2,1)} %get-tuple-element.198), channel_id=1, source_target_pairs={{0,0},{4,1},{5,2},{1,3},{2,4},{6,5},{7,6},{3,7},{8,8},{12,9},{13,1... | collective-permute-start | bytes 1572872 | tf_op jit(solution)/shard_map/ppermute | solution.py:1071
  445.5 65.7 %all-to-all-start.3 = ((bf16[4,4,4,128,256]{4,3,2,1,0:T(8,128)(2,1)}), bf16[4,4,4,128,256]{4,3,2,1,0:T(8,128)(2,1)}, u32[]{:S(2)}, u32[]{:S(2)}) async-start(bf16[4,4,4,128,256]{4,3,2,1,0:T(8,128)(2,1)} %weight_grad.13), calls=%async_computation.3 | async-start | bytes 8388608 | tf_op jit(solution)/shard_map/all_to_all | solution.py:1317
  450.7 26.4 %collective-permute-start.36 = (bf16[256,1024]{1,0:T(8,128)(2,1)S(1)}, bf16[256,1024]{1,0:T(8,128)(2,1)S(1)}, u32[]{:S(2)}, u32[]{:S(2)}) collective-permute-start(bf16[256,1024]{1,0:T(8,128)(2,1)S(1)} %copy-done.49), channel_id=1, source_target_pairs={{0,0},{4,1},{5,2},{1,3},{2,4},{6,5},{7,6},{3,7},{8,8},{12,9},{13,1... | collective-permute-start | bytes 1572872 | tf_op jit(solution)/shard_map/ppermute | solution.py:1071
  451.4 25.8 %collective-permute-start.37 = (bf16[256,1024]{1,0:T(8,128)(2,1)S(1)}, bf16[256,1024]{1,0:T(8,128)(2,1)S(1)}, u32[]{:S(2)}, u32[]{:S(2)}) collective-permute-start(bf16[256,1024]{1,0:T(8,128)(2,1)S(1)} %copy-done.48), channel_id=1, source_target_pairs={{1,0},{5,1},{4,2},{0,3},{3,4},{7,5},{6,6},{2,7},{9,8},{13,9},{12,1... | collective-permute-start | bytes 1572872 | tf_op jit(solution)/shard_map/ppermute | solution.py:1071
  511.2 29.8 %all-to-all-start.4 = ((bf16[32,32,512]{2,1,0:T(8,128)(2,1)}), bf16[32,32,512]{2,1,0:T(8,128)(2,1)S(1)}, u32[]{:S(2)}, u32[]{:S(2)}) async-start(bf16[32,32,512]{2,1,0:T(8,128)(2,1)} %bitcast.171), calls=%async_computation.4 | async-start | bytes 2097152 | tf_op jit(solution)/shard_map/all_to_all | solution.py:1327
  515.9 123.9 %reduce-scatter.8.cloned.1.call-start = ((), (), s32[]{:S(2)}) async-start(), calls=%async_computation.9 | async-start | bytes 4259840 | tf_op jit(solution)/shard_map/reduce_scatter | solution.py:1141
  544.4 66.0 %all-to-all-start.5 = ((bf16[4,4,3,128,256]{4,3,2,1,0:T(8,128)(2,1)}), bf16[4,4,3,128,256]{4,3,2,1,0:T(8,128)(2,1)S(1)}, u32[]{:S(2)}, u32[]{:S(2)}) async-start(bf16[4,4,3,128,256]{4,3,2,1,0:T(8,128)(2,1)} %weight_grad.15), calls=%async_computation.5 | async-start | bytes 6291456 | tf_op jit(solution)/shard_map/all_to_all | solution.py:1339
  548.1 62.2 %collective-permute-start.47 = (f32[10,1024]{1,0:T(8,128)S(1)}, f32[10,1024]{1,0:T(8,128)S(1)}, u32[]{:S(2)}, u32[]{:S(2)}) collective-permute-start(f32[10,1024]{1,0:T(8,128)S(1)} %add_add_fusion.1), channel_id=1, source_target_pairs={{0,3},{1,0},{2,1},{3,2},{4,7},{5,4},{6,5},{7,6},{8,11},{9,8},{10,9... | collective-permute-start | bytes 122888 | tf_op jit(solution)/shard_map/ppermute | solution.py:1163
  551.4 59.0 %collective-permute-start.46 = (f32[10,1024]{1,0:T(8,128)S(1)}, f32[10,1024]{1,0:T(8,128)S(1)}, u32[]{:S(2)}, u32[]{:S(2)}) collective-permute-start(f32[10,1024]{1,0:T(8,128)S(1)} %add_add_fusion.1), channel_id=1, source_target_pairs={{0,2},{1,3},{2,0},{3,1},{4,6},{5,7},{6,4},{7,5},{8,10},{9,11},{10,... | collective-permute-start | bytes 122888 | tf_op jit(solution)/shard_map/ppermute | solution.py:1163
  552.7 57.6 %collective-permute-start.45 = (f32[10,1024]{1,0:T(8,128)S(1)}, f32[10,1024]{1,0:T(8,128)S(1)}, u32[]{:S(2)}, u32[]{:S(2)}) collective-permute-start(f32[10,1024]{1,0:T(8,128)S(1)} %add_add_fusion.1), channel_id=1, source_target_pairs={{0,1},{1,2},{2,3},{3,0},{4,5},{5,6},{6,7},{7,4},{8,9},{9,10},{10,1... | collective-permute-start | bytes 122888 | tf_op jit(solution)/shard_map/ppermute | solution.py:1163
  (82 other events, 893.6 us)
Sparse Core Ops, SparseCore 0:
  11.9 224.3 all-gather.2
  351.6 51.4 reduce-scatter.9
  406.4 96.2 reduce-scatter.11
  544.5 68.0 reduce-scatter.7

commit v4 on v3

--- a/solution.py
+++ b/solution.py
@@ -1,4 +1,5 @@
 import functools
+import math
 
 import jax
 import jax.numpy as jnp
@@ -202,13 +203,15 @@
 
 
 BATCH = 16
+WIDTH = 4096
+SENDERS = 8
 
 
 def scatter_kernel(
     groups, per_core, rows_ref, row_ref, group_ref, grad_ref, out_ref, pos_ref, acc, update, turned, sem
 ):
     step = pl.program_id(0)
-    feats, tokens = grad_ref.shape[1:]
+    senders, feats, tokens = grad_ref.shape
     height = acc.shape[0]
     width = turned.shape[2]
 
@@ -221,32 +224,39 @@
         lax.fori_loop(0, height // 256, clear, 0)
         pos_ref[...] = jnp.zeros_like(pos_ref)
 
-    grads = grad_ref[0].astype(f32)
-    core = lax.rem(lax.div(step, per_core), CORES)
-    pos_ref[core] += grads
-    tall = jnp.concatenate([grads] * groups, axis=0)
-    own = lax.broadcasted_iota(i32, (LANES, tokens), 0) // feats == group_ref[0]
-    tall = jnp.where(own, tall, 0.0).astype(bf16)
     row = lax.broadcasted_iota(i32, (LANES, LANES), 0)
     col = lax.broadcasted_iota(i32, (LANES, LANES), 1)
     near = row // BATCH == col // BATCH
-    for b in range(tokens // LANES):
-        at = slice(b * LANES, (b + 1) * LANES)
-        along = jnp.broadcast_to(row_ref[0][:, at].astype(f32), (LANES, LANES))
-        same = jnp.where((along == along.T) & near, 1.0, 0.0).astype(bf16)
-        update[at, :] = dot(same, tall[:, at], NT)
-    base = step * tokens
-
-    def some(k, carry):
-        where = [rows_ref[base + k * BATCH + u] for u in range(BATCH)]
-        fresh = [
-            acc[pl.ds(where[u], 1), :] + update[pl.ds(k * BATCH + u, 1), :] for u in range(BATCH)
-        ]
-        for u in range(BATCH):
-            acc[pl.ds(where[u], 1), :] = fresh[u]
+
+    def sender(d, carry):
+        place = step * senders + d
+        grads = grad_ref[d].astype(f32)
+        core = lax.rem(lax.div(place, per_core), CORES)
+        pos_ref[core] += grads
+        tall = jnp.concatenate([grads] * groups, axis=0)
+        own = lax.broadcasted_iota(i32, (LANES, tokens), 0) // feats == group_ref[d]
+        tall = jnp.where(own, tall, 0.0).astype(bf16)
+        for b in range(tokens // LANES):
+            at = slice(b * LANES, (b + 1) * LANES)
+            along = jnp.broadcast_to(row_ref[d][:, at].astype(f32), (LANES, LANES))
+            same = jnp.where((along == along.T) & near, 1.0, 0.0).astype(bf16)
+            update[at, :] = dot(same, tall[:, at], NT)
+        base = place * tokens
+
+        def some(k, carry):
+            where = [rows_ref[base + k * BATCH + u] for u in range(BATCH)]
+            fresh = [
+                acc[pl.ds(where[u], 1), :] + update[pl.ds(k * BATCH + u, 1), :]
+                for u in range(BATCH)
+            ]
+            for u in range(BATCH):
+                acc[pl.ds(where[u], 1), :] = fresh[u]
+            return carry
+
+        lax.fori_loop(0, tokens // BATCH, some, 0, unroll=True)
         return carry
 
-    lax.fori_loop(0, tokens // BATCH, some, 0)
+    lax.fori_loop(0, senders, sender, 0)
 
     @pl.when(step == pl.num_programs(0) - 1)
     def _():
@@ -283,8 +293,9 @@
     n, feats, tokens = grads.shape
     groups = LANES // feats
     height = vocab // groups
-    width = min(1024, height)
-    token_spec = pl.BlockSpec((1, 1, tokens), lambda s, r: (s, 0, 0))
+    width = min(WIDTH, height)
+    senders = math.gcd(n, SENDERS)
+    token_spec = pl.BlockSpec((senders, 1, tokens), lambda s, r: (s, 0, 0))
     return pl.pallas_call(
         functools.partial(scatter_kernel, groups, per_core),
         out_shape=(
@@ -293,11 +304,11 @@
         ),
         grid_spec=pltpu.PrefetchScalarGridSpec(
             num_scalar_prefetch=1,
-            grid=(n,),
+            grid=(n // senders,),
             in_specs=[
                 token_spec,
                 token_spec,
-                pl.BlockSpec((1, feats, tokens), lambda s, r: (s, 0, 0)),
+                pl.BlockSpec((senders, feats, tokens), lambda s, r: (s, 0, 0)),
             ],
             out_specs=(
                 pl.BlockSpec(memory_space=pl.ANY),
@@ -311,7 +322,7 @@
             ],
         ),
         compiler_params=params(),
-        cost_estimate=cost(57),
+        cost_estimate=cost(39),
         name="scatter_tokens",
     )(rows, row, group, grads)
 
@@ -1213,9 +1224,10 @@
     )
     third = packed(split(feedforward_input_weight), split(feedforward_output_weight))
     sub = feedforward_input_weight.shape[1] // block
-    late = gathered(jnp.concatenate([second, third]), rows, chips, mp)
-    second = [(late, 0)], [(late, 2)]
-    third = [(late, 5)], [(late, 5 + sub)]
+    second = gathered(second, rows, chips, mp)
+    third = gathered(third, rows, chips, mp)
+    second = [(second, 0)], [(second, 2)]
+    third = [(third, 0)], [(third, sub)]
     stepped = chips == 4
     if stepped:
         copies = jnp.broadcast_to(first[None], (mp,) + first.shape)
@@ -1314,18 +1326,20 @@
     grads = weight_grad(info, g2b, g2b_par, o, o_par, shape, 1, grads)
     grads = weight_grad(info, states, states_par, dckv, dckv_after, shape, 2, grads)
     do = after(do, grads)
-    cross_terms = lax.all_to_all(grads, "chip", split_axis=0, concat_axis=0, tiled=True)
+    cross_grads = grads
     encoder_grad = from_chips(tied(enc_grad, grads), mp)
 
     outs = causal_back(info, q, kv, kv_par, probs, o, do)
-    (dq, dkv_own, dkv_par), encoder_grad = lax.optimization_barrier((outs, encoder_grad))
+    (dq, dkv_own, dkv_par), encoder_grad, part_two = lax.optimization_barrier(
+        (outs, encoder_grad, part_two)
+    )
+    cross_part = scattered(after(cross_grads, part_two), "chip")
     dkv_came = swap(dkv_par)
     dq_par = swap(dq)
     outs = exit_back(info, dq, dkv_own, dkv_came, first, x1, x0, g2, norm_gains)
-    (g0, dkv, sums01), dq_par, cross_terms = lax.optimization_barrier((outs, dq_par, cross_terms))
+    (g0, dkv, sums01), dq_par = lax.optimization_barrier((outs, dq_par))
     sent = g0.reshape(n, feats, tokens)
     arrived = lax.all_to_all(sent, ALL, split_axis=0, concat_axis=0, tiled=True)
-    cross_part = jnp.sum(cross_terms.astype(f32), axis=0).astype(bf16)
     sums = jnp.concatenate((sums01, sums2, sums34), axis=0)
     sums_par = swap(sums)
     shape = (chips, mp, 3, rows, block)
@@ -1334,7 +1348,7 @@
     grads, sums_par = lax.optimization_barrier((grads, sums_par))
     sums = total_over(sums + sums_par, "chip", chips)
     grads = weight_grad(info, a, a_par, dkv, dkv_after, shape, 1, grads)
-    sums, grads, arrived, part_two = lax.optimization_barrier((sums, grads, arrived, part_two))
+    sums, grads, arrived, cross_part = lax.optimization_barrier((sums, grads, arrived, cross_part))
     sums_up = scattered(jnp.concatenate([part_one, part_two, cross_part], axis=1), "mp")
     self_terms = lax.all_to_all(grads, "chip", split_axis=0, concat_axis=0, tiled=True)
     sums = total_over(sums, "mp", mp)

time: 662 us -> 632 us (0.955)
  Pallas kernels: 356 us -> 340 us
  waiting for transfers between devices: 138 us -> 124 us
    all_gather x1 -> x2, waiting for transfers between devices: 38.1 us -> 3.73 us  [gathered(): value = lax.all_gather(rows, ALL, axis=0, tiled=False)]
    pallas_call x1, Pallas kernels: 56.7 us -> 39.3 us  [scatter_tokens(): pl.pallas_call(functools.partial(scatter_kernel, groups, per_core), out_s...]
    ppermute x3, waiting for transfers between devices: 8.89 us -> 21.7 us  [sent_over(): terms.append(part if k == 0 else lax.ppermute(part, axis, perm))]
    all_to_all x2 -> x1, waiting for transfers between devices: 10.7 us -> 0.01 us  [body(): lax.all_to_all(grads, 'chip', split_axis=0, concat_axis=0, tiled=True)]
    unnamed x6 -> x9, waiting for transfers between devices: 2.91 us -> 13.6 us
    ppermute x4, waiting for transfers between devices: 2.44 us -> 12.7 us  [to_chips(): lax.ppermute(jnp.where(slot ^ turn == 0, value[0], value[1]), LINE, moves)]
    unnamed x114 -> x99, local copies, waits for them, and re-layouts: 22.6 us -> 24.6 us
  transfers between devices with their start and end apart: 64 -> 65, of which waited for: 18 -> 18; matrix products, arithmetic and copies ran while one was open for 4% -> 5% of each run, Pallas kernels for 48% -> 53%
where the time goes in v4:
time: 632 us; the launch traced here: 624 us
  Pallas kernels  340 us (54%)
  waiting for transfers between devices  124 us (20%)
  starting transfers between devices  83.7 us (13%)
  local copies, waits for them, and re-layouts  39.6 us (6%)
  other arithmetic  21.6 us (3%)
  between operations  15.5 us (2%)
    pallas_call x9, Pallas kernels, call(): pl.pallas_call(body, out_shape=[o for o, _ in outs], grid_spec=pltpu.Pref...  134 us
    pallas_call x8, Pallas kernels, weight_grad(): pl.pallas_call(functools.partial(weight_grad_kernel, chips, before is not...  55.4 us
    pallas_call x1, Pallas kernels, gather_tokens(): pl.pallas_call(functools.partial(gather_kernel, groups, fill), out_shape=...  45.7 us
    pallas_call x2, Pallas kernels, attend(): pl.pallas_call(functools.partial(attend_kernel, causal), out_shape=(jax.S...  43.5 us
    ppermute x4, waiting for transfers between devices, begin(): lax.ppermute(w, 'chip', p)  40.4 us
    pallas_call x1, Pallas kernels, scatter_tokens(): pl.pallas_call(functools.partial(scatter_kernel, groups, per_core), out_s...  39.3 us
    unnamed x99, local copies, waits for them, and re-layouts  24.6 us
    ppermute x3, waiting for transfers between devices, sent_over(): terms.append(part if k == 0 else lax.ppermute(part, axis, perm))  21.7 us
  transfers between devices with their start and end apart: 65, of which 18 were waited for; matrix products, arithmetic and copies ran while one was open for 5% of the time, Pallas kernels for 53%

profile of v4, /device:TPU:0, one launch (start us, length us, event | category | flops | bytes accessed | tf_op | source)
XLA Modules:
  0.0 623.7 jit_solution(13714162800034532268)
XLA Ops:
  13.0 7.3 %all-to-all-start.1 = ((s32[32,1,512]{2,1,0:T(1,128)}), s32[32,1,512]{2,1,0:T(1,128)S(1)}, u32[]{:S(2)}, u32[]{:S(2)}) async-start(s32[32,1,512]{2,1,0:T(1,128)} %broadcast_in_dim.59), calls=%async_computation.1 | async-start | bytes 131072 | tf_op jit(solution)/shard_map/all_to_all | solution.py:1219
  21.3 6.4 %all-to-all-done.1 = s32[32,1,512]{2,1,0:T(1,128)S(1)} async-done(((s32[32,1,512]{2,1,0:T(1,128)}), s32[32,1,512]{2,1,0:T(1,128)S(1)}, u32[]{:S(2)}, u32[]{:S(2)}) %all-to-all-start.1) | async-done | bytes 65568 | tf_op jit(solution)/shard_map/all_to_all | solution.py:1219
  34.1 45.7 %gather_tokens.1 = bf16[32,32,512]{2,1,0:T(8,128)(2,1)} custom-call(s32[16384]{0:T(1024)} %add_select_fusion.rows_ref, s32[32,1,512]{2,1,0:T(1,128)} %and_select_fusion.1.group_ref, bf16[32,131072]{1,0:T(8,128)(2,1)} %refs_3_.1, bf16[32,131072]{1,0:T(8,128)(2,1)} %refs_3_.1, bf16[32,131072]{1,0:T(8,128)(2,1)} %refs_3_.1, bf16[32,131072]{1,0:T(8,128)(2,1)} %refs_3_.1), custom_call_target="tpu_custom_call" | custom-call | bytes 144000000 | tf_op jit(solution)/shard_map/gather_tokens/pallas_call | solution.py:186
  90.0 30.1 %collective-permute-done.2 = bf16[4,2,128,256]{3,2,1,0:T(8,128)(2,1)S(1)} collective-permute-done((bf16[4,2,128,256]{3,2,1,0:T(8,128)(2,1)S(1)}, bf16[4,2,128,256]{3,2,1,0:T(8,128)(2,1)S(1)}, u32[]{:S(2)}, u32[]{:S(2)}) %collective-permute-start.2) | collective-permute-done | bytes 524320 | tf_op jit(solution)/shard_map/ppermute | solution.py:1118
  121.7 10.0 %collective-permute-done.10 = bf16[4,2,128,256]{3,2,1,0:T(8,128)(2,1)} collective-permute-done((bf16[4,2,128,256]{3,2,1,0:T(8,128)(2,1)S(1)}, bf16[4,2,128,256]{3,2,1,0:T(8,128)(2,1)}, u32[]{:S(2)}, u32[]{:S(2)}) %collective-permute-start.10) | collective-permute-done | bytes 524320 | tf_op jit(solution)/shard_map/ppermute | solution.py:1118
  133.7 9.1 %collective-permute-done.6 = bf16[4,2,128,256]{3,2,1,0:T(8,128)(2,1)} collective-permute-done((bf16[4,2,128,256]{3,2,1,0:T(8,128)(2,1)S(1)}, bf16[4,2,128,256]{3,2,1,0:T(8,128)(2,1)}, u32[]{:S(2)}, u32[]{:S(2)}) %collective-permute-start.6) | collective-permute-done | bytes 524320 | tf_op jit(solution)/shard_map/ppermute | solution.py:1123
  149.2 15.3 %entry.1 = (f32[512,1024]{1,0:T(8,128)}, f32[512,1024]{1,0:T(8,128)}, bf16[512,1024]{1,0:T(8,128)(2,1)}, bf16[1,512,1024]{2,1,0:T(8,128)(2,1)}, bf16[2,512,1024]{2,1,0:T(8,128)(2,1)}) custom-call(s32[10]{0:T(128)} %stack.70.info_ref, bf16[1024,512]{1,0:T(8,128)(2,1)} %bitcast.16.refs_0_, bf16[1,4,4,128,256]{4,3,2,1,0:T(8,128)(2,1)} %bitcast.141, ...), custom_call_target="tpu_custom_call" | custom-call | bytes 48000000 | tf_op jit(solution)/shard_map/entry/pallas_call | solution.py:117
  173.4 21.6 %attend.2 = (bf16[1,512,1024]{2,1,0:T(8,128)(2,1)}, bf16[16,2,512,512]{3,2,1,0:T(8,128)(2,1)}) custom-call(s32[10]{0:T(128)} %stack.70.info_ref, bf16[1,512,1024]{2,1,0:T(8,128)(2,1)} %get-tuple-element.145.q_ref.refs_0_, bf16[2,512,1024]{2,1,0:T(8,128)(2,1)} %get-tuple-element.146.own_ref.refs_1_, bf16[2,512,1024]{2,1,0:T(8,128)(2,1)} %copy-done.9), custom_call_target="tpu_custom_call" | custom-call | bytes 70400000 | tf_op jit(solution)/shard_map/attend/pallas_call | solution.py:507
  195.1 12.7 %collective-permute-done.16.refs_1_ = bf16[256,1024]{1,0:T(8,128)(2,1)S(1)} collective-permute-done((bf16[256,1024]{1,0:T(8,128)(2,1)S(1)}, bf16[256,1024]{1,0:T(8,128)(2,1)S(1)}, u32[]{:S(2)}, u32[]{:S(2)}) %collective-permute-start.16) | collective-permute-done | bytes 524320 | tf_op jit(solution)/shard_map/ppermute | solution.py:1075
  208.6 8.6 %source_keys.1 = (bf16[512,1024]{1,0:T(8,128)(2,1)}, bf16[2,512,1024]{2,1,0:T(8,128)(2,1)}) custom-call(s32[10]{0:T(128)} %stack.70.info_ref, bf16[256,1024]{1,0:T(8,128)(2,1)} %copy-done.34, bf16[256,1024]{1,0:T(8,128)(2,1)} %copy-done.35, bf16[8,4,5,128,256]{4,3,2,1,0:T(8,128)(2,1)} %bitcast.127), custom_call_target="tpu_custom_call" | custom-call | bytes 25600000 | tf_op jit(solution)/shard_map/source_keys/pallas_call | solution.py:117
  220.8 9.0 %middle.1 = (f32[512,1024]{1,0:T(8,128)}, bf16[512,1024]{1,0:T(8,128)(2,1)}, bf16[1,512,1024]{2,1,0:T(8,128)(2,1)}) custom-call(s32[10]{0:T(128)} %stack.70.info_ref, bf16[1,512,1024]{2,1,0:T(8,128)(2,1)} %get-tuple-element.184.refs_0_.yo_ref.refs_4_, bf16[8,4,5,128,256]{4,3,2,1,0:T(8,128)(2,1)} %bitcast.128, ...), custom_call_target="tpu_custom_call" | custom-call | bytes 28800000 | tf_op jit(solution)/shard_map/middle/pallas_call | solution.py:117
  231.2 21.8 %attend.3 = (bf16[1,512,1024]{2,1,0:T(8,128)(2,1)}, bf16[16,2,512,512]{3,2,1,0:T(8,128)(2,1)}) custom-call(s32[10]{0:T(128)} %stack.70.info_ref, bf16[1,512,1024]{2,1,0:T(8,128)(2,1)} %get-tuple-element.157.q_ref, bf16[2,512,1024]{2,1,0:T(8,128)(2,1)} %get-tuple-element.154.own_ref, bf16[2,512,1024]{2,1,0:T(8,128)(2,1)} %copy-done.8), custom_call_target="tpu_custom_call" | custom-call | bytes 70400000 | tf_op jit(solution)/shard_map/attend/pallas_call | solution.py:507
  264.4 22.8 %feed.1 = (f32[512,1024]{1,0:T(8,128)}, bf16[512,1024]{1,0:T(8,128)(2,1)}, bf16[4,512,1024]{2,1,0:T(8,128)(2,1)}, bf16[4,512,1024]{2,1,0:T(8,128)(2,1)}, f32[512,1024]{1,0:T(8,128)}) custom-call(s32[10]{0:T(128)} %stack.70.info_ref, bf16[1,512,1024]{2,1,0:T(8,128)(2,1)} %get-tuple-element.158.refs_0_.yo_ref.o_ref, bf16[8,4,5,128,256]{4,3,2,1,0:T(8,128)(2,1)} %bitcast.130, ...), custom_call_target="tpu_custom_call" | custom-call | bytes 89600000 | tf_op jit(solution)/shard_map/feed/pallas_call | solution.py:117
  288.6 27.1 %feed_back.1 = (bf16[256,1024]{1,0:T(8,128)(2,1)}, bf16[256,1024]{1,0:T(8,128)(2,1)}, bf16[512,1024]{1,0:T(8,128)(2,1)}, bf16[4,512,1024]{2,1,0:T(8,128)(2,1)}, ...) custom-call(s32[10]{0:T(128)} %stack.70.info_ref, ...), custom_call_target="tpu_custom_call" | custom-call | bytes 89600000 | tf_op jit(solution)/shard_map/feed_back/pallas_call | solution.py:117
  319.7 10.1 %weight_grad.8 = bf16[4,4,4,128,256]{4,3,2,1,0:T(8,128)(2,1)} custom-call(s32[10]{0:T(128)} %stack.70.info_ref, bf16[512,1024]{1,0:T(8,128)(2,1)} %get-tuple-element.189.xo_ref, bf16[512,1024]{1,0:T(8,128)(2,1)} %copy-done.27, bf16[4,512,1024]{2,1,0:T(8,128)(2,1)} %get-tuple-element.182.yo_ref, bf16[4,512,1024]{2,1,0:T(8,128)(2,1)} %collective-permute-done.23.yp_ref), custom_call_target="tpu_custom_call" | custom-call | bytes 35200000 | tf_op jit(solution)/shard_map/weight_grad/pallas_call | solution.py:1037
  332.9 6.8 %collective-permute-start.31 = (bf16[256,1024]{1,0:T(8,128)(2,1)}, bf16[256,1024]{1,0:T(8,128)(2,1)S(1)}, u32[]{:S(2)}, u32[]{:S(2)}) collective-permute-start(bf16[256,1024]{1,0:T(8,128)(2,1)} %get-tuple-element.200), channel_id=1, source_target_pairs={{1,0},{5,1},{4,2},{0,3},{3,4},{7,5},{6,6},{2,7},{9,8},{13,9},{12,1... | collective-permute-start | bytes 1572872 | tf_op jit(solution)/shard_map/ppermute | solution.py:1082
  340.7 5.2 weight_grad.9.refs_0_
  347.9 10.4 %weight_grad.10 = bf16[4,4,5,128,256]{4,3,2,1,0:T(8,128)(2,1)} custom-call(s32[10]{0:T(128)} %stack.70.info_ref, bf16[512,1024]{1,0:T(8,128)(2,1)} %get-tuple-element.193.xo_ref, bf16[512,1024]{1,0:T(8,128)(2,1)} %collective-permute-done.22.xp_ref, bf16[4,512,1024]{2,1,0:T(8,128)(2,1)} %get-tuple-element.195.yo_ref, ...), custom_call_target="tpu_custom_call", output_to_operand_aliasing={{}: (5, {})} | custom-call | bytes 35200000 | tf_op jit(solution)/shard_map/weight_grad/pallas_call | solution.py:1037
  358.4 21.4 %attend_back.1 = (bf16[1,512,1024]{2,1,0:T(8,128)(2,1)}, bf16[2,512,1024]{2,1,0:T(8,128)(2,1)}, bf16[2,512,1024]{2,1,0:T(8,128)(2,1)}) custom-call(bf16[1,512,1024]{2,1,0:T(8,128)(2,1)} %get-tuple-element.157.q_ref, bf16[2,512,1024]{2,1,0:T(8,128)(2,1)} %get-tuple-element.154.own_ref, bf16[2,512,1024]{2,1,0:T(8,128)(2,1)} %copy-done.8, ...), custom_call_target="tpu_custom_call" | custom-call | bytes 67200000 | tf_op jit(solution)/shard_map/attend_back/pallas_call | solution.py:769
  386.4 10.0 %middle_back.1 = (f32[512,1024]{1,0:T(8,128)}, bf16[512,1024]{1,0:T(8,128)(2,1)}, bf16[1,512,1024]{2,1,0:T(8,128)(2,1)}, f32[2,1024]{1,0:T(2,128)}) custom-call(s32[10]{0:T(128)} %stack.70.info_ref, bf16[1,512,1024]{2,1,0:T(8,128)(2,1)} %get-tuple-element.225.refs_0_.yo_ref, bf16[8,4,5,128,256]{4,3,2,1,0:T(8,128)(2,1)} %bitcast.132, ...), custom_call_target="tpu_custom_call" | custom-call | bytes 32000000 | tf_op jit(solution)/shard_map/middle_back/pallas_call | solution.py:117
  397.8 7.6 %source_back.1 = (bf16[256,1024]{1,0:T(8,128)(2,1)}, bf16[256,1024]{1,0:T(8,128)(2,1)}, bf16[2,512,1024]{2,1,0:T(8,128)(2,1)}) custom-call(s32[10]{0:T(128)} %stack.70.info_ref, bf16[2,512,1024]{2,1,0:T(8,128)(2,1)} %get-tuple-element.219.refs_0_, bf16[2,512,1024]{2,1,0:T(8,128)(2,1)} %copy-done.19, bf16[8,4,5,128,256]{4,3,2,1,0:T(8,128)(2,1)} %bitcast.134), custom_call_target="tpu_custom_call" | custom-call | bytes 22400000 | tf_op jit(solution)/shard_map/source_back/pallas_call | solution.py:117
  406.1 5.5 weight_grad.11.refs_0_
  412.6 5.4 weight_grad.12.refs_0_
  419.3 6.8 %weight_grad.13 = bf16[4,4,4,128,256]{4,3,2,1,0:T(8,128)(2,1)} custom-call(s32[10]{0:T(128)} %stack.70.info_ref, bf16[512,1024]{1,0:T(8,128)(2,1)} %get-tuple-element.186.xo_ref, bf16[512,1024]{1,0:T(8,128)(2,1)} %collective-permute-done.26.xp_ref, bf16[2,512,1024]{2,1,0:T(8,128)(2,1)} %get-tuple-element.221.yo_ref, ...), custom_call_target="tpu_custom_call", output_to_operand_aliasing={{}: (5, {})} | custom-call | bytes 22400000 | tf_op jit(solution)/shard_map/weight_grad/pallas_call | solution.py:1037
  427.9 5.8 collective-permute-start.37
  433.7 19.0 %causal_back.1 = (bf16[1,512,1024]{2,1,0:T(8,128)(2,1)}, bf16[2,512,1024]{2,1,0:T(8,128)(2,1)}, bf16[2,512,1024]{2,1,0:T(8,128)(2,1)}) custom-call(s32[10]{0:T(128)} %stack.70.info_ref, bf16[1,512,1024]{2,1,0:T(8,128)(2,1)} %get-tuple-element.145.q_ref.refs_0_, bf16[2,512,1024]{2,1,0:T(8,128)(2,1)} %get-tuple-element.146.own_ref.refs_1_, ...), custom_call_target="tpu_custom_call" | custom-call | bytes 60800000 | tf_op jit(solution)/shard_map/causal_back/pallas_call | solution.py:117
  461.3 15.0 %exit_back.1 = (bf16[1024,512]{1,0:T(8,128)(2,1)}, bf16[2,512,1024]{2,1,0:T(8,128)(2,1)}, f32[4,1024]{1,0:T(4,128)}) custom-call(s32[10]{0:T(128)} %stack.70.info_ref, bf16[1,512,1024]{2,1,0:T(8,128)(2,1)} %get-tuple-element.237.refs_0_.yo_ref, bf16[2,512,1024]{2,1,0:T(8,128)(2,1)} %get-tuple-element.238.refs_1_, bf16[2,512,1024]{2,1,0:T(8,128)(2,1)} %copy-done.17, ...), custom_call_target="tpu_custom_call" | custom-call | bytes 48000000 | tf_op jit(solution)/shard_map/exit_back/pallas_call | solution.py:117
  482.5 5.2 weight_grad.14.refs_0_
  497.6 6.8 %weight_grad.15 = bf16[4,4,3,128,256]{4,3,2,1,0:T(8,128)(2,1)} custom-call(s32[10]{0:T(128)} %stack.70.info_ref, bf16[512,1024]{1,0:T(8,128)(2,1)} %get-tuple-element.183.xo_ref, bf16[512,1024]{1,0:T(8,128)(2,1)} %copy-done.15, bf16[2,512,1024]{2,1,0:T(8,128)(2,1)} %get-tuple-element.251.yo_ref, ...), custom_call_target="tpu_custom_call", output_to_operand_aliasing={{}: (5, {})} | custom-call | bytes 22400000 | tf_op jit(solution)/shard_map/weight_grad/pallas_call | solution.py:1037
  504.3 9.8 %reduce-scatter.17.cloned.1.call-done = bf16[1,4,4,128,256]{4,3,2,1,0:T(8,128)(2,1)} async-done(((bf16[4,4,4,128,256]{4,3,2,1,0:T(8,128)(2,1)}), bf16[1,4,4,128,256]{4,3,2,1,0:T(8,128)(2,1)}) %reduce-scatter.17.cloned.1.call-update) | async-done | bytes 1048592
  528.4 39.3 %scatter_tokens.1 = (f32[32,131072]{1,0:T(8,128)}, f32[2,32,512]{2,1,0:T(8,128)}) custom-call(s32[16384]{0:T(1024)} %add_select_fusion.rows_ref, s32[32,1,512]{2,1,0:T(1,128)} %get-tuple-element.324.row_ref, s32[32,1,512]{2,1,0:T(1,128)} %and_select_fusion.1.group_ref, bf16[32,32,512]{2,1,0:T(8,128)(2,1)} %copy-done.12), custom_call_target="tpu_custom_call" | custom-call | bytes 124800000 | tf_op jit(solution)/shard_map/scatter_tokens/pallas_call | solution.py:299
  589.8 18.2 %collective-permute-done.52 = bf16[3,128,256]{2,1,0:T(8,128)(2,1)S(1)} collective-permute-done((bf16[3,128,256]{2,1,0:T(8,128)(2,1)S(1)}, bf16[3,128,256]{2,1,0:T(8,128)(2,1)S(1)}, u32[]{:S(2)}, u32[]{:S(2)}) %collective-permute-start.52) | collective-permute-done | bytes 196640 | tf_op jit(solution)/shard_map/ppermute | solution.py:1164
  (281 shorter events, 152.3 us)
Async XLA Ops:
  7.2 200.6 %all-gather.5.cloned.1.call-start = ((), (), s32[]{:S(2)}) async-start(), calls=%async_computation.10 | async-start | bytes 10813440 | tf_op jit(solution)/shard_map/all_gather | solution.py:1100
  9.9 254.5 %all-gather.7.cloned.1.call-start = ((), (), s32[]{:S(2)}) async-start(), calls=%async_computation.11 | async-start | bytes 17301504 | tf_op jit(solution)/shard_map/all_gather | solution.py:1100
  27.8 52.1 %all-to-all-start = ((bf16[4,512,256]{2,1,0:T(8,128)(2,1)}), bf16[4,512,256]{2,1,0:T(8,128)(2,1)S(1)}, u32[]{:S(2)}, u32[]{:S(2)}) async-start(bf16[4,512,256]{2,1,0:T(8,128)(2,1)} %broadcast_in_dim.57), calls=%async_computation | async-start | bytes 2097152 | tf_op jit(solution)/shard_map/all_to_all | solution.py:1234
  79.9 68.4 %all-to-all-start.2 = ((bf16[32,32,512]{2,1,0:T(8,128)(2,1)}), bf16[32,32,512]{2,1,0:T(8,128)(2,1)}, u32[]{:S(2)}, u32[]{:S(2)}) async-start(bf16[32,32,512]{2,1,0:T(8,128)(2,1)} %gather_tokens.1), calls=%async_computation.2 | async-start | bytes 2097152 | tf_op jit(solution)/shard_map/all_to_all | solution.py:1278
  84.2 299.3 %reduce-scatter.13.cloned.1.call-start = ((), (), s32[]{:S(2)}) async-start(), calls=%async_computation.12 | async-start | bytes 5242880
  84.3 48.8 %collective-permute-start.1 = (bf16[4,4,128,256]{3,2,1,0:T(8,128)(2,1)S(1)}, bf16[4,4,128,256]{3,2,1,0:T(8,128)(2,1)S(1)}, u32[]{:S(2)}, u32[]{:S(2)}) collective-permute-start(bf16[4,4,128,256]{3,2,1,0:T(8,128)(2,1)S(1)} %bitcast.139), channel_id=1, source_target_pairs={{0,4},{4,0},{1,5},{5,1},{2,6},{6,2},{3,7},{7,3},{8,12},{12,8},{9,1... | collective-permute-start | bytes 3145736 | tf_op jit(solution)/shard_map/ppermute | solution.py:1057
  84.6 35.5 %collective-permute-start.2 = (bf16[4,2,128,256]{3,2,1,0:T(8,128)(2,1)S(1)}, bf16[4,2,128,256]{3,2,1,0:T(8,128)(2,1)S(1)}, u32[]{:S(2)}, u32[]{:S(2)}) collective-permute-start(bf16[4,2,128,256]{3,2,1,0:T(8,128)(2,1)S(1)} %get-tuple-element.338), channel_id=1, source_target_pairs={{0,8},{8,0},{16,24},{24,16},{1,9},{9,1},{17,25},{25,17},{2,10},{10... | collective-permute-start | bytes 1572872 | tf_op jit(solution)/shard_map/ppermute | solution.py:1118
  86.4 34.0 %collective-permute-start.4 = (bf16[4,2,128,256]{3,2,1,0:T(8,128)(2,1)S(1)}, bf16[4,2,128,256]{3,2,1,0:T(8,128)(2,1)S(1)}, u32[]{:S(2)}, u32[]{:S(2)}) collective-permute-start(bf16[4,2,128,256]{3,2,1,0:T(8,128)(2,1)S(1)} %get-tuple-element.338), channel_id=1, source_target_pairs={{0,16},{16,0},{8,24},{24,8},{1,17},{17,1},{9,25},{25,9},{2,18},{18... | collective-permute-start | bytes 1572872 | tf_op jit(solution)/shard_map/ppermute | solution.py:1119
  87.9 43.9 %collective-permute-start.10 = (bf16[4,2,128,256]{3,2,1,0:T(8,128)(2,1)S(1)}, bf16[4,2,128,256]{3,2,1,0:T(8,128)(2,1)}, u32[]{:S(2)}, u32[]{:S(2)}) collective-permute-start(bf16[4,2,128,256]{3,2,1,0:T(8,128)(2,1)S(1)} %get-tuple-element.337), channel_id=1, source_target_pairs={{0,16},{16,0},{8,24},{24,8},{1,17},{17,1},{9,25},{25,9},{2,18},{18... | collective-permute-start | bytes 1572872 | tf_op jit(solution)/shard_map/ppermute | solution.py:1118
  89.6 43.4 %collective-permute-start.8 = (bf16[4,2,128,256]{3,2,1,0:T(8,128)(2,1)S(1)}, bf16[4,2,128,256]{3,2,1,0:T(8,128)(2,1)}, u32[]{:S(2)}, u32[]{:S(2)}) collective-permute-start(bf16[4,2,128,256]{3,2,1,0:T(8,128)(2,1)S(1)} %get-tuple-element.337), channel_id=1, source_target_pairs={{0,8},{8,0},{16,24},{24,16},{1,9},{9,1},{17,25},{25,17},{2,10},{10... | collective-permute-start | bytes 1572872 | tf_op jit(solution)/shard_map/ppermute | solution.py:1119
  166.4 28.7 %collective-permute-start.15 = (bf16[256,1024]{1,0:T(8,128)(2,1)S(1)}, bf16[256,1024]{1,0:T(8,128)(2,1)S(1)}, u32[]{:S(2)}, u32[]{:S(2)}) collective-permute-start(bf16[256,1024]{1,0:T(8,128)(2,1)S(1)} %get-tuple-element.336), channel_id=1, source_target_pairs={{0,0},{1,4},{2,5},{3,1},{4,2},{5,6},{6,7},{7,3},{8,8},{9,12},{10,1... | collective-permute-start | bytes 1572872 | tf_op jit(solution)/shard_map/ppermute | solution.py:1075
  167.1 40.7 %collective-permute-start.16 = (bf16[256,1024]{1,0:T(8,128)(2,1)S(1)}, bf16[256,1024]{1,0:T(8,128)(2,1)S(1)}, u32[]{:S(2)}, u32[]{:S(2)}) collective-permute-start(bf16[256,1024]{1,0:T(8,128)(2,1)S(1)} %get-tuple-element.335), channel_id=1, source_target_pairs={{0,1},{1,5},{2,4},{3,0},{4,3},{5,7},{6,6},{7,2},{8,9},{9,13},{10,1... | collective-permute-start | bytes 1572872 | tf_op jit(solution)/shard_map/ppermute | solution.py:1075
  253.0 34.2 %collective-permute-start.20 = (bf16[1,512,1024]{2,1,0:T(8,128)(2,1)}, bf16[1,512,1024]{2,1,0:T(8,128)(2,1)}, u32[]{:S(2)}, u32[]{:S(2)}) collective-permute-start(bf16[1,512,1024]{2,1,0:T(8,128)(2,1)} %get-tuple-element.158.refs_0_.yo_ref.o_ref), channel_id=1, source_target_pairs={{0,4},{4,0},{1,5},{5,1},{2,6},{6,2},{3,7},{7,3},{8,12},{12,8},{9,1... | collective-permute-start | bytes 3145736 | tf_op jit(solution)/shard_map/ppermute | solution.py:1057
  253.0 34.2 %collective-permute-start.21 = (bf16[512,1024]{1,0:T(8,128)(2,1)S(1)}, bf16[512,1024]{1,0:T(8,128)(2,1)}, u32[]{:S(2)}, u32[]{:S(2)}) collective-permute-start(bf16[512,1024]{1,0:T(8,128)(2,1)S(1)} %copy-done.21), channel_id=1, source_target_pairs={{0,4},{4,0},{1,5},{5,1},{2,6},{6,2},{3,7},{7,3},{8,12},{12,8},{9,1... | collective-permute-start | bytes 3145736 | tf_op jit(solution)/shard_map/ppermute | solution.py:1057
  254.7 32.5 %collective-permute-start.18 = (bf16[256,1024]{1,0:T(8,128)(2,1)}, bf16[256,1024]{1,0:T(8,128)(2,1)S(1)}, u32[]{:S(2)}, u32[]{:S(2)}) collective-permute-start(bf16[256,1024]{1,0:T(8,128)(2,1)} %get-tuple-element.334), channel_id=1, source_target_pairs={{0,0},{1,4},{2,5},{3,1},{4,2},{5,6},{6,7},{7,3},{8,8},{9,12},{10,1... | collective-permute-start | bytes 1572872 | tf_op jit(solution)/shard_map/ppermute | solution.py:1075
  256.4 30.8 %collective-permute-start.19 = (bf16[256,1024]{1,0:T(8,128)(2,1)}, bf16[256,1024]{1,0:T(8,128)(2,1)}, u32[]{:S(2)}, u32[]{:S(2)}) collective-permute-start(bf16[256,1024]{1,0:T(8,128)(2,1)} %get-tuple-element.333), channel_id=1, source_target_pairs={{0,1},{1,5},{2,4},{3,0},{4,3},{5,7},{6,6},{7,2},{8,9},{9,13},{10,1... | collective-permute-start | bytes 1572872 | tf_op jit(solution)/shard_map/ppermute | solution.py:1075
  287.2 28.5 %collective-permute-start.23 = (bf16[4,512,1024]{2,1,0:T(8,128)(2,1)}, bf16[4,512,1024]{2,1,0:T(8,128)(2,1)}, u32[]{:S(2)}, u32[]{:S(2)}) collective-permute-start(bf16[4,512,1024]{2,1,0:T(8,128)(2,1)} %get-tuple-element.182.yo_ref), channel_id=1, source_target_pairs={{0,4},{4,0},{1,5},{5,1},{2,6},{6,2},{3,7},{7,3},{8,12},{12,8},{9,1... | collective-permute-start | bytes 12582920 | tf_op jit(solution)/shard_map/ppermute | solution.py:1057
  287.6 28.1 %collective-permute-start.22 = (bf16[512,1024]{1,0:T(8,128)(2,1)}, bf16[512,1024]{1,0:T(8,128)(2,1)}, u32[]{:S(2)}, u32[]{:S(2)}) collective-permute-start(bf16[512,1024]{1,0:T(8,128)(2,1)} %get-tuple-element.193.xo_ref), channel_id=1, source_target_pairs={{0,4},{4,0},{1,5},{5,1},{2,6},{6,2},{3,7},{7,3},{8,12},{12,8},{9,1... | collective-permute-start | bytes 3145736 | tf_op jit(solution)/shard_map/ppermute | solution.py:1057
  287.8 27.9 %collective-permute-start.24 = (bf16[512,1024]{1,0:T(8,128)(2,1)S(1)}, bf16[512,1024]{1,0:T(8,128)(2,1)S(1)}, u32[]{:S(2)}, u32[]{:S(2)}) collective-permute-start(bf16[512,1024]{1,0:T(8,128)(2,1)S(1)} %copy-done.14), channel_id=1, source_target_pairs={{0,4},{4,0},{1,5},{5,1},{2,6},{6,2},{3,7},{7,3},{8,12},{12,8},{9,1... | collective-permute-start | bytes 3145736 | tf_op jit(solution)/shard_map/ppermute | solution.py:1057
  288.1 27.6 %collective-permute-start.25 = (bf16[1,512,1024]{2,1,0:T(8,128)(2,1)S(1)}, bf16[1,512,1024]{2,1,0:T(8,128)(2,1)}, u32[]{:S(2)}, u32[]{:S(2)}) collective-permute-start(bf16[1,512,1024]{2,1,0:T(8,128)(2,1)S(1)} %copy-done.2), channel_id=1, source_target_pairs={{0,4},{4,0},{1,5},{5,1},{2,6},{6,2},{3,7},{7,3},{8,12},{12,8},{9,1... | collective-permute-start | bytes 3145736 | tf_op jit(solution)/shard_map/ppermute | solution.py:1057
  288.3 27.4 %collective-permute-start.26 = (bf16[512,1024]{1,0:T(8,128)(2,1)}, bf16[512,1024]{1,0:T(8,128)(2,1)}, u32[]{:S(2)}, u32[]{:S(2)}) collective-permute-start(bf16[512,1024]{1,0:T(8,128)(2,1)} %get-tuple-element.186.xo_ref), channel_id=1, source_target_pairs={{0,4},{4,0},{1,5},{5,1},{2,6},{6,2},{3,7},{7,3},{8,12},{12,8},{9,1... | collective-permute-start | bytes 3145736 | tf_op jit(solution)/shard_map/ppermute | solution.py:1057
  329.8 123.0 %reduce-scatter.15.cloned.1.call-start = ((), (), s32[]{:S(2)}) async-start(), calls=%async_computation.13 | async-start | bytes 6553600
  331.2 27.1 %collective-permute-start.30 = (bf16[256,1024]{1,0:T(8,128)(2,1)}, bf16[256,1024]{1,0:T(8,128)(2,1)S(1)}, u32[]{:S(2)}, u32[]{:S(2)}) collective-permute-start(bf16[256,1024]{1,0:T(8,128)(2,1)} %get-tuple-element.199), channel_id=1, source_target_pairs={{0,0},{4,1},{5,2},{1,3},{2,4},{6,5},{7,6},{3,7},{8,8},{12,9},{13,1... | collective-permute-start | bytes 1572872 | tf_op jit(solution)/shard_map/ppermute | solution.py:1082
  385.2 128.9 %reduce-scatter.17.cloned.1.call-start = ((), (), s32[]{:S(2)}) async-start(), calls=%async_computation.14 | async-start | bytes 5242880
  426.2 28.3 %collective-permute-start.36 = (bf16[256,1024]{1,0:T(8,128)(2,1)}, bf16[256,1024]{1,0:T(8,128)(2,1)S(1)}, u32[]{:S(2)}, u32[]{:S(2)}) collective-permute-start(bf16[256,1024]{1,0:T(8,128)(2,1)} %get-tuple-element.233), channel_id=1, source_target_pairs={{0,0},{4,1},{5,2},{1,3},{2,4},{6,5},{7,6},{3,7},{8,8},{12,9},{13,1... | collective-permute-start | bytes 1572872 | tf_op jit(solution)/shard_map/ppermute | solution.py:1082
  427.9 26.7 %collective-permute-start.37 = (bf16[256,1024]{1,0:T(8,128)(2,1)}, bf16[256,1024]{1,0:T(8,128)(2,1)S(1)}, u32[]{:S(2)}, u32[]{:S(2)}) collective-permute-start(bf16[256,1024]{1,0:T(8,128)(2,1)} %get-tuple-element.234), channel_id=1, source_target_pairs={{1,0},{5,1},{4,2},{0,3},{3,4},{7,5},{6,6},{2,7},{9,8},{13,9},{12,1... | collective-permute-start | bytes 1572872 | tf_op jit(solution)/shard_map/ppermute | solution.py:1082
  477.7 38.7 %all-to-all-start.3 = ((bf16[32,32,512]{2,1,0:T(8,128)(2,1)}), bf16[32,32,512]{2,1,0:T(8,128)(2,1)S(1)}, u32[]{:S(2)}, u32[]{:S(2)}) async-start(bf16[32,32,512]{2,1,0:T(8,128)(2,1)} %bitcast.178), calls=%async_computation.3 | async-start | bytes 2097152 | tf_op jit(solution)/shard_map/all_to_all | solution.py:1342
  482.0 127.8 %reduce-scatter.11.cloned.1.call-start = ((), (), s32[]{:S(2)}) async-start(), calls=%async_computation.9 | async-start | bytes 4259840 | tf_op jit(solution)/shard_map/reduce_scatter | solution.py:1152
  519.8 48.0 %all-to-all-start.4 = ((bf16[4,4,3,128,256]{4,3,2,1,0:T(8,128)(2,1)}), bf16[4,4,3,128,256]{4,3,2,1,0:T(8,128)(2,1)S(1)}, u32[]{:S(2)}, u32[]{:S(2)}) async-start(bf16[4,4,3,128,256]{4,3,2,1,0:T(8,128)(2,1)} %weight_grad.15), calls=%async_computation.4 | async-start | bytes 6291456 | tf_op jit(solution)/shard_map/all_to_all | solution.py:1353
  523.8 43.9 %collective-permute-start.47 = (f32[10,1024]{1,0:T(8,128)S(1)}, f32[10,1024]{1,0:T(8,128)S(1)}, u32[]{:S(2)}, u32[]{:S(2)}) collective-permute-start(f32[10,1024]{1,0:T(8,128)S(1)} %add_add_fusion.1), channel_id=1, source_target_pairs={{0,3},{1,0},{2,1},{3,2},{4,7},{5,4},{6,5},{7,6},{8,11},{9,8},{10,9... | collective-permute-start | bytes 122888 | tf_op jit(solution)/shard_map/ppermute | solution.py:1174
  526.4 41.4 %collective-permute-start.46 = (f32[10,1024]{1,0:T(8,128)S(1)}, f32[10,1024]{1,0:T(8,128)S(1)}, u32[]{:S(2)}, u32[]{:S(2)}) collective-permute-start(f32[10,1024]{1,0:T(8,128)S(1)} %add_add_fusion.1), channel_id=1, source_target_pairs={{0,2},{1,3},{2,0},{3,1},{4,6},{5,7},{6,4},{7,5},{8,10},{9,11},{10,... | collective-permute-start | bytes 122888 | tf_op jit(solution)/shard_map/ppermute | solution.py:1174
  527.4 40.4 %collective-permute-start.45 = (f32[10,1024]{1,0:T(8,128)S(1)}, f32[10,1024]{1,0:T(8,128)S(1)}, u32[]{:S(2)}, u32[]{:S(2)}) collective-permute-start(f32[10,1024]{1,0:T(8,128)S(1)} %add_add_fusion.1), channel_id=1, source_target_pairs={{0,1},{1,2},{2,3},{3,0},{4,5},{5,6},{6,7},{7,4},{8,9},{9,10},{10,1... | collective-permute-start | bytes 122888 | tf_op jit(solution)/shard_map/ppermute | solution.py:1174
  (78 other events, 762.7 us)
Sparse Core Ops, SparseCore 0:
  11.4 121.3 all-gather.4
  135.9 128.4 all-gather.6
  329.9 53.6 reduce-scatter.12
  386.7 61.4 reduce-scatter.14
  455.7 58.4 reduce-scatter.16
  520.0 77.6 reduce-scatter.10

commit v5 on v4

--- a/solution.py
+++ b/solution.py
@@ -86,7 +86,7 @@
         store(pl.multiple_of(m * width, width), dot(x, columns(w_refs, m, info_ref)))
         return carry
 
-    lax.fori_loop(0, w_refs[0].shape[1], step, 0)
+    lax.fori_loop(0, w_refs[0].shape[1], step, 0, unroll=True)
 
 
 def weight_specs(weights, index):

time: 632 us -> 626 us (level)
  Pallas kernels: 340 us -> 326 us
  waiting for transfers between devices: 124 us -> 132 us
    pallas_call x9, Pallas kernels: 134 us -> 121 us  [call(): pl.pallas_call(body, out_shape=[o for o, _ in outs], grid_spec=pltpu.Pref...]
  transfers between devices with their start and end apart: 65 -> 65, of which waited for: 18 -> 19; matrix products, arithmetic and copies ran while one was open for 5% -> 5% of each run, Pallas kernels for 53% -> 51%
where the time goes in v5:
time: 626 us; the launch traced here: 616 us
  Pallas kernels  326 us (52%)
  waiting for transfers between devices  132 us (21%)
  starting transfers between devices  81 us (13%)
  local copies, waits for them, and re-layouts  39.5 us (6%)
  other arithmetic  21.9 us (3%)
  between operations  15.5 us (2%)
    pallas_call x9, Pallas kernels, call(): pl.pallas_call(body, out_shape=[o for o, _ in outs], grid_spec=pltpu.Pref...  121 us
    pallas_call x8, Pallas kernels, weight_grad(): pl.pallas_call(functools.partial(weight_grad_kernel, chips, before is not...  54.8 us
    pallas_call x1, Pallas kernels, gather_tokens(): pl.pallas_call(functools.partial(gather_kernel, groups, fill), out_shape=...  45.7 us
    pallas_call x2, Pallas kernels, attend(): pl.pallas_call(functools.partial(attend_kernel, causal), out_shape=(jax.S...  43.6 us
    ppermute x4, waiting for transfers between devices, begin(): lax.ppermute(w, 'chip', p)  40.4 us
    pallas_call x1, Pallas kernels, scatter_tokens(): pl.pallas_call(functools.partial(scatter_kernel, groups, per_core), out_s...  39.3 us
    unnamed x99, local copies, waits for them, and re-layouts  24.4 us
    ppermute x3, waiting for transfers between devices, sent_over(): terms.append(part if k == 0 else lax.ppermute(part, axis, perm))  21.7 us
  transfers between devices with their start and end apart: 65, of which 19 were waited for; matrix products, arithmetic and copies ran while one was open for 5% of the time, Pallas kernels for 51%

profile of v5, /device:TPU:0, one launch (start us, length us, event | category | flops | bytes accessed | tf_op | source)
XLA Modules:
  0.0 616.3 jit_solution(12095839507053205232)
XLA Ops:
  13.0 7.3 %all-to-all-start.1 = ((s32[32,1,512]{2,1,0:T(1,128)}), s32[32,1,512]{2,1,0:T(1,128)S(1)}, u32[]{:S(2)}, u32[]{:S(2)}) async-start(s32[32,1,512]{2,1,0:T(1,128)} %broadcast_in_dim.59), calls=%async_computation.1 | async-start | bytes 131072 | tf_op jit(solution)/shard_map/all_to_all | solution.py:1219
  21.3 6.4 %all-to-all-done.1 = s32[32,1,512]{2,1,0:T(1,128)S(1)} async-done(((s32[32,1,512]{2,1,0:T(1,128)}), s32[32,1,512]{2,1,0:T(1,128)S(1)}, u32[]{:S(2)}, u32[]{:S(2)}) %all-to-all-start.1) | async-done | bytes 65568 | tf_op jit(solution)/shard_map/all_to_all | solution.py:1219
  34.1 45.7 %gather_tokens.1 = bf16[32,32,512]{2,1,0:T(8,128)(2,1)} custom-call(s32[16384]{0:T(1024)} %add_select_fusion.rows_ref, s32[32,1,512]{2,1,0:T(1,128)} %and_select_fusion.1.group_ref, bf16[32,131072]{1,0:T(8,128)(2,1)} %refs_3_.1, bf16[32,131072]{1,0:T(8,128)(2,1)} %refs_3_.1, bf16[32,131072]{1,0:T(8,128)(2,1)} %refs_3_.1, bf16[32,131072]{1,0:T(8,128)(2,1)} %refs_3_.1), custom_call_target="tpu_custom_call" | custom-call | bytes 144000000 | tf_op jit(solution)/shard_map/gather_tokens/pallas_call | solution.py:186
  90.0 30.1 %collective-permute-done.2 = bf16[4,2,128,256]{3,2,1,0:T(8,128)(2,1)S(1)} collective-permute-done((bf16[4,2,128,256]{3,2,1,0:T(8,128)(2,1)S(1)}, bf16[4,2,128,256]{3,2,1,0:T(8,128)(2,1)S(1)}, u32[]{:S(2)}, u32[]{:S(2)}) %collective-permute-start.2) | collective-permute-done | bytes 524320 | tf_op jit(solution)/shard_map/ppermute | solution.py:1118
  121.7 10.0 %collective-permute-done.10 = bf16[4,2,128,256]{3,2,1,0:T(8,128)(2,1)} collective-permute-done((bf16[4,2,128,256]{3,2,1,0:T(8,128)(2,1)S(1)}, bf16[4,2,128,256]{3,2,1,0:T(8,128)(2,1)}, u32[]{:S(2)}, u32[]{:S(2)}) %collective-permute-start.10) | collective-permute-done | bytes 524320 | tf_op jit(solution)/shard_map/ppermute | solution.py:1118
  133.7 9.1 %collective-permute-done.6 = bf16[4,2,128,256]{3,2,1,0:T(8,128)(2,1)} collective-permute-done((bf16[4,2,128,256]{3,2,1,0:T(8,128)(2,1)S(1)}, bf16[4,2,128,256]{3,2,1,0:T(8,128)(2,1)}, u32[]{:S(2)}, u32[]{:S(2)}) %collective-permute-start.6) | collective-permute-done | bytes 524320 | tf_op jit(solution)/shard_map/ppermute | solution.py:1123
  149.2 13.9 %entry.1 = (f32[512,1024]{1,0:T(8,128)}, f32[512,1024]{1,0:T(8,128)}, bf16[512,1024]{1,0:T(8,128)(2,1)}, bf16[1,512,1024]{2,1,0:T(8,128)(2,1)}, bf16[2,512,1024]{2,1,0:T(8,128)(2,1)}) custom-call(s32[10]{0:T(128)} %stack.70.info_ref, bf16[1024,512]{1,0:T(8,128)(2,1)} %bitcast.16.refs_0_, bf16[1,4,4,128,256]{4,3,2,1,0:T(8,128)(2,1)} %bitcast.141, ...), custom_call_target="tpu_custom_call" | custom-call | bytes 48000000 | tf_op jit(solution)/shard_map/entry/pallas_call | solution.py:117
  172.0 21.6 %attend.2 = (bf16[1,512,1024]{2,1,0:T(8,128)(2,1)}, bf16[16,2,512,512]{3,2,1,0:T(8,128)(2,1)}) custom-call(s32[10]{0:T(128)} %stack.70.info_ref, bf16[1,512,1024]{2,1,0:T(8,128)(2,1)} %get-tuple-element.145.q_ref.refs_0_, bf16[2,512,1024]{2,1,0:T(8,128)(2,1)} %get-tuple-element.146.own_ref.refs_1_, bf16[2,512,1024]{2,1,0:T(8,128)(2,1)} %copy-done.9), custom_call_target="tpu_custom_call" | custom-call | bytes 70400000 | tf_op jit(solution)/shard_map/attend/pallas_call | solution.py:507
  193.7 14.1 %collective-permute-done.16.refs_1_ = bf16[256,1024]{1,0:T(8,128)(2,1)S(1)} collective-permute-done((bf16[256,1024]{1,0:T(8,128)(2,1)S(1)}, bf16[256,1024]{1,0:T(8,128)(2,1)S(1)}, u32[]{:S(2)}, u32[]{:S(2)}) %collective-permute-start.16) | collective-permute-done | bytes 524320 | tf_op jit(solution)/shard_map/ppermute | solution.py:1075
  208.6 6.6 %source_keys.1 = (bf16[512,1024]{1,0:T(8,128)(2,1)}, bf16[2,512,1024]{2,1,0:T(8,128)(2,1)}) custom-call(s32[10]{0:T(128)} %stack.70.info_ref, bf16[256,1024]{1,0:T(8,128)(2,1)} %copy-done.34, bf16[256,1024]{1,0:T(8,128)(2,1)} %copy-done.35, bf16[8,4,5,128,256]{4,3,2,1,0:T(8,128)(2,1)} %bitcast.127), custom_call_target="tpu_custom_call" | custom-call | bytes 25600000 | tf_op jit(solution)/shard_map/source_keys/pallas_call | solution.py:117
  219.2 7.8 %middle.1 = (f32[512,1024]{1,0:T(8,128)}, bf16[512,1024]{1,0:T(8,128)(2,1)}, bf16[1,512,1024]{2,1,0:T(8,128)(2,1)}) custom-call(s32[10]{0:T(128)} %stack.70.info_ref, bf16[1,512,1024]{2,1,0:T(8,128)(2,1)} %get-tuple-element.184.refs_0_.yo_ref.refs_4_, bf16[8,4,5,128,256]{4,3,2,1,0:T(8,128)(2,1)} %bitcast.128, ...), custom_call_target="tpu_custom_call" | custom-call | bytes 28800000 | tf_op jit(solution)/shard_map/middle/pallas_call | solution.py:117
  228.3 22.0 %attend.3 = (bf16[1,512,1024]{2,1,0:T(8,128)(2,1)}, bf16[16,2,512,512]{3,2,1,0:T(8,128)(2,1)}) custom-call(s32[10]{0:T(128)} %stack.70.info_ref, bf16[1,512,1024]{2,1,0:T(8,128)(2,1)} %get-tuple-element.157.q_ref, bf16[2,512,1024]{2,1,0:T(8,128)(2,1)} %get-tuple-element.154.own_ref, bf16[2,512,1024]{2,1,0:T(8,128)(2,1)} %copy-done.8), custom_call_target="tpu_custom_call" | custom-call | bytes 70400000 | tf_op jit(solution)/shard_map/attend/pallas_call | solution.py:507
  257.9 9.6 %all-gather.7.cloned.1.call-done = bf16[32768,256]{1,0:T(8,128)(2,1)} async-done(((bf16[1024,256]{1,0:T(8,128)(2,1)}), bf16[32768,256]{1,0:T(8,128)(2,1)}) %all-gather.7.cloned.1.call-update) | async-done | bytes 16777232 | tf_op jit(solution)/shard_map/all_gather | solution.py:1100
  267.6 19.4 %feed.1 = (f32[512,1024]{1,0:T(8,128)}, bf16[512,1024]{1,0:T(8,128)(2,1)}, bf16[4,512,1024]{2,1,0:T(8,128)(2,1)}, bf16[4,512,1024]{2,1,0:T(8,128)(2,1)}, f32[512,1024]{1,0:T(8,128)}) custom-call(s32[10]{0:T(128)} %stack.70.info_ref, bf16[1,512,1024]{2,1,0:T(8,128)(2,1)} %get-tuple-element.158.refs_0_.yo_ref.o_ref, bf16[8,4,5,128,256]{4,3,2,1,0:T(8,128)(2,1)} %bitcast.130, ...), custom_call_target="tpu_custom_call" | custom-call | bytes 89600000 | tf_op jit(solution)/shard_map/feed/pallas_call | solution.py:117
  288.4 23.3 %feed_back.1 = (bf16[256,1024]{1,0:T(8,128)(2,1)}, bf16[256,1024]{1,0:T(8,128)(2,1)}, bf16[512,1024]{1,0:T(8,128)(2,1)}, bf16[4,512,1024]{2,1,0:T(8,128)(2,1)}, ...) custom-call(s32[10]{0:T(128)} %stack.70.info_ref, ...), custom_call_target="tpu_custom_call" | custom-call | bytes 89600000 | tf_op jit(solution)/shard_map/feed_back/pallas_call | solution.py:117
  315.7 10.1 %weight_grad.8 = bf16[4,4,4,128,256]{4,3,2,1,0:T(8,128)(2,1)} custom-call(s32[10]{0:T(128)} %stack.70.info_ref, bf16[512,1024]{1,0:T(8,128)(2,1)} %get-tuple-element.189.xo_ref, bf16[512,1024]{1,0:T(8,128)(2,1)} %copy-done.27, bf16[4,512,1024]{2,1,0:T(8,128)(2,1)} %get-tuple-element.182.yo_ref, bf16[4,512,1024]{2,1,0:T(8,128)(2,1)} %collective-permute-done.23.yp_ref), custom_call_target="tpu_custom_call" | custom-call | bytes 35200000 | tf_op jit(solution)/shard_map/weight_grad/pallas_call | solution.py:1037
  335.8 5.4 weight_grad.9.refs_0_
  343.2 10.1 %weight_grad.10 = bf16[4,4,5,128,256]{4,3,2,1,0:T(8,128)(2,1)} custom-call(s32[10]{0:T(128)} %stack.70.info_ref, bf16[512,1024]{1,0:T(8,128)(2,1)} %get-tuple-element.193.xo_ref, bf16[512,1024]{1,0:T(8,128)(2,1)} %collective-permute-done.22.xp_ref, bf16[4,512,1024]{2,1,0:T(8,128)(2,1)} %get-tuple-element.195.yo_ref, ...), custom_call_target="tpu_custom_call", output_to_operand_aliasing={{}: (5, {})} | custom-call | bytes 35200000 | tf_op jit(solution)/shard_map/weight_grad/pallas_call | solution.py:1037
  353.4 21.4 %attend_back.1 = (bf16[1,512,1024]{2,1,0:T(8,128)(2,1)}, bf16[2,512,1024]{2,1,0:T(8,128)(2,1)}, bf16[2,512,1024]{2,1,0:T(8,128)(2,1)}) custom-call(bf16[1,512,1024]{2,1,0:T(8,128)(2,1)} %get-tuple-element.157.q_ref, bf16[2,512,1024]{2,1,0:T(8,128)(2,1)} %get-tuple-element.154.own_ref, bf16[2,512,1024]{2,1,0:T(8,128)(2,1)} %copy-done.8, ...), custom_call_target="tpu_custom_call" | custom-call | bytes 67200000 | tf_op jit(solution)/shard_map/attend_back/pallas_call | solution.py:769
  380.5 8.8 %middle_back.1 = (f32[512,1024]{1,0:T(8,128)}, bf16[512,1024]{1,0:T(8,128)(2,1)}, bf16[1,512,1024]{2,1,0:T(8,128)(2,1)}, f32[2,1024]{1,0:T(2,128)}) custom-call(s32[10]{0:T(128)} %stack.70.info_ref, bf16[1,512,1024]{2,1,0:T(8,128)(2,1)} %get-tuple-element.225.refs_0_.yo_ref, bf16[8,4,5,128,256]{4,3,2,1,0:T(8,128)(2,1)} %bitcast.132, ...), custom_call_target="tpu_custom_call" | custom-call | bytes 32000000 | tf_op jit(solution)/shard_map/middle_back/pallas_call | solution.py:117
  390.8 7.4 %source_back.1 = (bf16[256,1024]{1,0:T(8,128)(2,1)}, bf16[256,1024]{1,0:T(8,128)(2,1)}, bf16[2,512,1024]{2,1,0:T(8,128)(2,1)}) custom-call(s32[10]{0:T(128)} %stack.70.info_ref, bf16[2,512,1024]{2,1,0:T(8,128)(2,1)} %get-tuple-element.219.refs_0_, bf16[2,512,1024]{2,1,0:T(8,128)(2,1)} %copy-done.19, bf16[8,4,5,128,256]{4,3,2,1,0:T(8,128)(2,1)} %bitcast.134), custom_call_target="tpu_custom_call" | custom-call | bytes 22400000 | tf_op jit(solution)/shard_map/source_back/pallas_call | solution.py:117
  398.9 5.2 weight_grad.11.refs_0_
  405.1 5.3 weight_grad.12.refs_0_
  411.7 6.7 %weight_grad.13 = bf16[4,4,4,128,256]{4,3,2,1,0:T(8,128)(2,1)} custom-call(s32[10]{0:T(128)} %stack.70.info_ref, bf16[512,1024]{1,0:T(8,128)(2,1)} %get-tuple-element.186.xo_ref, bf16[512,1024]{1,0:T(8,128)(2,1)} %collective-permute-done.26.xp_ref, bf16[2,512,1024]{2,1,0:T(8,128)(2,1)} %get-tuple-element.221.yo_ref, ...), custom_call_target="tpu_custom_call", output_to_operand_aliasing={{}: (5, {})} | custom-call | bytes 22400000 | tf_op jit(solution)/shard_map/weight_grad/pallas_call | solution.py:1037
  420.2 6.5 %collective-permute-start.37 = (bf16[256,1024]{1,0:T(8,128)(2,1)}, bf16[256,1024]{1,0:T(8,128)(2,1)S(1)}, u32[]{:S(2)}, u32[]{:S(2)}) collective-permute-start(bf16[256,1024]{1,0:T(8,128)(2,1)} %get-tuple-element.234), channel_id=1, source_target_pairs={{1,0},{5,1},{4,2},{0,3},{3,4},{7,5},{6,6},{2,7},{9,8},{13,9},{12,1... | collective-permute-start | bytes 1572872 | tf_op jit(solution)/shard_map/ppermute | solution.py:1082
  426.7 19.0 %causal_back.1 = (bf16[1,512,1024]{2,1,0:T(8,128)(2,1)}, bf16[2,512,1024]{2,1,0:T(8,128)(2,1)}, bf16[2,512,1024]{2,1,0:T(8,128)(2,1)}) custom-call(s32[10]{0:T(128)} %stack.70.info_ref, bf16[1,512,1024]{2,1,0:T(8,128)(2,1)} %get-tuple-element.145.q_ref.refs_0_, bf16[2,512,1024]{2,1,0:T(8,128)(2,1)} %get-tuple-element.146.own_ref.refs_1_, ...), custom_call_target="tpu_custom_call" | custom-call | bytes 60800000 | tf_op jit(solution)/shard_map/causal_back/pallas_call | solution.py:117
  454.3 15.1 %exit_back.1 = (bf16[1024,512]{1,0:T(8,128)(2,1)}, bf16[2,512,1024]{2,1,0:T(8,128)(2,1)}, f32[4,1024]{1,0:T(4,128)}) custom-call(s32[10]{0:T(128)} %stack.70.info_ref, bf16[1,512,1024]{2,1,0:T(8,128)(2,1)} %get-tuple-element.237.refs_0_.yo_ref, bf16[2,512,1024]{2,1,0:T(8,128)(2,1)} %get-tuple-element.238.refs_1_, bf16[2,512,1024]{2,1,0:T(8,128)(2,1)} %copy-done.17, ...), custom_call_target="tpu_custom_call" | custom-call | bytes 48000000 | tf_op jit(solution)/shard_map/exit_back/pallas_call | solution.py:117
  475.1 5.2 weight_grad.14.refs_0_
  490.2 6.8 %weight_grad.15 = bf16[4,4,3,128,256]{4,3,2,1,0:T(8,128)(2,1)} custom-call(s32[10]{0:T(128)} %stack.70.info_ref, bf16[512,1024]{1,0:T(8,128)(2,1)} %get-tuple-element.183.xo_ref, bf16[512,1024]{1,0:T(8,128)(2,1)} %copy-done.15, bf16[2,512,1024]{2,1,0:T(8,128)(2,1)} %get-tuple-element.251.yo_ref, ...), custom_call_target="tpu_custom_call", output_to_operand_aliasing={{}: (5, {})} | custom-call | bytes 22400000 | tf_op jit(solution)/shard_map/weight_grad/pallas_call | solution.py:1037
  497.0 9.8 %reduce-scatter.17.cloned.1.call-done = bf16[1,4,4,128,256]{4,3,2,1,0:T(8,128)(2,1)} async-done(((bf16[4,4,4,128,256]{4,3,2,1,0:T(8,128)(2,1)}), bf16[1,4,4,128,256]{4,3,2,1,0:T(8,128)(2,1)}) %reduce-scatter.17.cloned.1.call-update) | async-done | bytes 1048592
  521.1 39.3 %scatter_tokens.1 = (f32[32,131072]{1,0:T(8,128)}, f32[2,32,512]{2,1,0:T(8,128)}) custom-call(s32[16384]{0:T(1024)} %add_select_fusion.rows_ref, s32[32,1,512]{2,1,0:T(1,128)} %get-tuple-element.324.row_ref, s32[32,1,512]{2,1,0:T(1,128)} %and_select_fusion.1.group_ref, bf16[32,32,512]{2,1,0:T(8,128)(2,1)} %copy-done.12), custom_call_target="tpu_custom_call" | custom-call | bytes 124800000 | tf_op jit(solution)/shard_map/scatter_tokens/pallas_call | solution.py:299
  582.4 18.2 %collective-permute-done.52 = bf16[3,128,256]{2,1,0:T(8,128)(2,1)S(1)} collective-permute-done((bf16[3,128,256]{2,1,0:T(8,128)(2,1)S(1)}, bf16[3,128,256]{2,1,0:T(8,128)(2,1)S(1)}, u32[]{:S(2)}, u32[]{:S(2)}) %collective-permute-start.52) | collective-permute-done | bytes 196640 | tf_op jit(solution)/shard_map/ppermute | solution.py:1164
  (281 shorter events, 153.6 us)
Async XLA Ops:
  7.2 200.6 %all-gather.5.cloned.1.call-start = ((), (), s32[]{:S(2)}) async-start(), calls=%async_computation.10 | async-start | bytes 10813440 | tf_op jit(solution)/shard_map/all_gather | solution.py:1100
  9.9 257.7 %all-gather.7.cloned.1.call-start = ((), (), s32[]{:S(2)}) async-start(), calls=%async_computation.11 | async-start | bytes 17301504 | tf_op jit(solution)/shard_map/all_gather | solution.py:1100
  27.8 52.1 %all-to-all-start = ((bf16[4,512,256]{2,1,0:T(8,128)(2,1)}), bf16[4,512,256]{2,1,0:T(8,128)(2,1)S(1)}, u32[]{:S(2)}, u32[]{:S(2)}) async-start(bf16[4,512,256]{2,1,0:T(8,128)(2,1)} %broadcast_in_dim.57), calls=%async_computation | async-start | bytes 2097152 | tf_op jit(solution)/shard_map/all_to_all | solution.py:1234
  79.9 68.4 %all-to-all-start.2 = ((bf16[32,32,512]{2,1,0:T(8,128)(2,1)}), bf16[32,32,512]{2,1,0:T(8,128)(2,1)}, u32[]{:S(2)}, u32[]{:S(2)}) async-start(bf16[32,32,512]{2,1,0:T(8,128)(2,1)} %gather_tokens.1), calls=%async_computation.2 | async-start | bytes 2097152 | tf_op jit(solution)/shard_map/all_to_all | solution.py:1278
  84.2 293.4 %reduce-scatter.13.cloned.1.call-start = ((), (), s32[]{:S(2)}) async-start(), calls=%async_computation.12 | async-start | bytes 5242880
  84.3 48.8 %collective-permute-start.1 = (bf16[4,4,128,256]{3,2,1,0:T(8,128)(2,1)S(1)}, bf16[4,4,128,256]{3,2,1,0:T(8,128)(2,1)S(1)}, u32[]{:S(2)}, u32[]{:S(2)}) collective-permute-start(bf16[4,4,128,256]{3,2,1,0:T(8,128)(2,1)S(1)} %bitcast.139), channel_id=1, source_target_pairs={{0,4},{4,0},{1,5},{5,1},{2,6},{6,2},{3,7},{7,3},{8,12},{12,8},{9,1... | collective-permute-start | bytes 3145736 | tf_op jit(solution)/shard_map/ppermute | solution.py:1057
  84.6 35.5 %collective-permute-start.2 = (bf16[4,2,128,256]{3,2,1,0:T(8,128)(2,1)S(1)}, bf16[4,2,128,256]{3,2,1,0:T(8,128)(2,1)S(1)}, u32[]{:S(2)}, u32[]{:S(2)}) collective-permute-start(bf16[4,2,128,256]{3,2,1,0:T(8,128)(2,1)S(1)} %get-tuple-element.338), channel_id=1, source_target_pairs={{0,8},{8,0},{16,24},{24,16},{1,9},{9,1},{17,25},{25,17},{2,10},{10... | collective-permute-start | bytes 1572872 | tf_op jit(solution)/shard_map/ppermute | solution.py:1118
  86.4 34.0 %collective-permute-start.4 = (bf16[4,2,128,256]{3,2,1,0:T(8,128)(2,1)S(1)}, bf16[4,2,128,256]{3,2,1,0:T(8,128)(2,1)S(1)}, u32[]{:S(2)}, u32[]{:S(2)}) collective-permute-start(bf16[4,2,128,256]{3,2,1,0:T(8,128)(2,1)S(1)} %get-tuple-element.338), channel_id=1, source_target_pairs={{0,16},{16,0},{8,24},{24,8},{1,17},{17,1},{9,25},{25,9},{2,18},{18... | collective-permute-start | bytes 1572872 | tf_op jit(solution)/shard_map/ppermute | solution.py:1119
  87.9 43.9 %collective-permute-start.10 = (bf16[4,2,128,256]{3,2,1,0:T(8,128)(2,1)S(1)}, bf16[4,2,128,256]{3,2,1,0:T(8,128)(2,1)}, u32[]{:S(2)}, u32[]{:S(2)}) collective-permute-start(bf16[4,2,128,256]{3,2,1,0:T(8,128)(2,1)S(1)} %get-tuple-element.337), channel_id=1, source_target_pairs={{0,16},{16,0},{8,24},{24,8},{1,17},{17,1},{9,25},{25,9},{2,18},{18... | collective-permute-start | bytes 1572872 | tf_op jit(solution)/shard_map/ppermute | solution.py:1118
  89.6 43.4 %collective-permute-start.8 = (bf16[4,2,128,256]{3,2,1,0:T(8,128)(2,1)S(1)}, bf16[4,2,128,256]{3,2,1,0:T(8,128)(2,1)}, u32[]{:S(2)}, u32[]{:S(2)}) collective-permute-start(bf16[4,2,128,256]{3,2,1,0:T(8,128)(2,1)S(1)} %get-tuple-element.337), channel_id=1, source_target_pairs={{0,8},{8,0},{16,24},{24,16},{1,9},{9,1},{17,25},{25,17},{2,10},{10... | collective-permute-start | bytes 1572872 | tf_op jit(solution)/shard_map/ppermute | solution.py:1119
  165.3 28.4 %collective-permute-start.15 = (bf16[256,1024]{1,0:T(8,128)(2,1)S(1)}, bf16[256,1024]{1,0:T(8,128)(2,1)S(1)}, u32[]{:S(2)}, u32[]{:S(2)}) collective-permute-start(bf16[256,1024]{1,0:T(8,128)(2,1)S(1)} %get-tuple-element.336), channel_id=1, source_target_pairs={{0,0},{1,4},{2,5},{3,1},{4,2},{5,6},{6,7},{7,3},{8,8},{9,12},{10,1... | collective-permute-start | bytes 1572872 | tf_op jit(solution)/shard_map/ppermute | solution.py:1075
  166.0 41.8 %collective-permute-start.16 = (bf16[256,1024]{1,0:T(8,128)(2,1)S(1)}, bf16[256,1024]{1,0:T(8,128)(2,1)S(1)}, u32[]{:S(2)}, u32[]{:S(2)}) collective-permute-start(bf16[256,1024]{1,0:T(8,128)(2,1)S(1)} %get-tuple-element.335), channel_id=1, source_target_pairs={{0,1},{1,5},{2,4},{3,0},{4,3},{5,7},{6,6},{7,2},{8,9},{9,13},{10,1... | collective-permute-start | bytes 1572872 | tf_op jit(solution)/shard_map/ppermute | solution.py:1075
  250.3 36.8 %collective-permute-start.20 = (bf16[1,512,1024]{2,1,0:T(8,128)(2,1)}, bf16[1,512,1024]{2,1,0:T(8,128)(2,1)}, u32[]{:S(2)}, u32[]{:S(2)}) collective-permute-start(bf16[1,512,1024]{2,1,0:T(8,128)(2,1)} %get-tuple-element.158.refs_0_.yo_ref.o_ref), channel_id=1, source_target_pairs={{0,4},{4,0},{1,5},{5,1},{2,6},{6,2},{3,7},{7,3},{8,12},{12,8},{9,1... | collective-permute-start | bytes 3145736 | tf_op jit(solution)/shard_map/ppermute | solution.py:1057
  250.3 36.8 %collective-permute-start.21 = (bf16[512,1024]{1,0:T(8,128)(2,1)S(1)}, bf16[512,1024]{1,0:T(8,128)(2,1)}, u32[]{:S(2)}, u32[]{:S(2)}) collective-permute-start(bf16[512,1024]{1,0:T(8,128)(2,1)S(1)} %copy-done.21), channel_id=1, source_target_pairs={{0,4},{4,0},{1,5},{5,1},{2,6},{6,2},{3,7},{7,3},{8,12},{12,8},{9,1... | collective-permute-start | bytes 3145736 | tf_op jit(solution)/shard_map/ppermute | solution.py:1057
  252.0 35.0 %collective-permute-start.18 = (bf16[256,1024]{1,0:T(8,128)(2,1)}, bf16[256,1024]{1,0:T(8,128)(2,1)S(1)}, u32[]{:S(2)}, u32[]{:S(2)}) collective-permute-start(bf16[256,1024]{1,0:T(8,128)(2,1)} %get-tuple-element.334), channel_id=1, source_target_pairs={{0,0},{1,4},{2,5},{3,1},{4,2},{5,6},{6,7},{7,3},{8,8},{9,12},{10,1... | collective-permute-start | bytes 1572872 | tf_op jit(solution)/shard_map/ppermute | solution.py:1075
  253.7 33.4 %collective-permute-start.19 = (bf16[256,1024]{1,0:T(8,128)(2,1)}, bf16[256,1024]{1,0:T(8,128)(2,1)}, u32[]{:S(2)}, u32[]{:S(2)}) collective-permute-start(bf16[256,1024]{1,0:T(8,128)(2,1)} %get-tuple-element.333), channel_id=1, source_target_pairs={{0,1},{1,5},{2,4},{3,0},{4,3},{5,7},{6,6},{7,2},{8,9},{9,13},{10,1... | collective-permute-start | bytes 1572872 | tf_op jit(solution)/shard_map/ppermute | solution.py:1075
  287.1 24.7 %collective-permute-start.23 = (bf16[4,512,1024]{2,1,0:T(8,128)(2,1)}, bf16[4,512,1024]{2,1,0:T(8,128)(2,1)}, u32[]{:S(2)}, u32[]{:S(2)}) collective-permute-start(bf16[4,512,1024]{2,1,0:T(8,128)(2,1)} %get-tuple-element.182.yo_ref), channel_id=1, source_target_pairs={{0,4},{4,0},{1,5},{5,1},{2,6},{6,2},{3,7},{7,3},{8,12},{12,8},{9,1... | collective-permute-start | bytes 12582920 | tf_op jit(solution)/shard_map/ppermute | solution.py:1057
  287.4 24.3 %collective-permute-start.22 = (bf16[512,1024]{1,0:T(8,128)(2,1)}, bf16[512,1024]{1,0:T(8,128)(2,1)}, u32[]{:S(2)}, u32[]{:S(2)}) collective-permute-start(bf16[512,1024]{1,0:T(8,128)(2,1)} %get-tuple-element.193.xo_ref), channel_id=1, source_target_pairs={{0,4},{4,0},{1,5},{5,1},{2,6},{6,2},{3,7},{7,3},{8,12},{12,8},{9,1... | collective-permute-start | bytes 3145736 | tf_op jit(solution)/shard_map/ppermute | solution.py:1057
  287.7 24.1 %collective-permute-start.24 = (bf16[512,1024]{1,0:T(8,128)(2,1)S(1)}, bf16[512,1024]{1,0:T(8,128)(2,1)S(1)}, u32[]{:S(2)}, u32[]{:S(2)}) collective-permute-start(bf16[512,1024]{1,0:T(8,128)(2,1)S(1)} %copy-done.14), channel_id=1, source_target_pairs={{0,4},{4,0},{1,5},{5,1},{2,6},{6,2},{3,7},{7,3},{8,12},{12,8},{9,1... | collective-permute-start | bytes 3145736 | tf_op jit(solution)/shard_map/ppermute | solution.py:1057
  287.9 23.8 %collective-permute-start.25 = (bf16[1,512,1024]{2,1,0:T(8,128)(2,1)S(1)}, bf16[1,512,1024]{2,1,0:T(8,128)(2,1)}, u32[]{:S(2)}, u32[]{:S(2)}) collective-permute-start(bf16[1,512,1024]{2,1,0:T(8,128)(2,1)S(1)} %copy-done.2), channel_id=1, source_target_pairs={{0,4},{4,0},{1,5},{5,1},{2,6},{6,2},{3,7},{7,3},{8,12},{12,8},{9,1... | collective-permute-start | bytes 3145736 | tf_op jit(solution)/shard_map/ppermute | solution.py:1057
  325.8 119.9 %reduce-scatter.15.cloned.1.call-start = ((), (), s32[]{:S(2)}) async-start(), calls=%async_computation.13 | async-start | bytes 6553600
  327.3 26.1 %collective-permute-start.30 = (bf16[256,1024]{1,0:T(8,128)(2,1)}, bf16[256,1024]{1,0:T(8,128)(2,1)S(1)}, u32[]{:S(2)}, u32[]{:S(2)}) collective-permute-start(bf16[256,1024]{1,0:T(8,128)(2,1)} %get-tuple-element.199), channel_id=1, source_target_pairs={{0,0},{4,1},{5,2},{1,3},{2,4},{6,5},{7,6},{3,7},{8,8},{12,9},{13,1... | collective-permute-start | bytes 1572872 | tf_op jit(solution)/shard_map/ppermute | solution.py:1082
  329.0 24.4 %collective-permute-start.31 = (bf16[256,1024]{1,0:T(8,128)(2,1)}, bf16[256,1024]{1,0:T(8,128)(2,1)S(1)}, u32[]{:S(2)}, u32[]{:S(2)}) collective-permute-start(bf16[256,1024]{1,0:T(8,128)(2,1)} %get-tuple-element.200), channel_id=1, source_target_pairs={{1,0},{5,1},{4,2},{0,3},{3,4},{7,5},{6,6},{2,7},{9,8},{13,9},{12,1... | collective-permute-start | bytes 1572872 | tf_op jit(solution)/shard_map/ppermute | solution.py:1082
  379.3 127.4 %reduce-scatter.17.cloned.1.call-start = ((), (), s32[]{:S(2)}) async-start(), calls=%async_computation.14 | async-start | bytes 5242880
  418.5 29.1 %collective-permute-start.36 = (bf16[256,1024]{1,0:T(8,128)(2,1)}, bf16[256,1024]{1,0:T(8,128)(2,1)S(1)}, u32[]{:S(2)}, u32[]{:S(2)}) collective-permute-start(bf16[256,1024]{1,0:T(8,128)(2,1)} %get-tuple-element.233), channel_id=1, source_target_pairs={{0,0},{4,1},{5,2},{1,3},{2,4},{6,5},{7,6},{3,7},{8,8},{12,9},{13,1... | collective-permute-start | bytes 1572872 | tf_op jit(solution)/shard_map/ppermute | solution.py:1082
  420.2 27.4 %collective-permute-start.37 = (bf16[256,1024]{1,0:T(8,128)(2,1)}, bf16[256,1024]{1,0:T(8,128)(2,1)S(1)}, u32[]{:S(2)}, u32[]{:S(2)}) collective-permute-start(bf16[256,1024]{1,0:T(8,128)(2,1)} %get-tuple-element.234), channel_id=1, source_target_pairs={{1,0},{5,1},{4,2},{0,3},{3,4},{7,5},{6,6},{2,7},{9,8},{13,9},{12,1... | collective-permute-start | bytes 1572872 | tf_op jit(solution)/shard_map/ppermute | solution.py:1082
  470.9 38.1 %all-to-all-start.3 = ((bf16[32,32,512]{2,1,0:T(8,128)(2,1)}), bf16[32,32,512]{2,1,0:T(8,128)(2,1)S(1)}, u32[]{:S(2)}, u32[]{:S(2)}) async-start(bf16[32,32,512]{2,1,0:T(8,128)(2,1)} %bitcast.178), calls=%async_computation.3 | async-start | bytes 2097152 | tf_op jit(solution)/shard_map/all_to_all | solution.py:1342
  474.7 127.7 %reduce-scatter.11.cloned.1.call-start = ((), (), s32[]{:S(2)}) async-start(), calls=%async_computation.9 | async-start | bytes 4259840 | tf_op jit(solution)/shard_map/reduce_scatter | solution.py:1152
  512.5 48.0 %all-to-all-start.4 = ((bf16[4,4,3,128,256]{4,3,2,1,0:T(8,128)(2,1)}), bf16[4,4,3,128,256]{4,3,2,1,0:T(8,128)(2,1)S(1)}, u32[]{:S(2)}, u32[]{:S(2)}) async-start(bf16[4,4,3,128,256]{4,3,2,1,0:T(8,128)(2,1)} %weight_grad.15), calls=%async_computation.4 | async-start | bytes 6291456 | tf_op jit(solution)/shard_map/all_to_all | solution.py:1353
  516.4 44.0 %collective-permute-start.47 = (f32[10,1024]{1,0:T(8,128)S(1)}, f32[10,1024]{1,0:T(8,128)S(1)}, u32[]{:S(2)}, u32[]{:S(2)}) collective-permute-start(f32[10,1024]{1,0:T(8,128)S(1)} %add_add_fusion.1), channel_id=1, source_target_pairs={{0,3},{1,0},{2,1},{3,2},{4,7},{5,4},{6,5},{7,6},{8,11},{9,8},{10,9... | collective-permute-start | bytes 122888 | tf_op jit(solution)/shard_map/ppermute | solution.py:1174
  519.0 41.4 %collective-permute-start.46 = (f32[10,1024]{1,0:T(8,128)S(1)}, f32[10,1024]{1,0:T(8,128)S(1)}, u32[]{:S(2)}, u32[]{:S(2)}) collective-permute-start(f32[10,1024]{1,0:T(8,128)S(1)} %add_add_fusion.1), channel_id=1, source_target_pairs={{0,2},{1,3},{2,0},{3,1},{4,6},{5,7},{6,4},{7,5},{8,10},{9,11},{10,... | collective-permute-start | bytes 122888 | tf_op jit(solution)/shard_map/ppermute | solution.py:1174
  520.0 40.5 %collective-permute-start.45 = (f32[10,1024]{1,0:T(8,128)S(1)}, f32[10,1024]{1,0:T(8,128)S(1)}, u32[]{:S(2)}, u32[]{:S(2)}) collective-permute-start(f32[10,1024]{1,0:T(8,128)S(1)} %add_add_fusion.1), channel_id=1, source_target_pairs={{0,1},{1,2},{2,3},{3,0},{4,5},{5,6},{6,7},{7,4},{8,9},{9,10},{10,1... | collective-permute-start | bytes 122888 | tf_op jit(solution)/shard_map/ppermute | solution.py:1174
  (78 other events, 747.7 us)
Sparse Core Ops, SparseCore 0:
  11.4 121.3 all-gather.4
  135.9 131.6 all-gather.6
  325.9 51.6 reduce-scatter.12
  380.8 61.4 reduce-scatter.14
  448.7 58.0 reduce-scatter.16
  512.6 77.6 reduce-scatter.10

commit v6 on v5

--- a/solution.py
+++ b/solution.py
@@ -1047,7 +1047,7 @@
             scratch_shapes=[pltpu.VMEM((x_own.shape[1] // 2, 2 * tokens), bf16)],
         ),
         input_output_aliases={} if before is None else {5: 0},
-        compiler_params=params(),
+        compiler_params=params(30),
         cost_estimate=cost(3 + 2 * parts),
         name="weight_grad",
     )(info, x_own, x_par, y_own, y_par, *extra)
@@ -1321,10 +1321,11 @@
     outs = source_back(info, dckv_own, dckv_came, second[1])
     *enc_grad, dckv = outs
     dckv_after = swap(dckv)
-    shape = (chips, mp, 4, rows, block)
+    shape = (chips, mp, 3, rows, block)
     grads = weight_grad(info, c, c_par, after(dcq, dckv), dcq_par, shape, 0)
-    grads = weight_grad(info, g2b, g2b_par, o, o_par, shape, 1, grads)
-    grads = weight_grad(info, states, states_par, dckv, dckv_after, shape, 2, grads)
+    self_shape = (chips, mp, 4, rows, block)
+    held = weight_grad(info, after(g2b, grads), g2b_par, o, o_par, self_shape, 3)
+    grads = weight_grad(info, after(states, held), states_par, dckv, dckv_after, shape, 1, grads)
     do = after(do, grads)
     cross_grads = grads
     encoder_grad = from_chips(tied(enc_grad, grads), mp)
@@ -1342,12 +1343,11 @@
     arrived = lax.all_to_all(sent, ALL, split_axis=0, concat_axis=0, tiled=True)
     sums = jnp.concatenate((sums01, sums2, sums34), axis=0)
     sums_par = swap(sums)
-    shape = (chips, mp, 3, rows, block)
     dkv_after = swap(dkv)
-    grads = weight_grad(info, a, a_par, dq, dq_par, shape, 0)
+    grads = weight_grad(info, a, a_par, dq, dq_par, self_shape, 0, held)
     grads, sums_par = lax.optimization_barrier((grads, sums_par))
     sums = total_over(sums + sums_par, "chip", chips)
-    grads = weight_grad(info, a, a_par, dkv, dkv_after, shape, 1, grads)
+    grads = weight_grad(info, a, a_par, dkv, dkv_after, self_shape, 1, grads)
     sums, grads, arrived, cross_part = lax.optimization_barrier((sums, grads, arrived, cross_part))
     sums_up = scattered(jnp.concatenate([part_one, part_two, cross_part], axis=1), "mp")
     self_terms = lax.all_to_all(grads, "chip", split_axis=0, concat_axis=0, tiled=True)
@@ -1389,10 +1389,10 @@
         hidden_out,
         table_grad,
         pos_grad,
-        join(self_grads),
-        cross_grads[1],
+        join(self_grads[:3]),
+        self_grads[3],
         cross_grads[0],
-        join(cross_grads[2:4]),
+        join(cross_grads[1:3]),
         feed_in_grads[sub],
         join(feed_in_grads[:sub]).reshape(rows, -1),
         join(feed_out_grads).reshape(rows, -1),

time: 626 us -> 620 us (level)
  Pallas kernels: 326 us -> 310 us
  local copies, waits for them, and re-layouts: 39.5 us -> 47.6 us
    pallas_call x8, Pallas kernels: 54.8 us -> 38.4 us  [weight_grad(): pl.pallas_call(functools.partial(weight_grad_kernel, chips, before is not...]
    unnamed x99 -> x118, local copies, waits for them, and re-layouts: 24.4 us -> 31.7 us
  transfers between devices with their start and end apart: 65 -> 65, of which waited for: 19 -> 20; matrix products, arithmetic and copies ran while one was open for 5% -> 5% of each run, Pallas kernels for 51% -> 50%
where the time goes in v6:
time: 620 us; the launch traced here: 611 us
  Pallas kernels  310 us (50%)
  waiting for transfers between devices  130 us (21%)
  starting transfers between devices  86.6 us (14%)
  local copies, waits for them, and re-layouts  47.6 us (8%)
  other arithmetic  21 us (3%)
  between operations  15.5 us (2%)
    pallas_call x9, Pallas kernels, call(): pl.pallas_call(body, out_shape=[o for o, _ in outs], grid_spec=pltpu.Pref...  122 us
    pallas_call x1, Pallas kernels, gather_tokens(): pl.pallas_call(functools.partial(gather_kernel, groups, fill), out_shape=...  45.8 us
    pallas_call x2, Pallas kernels, attend(): pl.pallas_call(functools.partial(attend_kernel, causal), out_shape=(jax.S...  43.3 us
    ppermute x4, waiting for transfers between devices, begin(): lax.ppermute(w, 'chip', p)  40.5 us
    pallas_call x1, Pallas kernels, scatter_tokens(): pl.pallas_call(functools.partial(scatter_kernel, groups, per_core), out_s...  39.3 us
    pallas_call x8, Pallas kernels, weight_grad(): pl.pallas_call(functools.partial(weight_grad_kernel, chips, before is not...  38.4 us
    unnamed x118, local copies, waits for them, and re-layouts  31.7 us
    pallas_call x1, Pallas kernels, attend_back(): pl.pallas_call(attend_back_kernel, out_shape=(jax.ShapeDtypeStruct((1, to...  20.9 us
  transfers between devices with their start and end apart: 65, of which 20 were waited for; matrix products, arithmetic and copies ran while one was open for 5% of the time, Pallas kernels for 50%

profile of v6, /device:TPU:0, one launch (start us, length us, event | category | flops | bytes accessed | tf_op | source)
XLA Modules:
  0.0 610.6 jit_solution(228947395046017177)
XLA Ops:
  13.0 7.3 %all-to-all-start.1 = ((s32[32,1,512]{2,1,0:T(1,128)}), s32[32,1,512]{2,1,0:T(1,128)S(1)}, u32[]{:S(2)}, u32[]{:S(2)}) async-start(s32[32,1,512]{2,1,0:T(1,128)} %broadcast_in_dim.59), calls=%async_computation.1 | async-start | bytes 131072 | tf_op jit(solution)/shard_map/all_to_all | solution.py:1219
  21.3 6.4 %all-to-all-done.1 = s32[32,1,512]{2,1,0:T(1,128)S(1)} async-done(((s32[32,1,512]{2,1,0:T(1,128)}), s32[32,1,512]{2,1,0:T(1,128)S(1)}, u32[]{:S(2)}, u32[]{:S(2)}) %all-to-all-start.1) | async-done | bytes 65568 | tf_op jit(solution)/shard_map/all_to_all | solution.py:1219
  34.1 45.8 %gather_tokens.1 = bf16[32,32,512]{2,1,0:T(8,128)(2,1)} custom-call(s32[16384]{0:T(1024)} %add_select_fusion.rows_ref, s32[32,1,512]{2,1,0:T(1,128)} %and_select_fusion.1.group_ref, bf16[32,131072]{1,0:T(8,128)(2,1)} %refs_3_.1, bf16[32,131072]{1,0:T(8,128)(2,1)} %refs_3_.1, bf16[32,131072]{1,0:T(8,128)(2,1)} %refs_3_.1, bf16[32,131072]{1,0:T(8,128)(2,1)} %refs_3_.1), custom_call_target="tpu_custom_call" | custom-call | bytes 144000000 | tf_op jit(solution)/shard_map/gather_tokens/pallas_call | solution.py:186
  90.0 30.1 %collective-permute-done.2 = bf16[4,2,128,256]{3,2,1,0:T(8,128)(2,1)S(1)} collective-permute-done((bf16[4,2,128,256]{3,2,1,0:T(8,128)(2,1)S(1)}, bf16[4,2,128,256]{3,2,1,0:T(8,128)(2,1)S(1)}, u32[]{:S(2)}, u32[]{:S(2)}) %collective-permute-start.2) | collective-permute-done | bytes 524320 | tf_op jit(solution)/shard_map/ppermute | solution.py:1118
  121.7 10.1 %collective-permute-done.10 = bf16[4,2,128,256]{3,2,1,0:T(8,128)(2,1)} collective-permute-done((bf16[4,2,128,256]{3,2,1,0:T(8,128)(2,1)S(1)}, bf16[4,2,128,256]{3,2,1,0:T(8,128)(2,1)}, u32[]{:S(2)}, u32[]{:S(2)}) %collective-permute-start.10) | collective-permute-done | bytes 524320 | tf_op jit(solution)/shard_map/ppermute | solution.py:1118
  133.7 9.1 %collective-permute-done.6 = bf16[4,2,128,256]{3,2,1,0:T(8,128)(2,1)} collective-permute-done((bf16[4,2,128,256]{3,2,1,0:T(8,128)(2,1)S(1)}, bf16[4,2,128,256]{3,2,1,0:T(8,128)(2,1)}, u32[]{:S(2)}, u32[]{:S(2)}) %collective-permute-start.6) | collective-permute-done | bytes 524320 | tf_op jit(solution)/shard_map/ppermute | solution.py:1123
  149.2 13.9 %entry.1 = (f32[512,1024]{1,0:T(8,128)}, f32[512,1024]{1,0:T(8,128)}, bf16[512,1024]{1,0:T(8,128)(2,1)}, bf16[1,512,1024]{2,1,0:T(8,128)(2,1)}, bf16[2,512,1024]{2,1,0:T(8,128)(2,1)}) custom-call(s32[10]{0:T(128)} %stack.70.info_ref, bf16[1024,512]{1,0:T(8,128)(2,1)} %bitcast.16.refs_0_, bf16[1,4,4,128,256]{4,3,2,1,0:T(8,128)(2,1)} %bitcast.141, ...), custom_call_target="tpu_custom_call" | custom-call | bytes 48000000 | tf_op jit(solution)/shard_map/entry/pallas_call | solution.py:117
  165.9 4.7 collective-permute-start.16
  172.0 21.6 %attend.2 = (bf16[1,512,1024]{2,1,0:T(8,128)(2,1)}, bf16[16,2,512,512]{3,2,1,0:T(8,128)(2,1)}) custom-call(s32[10]{0:T(128)} %stack.70.info_ref, bf16[1,512,1024]{2,1,0:T(8,128)(2,1)} %get-tuple-element.147.q_ref.refs_0_, bf16[2,512,1024]{2,1,0:T(8,128)(2,1)} %get-tuple-element.148.own_ref.refs_1_, bf16[2,512,1024]{2,1,0:T(8,128)(2,1)} %copy-done.34), custom_call_target="tpu_custom_call" | custom-call | bytes 70400000 | tf_op jit(solution)/shard_map/attend/pallas_call | solution.py:507
  193.6 14.1 %collective-permute-done.16.refs_1_ = bf16[256,1024]{1,0:T(8,128)(2,1)S(1)} collective-permute-done((bf16[256,1024]{1,0:T(8,128)(2,1)S(1)}, bf16[256,1024]{1,0:T(8,128)(2,1)S(1)}, u32[]{:S(2)}, u32[]{:S(2)}) %collective-permute-start.16) | collective-permute-done | bytes 524320 | tf_op jit(solution)/shard_map/ppermute | solution.py:1075
  208.5 6.6 %source_keys.1 = (bf16[512,1024]{1,0:T(8,128)(2,1)}, bf16[2,512,1024]{2,1,0:T(8,128)(2,1)}) custom-call(s32[10]{0:T(128)} %stack.70.info_ref, bf16[256,1024]{1,0:T(8,128)(2,1)} %copy-done.44, bf16[256,1024]{1,0:T(8,128)(2,1)} %copy-done.45, bf16[8,4,5,128,256]{4,3,2,1,0:T(8,128)(2,1)} %bitcast.127), custom_call_target="tpu_custom_call" | custom-call | bytes 25600000 | tf_op jit(solution)/shard_map/source_keys/pallas_call | solution.py:117
  219.2 7.8 %middle.1 = (f32[512,1024]{1,0:T(8,128)}, bf16[512,1024]{1,0:T(8,128)(2,1)}, bf16[1,512,1024]{2,1,0:T(8,128)(2,1)}) custom-call(s32[10]{0:T(128)} %stack.70.info_ref, bf16[1,512,1024]{2,1,0:T(8,128)(2,1)} %get-tuple-element.186.refs_0_.yo_ref.refs_4_, bf16[8,4,5,128,256]{4,3,2,1,0:T(8,128)(2,1)} %bitcast.128, ...), custom_call_target="tpu_custom_call" | custom-call | bytes 28800000 | tf_op jit(solution)/shard_map/middle/pallas_call | solution.py:117
  228.3 21.6 %attend.3 = (bf16[1,512,1024]{2,1,0:T(8,128)(2,1)}, bf16[16,2,512,512]{3,2,1,0:T(8,128)(2,1)}) custom-call(s32[10]{0:T(128)} %stack.70.info_ref, bf16[1,512,1024]{2,1,0:T(8,128)(2,1)} %get-tuple-element.159.q_ref, bf16[2,512,1024]{2,1,0:T(8,128)(2,1)} %get-tuple-element.156.own_ref, bf16[2,512,1024]{2,1,0:T(8,128)(2,1)} %copy-done.33), custom_call_target="tpu_custom_call" | custom-call | bytes 70400000 | tf_op jit(solution)/shard_map/attend/pallas_call | solution.py:507
  251.7 5.4 collective-permute-start.18
  259.4 8.2 %all-gather.7.cloned.1.call-done = bf16[32768,256]{1,0:T(8,128)(2,1)} async-done(((bf16[1024,256]{1,0:T(8,128)(2,1)}), bf16[32768,256]{1,0:T(8,128)(2,1)}) %all-gather.7.cloned.1.call-update) | async-done | bytes 16777232 | tf_op jit(solution)/shard_map/all_gather | solution.py:1100
  267.6 19.4 %feed.1 = (f32[512,1024]{1,0:T(8,128)}, bf16[512,1024]{1,0:T(8,128)(2,1)}, bf16[4,512,1024]{2,1,0:T(8,128)(2,1)}, bf16[4,512,1024]{2,1,0:T(8,128)(2,1)}, f32[512,1024]{1,0:T(8,128)}) custom-call(s32[10]{0:T(128)} %stack.70.info_ref, bf16[1,512,1024]{2,1,0:T(8,128)(2,1)} %get-tuple-element.160.refs_0_.yo_ref.o_ref, bf16[8,4,5,128,256]{4,3,2,1,0:T(8,128)(2,1)} %bitcast.130, ...), custom_call_target="tpu_custom_call" | custom-call | bytes 89600000 | tf_op jit(solution)/shard_map/feed/pallas_call | solution.py:117
  289.4 23.3 %feed_back.1 = (bf16[256,1024]{1,0:T(8,128)(2,1)}, bf16[256,1024]{1,0:T(8,128)(2,1)}, bf16[512,1024]{1,0:T(8,128)(2,1)}, bf16[4,512,1024]{2,1,0:T(8,128)(2,1)}, ...) custom-call(s32[10]{0:T(128)} %stack.70.info_ref, ...), custom_call_target="tpu_custom_call" | custom-call | bytes 89600000 | tf_op jit(solution)/shard_map/feed_back/pallas_call | solution.py:117
  319.1 7.4 %weight_grad.8 = bf16[4,4,4,128,256]{4,3,2,1,0:T(8,128)(2,1)S(1)} custom-call(s32[10]{0:T(128)S(1)} %copy-done.23, bf16[512,1024]{1,0:T(8,128)(2,1)S(1)} %copy-done.21, bf16[512,1024]{1,0:T(8,128)(2,1)S(1)} %collective-permute-done.27.xp_ref, bf16[4,512,1024]{2,1,0:T(8,128)(2,1)S(1)} %copy-done.7, bf16[4,512,1024]{2,1,0:T(8,128)(2,1)} %collective-permute-done.23.yp_ref), custom_call_target="tpu_custom_call" | custom-call | bytes 35200000 | tf_op jit(solution)/shard_map/weight_grad/pallas_call | solution.py:1037
  329.3 5.4 collective-permute-start.30
  342.8 7.6 %weight_grad.10 = bf16[4,4,5,128,256]{4,3,2,1,0:T(8,128)(2,1)S(1)} custom-call(s32[10]{0:T(128)S(1)} %copy-done.23, bf16[512,1024]{1,0:T(8,128)(2,1)S(1)} %copy-done.19, bf16[512,1024]{1,0:T(8,128)(2,1)} %collective-permute-done.22.xp_ref, bf16[4,512,1024]{2,1,0:T(8,128)(2,1)S(1)} %copy-done.11, ...), custom_call_target="tpu_custom_call", output_to_operand_aliasing={{}: (5, {})} | custom-call | bytes 35200000 | tf_op jit(solution)/shard_map/weight_grad/pallas_call | solution.py:1037
  352.7 20.9 %attend_back.1 = (bf16[1,512,1024]{2,1,0:T(8,128)(2,1)}, bf16[2,512,1024]{2,1,0:T(8,128)(2,1)}, bf16[2,512,1024]{2,1,0:T(8,128)(2,1)}) custom-call(bf16[1,512,1024]{2,1,0:T(8,128)(2,1)} %get-tuple-element.159.q_ref, bf16[2,512,1024]{2,1,0:T(8,128)(2,1)} %get-tuple-element.156.own_ref, bf16[2,512,1024]{2,1,0:T(8,128)(2,1)} %copy-done.33, ...), custom_call_target="tpu_custom_call" | custom-call | bytes 67200000 | tf_op jit(solution)/shard_map/attend_back/pallas_call | solution.py:769
  373.6 6.9 %reduce-scatter.13.cloned.1.call-done = bf16[1,4,4,128,256]{4,3,2,1,0:T(8,128)(2,1)} async-done(((bf16[4,4,4,128,256]{4,3,2,1,0:T(8,128)(2,1)}), bf16[1,4,4,128,256]{4,3,2,1,0:T(8,128)(2,1)}) %reduce-scatter.13.cloned.1.call-update) | async-done | bytes 1048592
  384.0 8.8 %middle_back.1 = (f32[512,1024]{1,0:T(8,128)}, bf16[512,1024]{1,0:T(8,128)(2,1)}, bf16[1,512,1024]{2,1,0:T(8,128)(2,1)}, f32[2,1024]{1,0:T(2,128)}) custom-call(s32[10]{0:T(128)} %stack.70.info_ref, bf16[1,512,1024]{2,1,0:T(8,128)(2,1)} %get-tuple-element.225.refs_0_.yo_ref, bf16[8,4,5,128,256]{4,3,2,1,0:T(8,128)(2,1)} %bitcast.132, ...), custom_call_target="tpu_custom_call" | custom-call | bytes 32000000 | tf_op jit(solution)/shard_map/middle_back/pallas_call | solution.py:117
  394.1 7.6 %source_back.1 = (bf16[256,1024]{1,0:T(8,128)(2,1)}, bf16[256,1024]{1,0:T(8,128)(2,1)}, bf16[2,512,1024]{2,1,0:T(8,128)(2,1)}) custom-call(s32[10]{0:T(128)} %stack.70.info_ref, bf16[2,512,1024]{2,1,0:T(8,128)(2,1)} %get-tuple-element.222.refs_0_, bf16[2,512,1024]{2,1,0:T(8,128)(2,1)} %copy-done.39, bf16[8,4,5,128,256]{4,3,2,1,0:T(8,128)(2,1)} %bitcast.134), custom_call_target="tpu_custom_call" | custom-call | bytes 22400000 | tf_op jit(solution)/shard_map/source_back/pallas_call | solution.py:117
  412.9 5.7 weight_grad.13
  420.3 6.0 collective-permute-start.37
  426.3 19.4 %causal_back.1 = (bf16[1,512,1024]{2,1,0:T(8,128)(2,1)}, bf16[2,512,1024]{2,1,0:T(8,128)(2,1)}, bf16[2,512,1024]{2,1,0:T(8,128)(2,1)}) custom-call(s32[10]{0:T(128)} %stack.70.info_ref, bf16[1,512,1024]{2,1,0:T(8,128)(2,1)} %get-tuple-element.147.q_ref.refs_0_, bf16[2,512,1024]{2,1,0:T(8,128)(2,1)} %get-tuple-element.148.own_ref.refs_1_, ...), custom_call_target="tpu_custom_call" | custom-call | bytes 60800000 | tf_op jit(solution)/shard_map/causal_back/pallas_call | solution.py:117
  453.9 15.3 %exit_back.1 = (bf16[1024,512]{1,0:T(8,128)(2,1)}, bf16[2,512,1024]{2,1,0:T(8,128)(2,1)}, f32[4,1024]{1,0:T(4,128)}) custom-call(s32[10]{0:T(128)} %stack.70.info_ref, bf16[1,512,1024]{2,1,0:T(8,128)(2,1)} %get-tuple-element.241.refs_0_.yo_ref, bf16[2,512,1024]{2,1,0:T(8,128)(2,1)} %get-tuple-element.242.refs_1_, bf16[2,512,1024]{2,1,0:T(8,128)(2,1)} %copy-done.37, ...), custom_call_target="tpu_custom_call" | custom-call | bytes 48000000 | tf_op jit(solution)/shard_map/exit_back/pallas_call | solution.py:117
  492.7 4.8 weight_grad.15
  505.7 4.9 all-to-all-start.4
  515.3 39.3 %scatter_tokens.1 = (f32[32,131072]{1,0:T(8,128)}, f32[2,32,512]{2,1,0:T(8,128)}) custom-call(s32[16384]{0:T(1024)} %add_select_fusion.rows_ref, s32[32,1,512]{2,1,0:T(1,128)} %get-tuple-element.328.row_ref, s32[32,1,512]{2,1,0:T(1,128)} %and_select_fusion.1.group_ref, bf16[32,32,512]{2,1,0:T(8,128)(2,1)} %all-to-all-done.3.grad_ref), custom_call_target="tpu_custom_call" | custom-call | bytes 124800000 | tf_op jit(solution)/shard_map/scatter_tokens/pallas_call | solution.py:299
  577.6 18.3 %collective-permute-done.52 = bf16[4,128,256]{2,1,0:T(8,128)(2,1)S(1)} collective-permute-done((bf16[4,128,256]{2,1,0:T(8,128)(2,1)S(1)}, bf16[4,128,256]{2,1,0:T(8,128)(2,1)S(1)}, u32[]{:S(2)}, u32[]{:S(2)}) %collective-permute-start.52) | collective-permute-done | bytes 262176 | tf_op jit(solution)/shard_map/ppermute | solution.py:1164
  (302 shorter events, 161.2 us)
Async XLA Ops:
  7.2 200.5 %all-gather.5.cloned.1.call-start = ((), (), s32[]{:S(2)}) async-start(), calls=%async_computation.10 | async-start | bytes 10813440 | tf_op jit(solution)/shard_map/all_gather | solution.py:1100
  9.9 257.7 %all-gather.7.cloned.1.call-start = ((), (), s32[]{:S(2)}) async-start(), calls=%async_computation.11 | async-start | bytes 17301504 | tf_op jit(solution)/shard_map/all_gather | solution.py:1100
  27.8 52.1 %all-to-all-start = ((bf16[4,512,256]{2,1,0:T(8,128)(2,1)}), bf16[4,512,256]{2,1,0:T(8,128)(2,1)S(1)}, u32[]{:S(2)}, u32[]{:S(2)}) async-start(bf16[4,512,256]{2,1,0:T(8,128)(2,1)} %broadcast_in_dim.57), calls=%async_computation | async-start | bytes 2097152 | tf_op jit(solution)/shard_map/all_to_all | solution.py:1234
  79.9 68.4 %all-to-all-start.2 = ((bf16[32,32,512]{2,1,0:T(8,128)(2,1)}), bf16[32,32,512]{2,1,0:T(8,128)(2,1)}, u32[]{:S(2)}, u32[]{:S(2)}) async-start(bf16[32,32,512]{2,1,0:T(8,128)(2,1)} %gather_tokens.1), calls=%async_computation.2 | async-start | bytes 2097152 | tf_op jit(solution)/shard_map/all_to_all | solution.py:1278
  84.2 296.3 %reduce-scatter.13.cloned.1.call-start = ((), (), s32[]{:S(2)}) async-start(), calls=%async_computation.12 | async-start | bytes 5242880
  84.3 48.8 %collective-permute-start.1 = (bf16[4,4,128,256]{3,2,1,0:T(8,128)(2,1)S(1)}, bf16[4,4,128,256]{3,2,1,0:T(8,128)(2,1)S(1)}, u32[]{:S(2)}, u32[]{:S(2)}) collective-permute-start(bf16[4,4,128,256]{3,2,1,0:T(8,128)(2,1)S(1)} %bitcast.139), channel_id=1, source_target_pairs={{0,4},{4,0},{1,5},{5,1},{2,6},{6,2},{3,7},{7,3},{8,12},{12,8},{9,1... | collective-permute-start | bytes 3145736 | tf_op jit(solution)/shard_map/ppermute | solution.py:1057
  84.6 35.5 %collective-permute-start.2 = (bf16[4,2,128,256]{3,2,1,0:T(8,128)(2,1)S(1)}, bf16[4,2,128,256]{3,2,1,0:T(8,128)(2,1)S(1)}, u32[]{:S(2)}, u32[]{:S(2)}) collective-permute-start(bf16[4,2,128,256]{3,2,1,0:T(8,128)(2,1)S(1)} %get-tuple-element.344), channel_id=1, source_target_pairs={{0,8},{8,0},{16,24},{24,16},{1,9},{9,1},{17,25},{25,17},{2,10},{10... | collective-permute-start | bytes 1572872 | tf_op jit(solution)/shard_map/ppermute | solution.py:1118
  86.4 34.0 %collective-permute-start.4 = (bf16[4,2,128,256]{3,2,1,0:T(8,128)(2,1)S(1)}, bf16[4,2,128,256]{3,2,1,0:T(8,128)(2,1)S(1)}, u32[]{:S(2)}, u32[]{:S(2)}) collective-permute-start(bf16[4,2,128,256]{3,2,1,0:T(8,128)(2,1)S(1)} %get-tuple-element.344), channel_id=1, source_target_pairs={{0,16},{16,0},{8,24},{24,8},{1,17},{17,1},{9,25},{25,9},{2,18},{18... | collective-permute-start | bytes 1572872 | tf_op jit(solution)/shard_map/ppermute | solution.py:1119
  87.8 43.9 %collective-permute-start.10 = (bf16[4,2,128,256]{3,2,1,0:T(8,128)(2,1)S(1)}, bf16[4,2,128,256]{3,2,1,0:T(8,128)(2,1)}, u32[]{:S(2)}, u32[]{:S(2)}) collective-permute-start(bf16[4,2,128,256]{3,2,1,0:T(8,128)(2,1)S(1)} %get-tuple-element.343), channel_id=1, source_target_pairs={{0,16},{16,0},{8,24},{24,8},{1,17},{17,1},{9,25},{25,9},{2,18},{18... | collective-permute-start | bytes 1572872 | tf_op jit(solution)/shard_map/ppermute | solution.py:1118
  89.6 43.5 %collective-permute-start.8 = (bf16[4,2,128,256]{3,2,1,0:T(8,128)(2,1)S(1)}, bf16[4,2,128,256]{3,2,1,0:T(8,128)(2,1)}, u32[]{:S(2)}, u32[]{:S(2)}) collective-permute-start(bf16[4,2,128,256]{3,2,1,0:T(8,128)(2,1)S(1)} %get-tuple-element.343), channel_id=1, source_target_pairs={{0,8},{8,0},{16,24},{24,16},{1,9},{9,1},{17,25},{25,17},{2,10},{10... | collective-permute-start | bytes 1572872 | tf_op jit(solution)/shard_map/ppermute | solution.py:1119
  165.2 28.4 %collective-permute-start.15 = (bf16[256,1024]{1,0:T(8,128)(2,1)S(1)}, bf16[256,1024]{1,0:T(8,128)(2,1)S(1)}, u32[]{:S(2)}, u32[]{:S(2)}) collective-permute-start(bf16[256,1024]{1,0:T(8,128)(2,1)S(1)} %get-tuple-element.342), channel_id=1, source_target_pairs={{0,0},{1,4},{2,5},{3,1},{4,2},{5,6},{6,7},{7,3},{8,8},{9,12},{10,1... | collective-permute-start | bytes 1572872 | tf_op jit(solution)/shard_map/ppermute | solution.py:1075
  165.9 41.8 %collective-permute-start.16 = (bf16[256,1024]{1,0:T(8,128)(2,1)S(1)}, bf16[256,1024]{1,0:T(8,128)(2,1)S(1)}, u32[]{:S(2)}, u32[]{:S(2)}) collective-permute-start(bf16[256,1024]{1,0:T(8,128)(2,1)S(1)} %get-tuple-element.341), channel_id=1, source_target_pairs={{0,1},{1,5},{2,4},{3,0},{4,3},{5,7},{6,6},{7,2},{8,9},{9,13},{10,1... | collective-permute-start | bytes 1572872 | tf_op jit(solution)/shard_map/ppermute | solution.py:1075
  249.9 37.1 %collective-permute-start.20 = (bf16[1,512,1024]{2,1,0:T(8,128)(2,1)}, bf16[1,512,1024]{2,1,0:T(8,128)(2,1)S(1)}, u32[]{:S(2)}, u32[]{:S(2)}) collective-permute-start(bf16[1,512,1024]{2,1,0:T(8,128)(2,1)} %get-tuple-element.160.refs_0_.yo_ref.o_ref), channel_id=1, source_target_pairs={{0,4},{4,0},{1,5},{5,1},{2,6},{6,2},{3,7},{7,3},{8,12},{12,8},{9,1... | collective-permute-start | bytes 3145736 | tf_op jit(solution)/shard_map/ppermute | solution.py:1057
  249.9 38.1 %collective-permute-start.21 = (bf16[512,1024]{1,0:T(8,128)(2,1)}, bf16[512,1024]{1,0:T(8,128)(2,1)}, u32[]{:S(2)}, u32[]{:S(2)}) collective-permute-start(bf16[512,1024]{1,0:T(8,128)(2,1)} %get-tuple-element.169.xo_ref), channel_id=1, source_target_pairs={{0,4},{4,0},{1,5},{5,1},{2,6},{6,2},{3,7},{7,3},{8,12},{12,8},{9,1... | collective-permute-start | bytes 3145736 | tf_op jit(solution)/shard_map/ppermute | solution.py:1057
  251.7 35.3 %collective-permute-start.18 = (bf16[256,1024]{1,0:T(8,128)(2,1)}, bf16[256,1024]{1,0:T(8,128)(2,1)}, u32[]{:S(2)}, u32[]{:S(2)}) collective-permute-start(bf16[256,1024]{1,0:T(8,128)(2,1)} %get-tuple-element.340), channel_id=1, source_target_pairs={{0,0},{1,4},{2,5},{3,1},{4,2},{5,6},{6,7},{7,3},{8,8},{9,12},{10,1... | collective-permute-start | bytes 1572872 | tf_op jit(solution)/shard_map/ppermute | solution.py:1075
  257.1 30.0 %collective-permute-start.19 = (bf16[256,1024]{1,0:T(8,128)(2,1)}, bf16[256,1024]{1,0:T(8,128)(2,1)}, u32[]{:S(2)}, u32[]{:S(2)}) collective-permute-start(bf16[256,1024]{1,0:T(8,128)(2,1)} %get-tuple-element.339), channel_id=1, source_target_pairs={{0,1},{1,5},{2,4},{3,0},{4,3},{5,7},{6,6},{7,2},{8,9},{9,13},{10,1... | collective-permute-start | bytes 1572872 | tf_op jit(solution)/shard_map/ppermute | solution.py:1075
  288.1 24.6 %collective-permute-start.23 = (bf16[4,512,1024]{2,1,0:T(8,128)(2,1)}, bf16[4,512,1024]{2,1,0:T(8,128)(2,1)}, u32[]{:S(2)}, u32[]{:S(2)}) collective-permute-start(bf16[4,512,1024]{2,1,0:T(8,128)(2,1)} %get-tuple-element.184.yo_ref), channel_id=1, source_target_pairs={{0,4},{4,0},{1,5},{5,1},{2,6},{6,2},{3,7},{7,3},{8,12},{12,8},{9,1... | collective-permute-start | bytes 12582920 | tf_op jit(solution)/shard_map/ppermute | solution.py:1057
  288.3 24.3 %collective-permute-start.22 = (bf16[512,1024]{1,0:T(8,128)(2,1)}, bf16[512,1024]{1,0:T(8,128)(2,1)}, u32[]{:S(2)}, u32[]{:S(2)}) collective-permute-start(bf16[512,1024]{1,0:T(8,128)(2,1)} %get-tuple-element.195.xo_ref), channel_id=1, source_target_pairs={{0,4},{4,0},{1,5},{5,1},{2,6},{6,2},{3,7},{7,3},{8,12},{12,8},{9,1... | collective-permute-start | bytes 3145736 | tf_op jit(solution)/shard_map/ppermute | solution.py:1057
  288.6 24.1 %collective-permute-start.24 = (bf16[512,1024]{1,0:T(8,128)(2,1)S(1)}, bf16[512,1024]{1,0:T(8,128)(2,1)S(1)}, u32[]{:S(2)}, u32[]{:S(2)}) collective-permute-start(bf16[512,1024]{1,0:T(8,128)(2,1)S(1)} %copy-done.8), channel_id=1, source_target_pairs={{0,4},{4,0},{1,5},{5,1},{2,6},{6,2},{3,7},{7,3},{8,12},{12,8},{9,1... | collective-permute-start | bytes 3145736 | tf_op jit(solution)/shard_map/ppermute | solution.py:1057
  288.8 23.9 %collective-permute-start.25 = (bf16[1,512,1024]{2,1,0:T(8,128)(2,1)S(1)}, bf16[1,512,1024]{2,1,0:T(8,128)(2,1)}, u32[]{:S(2)}, u32[]{:S(2)}) collective-permute-start(bf16[1,512,1024]{2,1,0:T(8,128)(2,1)S(1)} %copy-done.6), channel_id=1, source_target_pairs={{0,4},{4,0},{1,5},{5,1},{2,6},{6,2},{3,7},{7,3},{8,12},{12,8},{9,1... | collective-permute-start | bytes 3145736 | tf_op jit(solution)/shard_map/ppermute | solution.py:1057
  289.1 23.6 %collective-permute-start.26 = (bf16[512,1024]{1,0:T(8,128)(2,1)}, bf16[512,1024]{1,0:T(8,128)(2,1)}, u32[]{:S(2)}, u32[]{:S(2)}) collective-permute-start(bf16[512,1024]{1,0:T(8,128)(2,1)} %get-tuple-element.229.xo_ref), channel_id=1, source_target_pairs={{0,4},{4,0},{1,5},{5,1},{2,6},{6,2},{3,7},{7,3},{8,12},{12,8},{9,1... | collective-permute-start | bytes 3145736 | tf_op jit(solution)/shard_map/ppermute | solution.py:1057
  328.5 117.2 %reduce-scatter.15.cloned.1.call-start = ((), (), s32[]{:S(2)}) async-start(), calls=%async_computation.13 | async-start | bytes 6553600
  329.3 23.4 %collective-permute-start.30 = (bf16[256,1024]{1,0:T(8,128)(2,1)}, bf16[256,1024]{1,0:T(8,128)(2,1)}, u32[]{:S(2)}, u32[]{:S(2)}) collective-permute-start(bf16[256,1024]{1,0:T(8,128)(2,1)} %get-tuple-element.201), channel_id=1, source_target_pairs={{0,0},{4,1},{5,2},{1,3},{2,4},{6,5},{7,6},{3,7},{8,8},{12,9},{13,1... | collective-permute-start | bytes 1572872 | tf_op jit(solution)/shard_map/ppermute | solution.py:1082
  382.8 118.3 %reduce-scatter.17.cloned.1.call-start = ((), (), s32[]{:S(2)}) async-start(), calls=%async_computation.14 | async-start | bytes 3932160
  418.6 29.6 %collective-permute-start.36 = (bf16[256,1024]{1,0:T(8,128)(2,1)}, bf16[256,1024]{1,0:T(8,128)(2,1)S(1)}, u32[]{:S(2)}, u32[]{:S(2)}) collective-permute-start(bf16[256,1024]{1,0:T(8,128)(2,1)} %get-tuple-element.237), channel_id=1, source_target_pairs={{0,0},{4,1},{5,2},{1,3},{2,4},{6,5},{7,6},{3,7},{8,8},{12,9},{13,1... | collective-permute-start | bytes 1572872 | tf_op jit(solution)/shard_map/ppermute | solution.py:1082
  420.3 27.9 %collective-permute-start.37 = (bf16[256,1024]{1,0:T(8,128)(2,1)}, bf16[256,1024]{1,0:T(8,128)(2,1)S(1)}, u32[]{:S(2)}, u32[]{:S(2)}) collective-permute-start(bf16[256,1024]{1,0:T(8,128)(2,1)} %get-tuple-element.238), channel_id=1, source_target_pairs={{1,0},{5,1},{4,2},{0,3},{3,4},{7,5},{6,6},{2,7},{9,8},{13,9},{12,1... | collective-permute-start | bytes 1572872 | tf_op jit(solution)/shard_map/ppermute | solution.py:1082
  469.6 33.1 %all-to-all-start.3 = ((bf16[32,32,512]{2,1,0:T(8,128)(2,1)}), bf16[32,32,512]{2,1,0:T(8,128)(2,1)}, u32[]{:S(2)}, u32[]{:S(2)}) async-start(bf16[32,32,512]{2,1,0:T(8,128)(2,1)} %bitcast.178), calls=%async_computation.3 | async-start | bytes 2097152 | tf_op jit(solution)/shard_map/all_to_all | solution.py:1343
  474.1 123.4 %reduce-scatter.11.cloned.1.call-start = ((), (), s32[]{:S(2)}) async-start(), calls=%async_computation.9 | async-start | bytes 3932160 | tf_op jit(solution)/shard_map/reduce_scatter | solution.py:1152
  505.7 52.8 %all-to-all-start.4 = ((bf16[4,4,4,128,256]{4,3,2,1,0:T(8,128)(2,1)}), bf16[4,4,4,128,256]{4,3,2,1,0:T(8,128)(2,1)}, u32[]{:S(2)}, u32[]{:S(2)}) async-start(bf16[4,4,4,128,256]{4,3,2,1,0:T(8,128)(2,1)} %copy-done.2), calls=%async_computation.4 | async-start | bytes 8388608 | tf_op jit(solution)/shard_map/all_to_all | solution.py:1353
  510.6 44.0 %collective-permute-start.47 = (f32[10,1024]{1,0:T(8,128)S(1)}, f32[10,1024]{1,0:T(8,128)S(1)}, u32[]{:S(2)}, u32[]{:S(2)}) collective-permute-start(f32[10,1024]{1,0:T(8,128)S(1)} %add_add_fusion.1), channel_id=1, source_target_pairs={{0,3},{1,0},{2,1},{3,2},{4,7},{5,4},{6,5},{7,6},{8,11},{9,8},{10,9... | collective-permute-start | bytes 122888 | tf_op jit(solution)/shard_map/ppermute | solution.py:1174
  513.8 40.8 %collective-permute-start.46 = (f32[10,1024]{1,0:T(8,128)S(1)}, f32[10,1024]{1,0:T(8,128)S(1)}, u32[]{:S(2)}, u32[]{:S(2)}) collective-permute-start(f32[10,1024]{1,0:T(8,128)S(1)} %add_add_fusion.1), channel_id=1, source_target_pairs={{0,2},{1,3},{2,0},{3,1},{4,6},{5,7},{6,4},{7,5},{8,10},{9,11},{10,... | collective-permute-start | bytes 122888 | tf_op jit(solution)/shard_map/ppermute | solution.py:1174
  513.8 40.8 %collective-permute-start.45 = (f32[10,1024]{1,0:T(8,128)S(1)}, f32[10,1024]{1,0:T(8,128)S(1)}, u32[]{:S(2)}, u32[]{:S(2)}) collective-permute-start(f32[10,1024]{1,0:T(8,128)S(1)} %add_add_fusion.1), channel_id=1, source_target_pairs={{0,1},{1,2},{2,3},{3,0},{4,5},{5,6},{6,7},{7,4},{8,9},{9,10},{10,1... | collective-permute-start | bytes 122888 | tf_op jit(solution)/shard_map/ppermute | solution.py:1174
  (88 other events, 787.7 us)
Sparse Core Ops, SparseCore 0:
  11.4 121.3 all-gather.4
  135.9 131.6 all-gather.6
  328.6 51.8 reduce-scatter.12
  383.6 61.4 reduce-scatter.14
  448.3 52.7 reduce-scatter.16
  505.8 66.3 reduce-scatter.10

commit v7 on v6

--- a/solution.py
+++ b/solution.py
@@ -203,7 +203,7 @@
 
 
 BATCH = 16
-WIDTH = 4096
+WIDTH = 8192
 SENDERS = 8
 
 

time: 620 us -> 620 us (level)
  transfers between devices with their start and end apart: 65 -> 65, of which waited for: 20 -> 20; matrix products, arithmetic and copies ran while one was open for 5% -> 5% of each run, Pallas kernels for 50% -> 49%
where the time goes in v7:
time: 620 us; the launch traced here: 611 us
  Pallas kernels  309 us (50%)
  waiting for transfers between devices  131 us (21%)
  starting transfers between devices  86.6 us (14%)
  local copies, waits for them, and re-layouts  47.6 us (8%)
  other arithmetic  21 us (3%)
  between operations  15.5 us (2%)
    pallas_call x9, Pallas kernels, call(): pl.pallas_call(body, out_shape=[o for o, _ in outs], grid_spec=pltpu.Pref...  122 us
    pallas_call x1, Pallas kernels, gather_tokens(): pl.pallas_call(functools.partial(gather_kernel, groups, fill), out_shape=...  45.8 us
    pallas_call x2, Pallas kernels, attend(): pl.pallas_call(functools.partial(attend_kernel, causal), out_shape=(jax.S...  43.3 us
    ppermute x4, waiting for transfers between devices, begin(): lax.ppermute(w, 'chip', p)  40.5 us
    pallas_call x1, Pallas kernels, scatter_tokens(): pl.pallas_call(functools.partial(scatter_kernel, groups, per_core), out_s...  38.6 us
    pallas_call x8, Pallas kernels, weight_grad(): pl.pallas_call(functools.partial(weight_grad_kernel, chips, before is not...  38.4 us
    unnamed x118, local copies, waits for them, and re-layouts  31.7 us
    pallas_call x1, Pallas kernels, attend_back(): pl.pallas_call(attend_back_kernel, out_shape=(jax.ShapeDtypeStruct((1, to...  20.9 us
  transfers between devices with their start and end apart: 65, of which 20 were waited for; matrix products, arithmetic and copies ran while one was open for 5% of the time, Pallas kernels for 49%

profile of v7, /device:TPU:0, one launch (start us, length us, event | category | flops | bytes accessed | tf_op | source)
XLA Modules:
  0.0 610.6 jit_solution(620268024259395115)
XLA Ops:
  13.0 7.3 %all-to-all-start.1 = ((s32[32,1,512]{2,1,0:T(1,128)}), s32[32,1,512]{2,1,0:T(1,128)S(1)}, u32[]{:S(2)}, u32[]{:S(2)}) async-start(s32[32,1,512]{2,1,0:T(1,128)} %broadcast_in_dim.59), calls=%async_computation.1 | async-start | bytes 131072 | tf_op jit(solution)/shard_map/all_to_all | solution.py:1219
  21.3 6.4 %all-to-all-done.1 = s32[32,1,512]{2,1,0:T(1,128)S(1)} async-done(((s32[32,1,512]{2,1,0:T(1,128)}), s32[32,1,512]{2,1,0:T(1,128)S(1)}, u32[]{:S(2)}, u32[]{:S(2)}) %all-to-all-start.1) | async-done | bytes 65568 | tf_op jit(solution)/shard_map/all_to_all | solution.py:1219
  34.1 45.8 %gather_tokens.1 = bf16[32,32,512]{2,1,0:T(8,128)(2,1)} custom-call(s32[16384]{0:T(1024)} %add_select_fusion.rows_ref, s32[32,1,512]{2,1,0:T(1,128)} %and_select_fusion.1.group_ref, bf16[32,131072]{1,0:T(8,128)(2,1)} %refs_3_.1, bf16[32,131072]{1,0:T(8,128)(2,1)} %refs_3_.1, bf16[32,131072]{1,0:T(8,128)(2,1)} %refs_3_.1, bf16[32,131072]{1,0:T(8,128)(2,1)} %refs_3_.1), custom_call_target="tpu_custom_call" | custom-call | bytes 144000000 | tf_op jit(solution)/shard_map/gather_tokens/pallas_call | solution.py:186
  90.0 30.1 %collective-permute-done.2 = bf16[4,2,128,256]{3,2,1,0:T(8,128)(2,1)S(1)} collective-permute-done((bf16[4,2,128,256]{3,2,1,0:T(8,128)(2,1)S(1)}, bf16[4,2,128,256]{3,2,1,0:T(8,128)(2,1)S(1)}, u32[]{:S(2)}, u32[]{:S(2)}) %collective-permute-start.2) | collective-permute-done | bytes 524320 | tf_op jit(solution)/shard_map/ppermute | solution.py:1118
  121.7 10.1 %collective-permute-done.10 = bf16[4,2,128,256]{3,2,1,0:T(8,128)(2,1)} collective-permute-done((bf16[4,2,128,256]{3,2,1,0:T(8,128)(2,1)S(1)}, bf16[4,2,128,256]{3,2,1,0:T(8,128)(2,1)}, u32[]{:S(2)}, u32[]{:S(2)}) %collective-permute-start.10) | collective-permute-done | bytes 524320 | tf_op jit(solution)/shard_map/ppermute | solution.py:1118
  133.7 9.1 %collective-permute-done.6 = bf16[4,2,128,256]{3,2,1,0:T(8,128)(2,1)} collective-permute-done((bf16[4,2,128,256]{3,2,1,0:T(8,128)(2,1)S(1)}, bf16[4,2,128,256]{3,2,1,0:T(8,128)(2,1)}, u32[]{:S(2)}, u32[]{:S(2)}) %collective-permute-start.6) | collective-permute-done | bytes 524320 | tf_op jit(solution)/shard_map/ppermute | solution.py:1123
  149.2 13.9 %entry.1 = (f32[512,1024]{1,0:T(8,128)}, f32[512,1024]{1,0:T(8,128)}, bf16[512,1024]{1,0:T(8,128)(2,1)}, bf16[1,512,1024]{2,1,0:T(8,128)(2,1)}, bf16[2,512,1024]{2,1,0:T(8,128)(2,1)}) custom-call(s32[10]{0:T(128)} %stack.70.info_ref, bf16[1024,512]{1,0:T(8,128)(2,1)} %bitcast.16.refs_0_, bf16[1,4,4,128,256]{4,3,2,1,0:T(8,128)(2,1)} %bitcast.141, ...), custom_call_target="tpu_custom_call" | custom-call | bytes 48000000 | tf_op jit(solution)/shard_map/entry/pallas_call | solution.py:117
  165.9 4.7 collective-permute-start.16
  172.0 21.6 %attend.2 = (bf16[1,512,1024]{2,1,0:T(8,128)(2,1)}, bf16[16,2,512,512]{3,2,1,0:T(8,128)(2,1)}) custom-call(s32[10]{0:T(128)} %stack.70.info_ref, bf16[1,512,1024]{2,1,0:T(8,128)(2,1)} %get-tuple-element.147.q_ref.refs_0_, bf16[2,512,1024]{2,1,0:T(8,128)(2,1)} %get-tuple-element.148.own_ref.refs_1_, bf16[2,512,1024]{2,1,0:T(8,128)(2,1)} %copy-done.34), custom_call_target="tpu_custom_call" | custom-call | bytes 70400000 | tf_op jit(solution)/shard_map/attend/pallas_call | solution.py:507
  193.6 14.1 %collective-permute-done.16.refs_1_ = bf16[256,1024]{1,0:T(8,128)(2,1)S(1)} collective-permute-done((bf16[256,1024]{1,0:T(8,128)(2,1)S(1)}, bf16[256,1024]{1,0:T(8,128)(2,1)S(1)}, u32[]{:S(2)}, u32[]{:S(2)}) %collective-permute-start.16) | collective-permute-done | bytes 524320 | tf_op jit(solution)/shard_map/ppermute | solution.py:1075
  208.5 6.6 %source_keys.1 = (bf16[512,1024]{1,0:T(8,128)(2,1)}, bf16[2,512,1024]{2,1,0:T(8,128)(2,1)}) custom-call(s32[10]{0:T(128)} %stack.70.info_ref, bf16[256,1024]{1,0:T(8,128)(2,1)} %copy-done.44, bf16[256,1024]{1,0:T(8,128)(2,1)} %copy-done.45, bf16[8,4,5,128,256]{4,3,2,1,0:T(8,128)(2,1)} %bitcast.127), custom_call_target="tpu_custom_call" | custom-call | bytes 25600000 | tf_op jit(solution)/shard_map/source_keys/pallas_call | solution.py:117
  219.2 7.8 %middle.1 = (f32[512,1024]{1,0:T(8,128)}, bf16[512,1024]{1,0:T(8,128)(2,1)}, bf16[1,512,1024]{2,1,0:T(8,128)(2,1)}) custom-call(s32[10]{0:T(128)} %stack.70.info_ref, bf16[1,512,1024]{2,1,0:T(8,128)(2,1)} %get-tuple-element.186.refs_0_.yo_ref.refs_4_, bf16[8,4,5,128,256]{4,3,2,1,0:T(8,128)(2,1)} %bitcast.128, ...), custom_call_target="tpu_custom_call" | custom-call | bytes 28800000 | tf_op jit(solution)/shard_map/middle/pallas_call | solution.py:117
  228.3 21.6 %attend.3 = (bf16[1,512,1024]{2,1,0:T(8,128)(2,1)}, bf16[16,2,512,512]{3,2,1,0:T(8,128)(2,1)}) custom-call(s32[10]{0:T(128)} %stack.70.info_ref, bf16[1,512,1024]{2,1,0:T(8,128)(2,1)} %get-tuple-element.159.q_ref, bf16[2,512,1024]{2,1,0:T(8,128)(2,1)} %get-tuple-element.156.own_ref, bf16[2,512,1024]{2,1,0:T(8,128)(2,1)} %copy-done.33), custom_call_target="tpu_custom_call" | custom-call | bytes 70400000 | tf_op jit(solution)/shard_map/attend/pallas_call | solution.py:507
  251.7 5.4 collective-permute-start.18
  259.4 8.2 %all-gather.7.cloned.1.call-done = bf16[32768,256]{1,0:T(8,128)(2,1)} async-done(((bf16[1024,256]{1,0:T(8,128)(2,1)}), bf16[32768,256]{1,0:T(8,128)(2,1)}) %all-gather.7.cloned.1.call-update) | async-done | bytes 16777232 | tf_op jit(solution)/shard_map/all_gather | solution.py:1100
  267.6 19.4 %feed.1 = (f32[512,1024]{1,0:T(8,128)}, bf16[512,1024]{1,0:T(8,128)(2,1)}, bf16[4,512,1024]{2,1,0:T(8,128)(2,1)}, bf16[4,512,1024]{2,1,0:T(8,128)(2,1)}, f32[512,1024]{1,0:T(8,128)}) custom-call(s32[10]{0:T(128)} %stack.70.info_ref, bf16[1,512,1024]{2,1,0:T(8,128)(2,1)} %get-tuple-element.160.refs_0_.yo_ref.o_ref, bf16[8,4,5,128,256]{4,3,2,1,0:T(8,128)(2,1)} %bitcast.130, ...), custom_call_target="tpu_custom_call" | custom-call | bytes 89600000 | tf_op jit(solution)/shard_map/feed/pallas_call | solution.py:117
  289.4 23.3 %feed_back.1 = (bf16[256,1024]{1,0:T(8,128)(2,1)}, bf16[256,1024]{1,0:T(8,128)(2,1)}, bf16[512,1024]{1,0:T(8,128)(2,1)}, bf16[4,512,1024]{2,1,0:T(8,128)(2,1)}, ...) custom-call(s32[10]{0:T(128)} %stack.70.info_ref, ...), custom_call_target="tpu_custom_call" | custom-call | bytes 89600000 | tf_op jit(solution)/shard_map/feed_back/pallas_call | solution.py:117
  319.1 7.4 %weight_grad.8 = bf16[4,4,4,128,256]{4,3,2,1,0:T(8,128)(2,1)S(1)} custom-call(s32[10]{0:T(128)S(1)} %copy-done.23, bf16[512,1024]{1,0:T(8,128)(2,1)S(1)} %copy-done.21, bf16[512,1024]{1,0:T(8,128)(2,1)S(1)} %collective-permute-done.27.xp_ref, bf16[4,512,1024]{2,1,0:T(8,128)(2,1)S(1)} %copy-done.7, bf16[4,512,1024]{2,1,0:T(8,128)(2,1)} %collective-permute-done.23.yp_ref), custom_call_target="tpu_custom_call" | custom-call | bytes 35200000 | tf_op jit(solution)/shard_map/weight_grad/pallas_call | solution.py:1037
  329.3 5.4 collective-permute-start.30
  342.8 7.6 %weight_grad.10 = bf16[4,4,5,128,256]{4,3,2,1,0:T(8,128)(2,1)S(1)} custom-call(s32[10]{0:T(128)S(1)} %copy-done.23, bf16[512,1024]{1,0:T(8,128)(2,1)S(1)} %copy-done.19, bf16[512,1024]{1,0:T(8,128)(2,1)} %collective-permute-done.22.xp_ref, bf16[4,512,1024]{2,1,0:T(8,128)(2,1)S(1)} %copy-done.11, ...), custom_call_target="tpu_custom_call", output_to_operand_aliasing={{}: (5, {})} | custom-call | bytes 35200000 | tf_op jit(solution)/shard_map/weight_grad/pallas_call | solution.py:1037
  352.7 20.9 %attend_back.1 = (bf16[1,512,1024]{2,1,0:T(8,128)(2,1)}, bf16[2,512,1024]{2,1,0:T(8,128)(2,1)}, bf16[2,512,1024]{2,1,0:T(8,128)(2,1)}) custom-call(bf16[1,512,1024]{2,1,0:T(8,128)(2,1)} %get-tuple-element.159.q_ref, bf16[2,512,1024]{2,1,0:T(8,128)(2,1)} %get-tuple-element.156.own_ref, bf16[2,512,1024]{2,1,0:T(8,128)(2,1)} %copy-done.33, ...), custom_call_target="tpu_custom_call" | custom-call | bytes 67200000 | tf_op jit(solution)/shard_map/attend_back/pallas_call | solution.py:769
  373.6 6.9 %reduce-scatter.13.cloned.1.call-done = bf16[1,4,4,128,256]{4,3,2,1,0:T(8,128)(2,1)} async-done(((bf16[4,4,4,128,256]{4,3,2,1,0:T(8,128)(2,1)}), bf16[1,4,4,128,256]{4,3,2,1,0:T(8,128)(2,1)}) %reduce-scatter.13.cloned.1.call-update) | async-done | bytes 1048592
  384.0 8.8 %middle_back.1 = (f32[512,1024]{1,0:T(8,128)}, bf16[512,1024]{1,0:T(8,128)(2,1)}, bf16[1,512,1024]{2,1,0:T(8,128)(2,1)}, f32[2,1024]{1,0:T(2,128)}) custom-call(s32[10]{0:T(128)} %stack.70.info_ref, bf16[1,512,1024]{2,1,0:T(8,128)(2,1)} %get-tuple-element.225.refs_0_.yo_ref, bf16[8,4,5,128,256]{4,3,2,1,0:T(8,128)(2,1)} %bitcast.132, ...), custom_call_target="tpu_custom_call" | custom-call | bytes 32000000 | tf_op jit(solution)/shard_map/middle_back/pallas_call | solution.py:117
  394.1 7.6 %source_back.1 = (bf16[256,1024]{1,0:T(8,128)(2,1)}, bf16[256,1024]{1,0:T(8,128)(2,1)}, bf16[2,512,1024]{2,1,0:T(8,128)(2,1)}) custom-call(s32[10]{0:T(128)} %stack.70.info_ref, bf16[2,512,1024]{2,1,0:T(8,128)(2,1)} %get-tuple-element.222.refs_0_, bf16[2,512,1024]{2,1,0:T(8,128)(2,1)} %copy-done.39, bf16[8,4,5,128,256]{4,3,2,1,0:T(8,128)(2,1)} %bitcast.134), custom_call_target="tpu_custom_call" | custom-call | bytes 22400000 | tf_op jit(solution)/shard_map/source_back/pallas_call | solution.py:117
  412.9 5.7 weight_grad.13
  420.3 6.0 collective-permute-start.37
  426.3 19.4 %causal_back.1 = (bf16[1,512,1024]{2,1,0:T(8,128)(2,1)}, bf16[2,512,1024]{2,1,0:T(8,128)(2,1)}, bf16[2,512,1024]{2,1,0:T(8,128)(2,1)}) custom-call(s32[10]{0:T(128)} %stack.70.info_ref, bf16[1,512,1024]{2,1,0:T(8,128)(2,1)} %get-tuple-element.147.q_ref.refs_0_, bf16[2,512,1024]{2,1,0:T(8,128)(2,1)} %get-tuple-element.148.own_ref.refs_1_, ...), custom_call_target="tpu_custom_call" | custom-call | bytes 60800000 | tf_op jit(solution)/shard_map/causal_back/pallas_call | solution.py:117
  453.9 15.3 %exit_back.1 = (bf16[1024,512]{1,0:T(8,128)(2,1)}, bf16[2,512,1024]{2,1,0:T(8,128)(2,1)}, f32[4,1024]{1,0:T(4,128)}) custom-call(s32[10]{0:T(128)} %stack.70.info_ref, bf16[1,512,1024]{2,1,0:T(8,128)(2,1)} %get-tuple-element.241.refs_0_.yo_ref, bf16[2,512,1024]{2,1,0:T(8,128)(2,1)} %get-tuple-element.242.refs_1_, bf16[2,512,1024]{2,1,0:T(8,128)(2,1)} %copy-done.37, ...), custom_call_target="tpu_custom_call" | custom-call | bytes 48000000 | tf_op jit(solution)/shard_map/exit_back/pallas_call | solution.py:117
  492.7 4.8 weight_grad.15
  505.7 4.9 all-to-all-start.4
  515.3 38.6 %scatter_tokens.1 = (f32[32,131072]{1,0:T(8,128)}, f32[2,32,512]{2,1,0:T(8,128)}) custom-call(s32[16384]{0:T(1024)} %add_select_fusion.rows_ref, s32[32,1,512]{2,1,0:T(1,128)} %get-tuple-element.328.row_ref, s32[32,1,512]{2,1,0:T(1,128)} %and_select_fusion.1.group_ref, bf16[32,32,512]{2,1,0:T(8,128)(2,1)} %all-to-all-done.3.grad_ref), custom_call_target="tpu_custom_call" | custom-call | bytes 124800000 | tf_op jit(solution)/shard_map/scatter_tokens/pallas_call | solution.py:299
  577.6 18.3 %collective-permute-done.52 = bf16[4,128,256]{2,1,0:T(8,128)(2,1)S(1)} collective-permute-done((bf16[4,128,256]{2,1,0:T(8,128)(2,1)S(1)}, bf16[4,128,256]{2,1,0:T(8,128)(2,1)S(1)}, u32[]{:S(2)}, u32[]{:S(2)}) %collective-permute-start.52) | collective-permute-done | bytes 262176 | tf_op jit(solution)/shard_map/ppermute | solution.py:1164
  (302 shorter events, 162.0 us)
Async XLA Ops:
  7.2 200.5 %all-gather.5.cloned.1.call-start = ((), (), s32[]{:S(2)}) async-start(), calls=%async_computation.10 | async-start | bytes 10813440 | tf_op jit(solution)/shard_map/all_gather | solution.py:1100
  9.9 257.7 %all-gather.7.cloned.1.call-start = ((), (), s32[]{:S(2)}) async-start(), calls=%async_computation.11 | async-start | bytes 17301504 | tf_op jit(solution)/shard_map/all_gather | solution.py:1100
  27.8 52.1 %all-to-all-start = ((bf16[4,512,256]{2,1,0:T(8,128)(2,1)}), bf16[4,512,256]{2,1,0:T(8,128)(2,1)S(1)}, u32[]{:S(2)}, u32[]{:S(2)}) async-start(bf16[4,512,256]{2,1,0:T(8,128)(2,1)} %broadcast_in_dim.57), calls=%async_computation | async-start | bytes 2097152 | tf_op jit(solution)/shard_map/all_to_all | solution.py:1234
  79.9 68.4 %all-to-all-start.2 = ((bf16[32,32,512]{2,1,0:T(8,128)(2,1)}), bf16[32,32,512]{2,1,0:T(8,128)(2,1)}, u32[]{:S(2)}, u32[]{:S(2)}) async-start(bf16[32,32,512]{2,1,0:T(8,128)(2,1)} %gather_tokens.1), calls=%async_computation.2 | async-start | bytes 2097152 | tf_op jit(solution)/shard_map/all_to_all | solution.py:1278
  84.2 296.3 %reduce-scatter.13.cloned.1.call-start = ((), (), s32[]{:S(2)}) async-start(), calls=%async_computation.12 | async-start | bytes 5242880
  84.3 48.8 %collective-permute-start.1 = (bf16[4,4,128,256]{3,2,1,0:T(8,128)(2,1)S(1)}, bf16[4,4,128,256]{3,2,1,0:T(8,128)(2,1)S(1)}, u32[]{:S(2)}, u32[]{:S(2)}) collective-permute-start(bf16[4,4,128,256]{3,2,1,0:T(8,128)(2,1)S(1)} %bitcast.139), channel_id=1, source_target_pairs={{0,4},{4,0},{1,5},{5,1},{2,6},{6,2},{3,7},{7,3},{8,12},{12,8},{9,1... | collective-permute-start | bytes 3145736 | tf_op jit(solution)/shard_map/ppermute | solution.py:1057
  84.6 35.5 %collective-permute-start.2 = (bf16[4,2,128,256]{3,2,1,0:T(8,128)(2,1)S(1)}, bf16[4,2,128,256]{3,2,1,0:T(8,128)(2,1)S(1)}, u32[]{:S(2)}, u32[]{:S(2)}) collective-permute-start(bf16[4,2,128,256]{3,2,1,0:T(8,128)(2,1)S(1)} %get-tuple-element.344), channel_id=1, source_target_pairs={{0,8},{8,0},{16,24},{24,16},{1,9},{9,1},{17,25},{25,17},{2,10},{10... | collective-permute-start | bytes 1572872 | tf_op jit(solution)/shard_map/ppermute | solution.py:1118
  86.4 34.0 %collective-permute-start.4 = (bf16[4,2,128,256]{3,2,1,0:T(8,128)(2,1)S(1)}, bf16[4,2,128,256]{3,2,1,0:T(8,128)(2,1)S(1)}, u32[]{:S(2)}, u32[]{:S(2)}) collective-permute-start(bf16[4,2,128,256]{3,2,1,0:T(8,128)(2,1)S(1)} %get-tuple-element.344), channel_id=1, source_target_pairs={{0,16},{16,0},{8,24},{24,8},{1,17},{17,1},{9,25},{25,9},{2,18},{18... | collective-permute-start | bytes 1572872 | tf_op jit(solution)/shard_map/ppermute | solution.py:1119
  87.8 43.9 %collective-permute-start.10 = (bf16[4,2,128,256]{3,2,1,0:T(8,128)(2,1)S(1)}, bf16[4,2,128,256]{3,2,1,0:T(8,128)(2,1)}, u32[]{:S(2)}, u32[]{:S(2)}) collective-permute-start(bf16[4,2,128,256]{3,2,1,0:T(8,128)(2,1)S(1)} %get-tuple-element.343), channel_id=1, source_target_pairs={{0,16},{16,0},{8,24},{24,8},{1,17},{17,1},{9,25},{25,9},{2,18},{18... | collective-permute-start | bytes 1572872 | tf_op jit(solution)/shard_map/ppermute | solution.py:1118
  89.6 43.5 %collective-permute-start.8 = (bf16[4,2,128,256]{3,2,1,0:T(8,128)(2,1)S(1)}, bf16[4,2,128,256]{3,2,1,0:T(8,128)(2,1)}, u32[]{:S(2)}, u32[]{:S(2)}) collective-permute-start(bf16[4,2,128,256]{3,2,1,0:T(8,128)(2,1)S(1)} %get-tuple-element.343), channel_id=1, source_target_pairs={{0,8},{8,0},{16,24},{24,16},{1,9},{9,1},{17,25},{25,17},{2,10},{10... | collective-permute-start | bytes 1572872 | tf_op jit(solution)/shard_map/ppermute | solution.py:1119
  165.2 28.4 %collective-permute-start.15 = (bf16[256,1024]{1,0:T(8,128)(2,1)S(1)}, bf16[256,1024]{1,0:T(8,128)(2,1)S(1)}, u32[]{:S(2)}, u32[]{:S(2)}) collective-permute-start(bf16[256,1024]{1,0:T(8,128)(2,1)S(1)} %get-tuple-element.342), channel_id=1, source_target_pairs={{0,0},{1,4},{2,5},{3,1},{4,2},{5,6},{6,7},{7,3},{8,8},{9,12},{10,1... | collective-permute-start | bytes 1572872 | tf_op jit(solution)/shard_map/ppermute | solution.py:1075
  165.9 41.8 %collective-permute-start.16 = (bf16[256,1024]{1,0:T(8,128)(2,1)S(1)}, bf16[256,1024]{1,0:T(8,128)(2,1)S(1)}, u32[]{:S(2)}, u32[]{:S(2)}) collective-permute-start(bf16[256,1024]{1,0:T(8,128)(2,1)S(1)} %get-tuple-element.341), channel_id=1, source_target_pairs={{0,1},{1,5},{2,4},{3,0},{4,3},{5,7},{6,6},{7,2},{8,9},{9,13},{10,1... | collective-permute-start | bytes 1572872 | tf_op jit(solution)/shard_map/ppermute | solution.py:1075
  249.9 37.1 %collective-permute-start.20 = (bf16[1,512,1024]{2,1,0:T(8,128)(2,1)}, bf16[1,512,1024]{2,1,0:T(8,128)(2,1)S(1)}, u32[]{:S(2)}, u32[]{:S(2)}) collective-permute-start(bf16[1,512,1024]{2,1,0:T(8,128)(2,1)} %get-tuple-element.160.refs_0_.yo_ref.o_ref), channel_id=1, source_target_pairs={{0,4},{4,0},{1,5},{5,1},{2,6},{6,2},{3,7},{7,3},{8,12},{12,8},{9,1... | collective-permute-start | bytes 3145736 | tf_op jit(solution)/shard_map/ppermute | solution.py:1057
  249.9 38.1 %collective-permute-start.21 = (bf16[512,1024]{1,0:T(8,128)(2,1)}, bf16[512,1024]{1,0:T(8,128)(2,1)}, u32[]{:S(2)}, u32[]{:S(2)}) collective-permute-start(bf16[512,1024]{1,0:T(8,128)(2,1)} %get-tuple-element.169.xo_ref), channel_id=1, source_target_pairs={{0,4},{4,0},{1,5},{5,1},{2,6},{6,2},{3,7},{7,3},{8,12},{12,8},{9,1... | collective-permute-start | bytes 3145736 | tf_op jit(solution)/shard_map/ppermute | solution.py:1057
  251.7 35.3 %collective-permute-start.18 = (bf16[256,1024]{1,0:T(8,128)(2,1)}, bf16[256,1024]{1,0:T(8,128)(2,1)}, u32[]{:S(2)}, u32[]{:S(2)}) collective-permute-start(bf16[256,1024]{1,0:T(8,128)(2,1)} %get-tuple-element.340), channel_id=1, source_target_pairs={{0,0},{1,4},{2,5},{3,1},{4,2},{5,6},{6,7},{7,3},{8,8},{9,12},{10,1... | collective-permute-start | bytes 1572872 | tf_op jit(solution)/shard_map/ppermute | solution.py:1075
  257.1 30.0 %collective-permute-start.19 = (bf16[256,1024]{1,0:T(8,128)(2,1)}, bf16[256,1024]{1,0:T(8,128)(2,1)}, u32[]{:S(2)}, u32[]{:S(2)}) collective-permute-start(bf16[256,1024]{1,0:T(8,128)(2,1)} %get-tuple-element.339), channel_id=1, source_target_pairs={{0,1},{1,5},{2,4},{3,0},{4,3},{5,7},{6,6},{7,2},{8,9},{9,13},{10,1... | collective-permute-start | bytes 1572872 | tf_op jit(solution)/shard_map/ppermute | solution.py:1075
  288.1 24.6 %collective-permute-start.23 = (bf16[4,512,1024]{2,1,0:T(8,128)(2,1)}, bf16[4,512,1024]{2,1,0:T(8,128)(2,1)}, u32[]{:S(2)}, u32[]{:S(2)}) collective-permute-start(bf16[4,512,1024]{2,1,0:T(8,128)(2,1)} %get-tuple-element.184.yo_ref), channel_id=1, source_target_pairs={{0,4},{4,0},{1,5},{5,1},{2,6},{6,2},{3,7},{7,3},{8,12},{12,8},{9,1... | collective-permute-start | bytes 12582920 | tf_op jit(solution)/shard_map/ppermute | solution.py:1057
  288.3 24.3 %collective-permute-start.22 = (bf16[512,1024]{1,0:T(8,128)(2,1)}, bf16[512,1024]{1,0:T(8,128)(2,1)}, u32[]{:S(2)}, u32[]{:S(2)}) collective-permute-start(bf16[512,1024]{1,0:T(8,128)(2,1)} %get-tuple-element.195.xo_ref), channel_id=1, source_target_pairs={{0,4},{4,0},{1,5},{5,1},{2,6},{6,2},{3,7},{7,3},{8,12},{12,8},{9,1... | collective-permute-start | bytes 3145736 | tf_op jit(solution)/shard_map/ppermute | solution.py:1057
  288.6 24.1 %collective-permute-start.24 = (bf16[512,1024]{1,0:T(8,128)(2,1)S(1)}, bf16[512,1024]{1,0:T(8,128)(2,1)S(1)}, u32[]{:S(2)}, u32[]{:S(2)}) collective-permute-start(bf16[512,1024]{1,0:T(8,128)(2,1)S(1)} %copy-done.8), channel_id=1, source_target_pairs={{0,4},{4,0},{1,5},{5,1},{2,6},{6,2},{3,7},{7,3},{8,12},{12,8},{9,1... | collective-permute-start | bytes 3145736 | tf_op jit(solution)/shard_map/ppermute | solution.py:1057
  288.8 23.9 %collective-permute-start.25 = (bf16[1,512,1024]{2,1,0:T(8,128)(2,1)S(1)}, bf16[1,512,1024]{2,1,0:T(8,128)(2,1)}, u32[]{:S(2)}, u32[]{:S(2)}) collective-permute-start(bf16[1,512,1024]{2,1,0:T(8,128)(2,1)S(1)} %copy-done.6), channel_id=1, source_target_pairs={{0,4},{4,0},{1,5},{5,1},{2,6},{6,2},{3,7},{7,3},{8,12},{12,8},{9,1... | collective-permute-start | bytes 3145736 | tf_op jit(solution)/shard_map/ppermute | solution.py:1057
  289.1 23.6 %collective-permute-start.26 = (bf16[512,1024]{1,0:T(8,128)(2,1)}, bf16[512,1024]{1,0:T(8,128)(2,1)}, u32[]{:S(2)}, u32[]{:S(2)}) collective-permute-start(bf16[512,1024]{1,0:T(8,128)(2,1)} %get-tuple-element.229.xo_ref), channel_id=1, source_target_pairs={{0,4},{4,0},{1,5},{5,1},{2,6},{6,2},{3,7},{7,3},{8,12},{12,8},{9,1... | collective-permute-start | bytes 3145736 | tf_op jit(solution)/shard_map/ppermute | solution.py:1057
  328.5 117.2 %reduce-scatter.15.cloned.1.call-start = ((), (), s32[]{:S(2)}) async-start(), calls=%async_computation.13 | async-start | bytes 6553600
  329.3 23.4 %collective-permute-start.30 = (bf16[256,1024]{1,0:T(8,128)(2,1)}, bf16[256,1024]{1,0:T(8,128)(2,1)}, u32[]{:S(2)}, u32[]{:S(2)}) collective-permute-start(bf16[256,1024]{1,0:T(8,128)(2,1)} %get-tuple-element.201), channel_id=1, source_target_pairs={{0,0},{4,1},{5,2},{1,3},{2,4},{6,5},{7,6},{3,7},{8,8},{12,9},{13,1... | collective-permute-start | bytes 1572872 | tf_op jit(solution)/shard_map/ppermute | solution.py:1082
  382.8 118.3 %reduce-scatter.17.cloned.1.call-start = ((), (), s32[]{:S(2)}) async-start(), calls=%async_computation.14 | async-start | bytes 3932160
  418.6 29.6 %collective-permute-start.36 = (bf16[256,1024]{1,0:T(8,128)(2,1)}, bf16[256,1024]{1,0:T(8,128)(2,1)S(1)}, u32[]{:S(2)}, u32[]{:S(2)}) collective-permute-start(bf16[256,1024]{1,0:T(8,128)(2,1)} %get-tuple-element.237), channel_id=1, source_target_pairs={{0,0},{4,1},{5,2},{1,3},{2,4},{6,5},{7,6},{3,7},{8,8},{12,9},{13,1... | collective-permute-start | bytes 1572872 | tf_op jit(solution)/shard_map/ppermute | solution.py:1082
  420.3 27.9 %collective-permute-start.37 = (bf16[256,1024]{1,0:T(8,128)(2,1)}, bf16[256,1024]{1,0:T(8,128)(2,1)S(1)}, u32[]{:S(2)}, u32[]{:S(2)}) collective-permute-start(bf16[256,1024]{1,0:T(8,128)(2,1)} %get-tuple-element.238), channel_id=1, source_target_pairs={{1,0},{5,1},{4,2},{0,3},{3,4},{7,5},{6,6},{2,7},{9,8},{13,9},{12,1... | collective-permute-start | bytes 1572872 | tf_op jit(solution)/shard_map/ppermute | solution.py:1082
  469.6 33.1 %all-to-all-start.3 = ((bf16[32,32,512]{2,1,0:T(8,128)(2,1)}), bf16[32,32,512]{2,1,0:T(8,128)(2,1)}, u32[]{:S(2)}, u32[]{:S(2)}) async-start(bf16[32,32,512]{2,1,0:T(8,128)(2,1)} %bitcast.178), calls=%async_computation.3 | async-start | bytes 2097152 | tf_op jit(solution)/shard_map/all_to_all | solution.py:1343
  474.1 123.4 %reduce-scatter.11.cloned.1.call-start = ((), (), s32[]{:S(2)}) async-start(), calls=%async_computation.9 | async-start | bytes 3932160 | tf_op jit(solution)/shard_map/reduce_scatter | solution.py:1152
  505.7 52.8 %all-to-all-start.4 = ((bf16[4,4,4,128,256]{4,3,2,1,0:T(8,128)(2,1)}), bf16[4,4,4,128,256]{4,3,2,1,0:T(8,128)(2,1)}, u32[]{:S(2)}, u32[]{:S(2)}) async-start(bf16[4,4,4,128,256]{4,3,2,1,0:T(8,128)(2,1)} %copy-done.2), calls=%async_computation.4 | async-start | bytes 8388608 | tf_op jit(solution)/shard_map/all_to_all | solution.py:1353
  510.6 43.3 %collective-permute-start.47 = (f32[10,1024]{1,0:T(8,128)S(1)}, f32[10,1024]{1,0:T(8,128)S(1)}, u32[]{:S(2)}, u32[]{:S(2)}) collective-permute-start(f32[10,1024]{1,0:T(8,128)S(1)} %add_add_fusion.1), channel_id=1, source_target_pairs={{0,3},{1,0},{2,1},{3,2},{4,7},{5,4},{6,5},{7,6},{8,11},{9,8},{10,9... | collective-permute-start | bytes 122888 | tf_op jit(solution)/shard_map/ppermute | solution.py:1174
  513.8 40.1 %collective-permute-start.46 = (f32[10,1024]{1,0:T(8,128)S(1)}, f32[10,1024]{1,0:T(8,128)S(1)}, u32[]{:S(2)}, u32[]{:S(2)}) collective-permute-start(f32[10,1024]{1,0:T(8,128)S(1)} %add_add_fusion.1), channel_id=1, source_target_pairs={{0,2},{1,3},{2,0},{3,1},{4,6},{5,7},{6,4},{7,5},{8,10},{9,11},{10,... | collective-permute-start | bytes 122888 | tf_op jit(solution)/shard_map/ppermute | solution.py:1174
  513.8 40.1 %collective-permute-start.45 = (f32[10,1024]{1,0:T(8,128)S(1)}, f32[10,1024]{1,0:T(8,128)S(1)}, u32[]{:S(2)}, u32[]{:S(2)}) collective-permute-start(f32[10,1024]{1,0:T(8,128)S(1)} %add_add_fusion.1), channel_id=1, source_target_pairs={{0,1},{1,2},{2,3},{3,0},{4,5},{5,6},{6,7},{7,4},{8,9},{9,10},{10,1... | collective-permute-start | bytes 122888 | tf_op jit(solution)/shard_map/ppermute | solution.py:1174
  (88 other events, 787.7 us)
Sparse Core Ops, SparseCore 0:
  11.4 121.3 all-gather.4
  135.9 131.6 all-gather.6
  328.6 51.8 reduce-scatter.12
  383.6 61.4 reduce-scatter.14
  448.3 52.7 reduce-scatter.16
  505.8 66.3 reduce-scatter.10
